TPU v7x, 256 devices: a whole 4x4x8 slice. The times are simulated.
256 devices in a mesh: section: 2 (over core), req: 32 (over z, x), head: 4 (over y).
Axes of the slice: x: 4, y: 4, z: 8, core: 2. Of those that a mesh axis runs over, the one named last changes fastest.
Arguments:
- tokens: bfloat16 [256, 1792], P('req', 'head'), may hold values from -6 to 6
- norm_gain: float32 [2, 1792], P('section'), may hold values from 0.1 to 1.9
- feature_w: bfloat16 [1792, 512], P(None, 'head'), may hold values from -0.125 to 0.125
- query_key_w: bfloat16 [1792, 3584], P(None, 'head'), may hold values from -0.125 to 0.125
- value_w: bfloat16 [2, 1792, 1792], P('section', None, 'head'), may hold values from -0.125 to 0.125
- out_w: bfloat16 [2, 1792, 1792], P('section', 'head'), may hold values from -0.125 to 0.125
- conv_w: float32 [3, 1792], P(None, 'head'), may hold values from -4 to 4
- conv_state: bfloat16 [256, 2, 1792], P('req', None, 'head'), may hold values from -6 to 6
- lin_state: bfloat16 [256, 16, 273, 112], P('req', 'head'), may hold values from -6 to 6
- lin_norm: float32 [256, 16, 273], P('req', 'head'), may hold values from -6 to 6, as said below
- own_pages: bfloat16 [512, 2, 128, 1792], P('req', None, None, 'head'), may hold values from -110 to 110
- prompt_pages: bfloat16 [32, 2, 128, 1792], P('req', None, None, 'head'), may hold values from -110 to 110
- page_table: int32 [256, 256], P('req'), may hold values from 0 to 543, as said below
- lengths: int32 [256], P('req'), may hold values from 129 to 32768, as said below
Outputs:
- hidden_states: bfloat16 [2, 256, 1792], P('section', 'req', 'head')
Inputs may be any that keep to these rules, and one draw needn't show every extreme that they name: `page_table`: entry 0 of a request's row is its prompt group, whose page is prompt_pages row (entry 0). Entries of logical pages 1 and above are 32 plus a row of own_pages within the block of 16 rows that matches the request's block of 8 rows; two consecutive logical pages of a request are different pages. `lengths`: the new token sits at position length - 1; positions below 128 are the group's prompt. Some request has length 32768. `lin_norm`: the inner product with the feature vector phi(u) of any 16-vector u is at least one half.
All inputs are finite; a program needn't handle non-finite values.
Results may differ from a plain program's by a relative error of at most 0.024.
Values may be sent and summed in bfloat16 or wider, within the bound.
No kernel may reach another device: no remote copies, remote signals or barrier semaphores. Data moves between devices by JAX's collectives and lax.ppermute only.
A program may use at most 128 MiB of HBM per device.

v0:
```python
import jax
import jax.numpy as jnp
from jax import lax
from jax.sharding import PartitionSpec as P

HD = 112
FEAT = 16
WINDOW = 64
PAGE = 128
MB = 2


EPSILON = 1e-06
MASKED = -1e30


def from_behind(value, axis, steps):
    count = lax.axis_size(axis)
    initial, last = (max(0, -steps), min(count, count - steps))
    return lax.ppermute(value, axis, [(source, source + steps) for source in range(initial, last)])


def rms_norm(token_rows, gain_row):
    values = token_rows.astype(jnp.float32)
    factor = lax.rsqrt(jnp.mean(values * values, axis=-1, keepdims=True) + EPSILON)
    return (values * factor * gain_row).astype(jnp.bfloat16)


def taylor(raw_feats):
    scaled = raw_feats * FEAT ** (-0.25)
    outer = scaled[..., :, None] * scaled[..., None, :]
    flat = outer.reshape(scaled.shape[:-1] + (FEAT * FEAT,)) * 0.5**0.5
    constant = jnp.ones(scaled.shape[:-1] + (1,), jnp.float32)
    return jnp.concatenate([constant, scaled, flat], axis=-1)


def linear_local(normed, feature_w, value_w, out_w, conv_w, conv_part, state_part, norm_part):
    batch_rows = normed.shape[0]
    heads = state_part.shape[1]
    features = jnp.dot(normed, feature_w, preferred_element_type=jnp.float32).reshape(
        batch_rows, heads, 2, FEAT
    )
    query_feats = taylor(features[:, :, 0])
    key_feats = taylor(features[:, :, 1])
    fresh_values = jnp.dot(normed, value_w, preferred_element_type=jnp.float32)
    older_values = conv_part.astype(jnp.float32)
    mixed_values = (
        conv_w[0] * older_values[:, 0] + conv_w[1] * older_values[:, 1] + conv_w[2] * fresh_values
    )
    mixed_values = mixed_values.reshape(batch_rows, heads, HD)
    from_state = jnp.einsum(
        "rhf,rhfd->rhd",
        query_feats.astype(jnp.bfloat16),
        state_part,
        preferred_element_type=jnp.float32,
    )
    intersection = jnp.sum(query_feats * key_feats, axis=-1)
    denominator = jnp.sum(query_feats * norm_part, axis=-1) + intersection
    attended = (
        (from_state + intersection[..., None] * mixed_values) / denominator[..., None]
    ).astype(jnp.bfloat16)
    return jnp.dot(
        attended.reshape(batch_rows, heads * HD), out_w, preferred_element_type=jnp.float32
    )


def window_local(
    normed,
    query_key_w,
    value_w,
    out_w,
    own_pages,
    prompt_source,
    table_part,
    length_part,
    groups,
    req_index,
):
    batch_rows = normed.shape[0]
    heads = query_key_w.shape[1] // (2 * HD)
    query_key = (
        jnp.dot(normed, query_key_w, preferred_element_type=jnp.float32)
        .reshape(batch_rows, heads, 2, HD)
        .astype(jnp.bfloat16)
    )
    queries = query_key[:, :, 0]
    key_new = query_key[:, :, 1]
    value_new = (
        jnp.dot(normed, value_w, preferred_element_type=jnp.float32)
        .reshape(batch_rows, heads, HD)
        .astype(jnp.bfloat16)
    )
    window_start = length_part - WINDOW
    first_page = jnp.maximum(window_start // PAGE, 1)
    last_page = jnp.maximum((length_part - 2) // PAGE, 1)
    page_picks = jnp.stack([first_page, last_page], axis=1)
    own_ids = (
        jnp.take_along_axis(table_part, page_picks, axis=1)
        - groups
        - req_index * own_pages.shape[0]
    )
    own_ids = jnp.clip(own_ids, 0, own_pages.shape[0] - 1)
    own_rows = jnp.take(own_pages, own_ids, axis=0)
    own_keys = own_rows[:, :, 0].reshape(batch_rows, 2 * PAGE, heads, HD)
    own_values = own_rows[:, :, 1].reshape(batch_rows, 2 * PAGE, heads, HD)
    offsets = jnp.arange(PAGE, dtype=jnp.int32)
    own_positions = (page_picks[:, :, None] * PAGE + offsets[None, None, :]).reshape(
        batch_rows, 2 * PAGE
    )
    second = jnp.concatenate(
        [
            jnp.ones((batch_rows, PAGE), bool),
            jnp.broadcast_to((last_page != first_page)[:, None], (batch_rows, PAGE)),
        ],
        axis=1,
    )
    own_usable = (
        (own_positions >= window_start[:, None])
        & (own_positions <= (length_part - 2)[:, None])
        & second
    )
    prompt_len = prompt_source.shape[2]
    prompt_offsets = jnp.arange(prompt_len, dtype=jnp.int32)
    prompt_usable = prompt_offsets[None, :] >= window_start[:, None]
    score_scale = HD ** (-0.5)
    own_scores = (
        jnp.einsum("rhd,rthd->rht", queries, own_keys, preferred_element_type=jnp.float32)
        * score_scale
    )
    new_score = (
        jnp.sum(queries.astype(jnp.float32) * key_new.astype(jnp.float32), axis=-1) * score_scale
    )
    group_ids = jnp.clip(table_part[:, 0], 0, prompt_source.shape[0] - 1)
    prompt_rows = jnp.take(prompt_source, group_ids, axis=0)
    prompt_keys = prompt_rows[:, 0].reshape(batch_rows, prompt_len, heads, HD)
    prompt_scores = (
        jnp.einsum("rhd,rthd->rht", queries, prompt_keys, preferred_element_type=jnp.float32)
        * score_scale
    )
    prompt_scores = jnp.where(prompt_usable[:, None, :], prompt_scores, MASKED)
    own_scores = jnp.where(own_usable[:, None, :], own_scores, MASKED)
    highest = jnp.maximum(
        jnp.maximum(jnp.max(prompt_scores, axis=-1), jnp.max(own_scores, axis=-1)), new_score
    )
    prompt_exp = jnp.exp(prompt_scores - highest[..., None])
    own_exp = jnp.exp(own_scores - highest[..., None])
    new_exp = jnp.exp(new_score - highest)
    exp_total = jnp.sum(prompt_exp, axis=-1) + jnp.sum(own_exp, axis=-1) + new_exp
    prompt_weights = (prompt_exp / exp_total[..., None]).astype(jnp.bfloat16)
    own_weights = (own_exp / exp_total[..., None]).astype(jnp.bfloat16)
    new_weight = (new_exp / exp_total).astype(jnp.bfloat16)
    own_part = jnp.einsum(
        "rht,rthd->rhd", own_weights, own_values, preferred_element_type=jnp.float32
    )
    own_part = own_part + new_weight.astype(jnp.float32)[..., None] * value_new.astype(jnp.float32)
    prompt_values = prompt_rows[:, 1].reshape(batch_rows, prompt_len, heads, HD)
    prompt_part = jnp.einsum(
        "rht,rthd->rhd", prompt_weights, prompt_values, preferred_element_type=jnp.float32
    )
    attended = (prompt_part + own_part).astype(jnp.bfloat16).reshape(batch_rows, heads * HD)
    return jnp.dot(attended, out_w, preferred_element_type=jnp.float32)


def body(
    tokens,
    norm_gain,
    feature_w,
    query_key_w,
    value_w,
    out_w,
    conv_w,
    conv_state,
    lin_state,
    lin_norm,
    own_pages,
    prompt_pages,
    page_table,
    lengths,
):
    section_index = lax.axis_index("section")
    req_index = lax.axis_index("req")
    groups = lax.axis_size("req")
    slab_rows = tokens.shape[0] // MB
    layer_gain = norm_gain[0]
    prompt_source = lax.all_gather(prompt_pages, "req", axis=0, tiled=True)
    incoming = jnp.zeros_like(tokens[:slab_rows])
    results = []
    for moment in range(MB + 1):
        early_batch = min(moment, MB - 1)
        late_batch = max(moment - 1, 0)
        early_lo = early_batch * slab_rows
        early_hi = early_lo + slab_rows
        late_lo = late_batch * slab_rows
        late_hi = late_lo + slab_rows
        rows_in = jnp.where(section_index == 0, tokens[early_lo:early_hi], incoming)
        whole = lax.all_gather(rows_in, "head", axis=1, tiled=True)
        normed = rms_norm(whole, layer_gain)

        def run_linear(normed_rows):
            return linear_local(
                normed_rows,
                feature_w,
                value_w[0],
                out_w[0],
                conv_w,
                conv_state[early_lo:early_hi],
                lin_state[early_lo:early_hi],
                lin_norm[early_lo:early_hi],
            )

        def run_window(normed_rows):
            return window_local(
                normed_rows,
                query_key_w,
                value_w[0],
                out_w[0],
                own_pages,
                prompt_source,
                page_table[late_lo:late_hi],
                lengths[late_lo:late_hi],
                groups,
                req_index,
            )

        update = lax.cond(section_index == 0, run_linear, run_window, normed)
        summed = lax.psum_scatter(update, "head", scatter_dimension=1, tiled=True)
        output = (rows_in.astype(jnp.float32) + summed).astype(jnp.bfloat16)
        results.append(output)
        if moment < MB:
            incoming = from_behind(output, "section", 1)
    pieces = [
        jnp.where(section_index == 0, results[batch_index], results[batch_index + 1])
        for batch_index in range(MB)
    ]
    return jnp.concatenate(pieces, axis=0)[None]


def solution(mesh):
    placed = (
        P("req", "head"),
        P("section", None),
        P(None, "head"),
        P(None, "head"),
        P("section", None, "head"),
        P("section", "head", None),
        P(None, "head"),
        P("req", None, "head"),
        P("req", "head", None, None),
        P("req", "head", None),
        P("req", None, None, "head"),
        P("req", None, None, "head"),
        P("req", None),
        P("req"),
    )
    return jax.shard_map(
        body, mesh=mesh, in_specs=placed, out_specs=P("section", "req", "head"), check_vma=False
    )
```

profile of v0, /device:TPU:1, one launch (start us, length us, event | category | flops | bytes accessed | tf_op | source)
XLA Modules:
  0.0 342.1 jit_solution(4560962319637339431)
XLA Ops:
  8.0 10.4 %all-gather = bf16[4,448,4]{1,2,0:T(4,128)(2,1)S(1)} all-gather(bf16[1,448,4]{1,2,0:T(4,128)(2,1)S(1)} %fusion.145), channel_id=1, replica_groups=mesh['section'=2,'req'=32,'head'=4] {'head'}, dimensions={0}, use_global_device_ids=true | all-gather | bytes 17920 | tf_op jit(solution)/shard_map/all_gather | solution.py:196
  19.5 87.2 %all-gather.5.cloned.1.call-done = bf16[32,2,128,448]{2,3,1,0:T(8,128)(2,1)} async-done(((bf16[1,2,128,448]{2,3,1,0:T(8,128)(2,1)}), bf16[32,2,128,448]{2,3,1,0:T(8,128)(2,1)}) %all-gather.5.cloned.1.call-update) | async-done | bytes 7340048 | tf_op jit(solution)/shard_map/all_gather | solution.py:185
  106.6 39.0 %conditional.3 = (f32[4,1792]{1,0:T(4,128)S(1)}) conditional(s32[]{:T(128)} %convert_element_type.201, (s32[8]{0:T(128)}, bf16[4,1792]{1,0:T(4,128)(2,1)S(1)}, bf16[1792,896]{1,0:T(8,128)(2,1)}, s32[8,256]{1,0:T(8,128)}, bf16[32,2,128,448]{2,3,1,0:T(8,128)(2,1)}, /*index=5*/s32[]{:T(128)}, bf16[16,2,128,448]{2,3,1,0:T(8,128)(2,1)}, ...), branch_computations={%region_1.10_spmd, %region_7.13_spmd} | conditional | flops 29922272 | bytes 66392968 | solution.py:225
  109.4 6.2 %copy.280 = bf16[16,2,128,448]{3,2,1,0:T(8,128)(2,1)} copy(bf16[16,2,128,448]{2,3,1,0:T(8,128)(2,1)} %get-tuple-element.380) | data formatting | bytes 7340032 | tf_op jit(solution)/shard_map
  115.6 2.9 gather_fusion.2
  118.4 3.8 %copy.254 = bf16[4,2,2,128,448]{3,1,4,0,2:T(2,128)(2,1)} copy(bf16[4,2,2,128,448]{4,3,2,1,0:T(8,128)(2,1)S(1)} %bitcast.405) | data formatting | bytes 3670016 | tf_op jit(solution)/shard_map/cond/branch_0_fun/jit(_take)/gather | solution.py:103
  122.3 3.1 broadcast_select_fusion
  125.5 2.6 fusion.163
  128.1 3.4 %squeeze.61 = bf16[4,256,4,112]{1,3,2,0:T(8,128)(2,1)} reshape(bf16[4,2,1,128,448]{3,1,4,0,2:T(2,128)(2,1)} %get-tuple-element.481) | data formatting | bytes 1835008 | tf_op jit(solution)/shard_map/cond/branch_0_fun/reshape;cond/branch_0_fun/squeeze | solution.py:104
  132.1 1.4 fusion.70
  134.0 3.8 %gather_fusion = bf16[4,2,128,448]{2,3,1,0:T(8,128)(2,1)S(1)} fusion(bf16[32,2,128,448]{2,3,1,0:T(8,128)(2,1)} %get-tuple-element.120, s32[1024]{0:T(1024)S(1)} %pad_clamp_fusion.1), kind=kCustom, calls=%fused_computation.clone | custom fusion | bytes 1835024 | tf_op jit(solution)/shard_map/cond/branch_0_fun/jit(_take)/gather | solution.py:134
  139.5 3.6 %squeeze.67 = bf16[4,256,4,112]{1,3,2,0:T(8,128)(2,1)} reshape(bf16[4,2,1,128,448]{3,1,4,0,2:T(2,128)(2,1)} %get-tuple-element.482) | data formatting | bytes 1835008 | tf_op jit(solution)/shard_map/cond/branch_0_fun/reshape;cond/branch_0_fun/squeeze | solution.py:105
  143.1 1.5 fusion.62
  145.7 1.3 copy.323
  147.1 20.7 %reduce-scatter.10.cloned.1.call-done = f32[448,4]{1,0:T(8,128)} async-done(((f32[1792,4]{1,0:T(8,128)}), f32[448,4]{1,0:T(8,128)}) %reduce-scatter.10.cloned.1.call-update) | async-done | bytes 7184
  168.8 1.3 collective-permute-start
  170.1 2.9 collective-permute-done
  173.1 9.2 %all-gather.1 = bf16[4,448,4]{1,2,0:T(4,128)(2,1)S(1)} all-gather(bf16[1,448,4]{1,2,0:T(4,128)(2,1)S(1)} %fusion.147), channel_id=1, replica_groups=mesh['section'=2,'req'=32,'head'=4] {'head'}, dimensions={0}, use_global_device_ids=true | all-gather | bytes 17920 | tf_op jit(solution)/shard_map/all_gather | solution.py:196
  182.7 40.0 %conditional.4 = (f32[4,1792]{1,0:T(4,128)S(1)}) conditional(s32[]{:T(128)} %convert_element_type.201, (s32[8]{0:T(128)S(1)}, bf16[4,1792]{1,0:T(4,128)(2,1)S(1)}, bf16[1792,896]{1,0:T(8,128)(2,1)}, s32[8,256]{1,0:T(8,128)S(1)}, bf16[32,2,128,448]{2,3,1,0:T(8,128)(2,1)}, /*index=5*/s32[]{:T(128)}, bf16[16,2,128,448]{2,3,1,0:T(8,128)(2,1)}, ...), branch_computations={%region_12.21_spmd, %region_18.24_spmd} | conditional | flops 29922272 | bytes 50795216 | solution.py:225
  184.1 6.2 %copy.286 = bf16[16,2,128,448]{3,2,1,0:T(8,128)(2,1)} copy(bf16[16,2,128,448]{2,3,1,0:T(8,128)(2,1)} %get-tuple-element.397) | data formatting | bytes 7340032 | tf_op jit(solution)/shard_map
  190.3 4.3 %gather_fusion.5 = bf16[8,2,128,448]{3,2,1,0:T(8,128)(2,1)} fusion(bf16[16,2,128,448]{3,2,1,0:T(8,128)(2,1)} %copy.286, s32[1024]{0:T(1024)S(1)} %pad_clamp_fusion.2), kind=kCustom, calls=%fused_computation.7.clone | custom fusion | bytes 3670048 | tf_op jit(solution)/shard_map/cond/branch_0_fun/jit(_take)/gather | solution.py:103
  194.6 6.1 %copy.264 = bf16[4,2,2,128,448]{3,1,4,0,2:T(2,128)(2,1)} copy(bf16[4,2,2,128,448]{4,3,2,1,0:T(8,128)(2,1)} %bitcast.406) | data formatting | bytes 3670016 | tf_op jit(solution)/shard_map/cond/branch_0_fun/jit(_take)/gather | solution.py:103
  200.8 3.1 broadcast_select_fusion.2
  204.0 2.2 fusion.166
  206.2 1.6 squeeze.91
  207.7 2.5 convolution_convert_fusion.2
  211.1 3.8 %gather_fusion.3 = bf16[4,2,128,448]{2,3,1,0:T(8,128)(2,1)S(1)} fusion(bf16[32,2,128,448]{2,3,1,0:T(8,128)(2,1)} %get-tuple-element.139, s32[1024]{0:T(1024)S(1)} %pad_clamp_fusion.3), kind=kCustom, calls=%fused_computation.3.clone | custom fusion | bytes 1835024 | tf_op jit(solution)/shard_map/cond/branch_0_fun/jit(_take)/gather | solution.py:134
  216.5 3.6 %squeeze.93 = bf16[4,256,4,112]{1,3,2,0:T(8,128)(2,1)} reshape(bf16[4,2,1,128,448]{3,1,4,0,2:T(2,128)(2,1)} %get-tuple-element.490) | data formatting | bytes 1835008 | tf_op jit(solution)/shard_map/cond/branch_0_fun/reshape;cond/branch_0_fun/squeeze | solution.py:105
  220.1 1.5 fusion.91
  222.7 1.3 copy.325
  224.1 23.4 %reduce-scatter.12.cloned.1.call-done = f32[448,4]{1,0:T(8,128)} async-done(((f32[1792,4]{1,0:T(8,128)}), f32[448,4]{1,0:T(8,128)}) %reduce-scatter.12.cloned.1.call-update) | async-done | bytes 7184
  249.1 1.3 collective-permute-start.1
  250.4 2.9 collective-permute-done.1
  253.9 9.0 %all-gather.2 = bf16[4,448,4]{1,2,0:T(4,128)(2,1)S(1)} all-gather(bf16[1,448,4]{1,2,0:T(4,128)(2,1)S(1)} %fusion.146), channel_id=1, replica_groups=mesh['section'=2,'req'=32,'head'=4] {'head'}, dimensions={0}, use_global_device_ids=true | all-gather | bytes 17920 | tf_op jit(solution)/shard_map/all_gather | solution.py:196
  263.3 46.0 %conditional.5 = (f32[4,1792]{1,0:T(4,128)S(1)}) conditional(s32[]{:T(128)} %convert_element_type.201, (s32[8]{0:T(128)S(1)}, bf16[4,1792]{1,0:T(4,128)(2,1)S(1)}, bf16[1792,896]{1,0:T(8,128)(2,1)}, s32[8,256]{1,0:T(8,128)S(1)}, bf16[32,2,128,448]{2,3,1,0:T(8,128)(2,1)}, /*index=5*/s32[]{:T(128)}, bf16[16,2,128,448]{2,3,1,0:T(8,128)(2,1)}, ...), branch_computations={%region_23.32_spmd, %region_29.35_spmd} | conditional | flops 29922272 | bytes 40711120 | solution.py:225
  265.3 6.2 %copy.292 = bf16[16,2,128,448]{3,2,1,0:T(8,128)(2,1)} copy(bf16[16,2,128,448]{2,3,1,0:T(8,128)(2,1)} %get-tuple-element.414) | data formatting | bytes 7340032 | tf_op jit(solution)/shard_map
  271.5 4.3 %gather_fusion.8 = bf16[8,2,128,448]{3,2,1,0:T(8,128)(2,1)} fusion(bf16[16,2,128,448]{3,2,1,0:T(8,128)(2,1)} %copy.292, s32[1024]{0:T(1024)S(1)} %pad_clamp_fusion.4), kind=kCustom, calls=%fused_computation.8.clone | custom fusion | bytes 3670048 | tf_op jit(solution)/shard_map/cond/branch_0_fun/jit(_take)/gather | solution.py:103
  275.7 6.1 %copy.274 = bf16[4,2,2,128,448]{3,1,4,0,2:T(2,128)(2,1)} copy(bf16[4,2,2,128,448]{4,3,2,1,0:T(8,128)(2,1)} %bitcast.407) | data formatting | bytes 3670016 | tf_op jit(solution)/shard_map/cond/branch_0_fun/jit(_take)/gather | solution.py:103
  282.0 3.1 broadcast_select_fusion.4
  285.1 2.6 fusion.169
  287.7 3.4 %squeeze.102 = bf16[4,256,4,112]{1,3,2,0:T(8,128)(2,1)} reshape(bf16[4,2,1,128,448]{3,1,4,0,2:T(2,128)(2,1)} %get-tuple-element.497) | data formatting | bytes 1835008 | tf_op jit(solution)/shard_map/cond/branch_0_fun/reshape;cond/branch_0_fun/squeeze | solution.py:104
  291.1 2.4 convolution_convert_fusion.4
  293.7 1.4 fusion.128
  295.7 4.7 %gather_fusion.6 = bf16[4,2,128,448]{2,3,1,0:T(8,128)(2,1)} fusion(bf16[32,2,128,448]{2,3,1,0:T(8,128)(2,1)} %get-tuple-element.156, s32[1024]{0:T(1024)S(1)} %pad_clamp_fusion.5), kind=kCustom, calls=%fused_computation.4.clone | custom fusion | bytes 1835024 | tf_op jit(solution)/shard_map/cond/branch_0_fun/jit(_take)/gather | solution.py:134
  300.5 1.3 broadcast_select_fusion.5
  303.2 3.5 %squeeze.104 = bf16[4,256,4,112]{1,3,2,0:T(8,128)(2,1)} reshape(bf16[4,2,1,128,448]{3,1,4,0,2:T(2,128)(2,1)} %get-tuple-element.498) | data formatting | bytes 1835008 | tf_op jit(solution)/shard_map/cond/branch_0_fun/reshape;cond/branch_0_fun/squeeze | solution.py:105
  306.7 1.5 fusion.120
  310.6 23.2 %reduce-scatter.14.cloned.1.call-done = f32[448,4]{1,0:T(8,128)} async-done(((f32[1792,4]{1,0:T(8,128)}), f32[448,4]{1,0:T(8,128)}) %reduce-scatter.14.cloned.1.call-update) | async-done | bytes 7184
  (213 shorter events, 26.3 us)
Async XLA Ops:
  6.5 100.1 %all-gather.5.cloned.1.call-start = ((), (), s32[]{:S(2)}) async-start(), calls=%async_computation.3 | async-start | bytes 7569408 | tf_op jit(solution)/shard_map/all_gather | solution.py:185
  7.3 160.5 %reduce-scatter.10.cloned.1.call-start = ((), (), s32[]{:S(2)}) async-start(), calls=%async_computation.4 | async-start | bytes 1146880
  125.5 6.0 %copy-start.8 = (bf16[1792,896]{1,0:T(8,128)(2,1)S(1)}, bf16[1792,896]{1,0:T(8,128)(2,1)}, u32[]{:S(2)}) copy-start(bf16[1792,896]{1,0:T(8,128)(2,1)} %get-tuple-element.110) | copy-start | bytes 9633796 | tf_op jit(solution)/shard_map/cond
  131.5 2.3 copy-start.25
  138.1 6.6 %copy-start.1 = (bf16[1,1792,448]{1,2,0:T(8,128)(2,1)S(1)}, bf16[1,1792,448]{1,2,0:T(8,128)(2,1)}, u32[]{:S(2)}) copy-start(bf16[1,1792,448]{1,2,0:T(8,128)(2,1)} %get-tuple-element.126) | copy-start | bytes 4816900 | tf_op jit(solution)/shard_map/cond
  139.5 5.9 %copy-start.4 = (bf16[1,448,1792]{2,1,0:T(8,128)(2,1)S(1)}, bf16[1,448,1792]{2,1,0:T(8,128)(2,1)}, u32[]{:S(2)}) copy-start(bf16[1,448,1792]{2,1,0:T(8,128)(2,1)} %get-tuple-element.127) | copy-start | bytes 4816900 | tf_op jit(solution)/shard_map/cond
  145.7 23.1 %copy-start.14 = (bf16[8,448]{1,0:T(8,128)(2,1)S(1)}, bf16[8,448]{1,0:T(8,128)(2,1)}, u32[]{:S(2)}) copy-start(bf16[8,448]{1,0:T(8,128)(2,1)} %param.26) | copy-start | bytes 21508
  145.7 37.0 %copy-start = (bf16[1,1792,448]{1,2,0:T(8,128)(2,1)S(1)}, bf16[1,1792,448]{1,2,0:T(8,128)(2,1)}, u32[]{:S(2)}) copy-start(bf16[1,1792,448]{1,2,0:T(8,128)(2,1)} %param.30) | copy-start | bytes 4816900
  145.7 37.0 %copy-start.10 = (bf16[8,2,448]{2,1,0:T(2,128)(2,1)S(1)}, bf16[8,2,448]{2,1,0:T(2,128)(2,1)}, u32[]{:S(2)}) copy-start(bf16[8,2,448]{2,1,0:T(2,128)(2,1)} %param.33) | copy-start | bytes 43012
  145.7 37.0 %copy-start.12 = (f32[8,4,273]{2,1,0:T(4,128)S(1)}, f32[8,4,273]{2,1,0:T(4,128)}, u32[]{:S(2)}) copy-start(f32[8,4,273]{2,1,0:T(4,128)} %param.35) | copy-start | bytes 104836
  145.7 37.0 %copy-start.13 = (s32[8,256]{1,0:T(8,128)S(1)}, s32[8,256]{1,0:T(8,128)}, u32[]{:S(2)}) copy-start(s32[8,256]{1,0:T(8,128)} %param.38) | copy-start | bytes 24580
  145.7 37.0 %copy-start.16 = (f32[3,448]{1,0:T(4,128)S(1)}, f32[3,448]{1,0:T(4,128)}, u32[]{:S(2)}) copy-start(f32[3,448]{1,0:T(4,128)} %param.32) | copy-start | bytes 16132
  145.7 37.0 %copy-start.24 = (s32[8]{0:T(128)S(1)}, s32[8]{0:T(128)}, u32[]{:S(2)}) copy-start(s32[8]{0:T(128)} %param.39) | copy-start | bytes 100
  147.0 100.4 %reduce-scatter.12.cloned.1.call-start = ((), (), s32[]{:S(2)}) async-start(), calls=%async_computation.5 | async-start | bytes 1146880
  168.8 4.2 %collective-permute-start = (bf16[4,448]{1,0:T(4,128)(2,1)S(1)}, bf16[4,448]{1,0:T(4,128)(2,1)S(1)}, u32[]{:S(2)}, u32[]{:S(2)}) collective-permute-start(bf16[4,448]{1,0:T(4,128)(2,1)S(1)} %add_convert_fusion.2), channel_id=1, source_target_pairs={{0,128},{1,129},{2,130},{3,131},{4,132},{5,133},{6,134},{7,135},{8... | collective-permute-start | bytes 10760 | tf_op jit(solution)/shard_map/ppermute | solution.py:20
  207.7 2.7 copy-start.9
  216.5 5.9 %copy-start.6 = (bf16[1,448,1792]{2,1,0:T(8,128)(2,1)S(1)}, bf16[1,448,1792]{2,1,0:T(8,128)(2,1)}, u32[]{:S(2)}) copy-start(bf16[1,448,1792]{2,1,0:T(8,128)(2,1)} %get-tuple-element.144) | copy-start | bytes 4816900 | tf_op jit(solution)/shard_map/cond
  222.7 40.5 %copy-start.3 = (bf16[1,448,1792]{2,1,0:T(8,128)(2,1)S(1)}, bf16[1,448,1792]{2,1,0:T(8,128)(2,1)}, u32[]{:S(2)}) copy-start(bf16[1,448,1792]{2,1,0:T(8,128)(2,1)} %param.31) | copy-start | bytes 4816900
  224.0 109.8 %reduce-scatter.14.cloned.1.call-start = ((), (), s32[]{:S(2)}) async-start(), calls=%async_computation.6 | async-start | bytes 1146880
  249.1 4.2 %copy-start.19 = (bf16[4,448]{1,0:T(4,128)(2,1)}, bf16[4,448]{1,0:T(4,128)(2,1)S(1)}, u32[]{:S(2)}) copy-start(bf16[4,448]{1,0:T(4,128)(2,1)S(1)} %get-tuple-element.459) | copy-start | bytes 10756
  249.1 4.1 %collective-permute-start.1 = (bf16[4,448]{1,0:T(4,128)(2,1)S(1)}, bf16[4,448]{1,0:T(4,128)(2,1)S(1)}, u32[]{:S(2)}, u32[]{:S(2)}) collective-permute-start(bf16[4,448]{1,0:T(4,128)(2,1)S(1)} %get-tuple-element.459), channel_id=1, source_target_pairs={{0,128},{1,129},{2,130},{3,131},{4,132},{5,133},{6,134},{7,135},{8... | collective-permute-start | bytes 10760 | tf_op jit(solution)/shard_map/ppermute | solution.py:20
  253.3 0.6 copy-start.21
  263.5 0.5 copy-start.26
  291.1 4.2 %copy-start.27 = (s32[8]{0:T(128)S(1)}, s32[8]{0:T(128)}, u32[]{:S(2)}) copy-start(s32[8]{0:T(128)} %copy-done.26) | copy-start | bytes 100 | tf_op jit(solution)/shard_map/cond
  309.3 25.6 %copy-start.15 = (bf16[8,448]{1,0:T(8,128)(2,1)S(1)}, bf16[8,448]{1,0:T(8,128)(2,1)}, u32[]{:S(2)}) copy-start(bf16[8,448]{1,0:T(8,128)(2,1)} %param.26) | copy-start | bytes 21508
  309.3 25.6 %copy-start.20 = (bf16[4,448]{1,0:T(4,128)(2,1)S(1)}, bf16[4,448]{1,0:T(4,128)(2,1)}, u32[]{:S(2)}) copy-start(bf16[4,448]{1,0:T(4,128)(2,1)} %copy-done.19) | copy-start | bytes 10756
  309.3 25.6 %copy-start.22 = (bf16[4,448]{1,0:T(4,128)(2,1)S(1)}, bf16[4,448]{1,0:T(4,128)(2,1)}, u32[]{:S(2)}) copy-start(bf16[4,448]{1,0:T(4,128)(2,1)} %copy-done.21) | copy-start | bytes 10756
  309.3 25.6 %copy-start.23 = (bf16[4,448]{1,0:T(4,128)(2,1)S(1)}, bf16[4,448]{1,0:T(4,128)(2,1)}, u32[]{:S(2)}) copy-start(bf16[4,448]{1,0:T(4,128)(2,1)} %get-tuple-element.458) | copy-start | bytes 10756
Sparse Core Ops, SparseCore 0:
  9.9 96.6 all-gather.4
  147.1 20.5 reduce-scatter.9
  224.2 23.2 reduce-scatter.11
  310.7 23.0 reduce-scatter.13
where the time goes:
time: 345 us; the launch traced here: 342 us
  waiting for transfers between devices  161 us (47%)
  local copies, waits for them, and re-layouts  99.9 us (29%)
  blocking collectives  28.6 us (8%)
  other arithmetic  18.5 us (5%)
  matrix products  17.3 us (5%)
  between operations  13.3 us (4%)
    all_gather x1, waiting for transfers between devices, body(): prompt_source = lax.all_gather(prompt_pages, 'req', axis=0, tiled=True)  87.2 us
    unnamed x7, waiting for transfers between devices  68 us
    all_gather x3, blocking collectives, body(): whole = lax.all_gather(rows_in, 'head', axis=1, tiled=True)  28.6 us
    gather x6, local copies, waits for them, and re-layouts, window_local(): own_rows = jnp.take(own_pages, own_ids, axis=0)  27.5 us
    another operation x6, local copies, waits for them, and re-layouts  19.6 us
    gather x3, local copies, waits for them, and re-layouts, window_local(): prompt_rows = jnp.take(prompt_source, group_ids, axis=0)  12.4 us
    squeeze x3, local copies, waits for them, and re-layouts, window_local(): own_values = own_rows[:, :, 1].reshape(batch_rows, 2 * PAGE, heads, HD)  10.7 us
    select_n x3, other arithmetic, window_local(): own_rows = jnp.take(own_pages, own_ids, axis=0)  9.42 us
  transfers between devices with their start and end apart: 6, of which 6 were waited for; matrix products, arithmetic and copies ran while one was open for 1% of the time, Pallas kernels for 0%

commit v1 on v0

v1 whole, which is shorter than its diff:
```python
import jax
import jax.numpy as jnp
from jax import lax
from jax.sharding import PartitionSpec as P

HD = 112
FEAT = 16
WINDOW = 64
PAGE = 128
HALF = 64
XN = 4
ZN = 8
LANES = 512

EPSILON = 1e-06
MASKED = -1e30
Z_OFFSETS = (-1, 0, 1, 2, 3, 4, -3, -2)


def head_shift(value, steps):
    count = lax.axis_size("head")
    return lax.ppermute(value, "head", [(i, (i + steps) % count) for i in range(count)])


def x_shift(value, steps):
    return lax.ppermute(
        value,
        "req",
        [(z * XN + i, z * XN + (i + steps) % XN) for z in range(ZN) for i in range(XN)],
    )


def z_shift(value, steps):
    base = XN * ZN
    return lax.ppermute(
        value,
        ("section", "req"),
        [
            (base + z * XN + i, base + ((z + steps) % ZN) * XN + i)
            for z in range(ZN)
            for i in range(XN)
        ],
    )


def section_swap(value, steps):
    count = lax.axis_size("head")
    there = [(i, count + (i + steps) % count) for i in range(count)]
    return lax.ppermute(value, ("section", "head"), there + [(b, a) for a, b in there])


def rms_norm(token_rows, gain_row):
    values = token_rows.astype(jnp.float32)
    factor = lax.rsqrt(jnp.mean(values * values, axis=-1, keepdims=True) + EPSILON)
    return (values * factor * gain_row).astype(jnp.bfloat16)


def taylor(raw_feats):
    scaled = raw_feats * FEAT ** (-0.25)
    outer = scaled[..., :, None] * scaled[..., None, :]
    flat = outer.reshape(scaled.shape[:-1] + (FEAT * FEAT,)) * 0.5**0.5
    constant = jnp.ones(scaled.shape[:-1] + (1,), jnp.float32)
    return jnp.concatenate([constant, scaled, flat], axis=-1)


def linear_local(normed, feature_w, value_w, out_w, conv_w, conv_part, state_part, norm_part):
    batch_rows = normed.shape[0]
    heads = state_part.shape[1]
    features = jnp.dot(normed, feature_w, preferred_element_type=jnp.float32).reshape(
        batch_rows, heads, 2, FEAT
    )
    query_feats = taylor(features[:, :, 0])
    key_feats = taylor(features[:, :, 1])
    fresh_values = jnp.dot(normed, value_w, preferred_element_type=jnp.float32)
    older_values = conv_part.astype(jnp.float32)
    mixed_values = (
        conv_w[0] * older_values[:, 0] + conv_w[1] * older_values[:, 1] + conv_w[2] * fresh_values
    )
    mixed_values = mixed_values.reshape(batch_rows, heads, HD)
    from_state = jnp.einsum(
        "rhf,rhfd->rhd",
        query_feats.astype(jnp.bfloat16),
        state_part,
        preferred_element_type=jnp.float32,
    )
    intersection = jnp.sum(query_feats * key_feats, axis=-1)
    denominator = jnp.sum(query_feats * norm_part, axis=-1) + intersection
    attended = (
        (from_state + intersection[..., None] * mixed_values) / denominator[..., None]
    ).astype(jnp.bfloat16)
    return jnp.dot(
        attended.reshape(batch_rows, heads * HD), out_w, preferred_element_type=jnp.float32
    )


def gather_own(own_pages, page_table, lengths, groups, req_index):
    rows = lengths.shape[0]
    window_start = lengths - WINDOW
    halves = jnp.stack([window_start // HALF, (lengths - 2) // HALF], axis=1)
    pages = halves // 2
    own_ids = jnp.take_along_axis(page_table, pages, axis=1) - groups
    own_ids = jnp.clip(own_ids - req_index * own_pages.shape[0], 0, own_pages.shape[0] - 1)
    split = own_pages.reshape(own_pages.shape[0], 2, 2, HALF, own_pages.shape[-1])
    picked = split[own_ids, :, halves % 2]
    positions = (halves[:, :, None] * HALF + jnp.arange(HALF, dtype=jnp.int32)).reshape(
        rows, 2 * HALF
    )
    second = jnp.concatenate(
        [
            jnp.ones((rows, HALF), bool),
            jnp.broadcast_to((halves[:, 1] != halves[:, 0])[:, None], (rows, HALF)),
        ],
        axis=1,
    )
    usable = (
        (positions >= jnp.maximum(window_start, PAGE)[:, None])
        & (positions <= (lengths - 2)[:, None])
        & second
    )
    keys = picked[:, :, 0].reshape(rows, 2 * HALF, -1)
    values = picked[:, :, 1].reshape(rows, 2 * HALF, -1)
    return keys, values, usable


def project(layer_one, gain, query_key_w, value_w):
    rows = layer_one.shape[0]
    normed = rms_norm(layer_one, gain)
    query_key = jnp.dot(normed, query_key_w, preferred_element_type=jnp.float32).reshape(
        rows, -1, 2, HD
    )
    value_new = jnp.dot(normed, value_w, preferred_element_type=jnp.float32)
    return (
        query_key[:, :, 0].reshape(rows, -1).astype(jnp.bfloat16),
        query_key[:, :, 1].reshape(rows, -1).astype(jnp.bfloat16),
        value_new.astype(jnp.bfloat16),
    )


def prompt_local(queries, groups_of, starts, pages, slot_groups):
    rows = queries.shape[0]
    heads = queries.shape[1] // HD
    keys = pages[:, :HALF].reshape(ZN * HALF, heads, HD)
    values = pages[:, HALF:].reshape(ZN * HALF, heads, HD)
    scores = jnp.einsum(
        "rhd,thd->rht", queries.reshape(rows, heads, HD), keys, preferred_element_type=jnp.float32
    ) * HD ** (-0.5)
    offsets = jnp.arange(ZN * HALF, dtype=jnp.int32) % HALF + HALF
    usable = (groups_of[:, None] == jnp.repeat(slot_groups, HALF)[None]) & (
        offsets[None] >= starts[:, None]
    )
    scores = jnp.where(usable[:, None], scores, MASKED)
    highest = jnp.max(scores, axis=-1)
    exps = jnp.where(usable[:, None], jnp.exp(scores - highest[..., None]), 0.0)
    total = jnp.sum(exps, axis=-1)
    summed = jnp.einsum(
        "rht,thd->rhd", exps.astype(jnp.bfloat16), values, preferred_element_type=jnp.float32
    )
    pad = jnp.zeros((rows, LANES - heads * HD - 2 * heads), jnp.float32)
    return jnp.concatenate([summed.reshape(rows, heads * HD), highest, total, pad], axis=1)


def own_local(query, key_new, value_new, keys, values, usable):
    rows = query.shape[0]
    heads = query.shape[1] // HD
    query = query.reshape(rows, heads, HD)
    key_new = key_new.reshape(rows, heads, HD)
    value_new = value_new.reshape(rows, heads, HD)
    keys = keys.reshape(rows, 2 * HALF, heads, HD)
    values = values.reshape(rows, 2 * HALF, heads, HD)
    scale = HD ** (-0.5)
    scores = jnp.einsum("rhd,rthd->rht", query, keys, preferred_element_type=jnp.float32) * scale
    new_score = jnp.sum(query.astype(jnp.float32) * key_new.astype(jnp.float32), axis=-1) * scale
    scores = jnp.where(usable[:, None], scores, MASKED)
    highest = jnp.maximum(jnp.max(scores, axis=-1), new_score)
    exps = jnp.exp(scores - highest[..., None])
    exp_new = jnp.exp(new_score - highest)
    total = jnp.sum(exps, axis=-1) + exp_new
    summed = jnp.einsum(
        "rht,rthd->rhd", exps.astype(jnp.bfloat16), values, preferred_element_type=jnp.float32
    ) + exp_new.astype(jnp.bfloat16).astype(jnp.float32)[..., None] * value_new.astype(jnp.float32)
    return summed, highest, total


def combine(own_summed, own_highest, own_total, parts, out_w):
    rows, heads = own_highest.shape
    wide = heads * HD
    prompt_highest = parts[0][:, wide : wide + heads]
    merged = parts[0]
    for part in parts[1:]:
        prompt_highest = jnp.maximum(prompt_highest, part[:, wide : wide + heads])
        merged = merged + part
    prompt_total = merged[:, wide + heads : wide + 2 * heads]
    prompt_summed = merged[:, :wide].reshape(rows, heads, HD)
    highest = jnp.maximum(own_highest, prompt_highest)
    own_factor = jnp.exp(own_highest - highest)
    prompt_factor = jnp.exp(prompt_highest - highest)
    total = own_total * own_factor + prompt_total * prompt_factor
    attended = (
        own_summed * (own_factor / total)[..., None]
        + prompt_summed * (prompt_factor / total)[..., None]
    )
    attended = attended.astype(jnp.bfloat16).reshape(rows, wide)
    return jnp.dot(attended, out_w, preferred_element_type=jnp.float32)


def on_section(index, wanted, run, *operands):
    shapes = jax.eval_shape(run, *operands)

    def skip(*_):
        return jax.tree.map(lambda leaf: jnp.zeros(leaf.shape, leaf.dtype), shapes)

    return lax.cond(index == wanted, run, skip, *operands)


def body(
    tokens,
    norm_gain,
    feature_w,
    query_key_w,
    value_w,
    out_w,
    conv_w,
    conv_state,
    lin_state,
    lin_norm,
    own_pages,
    prompt_pages,
    page_table,
    lengths,
):
    section_index = lax.axis_index("section")
    req_index = lax.axis_index("req")
    head_index = lax.axis_index("head")
    groups = lax.axis_size("req")
    head_count = lax.axis_size("head")
    rows, share = tokens.shape
    gain = norm_gain[0]

    pieces = [tokens] + [head_shift(tokens, k) for k in (1, 3, 2)]
    order = jnp.stack([(head_index - k) % head_count for k in (0, 1, 3, 2)])
    whole = jnp.zeros((head_count, rows, share), tokens.dtype)
    for at, piece in enumerate(pieces):
        whole = lax.dynamic_update_slice(whole, piece[None], (order[at], 0, 0))
    whole = whole.transpose(1, 0, 2).reshape(rows, head_count * share)

    page = prompt_pages[0, :, HALF:, :].reshape(2 * HALF, share)
    trio = jnp.stack([z_shift(page, 1), page, z_shift(page, -1)])
    pages = jnp.concatenate([trio, z_shift(trio, -3), z_shift(trio[1:], 3)])
    slot_groups = (req_index // XN + jnp.array(Z_OFFSETS, jnp.int32)) % ZN * XN + req_index % XN
    own_keys, own_values, usable = on_section(
        section_index,
        1,
        lambda *a: gather_own(*a, groups, req_index),
        own_pages,
        page_table,
        lengths,
    )

    def run_linear(whole_rows):
        normed = rms_norm(whole_rows, gain)
        return linear_local(
            normed, feature_w, value_w[0], out_w[0], conv_w, conv_state, lin_state, lin_norm
        )

    update = on_section(section_index, 0, run_linear, whole)
    swapped = [section_swap(update, k) for k in (0, 1, 3, 2)]
    summed = whole.astype(jnp.float32)
    for piece in swapped:
        summed = summed + piece
    layer_one = summed.astype(jnp.bfloat16)
    one_share = lax.dynamic_slice(layer_one, (0, head_index * share), (rows, share))
    one_back = lax.ppermute(one_share, "section", [(1, 0)])

    query, key_new, value_new = on_section(
        section_index, 1, lambda a: project(a, gain, query_key_w, value_w[0]), layer_one
    )
    window_start = jnp.minimum(lengths - WINDOW, PAGE)
    tags = jnp.stack([page_table[:, 0], window_start], axis=1).astype(jnp.bfloat16)
    packed = jnp.concatenate(
        [query, tags, jnp.zeros((rows, LANES - share - 2), jnp.bfloat16)], axis=1
    )
    asked = [packed] + [x_shift(packed, k) for k in (1, 3, 2)]

    def run_own(*operands):
        return own_local(*operands)

    own_summed, own_highest, own_total = on_section(
        section_index, 1, run_own, query, key_new, value_new, own_keys, own_values, usable
    )

    def run_prompt(asked_rows, pages_here):
        return prompt_local(
            asked_rows[:, :share],
            asked_rows[:, share].astype(jnp.int32),
            asked_rows[:, share + 1].astype(jnp.int32),
            pages_here,
            slot_groups,
        )

    answers = on_section(section_index, 1, run_prompt, jnp.concatenate(asked), pages)
    parts = [answers[:rows]] + [
        x_shift(answers[(at + 1) * rows : (at + 2) * rows], -k) for at, k in enumerate((1, 3, 2))
    ]
    second = on_section(
        section_index,
        1,
        lambda a, b, c, d: combine(a, b, c, d, out_w[0]),
        own_summed,
        own_highest,
        own_total,
        parts,
    )
    by_head = second.reshape(rows, head_count, share).transpose(1, 0, 2)

    def slab(k):
        return lax.dynamic_index_in_dim(by_head, (head_index + k) % head_count, 0, keepdims=False)

    total = one_share.astype(jnp.float32) + slab(0)
    for piece in [head_shift(slab(k), k) for k in (1, 3, 2)]:
        total = total + piece
    output = jnp.where(section_index == 0, one_back, total.astype(jnp.bfloat16))
    return output[None]


def solution(mesh):
    placed = (
        P("req", "head"),
        P("section", None),
        P(None, "head"),
        P(None, "head"),
        P("section", None, "head"),
        P("section", "head", None),
        P(None, "head"),
        P("req", None, "head"),
        P("req", "head", None, None),
        P("req", "head", None),
        P("req", None, None, "head"),
        P("req", None, None, "head"),
        P("req", None),
        P("req"),
    )
    return jax.shard_map(
        body, mesh=mesh, in_specs=placed, out_specs=P("section", "req", "head"), check_vma=False
    )
```

time: 345 us -> 104 us (0.30)
  waiting for transfers between devices: 161 us -> 17 us
  local copies, waits for them, and re-layouts: 99.9 us -> 22.1 us
  starting transfers between devices: 2.7 us -> 49.6 us
  blocking collectives: 28.6 us -> 0 us
  between operations: 13.3 us -> 0.38 us
  other arithmetic: 18.5 us -> 6.66 us
  matrix products: 17.3 us -> 6.27 us
    all_gather x1 -> x0, waiting for transfers between devices: 87.2 us -> none  [body(): prompt_source = lax.all_gather(prompt_pages, 'req', axis=0, tiled=True)]
    unnamed x7 -> x0, waiting for transfers between devices: 68 us -> none
    ppermute x2 -> x21, starting transfers between devices: 2.57 us -> 49.6 us  [the longest x4 17.9 us: z_shift(): lax.ppermute(value, ('section', 'req'), [(base + z * XN + i, base + (z +...]
    gather x24 -> x7, local copies, waits for them, and re-layouts: 42.9 us -> 4.07 us  [the longest x2 3.09 us: gather_own(): picked = split[own_ids, :, halves % 2]]
    all_gather x3 -> x0, blocking collectives: 28.6 us -> none  [body(): whole = lax.all_gather(rows_in, 'head', axis=1, tiled=True)]
    squeeze x6 -> x1, local copies, waits for them, and re-layouts: 19.1 us -> 0.01 us  [slab(): lax.dynamic_index_in_dim(by_head, (head_index + k) % head_count, 0, keepd...]
    select_n x8 -> x0, other arithmetic: 11.7 us -> none  [the longest x3 9.42 us: window_local(): own_rows = jnp.take(own_pages, own_ids, axis=0)]
    ppermute x2 -> x21, waiting for transfers between devices: 5.79 us -> 17 us  [the longest x4 11.4 us: z_shift(): lax.ppermute(value, ('section', 'req'), [(base + z * XN + i, base + (z +...]
  transfers between devices with their start and end apart: 6 -> 21, of which waited for: 6 -> 9; matrix products, arithmetic and copies ran while one was open for 1% -> 22% of each run, Pallas kernels for 0% -> 0%
where the time goes in v1:
time: 104 us; the launch traced here: 103 us
  starting transfers between devices  49.6 us (48%)
  local copies, waits for them, and re-layouts  22.1 us (21%)
  waiting for transfers between devices  17 us (16%)
  other arithmetic  6.66 us (6%)
  matrix products  6.27 us (6%)
    ppermute x4, starting transfers between devices, z_shift(): lax.ppermute(value, ('section', 'req'), [(base + z * XN + i, base + (z +...  17.9 us
    ppermute x4, starting transfers between devices, section_swap(): lax.ppermute(value, ('section', 'head'), there + [(b, a) for a, b in there])  15 us
    another operation x10, local copies, waits for them, and re-layouts  11.7 us
    ppermute x4, waiting for transfers between devices, z_shift(): lax.ppermute(value, ('section', 'req'), [(base + z * XN + i, base + (z +...  11.4 us
    ppermute x6, starting transfers between devices, head_shift(): lax.ppermute(value, 'head', [(i, (i + steps) % count) for i in range(coun...  8.11 us
    ppermute x6, starting transfers between devices, x_shift(): lax.ppermute(value, 'req', [(z * XN + i, z * XN + (i + steps) % XN) for z...  7.29 us
    gather x2, local copies, waits for them, and re-layouts, gather_own(): picked = split[own_ids, :, halves % 2]  3.09 us
    ppermute x6, waiting for transfers between devices, head_shift(): lax.ppermute(value, 'head', [(i, (i + steps) % count) for i in range(coun...  2.68 us
  transfers between devices with their start and end apart: 21, of which 9 were waited for; matrix products, arithmetic and copies ran while one was open for 22% of the time, Pallas kernels for 0%

profile of v1, /device:TPU:1, one launch (start us, length us, event | category | flops | bytes accessed | tf_op | source)
XLA Modules:
  0.0 102.5 jit_solution(8251512504643029074)
XLA Ops:
  0.0 2.1 %collective-permute-start = (bf16[8,448]{1,0:T(8,128)(2,1)}, bf16[8,448]{1,0:T(8,128)(2,1)S(1)}, u32[]{:S(2)}, u32[]{:S(2)}) collective-permute-start(bf16[8,448]{1,0:T(8,128)(2,1)} %param.27), channel_id=1, source_target_pairs={{0,1},{1,2},{2,3},{3,0},{4,5},{5,6},{6,7},{7,4},{8,9},{9,10},{10,1... | collective-permute-start | bytes 21512 | tf_op jit(solution)/shard_map/ppermute | solution.py:22
  2.1 1.4 %collective-permute-start.1 = (bf16[8,448]{1,0:T(8,128)(2,1)}, bf16[8,448]{1,0:T(8,128)(2,1)S(1)}, u32[]{:S(2)}, u32[]{:S(2)}) collective-permute-start(bf16[8,448]{1,0:T(8,128)(2,1)} %param.27), channel_id=1, source_target_pairs={{0,3},{1,0},{2,1},{3,2},{4,7},{5,4},{6,5},{7,6},{8,11},{9,8},{10,9... | collective-permute-start | bytes 21512 | tf_op jit(solution)/shard_map/ppermute | solution.py:22
  3.6 1.6 %collective-permute-start.2 = (bf16[8,448]{1,0:T(8,128)(2,1)}, bf16[8,448]{1,0:T(8,128)(2,1)S(1)}, u32[]{:S(2)}, u32[]{:S(2)}) collective-permute-start(bf16[8,448]{1,0:T(8,128)(2,1)} %param.27), channel_id=1, source_target_pairs={{0,2},{1,3},{2,0},{3,1},{4,6},{5,7},{6,4},{7,5},{8,10},{9,11},{10,... | collective-permute-start | bytes 21512 | tf_op jit(solution)/shard_map/ppermute | solution.py:22
  5.2 0.7 slice_convert_fusion
  5.9 0.7 copy.209
  6.8 1.0 collective-permute-done.2
  8.2 11.5 %collective-permute-start.3 = (f32[8,1792]{1,0:T(8,128)S(1)}, f32[8,1792]{1,0:T(8,128)S(1)}, u32[]{:S(2)}, u32[]{:S(2)}) collective-permute-start(f32[8,1792]{1,0:T(8,128)S(1)} %get-tuple-element.632), channel_id=1, source_target_pairs={{0,128},{1,129},{2,130},{3,131},{128,0},{129,1},{130,2},{131,3},{4... | collective-permute-start | bytes 172040 | tf_op jit(solution)/shard_map/ppermute | solution.py:49
  19.7 3.5 %collective-permute-start.6 = (f32[8,1792]{1,0:T(8,128)S(1)}, f32[8,1792]{1,0:T(8,128)S(1)}, u32[]{:S(2)}, u32[]{:S(2)}) collective-permute-start(f32[8,1792]{1,0:T(8,128)S(1)} %get-tuple-element.632), channel_id=1, source_target_pairs={{0,130},{1,131},{2,128},{3,129},{130,0},{131,1},{128,2},{129,3},{4... | collective-permute-start | bytes 172040 | tf_op jit(solution)/shard_map/ppermute | solution.py:49
  23.3 1.8 %collective-permute-done.4 = f32[8,1792]{1,0:T(8,128)S(1)} collective-permute-done((f32[8,1792]{1,0:T(8,128)S(1)}, f32[8,1792]{1,0:T(8,128)S(1)}, u32[]{:S(2)}, u32[]{:S(2)}) %collective-permute-start.4) | collective-permute-done | bytes 57376 | tf_op jit(solution)/shard_map/ppermute | solution.py:49
  25.4 4.4 %conditional.7 = (bf16[8,448]{1,0:T(8,128)(2,1)S(1)}, bf16[8,448]{1,0:T(8,128)(2,1)S(1)}, bf16[8,448]{1,0:T(8,128)(2,1)S(1)}) conditional(s32[]{:T(128)} %convert_element_type.113, () %tuple.65, (bf16[8,1792]{1,0:T(8,128)(2,1)S(1)}, f32[1,1792]{1,0:T(1,128)}, bf16[1792,896]{1,0:T(8,128)(2,1)}, bf16[1,1792,448]{1,2,0:T(8,128)(2,1)}) %tuple.66), branch_computations={%region_5.6_spmd, %region_6.8_spmd} | conditional | flops 38703624 | bytes 11461848 | solution.py:212
  25.6 0.9 reduce.1
  26.4 2.5 %convolution_convert_fusion = bf16[8,896]{1,0:T(8,128)(2,1)S(1)} fusion(bf16[1792,896]{1,0:T(8,128)(2,1)} %get-tuple-element.296, bf16[8,1792]{1,0:T(8,128)(2,1)S(1)} %get-tuple-element.241, f32[1792]{0:T(1024)S(1)} %reduce.1, f32[8]{0:T(128)S(1)} %add_rsqrt_fusion.1), kind=kOutput, calls=%fused_computation.125 | convolution fusion | flops 25754624 | bytes 3261472 | tf_op jit(solution)/shard_map/cond/branch_1_fun/dot_general | solution.py:128
  29.9 3.1 %collective-permute-start.10 = (bf16[8,512]{1,0:T(8,128)(2,1)S(1)}, bf16[8,512]{1,0:T(8,128)(2,1)S(1)}, u32[]{:S(2)}, u32[]{:S(2)}) collective-permute-start(bf16[8,512]{1,0:T(8,128)(2,1)S(1)} %pad_maximum_fusion.4), channel_id=1, source_target_pairs={{0,8},{4,12},{8,0},{12,4},{16,24},{20,28},{24,16},{28,20},{32,40},... | collective-permute-start | bytes 24584 | tf_op jit(solution)/shard_map/ppermute | solution.py:26
  33.3 2.4 %collective-permute-start.9 = (bf16[8,512]{1,0:T(8,128)(2,1)S(1)}, bf16[8,512]{1,0:T(8,128)(2,1)S(1)}, u32[]{:S(2)}, u32[]{:S(2)}) collective-permute-start(bf16[8,512]{1,0:T(8,128)(2,1)S(1)} %pad_maximum_fusion.4), channel_id=1, source_target_pairs={{0,12},{4,0},{8,4},{12,8},{16,28},{20,16},{24,20},{28,24},{32,44},... | collective-permute-start | bytes 24584 | tf_op jit(solution)/shard_map/ppermute | solution.py:26
  35.9 3.5 %collective-permute-start.11 = (bf16[128,448]{1,0:T(8,128)(2,1)S(1)}, bf16[128,448]{1,0:T(8,128)(2,1)S(1)}, u32[]{:S(2)}, u32[]{:S(2)}) collective-permute-start(bf16[128,448]{1,0:T(8,128)(2,1)S(1)} %bitcast.144), channel_id=1, source_target_pairs={{128,144},{132,148},{136,152},{140,156},{144,160},{148,164},{152,1... | collective-permute-start | bytes 344072 | tf_op jit(solution)/shard_map/ppermute | solution.py:35
  39.5 5.9 %collective-permute-start.12 = (bf16[128,448]{1,0:T(8,128)(2,1)S(1)}, bf16[128,448]{1,0:T(8,128)(2,1)S(1)}, u32[]{:S(2)}, u32[]{:S(2)}) collective-permute-start(bf16[128,448]{1,0:T(8,128)(2,1)S(1)} %bitcast.145), channel_id=1, source_target_pairs={{128,240},{132,244},{136,248},{140,252},{144,128},{148,132},{152,1... | collective-permute-start | bytes 344072 | tf_op jit(solution)/shard_map/ppermute | solution.py:35
  45.9 1.4 %collective-permute-done.12 = bf16[128,448]{1,0:T(8,128)(2,1)S(1)} collective-permute-done((bf16[128,448]{1,0:T(8,128)(2,1)S(1)}, bf16[128,448]{1,0:T(8,128)(2,1)S(1)}, u32[]{:S(2)}, u32[]{:S(2)}) %collective-permute-start.12) | collective-permute-done | bytes 114720 | tf_op jit(solution)/shard_map/ppermute | solution.py:35
  47.5 5.7 %collective-permute-start.13 = (bf16[3,128,448]{1,2,0:T(8,128)(2,1)S(1)}, bf16[3,128,448]{1,2,0:T(8,128)(2,1)S(1)}, u32[]{:S(2)}, u32[]{:S(2)}) collective-permute-start(bf16[3,128,448]{1,2,0:T(8,128)(2,1)S(1)} %pad_maximum_fusion.1), channel_id=1, source_target_pairs={{128,208},{132,212},{136,216},{140,220},{144,224},{148,228},{152,2... | collective-permute-start | bytes 1032200 | tf_op jit(solution)/shard_map/ppermute | solution.py:35
  53.2 2.8 %collective-permute-start.14 = (bf16[2,128,448]{1,2,0:T(8,128)(2,1)S(1)}, bf16[2,128,448]{1,2,0:T(8,128)(2,1)S(1)}, u32[]{:S(2)}, u32[]{:S(2)}) collective-permute-start(bf16[2,128,448]{1,2,0:T(8,128)(2,1)S(1)} %pad_maximum_fusion.2), channel_id=1, source_target_pairs={{128,176},{132,180},{136,184},{140,188},{144,192},{148,196},{152,2... | collective-permute-start | bytes 688136 | tf_op jit(solution)/shard_map/ppermute | solution.py:35
  56.1 7.3 %collective-permute-done.13 = bf16[3,128,448]{1,2,0:T(8,128)(2,1)S(1)} collective-permute-done((bf16[3,128,448]{1,2,0:T(8,128)(2,1)S(1)}, bf16[3,128,448]{1,2,0:T(8,128)(2,1)S(1)}, u32[]{:S(2)}, u32[]{:S(2)}) %collective-permute-start.13) | collective-permute-done | bytes 344096 | tf_op jit(solution)/shard_map/ppermute | solution.py:35
  63.5 2.6 %collective-permute-done.14 = bf16[2,128,448]{1,2,0:T(8,128)(2,1)S(1)} collective-permute-done((bf16[2,128,448]{1,2,0:T(8,128)(2,1)S(1)}, bf16[2,128,448]{1,2,0:T(8,128)(2,1)S(1)}, u32[]{:S(2)}, u32[]{:S(2)}) %collective-permute-start.14) | collective-permute-done | bytes 229408 | tf_op jit(solution)/shard_map/ppermute | solution.py:35
  66.1 4.1 %conditional.8 = (f32[32,512]{1,0:T(8,128)S(1)}) conditional(s32[]{:T(128)} %convert_element_type.113, () %tuple.64, (bf16[32,512]{1,0:T(8,128)(2,1)S(1)}, s32[]{:T(128)}, pred[]{:T(512)}, bf16[8,128,448]{1,2,0:T(8,128)(2,1)S(1)}, pred[]{:T(512)}, /*index=5*/s32[]{:T(128)}, s32[]{:T(128)}, s32[]{:T(128)}, s32[]{:T(128)}, s32[]{:T(128)}, ...), branch_computations={%region_8.9_spmd, %region_9.12_spmd.clone} | conditional | flops 30051776 | bytes 7792966 | solution.py:212
  66.4 0.7 fusion.63
  67.5 0.5 copy.225
  70.3 1.5 %collective-permute-start.16 = (f32[8,512]{1,0:T(8,128)S(1)}, f32[8,512]{1,0:T(8,128)S(1)}, u32[]{:S(2)}, u32[]{:S(2)}) collective-permute-start(f32[8,512]{1,0:T(8,128)S(1)} %get-tuple-element.612), channel_id=1, source_target_pairs={{0,4},{4,8},{8,12},{12,0},{16,20},{20,24},{24,28},{28,16},{32,36},... | collective-permute-start | bytes 49160 | tf_op jit(solution)/shard_map/ppermute | solution.py:26
  71.8 12.1 %conditional.9 = (bf16[8,128,448]{2,1,0:T(8,128)(2,1)S(1)}, bf16[8,128,448]{2,1,0:T(8,128)(2,1)}, pred[8,128]{1,0:T(8,128)(4,1)S(1)}) conditional(s32[]{:T(128)} %convert_element_type.113, () %tuple.69, (bf16[16,2,128,448]{2,3,1,0:T(8,128)(2,1)}, s32[8]{0:T(128)S(1)}, s32[8,256]{1,0:T(8,128)S(1)}, s32[]{:T(128)}) %tuple.150), branch_computations={%region_12.13_spmd, %region_13.14_spmd} | conditional | flops 6193 | bytes 18372856 | solution.py:212
  72.0 0.7 gather_fusion.1
  73.0 6.1 %copy.226 = bf16[16,2,128,448]{3,2,1,0:T(8,128)(2,1)} copy(bf16[16,2,128,448]{2,3,1,0:T(8,128)(2,1)} %get-tuple-element.549) | data formatting | bytes 7340032 | tf_op jit(solution)/shard_map
  79.1 2.9 %gather_fusion = bf16[16,2,64,448]{3,2,1,0:T(8,128)(2,1)S(1)} fusion(bf16[16,2,2,64,448]{4,3,2,1,0:T(8,128)(2,1)} %bitcast.135, s32[16]{0:T(128)S(1)} %reshape.595), kind=kCustom, calls=%fused_computation | custom fusion | bytes 3670144 | tf_op jit(solution)/shard_map/cond/branch_1_fun/gather | solution.py:104
  82.3 1.2 %fusion.87 = (bf16[8,2,1,64,448]{4,3,1,0,2:T(8,128)(2,1)}, bf16[8,2,1,64,448]{4,3,1,0,2:T(8,128)(2,1)S(1)}) fusion(bf16[8,2,2,64,448]{4,3,1,0,2:T(8,128)(2,1)S(1)} %bitcast.136), kind=kLoop, calls=%fused_computation.163 | loop fusion | bytes 3670016 | tf_op jit(solution)/shard_map/cond/branch_1_fun/slice | solution.py:121
  84.0 7.9 %conditional.10 = (f32[8,4,112]{2,1,0:T(4,128)S(1)}, f32[8,4]{0,1:T(4,128)}, f32[8,4]{0,1:T(4,128)S(1)}) conditional(s32[]{:T(128)} %convert_element_type.113, () %tuple.68, (pred[8,128]{1,0:T(8,128)(4,1)S(1)}, bf16[8,448]{1,0:T(8,128)(2,1)S(1)}, bf16[8,128,448]{2,1,0:T(8,128)(2,1)S(1)}, bf16[8,448]{1,0:T(8,128)(2,1)S(1)}, ...), branch_computations={%region_14.15_spmd, %region_15.19_spmd} | conditional | flops 1885856 | bytes 5732504 | solution.py:212
  84.1 1.3 %copy.227 = bf16[8,128,448]{1,2,0:T(8,128)(2,1)} copy(bf16[8,128,448]{2,1,0:T(8,128)(2,1)S(1)} %get-tuple-element.555) | data formatting | bytes 1835008 | tf_op jit(solution)/shard_map
  85.3 1.5 %fusion.89 = f32[8,4,1,128]{3,2,1,0:T(1,128)S(1)} fusion(bf16[8,4,112,1]{2,3,1,0:T(2,128)(2,1)S(1)} %reshape.616, bf16[8,128,4,112]{1,3,2,0:T(8,128)(2,1)} %bitcast.139), kind=kOutput, calls=%fused_computation.165 | convolution fusion | flops 917504 | bytes 941056 | tf_op jit(solution)/shard_map/cond/branch_1_fun/rhd,rthd->rht/dot_general | solution.py:171
  87.3 0.6 convert_convert_fusion
  87.9 0.8 fusion.3
  88.7 0.7 fusion.7
  89.4 1.6 %copy.228 = bf16[8,128,448]{1,2,0:T(8,128)(2,1)S(1)} copy(bf16[8,128,448]{2,1,0:T(8,128)(2,1)} %get-tuple-element.557) | data formatting | bytes 1835008 | tf_op jit(solution)/shard_map
  91.0 0.6 fusion.1
  91.9 3.2 %conditional.11 = (f32[8,4,448]{2,0,1:T(8,128)S(1)}) conditional(s32[]{:T(128)} %convert_element_type.113, () %tuple.63, (f32[32,512]{1,0:T(8,128)S(1)}, f32[8,512]{1,0:T(8,128)S(1)}, f32[8,512]{1,0:T(8,128)S(1)}, f32[8,512]{1,0:T(8,128)S(1)}, f32[8,4]{0,1:T(4,128)}, /*index=5*/f32[8,4]{0,1:T(4,128)S(1)}, f32[8,4,112]{2,1,0:T(4,128)S(1)}, ...), branch_computations={%region_19.20_spmd, %region_20.21_spmd} | conditional | flops 12872224 | bytes 5044744 | solution.py:212
  91.9 0.8 copy.229
  93.2 1.3 %copy.231 = bf16[1,448,1792]{1,2,0:T(8,128)(2,1)S(1)} copy(bf16[1,448,1792]{2,1,0:T(8,128)(2,1)S(1)} %get-tuple-element.566) | data formatting | bytes 3211264 | tf_op jit(solution)/shard_map
  94.5 0.6 fusion.90
  95.1 1.0 collective-permute-start.18
  96.1 1.7 %collective-permute-start.19 = (f32[8,448]{1,0:T(8,128)S(1)}, f32[8,448]{1,0:T(8,128)S(1)}, u32[]{:S(2)}, u32[]{:S(2)}) collective-permute-start(f32[8,448]{1,0:T(8,128)S(1)} %get-tuple-element.610), channel_id=1, source_target_pairs={{0,3},{1,0},{2,1},{3,2},{4,7},{5,4},{6,5},{7,6},{8,11},{9,8},{10,9... | collective-permute-start | bytes 43016 | tf_op jit(solution)/shard_map/ppermute | solution.py:22
  98.0 1.3 %collective-permute-start.7 = (bf16[8,448]{1,0:T(8,128)(2,1)S(1)}, bf16[8,448]{1,0:T(8,128)(2,1)S(1)}, u32[]{:S(2)}, u32[]{:S(2)}) collective-permute-start(bf16[8,448]{1,0:T(8,128)(2,1)S(1)} %constant_dynamic-slice_fusion), channel_id=1, source_target_pairs={{128,0},{129,1},{130,2},{131,3},{132,4},{133,5},{134,6},{135,7},{1... | collective-permute-start | bytes 21512 | tf_op jit(solution)/shard_map/ppermute | solution.py:272
  99.3 0.8 collective-permute-done.7
  100.1 1.7 %collective-permute-done.20 = f32[8,448]{1,0:T(8,128)S(1)} collective-permute-done((f32[8,448]{1,0:T(8,128)S(1)}, f32[8,448]{1,0:T(8,128)S(1)}, u32[]{:S(2)}, u32[]{:S(2)}) %collective-permute-start.20) | collective-permute-done | bytes 14368 | tf_op jit(solution)/shard_map/ppermute | solution.py:22
  101.8 0.7 fusion.80
  (131 shorter events, 9.0 us)
Async XLA Ops:
  0.0 6.8 %collective-permute-start = (bf16[8,448]{1,0:T(8,128)(2,1)}, bf16[8,448]{1,0:T(8,128)(2,1)S(1)}, u32[]{:S(2)}, u32[]{:S(2)}) collective-permute-start(bf16[8,448]{1,0:T(8,128)(2,1)} %param.27), channel_id=1, source_target_pairs={{0,1},{1,2},{2,3},{3,0},{4,5},{5,6},{6,7},{7,4},{8,9},{9,10},{10,1... | collective-permute-start | bytes 21512 | tf_op jit(solution)/shard_map/ppermute | solution.py:22
  2.1 4.7 %collective-permute-start.1 = (bf16[8,448]{1,0:T(8,128)(2,1)}, bf16[8,448]{1,0:T(8,128)(2,1)S(1)}, u32[]{:S(2)}, u32[]{:S(2)}) collective-permute-start(bf16[8,448]{1,0:T(8,128)(2,1)} %param.27), channel_id=1, source_target_pairs={{0,3},{1,0},{2,1},{3,2},{4,7},{5,4},{6,5},{7,6},{8,11},{9,8},{10,9... | collective-permute-start | bytes 21512 | tf_op jit(solution)/shard_map/ppermute | solution.py:22
  3.6 4.2 %collective-permute-start.2 = (bf16[8,448]{1,0:T(8,128)(2,1)}, bf16[8,448]{1,0:T(8,128)(2,1)S(1)}, u32[]{:S(2)}, u32[]{:S(2)}) collective-permute-start(bf16[8,448]{1,0:T(8,128)(2,1)} %param.27), channel_id=1, source_target_pairs={{0,2},{1,3},{2,0},{3,1},{4,6},{5,7},{6,4},{7,5},{8,10},{9,11},{10,... | collective-permute-start | bytes 21512 | tf_op jit(solution)/shard_map/ppermute | solution.py:22
  8.2 15.0 %copy-start.12 = (s32[8]{0:T(128)S(1)}, s32[8]{0:T(128)}, u32[]{:S(2)}) copy-start(s32[8]{0:T(128)} %param.40) | copy-start | bytes 100
  8.2 15.1 %collective-permute-start.3 = (f32[8,1792]{1,0:T(8,128)S(1)}, f32[8,1792]{1,0:T(8,128)S(1)}, u32[]{:S(2)}, u32[]{:S(2)}) collective-permute-start(f32[8,1792]{1,0:T(8,128)S(1)} %get-tuple-element.632), channel_id=1, source_target_pairs={{0,128},{1,129},{2,130},{3,131},{128,0},{129,1},{130,2},{131,3},{4... | collective-permute-start | bytes 172040 | tf_op jit(solution)/shard_map/ppermute | solution.py:49
  19.7 5.4 %collective-permute-start.4 = (f32[8,1792]{1,0:T(8,128)S(1)}, f32[8,1792]{1,0:T(8,128)S(1)}, u32[]{:S(2)}, u32[]{:S(2)}) collective-permute-start(f32[8,1792]{1,0:T(8,128)S(1)} %get-tuple-element.632), channel_id=1, source_target_pairs={{0,129},{1,130},{2,131},{3,128},{129,0},{130,1},{131,2},{128,3},{4... | collective-permute-start | bytes 172040 | tf_op jit(solution)/shard_map/ppermute | solution.py:49
  19.7 5.4 %collective-permute-start.5 = (f32[8,1792]{1,0:T(8,128)S(1)}, f32[8,1792]{1,0:T(8,128)S(1)}, u32[]{:S(2)}, u32[]{:S(2)}) collective-permute-start(f32[8,1792]{1,0:T(8,128)S(1)} %get-tuple-element.632), channel_id=1, source_target_pairs={{0,131},{1,128},{2,129},{3,130},{131,0},{128,1},{129,2},{130,3},{4... | collective-permute-start | bytes 172040 | tf_op jit(solution)/shard_map/ppermute | solution.py:49
  19.7 5.6 %collective-permute-start.6 = (f32[8,1792]{1,0:T(8,128)S(1)}, f32[8,1792]{1,0:T(8,128)S(1)}, u32[]{:S(2)}, u32[]{:S(2)}) collective-permute-start(f32[8,1792]{1,0:T(8,128)S(1)} %get-tuple-element.632), channel_id=1, source_target_pairs={{0,130},{1,131},{2,128},{3,129},{130,0},{131,1},{128,2},{129,3},{4... | collective-permute-start | bytes 172040 | tf_op jit(solution)/shard_map/ppermute | solution.py:49
  25.4 10.3 %copy-start.5 = (bf16[1,2,128,448]{2,3,1,0:T(8,128)(2,1)S(1)}, bf16[1,2,128,448]{2,3,1,0:T(8,128)(2,1)}, u32[]{:S(2)}) copy-start(bf16[1,2,128,448]{2,3,1,0:T(8,128)(2,1)} %param.38) | copy-start | bytes 688132
  25.4 3.9 %copy-start.2 = (bf16[1,1792,448]{1,2,0:T(8,128)(2,1)S(1)}, bf16[1,1792,448]{1,2,0:T(8,128)(2,1)}, u32[]{:S(2)}) copy-start(bf16[1,1792,448]{1,2,0:T(8,128)(2,1)} %get-tuple-element.538) | copy-start | bytes 4816900 | tf_op jit(solution)/shard_map/cond
  29.8 33.7 %copy-start.6 = (bf16[8,448]{1,0:T(8,128)(2,1)}, bf16[8,448]{1,0:T(8,128)(2,1)S(1)}, u32[]{:S(2)}) copy-start(bf16[8,448]{1,0:T(8,128)(2,1)S(1)} %get-tuple-element.279) | copy-start | bytes 21508
  29.8 33.7 %copy-start.8 = (bf16[8,448]{1,0:T(8,128)(2,1)}, bf16[8,448]{1,0:T(8,128)(2,1)S(1)}, u32[]{:S(2)}) copy-start(bf16[8,448]{1,0:T(8,128)(2,1)S(1)} %get-tuple-element.281) | copy-start | bytes 21508
  29.9 15.6 %collective-permute-start.10 = (bf16[8,512]{1,0:T(8,128)(2,1)S(1)}, bf16[8,512]{1,0:T(8,128)(2,1)S(1)}, u32[]{:S(2)}, u32[]{:S(2)}) collective-permute-start(bf16[8,512]{1,0:T(8,128)(2,1)S(1)} %pad_maximum_fusion.4), channel_id=1, source_target_pairs={{0,8},{4,12},{8,0},{12,4},{16,24},{20,28},{24,16},{28,20},{32,40},... | collective-permute-start | bytes 24584 | tf_op jit(solution)/shard_map/ppermute | solution.py:26
  33.0 12.5 %collective-permute-start.8 = (bf16[8,512]{1,0:T(8,128)(2,1)S(1)}, bf16[8,512]{1,0:T(8,128)(2,1)S(1)}, u32[]{:S(2)}, u32[]{:S(2)}) collective-permute-start(bf16[8,512]{1,0:T(8,128)(2,1)S(1)} %pad_maximum_fusion.4), channel_id=1, source_target_pairs={{0,4},{4,8},{8,12},{12,0},{16,20},{20,24},{24,28},{28,16},{32,36},... | collective-permute-start | bytes 24584 | tf_op jit(solution)/shard_map/ppermute | solution.py:26
  33.3 12.2 %collective-permute-start.9 = (bf16[8,512]{1,0:T(8,128)(2,1)S(1)}, bf16[8,512]{1,0:T(8,128)(2,1)S(1)}, u32[]{:S(2)}, u32[]{:S(2)}) collective-permute-start(bf16[8,512]{1,0:T(8,128)(2,1)S(1)} %pad_maximum_fusion.4), channel_id=1, source_target_pairs={{0,12},{4,0},{8,4},{12,8},{16,28},{20,16},{24,20},{28,24},{32,44},... | collective-permute-start | bytes 24584 | tf_op jit(solution)/shard_map/ppermute | solution.py:26
  35.9 9.8 %collective-permute-start.11 = (bf16[128,448]{1,0:T(8,128)(2,1)S(1)}, bf16[128,448]{1,0:T(8,128)(2,1)S(1)}, u32[]{:S(2)}, u32[]{:S(2)}) collective-permute-start(bf16[128,448]{1,0:T(8,128)(2,1)S(1)} %bitcast.144), channel_id=1, source_target_pairs={{128,144},{132,148},{136,152},{140,156},{144,160},{148,164},{152,1... | collective-permute-start | bytes 344072 | tf_op jit(solution)/shard_map/ppermute | solution.py:35
  39.5 7.8 %collective-permute-start.12 = (bf16[128,448]{1,0:T(8,128)(2,1)S(1)}, bf16[128,448]{1,0:T(8,128)(2,1)S(1)}, u32[]{:S(2)}, u32[]{:S(2)}) collective-permute-start(bf16[128,448]{1,0:T(8,128)(2,1)S(1)} %bitcast.145), channel_id=1, source_target_pairs={{128,240},{132,244},{136,248},{140,252},{144,128},{148,132},{152,1... | collective-permute-start | bytes 344072 | tf_op jit(solution)/shard_map/ppermute | solution.py:35
  47.5 15.9 %collective-permute-start.13 = (bf16[3,128,448]{1,2,0:T(8,128)(2,1)S(1)}, bf16[3,128,448]{1,2,0:T(8,128)(2,1)S(1)}, u32[]{:S(2)}, u32[]{:S(2)}) collective-permute-start(bf16[3,128,448]{1,2,0:T(8,128)(2,1)S(1)} %pad_maximum_fusion.1), channel_id=1, source_target_pairs={{128,208},{132,212},{136,216},{140,220},{144,224},{148,228},{152,2... | collective-permute-start | bytes 1032200 | tf_op jit(solution)/shard_map/ppermute | solution.py:35
  53.2 12.9 %collective-permute-start.14 = (bf16[2,128,448]{1,2,0:T(8,128)(2,1)S(1)}, bf16[2,128,448]{1,2,0:T(8,128)(2,1)S(1)}, u32[]{:S(2)}, u32[]{:S(2)}) collective-permute-start(bf16[2,128,448]{1,2,0:T(8,128)(2,1)S(1)} %pad_maximum_fusion.2), channel_id=1, source_target_pairs={{128,176},{132,180},{136,184},{140,188},{144,192},{148,196},{152,2... | collective-permute-start | bytes 688136 | tf_op jit(solution)/shard_map/ppermute | solution.py:35
  66.1 5.7 %copy-start = (s32[8,256]{1,0:T(8,128)S(1)}, s32[8,256]{1,0:T(8,128)}, u32[]{:S(2)}) copy-start(s32[8,256]{1,0:T(8,128)} %param.39) | copy-start | bytes 24580
  70.2 21.6 %collective-permute-start.15 = (f32[8,512]{1,0:T(8,128)S(1)}, f32[8,512]{1,0:T(8,128)S(1)}, u32[]{:S(2)}, u32[]{:S(2)}) collective-permute-start(f32[8,512]{1,0:T(8,128)S(1)} %get-tuple-element.613), channel_id=1, source_target_pairs={{0,12},{4,0},{8,4},{12,8},{16,28},{20,16},{24,20},{28,24},{32,44},... | collective-permute-start | bytes 49160 | tf_op jit(solution)/shard_map/ppermute | solution.py:26
  70.3 21.5 %collective-permute-start.16 = (f32[8,512]{1,0:T(8,128)S(1)}, f32[8,512]{1,0:T(8,128)S(1)}, u32[]{:S(2)}, u32[]{:S(2)}) collective-permute-start(f32[8,512]{1,0:T(8,128)S(1)} %get-tuple-element.612), channel_id=1, source_target_pairs={{0,4},{4,8},{8,12},{12,0},{16,20},{20,24},{24,28},{28,16},{32,36},... | collective-permute-start | bytes 49160 | tf_op jit(solution)/shard_map/ppermute | solution.py:26
  71.8 20.1 %collective-permute-start.17 = (f32[8,512]{1,0:T(8,128)S(1)}, f32[8,512]{1,0:T(8,128)S(1)}, u32[]{:S(2)}, u32[]{:S(2)}) collective-permute-start(f32[8,512]{1,0:T(8,128)S(1)} %get-tuple-element.611), channel_id=1, source_target_pairs={{0,8},{4,12},{8,0},{12,4},{16,24},{20,28},{24,16},{28,20},{32,40},... | collective-permute-start | bytes 49160 | tf_op jit(solution)/shard_map/ppermute | solution.py:26
  71.8 12.2 %copy-start.7 = (bf16[8,448]{1,0:T(8,128)(2,1)S(1)}, bf16[8,448]{1,0:T(8,128)(2,1)}, u32[]{:S(2)}) copy-start(bf16[8,448]{1,0:T(8,128)(2,1)} %copy-done.6) | copy-start | bytes 21508
  71.8 12.2 %copy-start.9 = (bf16[8,448]{1,0:T(8,128)(2,1)S(1)}, bf16[8,448]{1,0:T(8,128)(2,1)}, u32[]{:S(2)}) copy-start(bf16[8,448]{1,0:T(8,128)(2,1)} %copy-done.8) | copy-start | bytes 21508
  83.9 7.9 %copy-start.3 = (bf16[1,448,1792]{2,1,0:T(8,128)(2,1)S(1)}, bf16[1,448,1792]{2,1,0:T(8,128)(2,1)}, u32[]{:S(2)}) copy-start(bf16[1,448,1792]{2,1,0:T(8,128)(2,1)} %param.32) | copy-start | bytes 4816900
  95.1 5.1 %collective-permute-start.18 = (f32[8,448]{1,0:T(8,128)S(1)}, f32[8,448]{1,0:T(8,128)S(1)}, u32[]{:S(2)}, u32[]{:S(2)}) collective-permute-start(f32[8,448]{1,0:T(8,128)S(1)} %get-tuple-element.608), channel_id=1, source_target_pairs={{0,1},{1,2},{2,3},{3,0},{4,5},{5,6},{6,7},{7,4},{8,9},{9,10},{10,1... | collective-permute-start | bytes 43016 | tf_op jit(solution)/shard_map/ppermute | solution.py:22
  96.1 4.1 %collective-permute-start.19 = (f32[8,448]{1,0:T(8,128)S(1)}, f32[8,448]{1,0:T(8,128)S(1)}, u32[]{:S(2)}, u32[]{:S(2)}) collective-permute-start(f32[8,448]{1,0:T(8,128)S(1)} %get-tuple-element.610), channel_id=1, source_target_pairs={{0,3},{1,0},{2,1},{3,2},{4,7},{5,4},{6,5},{7,6},{8,11},{9,8},{10,9... | collective-permute-start | bytes 43016 | tf_op jit(solution)/shard_map/ppermute | solution.py:22
  97.8 4.1 %collective-permute-start.20 = (f32[8,448]{1,0:T(8,128)S(1)}, f32[8,448]{1,0:T(8,128)S(1)}, u32[]{:S(2)}, u32[]{:S(2)}) collective-permute-start(f32[8,448]{1,0:T(8,128)S(1)} %get-tuple-element.609), channel_id=1, source_target_pairs={{0,2},{1,3},{2,0},{3,1},{4,6},{5,7},{6,4},{7,5},{8,10},{9,11},{10,... | collective-permute-start | bytes 43016 | tf_op jit(solution)/shard_map/ppermute | solution.py:22
  98.0 2.1 %collective-permute-start.7 = (bf16[8,448]{1,0:T(8,128)(2,1)S(1)}, bf16[8,448]{1,0:T(8,128)(2,1)S(1)}, u32[]{:S(2)}, u32[]{:S(2)}) collective-permute-start(bf16[8,448]{1,0:T(8,128)(2,1)S(1)} %constant_dynamic-slice_fusion), channel_id=1, source_target_pairs={{128,0},{129,1},{130,2},{131,3},{132,4},{133,5},{134,6},{135,7},{1... | collective-permute-start | bytes 21512 | tf_op jit(solution)/shard_map/ppermute | solution.py:272

commit v2 on v0

v2 whole, which is shorter than its diff:
```python
import jax
import jax.numpy as jnp
from jax import lax
from jax.experimental import pallas as pl
from jax.experimental.pallas import tpu as pltpu
from jax.sharding import PartitionSpec as P

HD = 112
FEAT = 16
WINDOW = 64
PAGE = 128
HALF = 64
XN = 4
ZN = 8
LANES = 512
GROUPS = 32
TAYLOR = 273
TAYLOR_LANES = 384
SPREAD = 1152

EPSILON = 1e-06
MASKED = -1e30


def head_shift(value, steps):
    count = lax.axis_size("head")
    return lax.ppermute(value, "head", [(i, (i + steps) % count) for i in range(count)])


def x_shift(value, steps):
    return lax.ppermute(
        value,
        "req",
        [(z * XN + i, z * XN + (i + steps) % XN) for z in range(ZN) for i in range(XN)],
    )


def z_shift(value, steps):
    base = XN * ZN
    return lax.ppermute(
        value,
        ("section", "req"),
        [
            (base + z * XN + i, base + ((z + steps) % ZN) * XN + i)
            for z in range(ZN)
            for i in range(XN)
        ],
    )


def section_swap(value, steps):
    count = lax.axis_size("head")
    there = [(i, count + (i + steps) % count) for i in range(count)]
    return lax.ppermute(value, ("section", "head"), there + [(b, a) for a, b in there])


VMEM = pl.BlockSpec(memory_space=pltpu.VMEM)
SMEM = pl.BlockSpec(memory_space=pltpu.SMEM)
HBM = pl.BlockSpec(memory_space=pl.ANY)
FLAT = (((1,), (1,)), ((), ()))


def normed_rows(values, gain_row):
    factor = lax.rsqrt(jnp.mean(values * values, axis=-1, keepdims=True) + EPSILON)
    return (values * factor * gain_row).astype(jnp.bfloat16)


def lanes_of(shape):
    return lax.broadcasted_iota(jnp.int32, shape, len(shape) - 1)


def in_head(lane, h):
    return (lane >= h * HD) & (lane < (h + 1) * HD)


def kernel_call(kernel, section, name, out_shape, in_specs, scratch_shapes, args, vmem=24 << 20):
    def run(ids, *refs):
        @pl.when(ids[0] == section)
        def _():
            kernel(ids, *refs)

    return pl.pallas_call(
        run,
        out_shape=out_shape,
        in_specs=[SMEM] + in_specs,
        out_specs=jax.tree.map(lambda _: VMEM, out_shape),
        scratch_shapes=scratch_shapes,
        compiler_params=pltpu.CompilerParams(vmem_limit_bytes=vmem),
        name=name,
    )(*args)


def expansion(features, width, repeat):
    lane = lax.broadcasted_iota(jnp.int32, (features, 2 * width), 1)
    source = lax.broadcasted_iota(jnp.int32, (features, 2 * width), 0)
    left = lane < width
    at = jnp.where(left, lane, lane - width) >> (repeat.bit_length() - 1)
    linear = left & (at > 0) & (at <= FEAT) & (source == at - 1)
    pair = at - (FEAT + 1)
    wanted = jnp.where(left, pair >> 4, pair & (FEAT - 1))
    quad = (pair >= 0) & (pair < FEAT * FEAT) & (source == wanted)
    return jnp.where(linear | quad, 1.0, 0.0).astype(jnp.bfloat16)


def taylor_rows(left, right, feature):
    scale = FEAT ** (-0.25)
    left, right = left * scale, right * scale
    return jnp.where(
        feature == 0, 1.0, jnp.where(feature <= FEAT, left, left * right * 0.5**0.5)
    )


def linear_kernel(
    ids,
    t0,
    t1,
    t2,
    t3,
    gain,
    conv_w,
    conv_state,
    lin_norm,
    feature_w,
    value_w,
    out_w,
    state_hbm,
    update,
    state,
    sem,
):
    rows, share = t0.shape
    heads = share // HD
    span = TAYLOR * heads
    copy = pltpu.make_async_copy(state_hbm, state, sem)
    copy.start()
    by_state = expansion(128, SPREAD, heads)
    by_norm = expansion(128, TAYLOR_LANES, 1)
    expand = jnp.concatenate([by_state, by_norm], axis=1)

    own = ids[2]
    got = [ref[...].astype(jnp.float32) for ref in (t0, t1, t3, t2)]
    whole = []
    for place in range(heads):
        piece = got[0]
        for back in range(1, heads):
            piece = jnp.where(((own - back) & (heads - 1)) == place, got[back], piece)
        whole.append(piece)
    tokens = jnp.concatenate(whole, axis=1)
    normed = normed_rows(tokens, gain[...])
    feats = jnp.dot(normed, feature_w[...], preferred_element_type=jnp.float32)
    by_head = jnp.concatenate(
        [feats] + [pltpu.roll(feats, 128 - 2 * FEAT * h, 1) for h in range(1, heads)], axis=0
    )
    high = by_head.astype(jnp.bfloat16)
    rest = by_head - high.astype(jnp.float32)
    middle = rest.astype(jnp.bfloat16)
    low = (rest - middle.astype(jnp.float32)).astype(jnp.bfloat16)
    spread = jnp.dot(
        jnp.concatenate([high, middle, low], axis=0), expand, preferred_element_type=jnp.float32
    )
    count = heads * rows
    spread = spread[:count] + spread[count : 2 * count] + spread[2 * count :]
    lane = lanes_of((count, SPREAD))
    head = lax.broadcasted_iota(jnp.int32, (count, SPREAD), 0) >> 3
    query_wide = taylor_rows(spread[:, :SPREAD], spread[:, SPREAD : 2 * SPREAD], lane >> 2)
    query_wide = jnp.where(((lane & (heads - 1)) == head) & (lane < span), query_wide, 0.0)
    query_feats = taylor_rows(
        spread[:, 2 * SPREAD : 2 * SPREAD + TAYLOR_LANES],
        spread[:, 2 * SPREAD + TAYLOR_LANES :],
        lanes_of((count, TAYLOR_LANES)),
    )[:, :TAYLOR]
    both = by_head * pltpu.roll(by_head, 128 - FEAT, 1)
    near = jnp.sum(
        jnp.where(lanes_of(both.shape) < FEAT, both, 0.0), axis=-1, keepdims=True
    ) * FEAT ** (-0.5)
    intersection = 1.0 + near + 0.5 * near * near

    fresh = lax.dot_general(normed, value_w[0], FLAT, preferred_element_type=jnp.float32)
    older = conv_state[...].astype(jnp.float32)
    mixed = conv_w[0:1] * older[:, 0] + conv_w[1:2] * older[:, 1] + conv_w[2:3] * fresh

    length = span + 12
    queries = []
    for shift in range(0, 16, 4):
        moved = query_wide if shift == 0 else pltpu.roll(query_wide, shift, 1)
        queries.append(moved[:, :length].astype(jnp.bfloat16))
    row = lax.broadcasted_iota(jnp.int32, (count, HD), 0) & (rows - 1)
    found = jnp.zeros((count, HD), jnp.float32)
    copy.wait()
    for r in range(rows):
        first = span * r
        shift = first % 16
        product = jnp.dot(
            queries[shift // 4],
            state[first - shift : first - shift + length, :],
            preferred_element_type=jnp.float32,
        )
        found = jnp.where(row == r, product, found)
    total = tokens * 0.25
    for h in range(heads):
        here = slice(h * rows, (h + 1) * rows)
        denominator = (
            jnp.sum(query_feats[here] * lin_norm[:, h, :], axis=-1, keepdims=True)
            + intersection[here]
        )
        attended = (
            (found[here] + intersection[here] * mixed[:, h * HD : (h + 1) * HD]) / denominator
        ).astype(jnp.bfloat16)
        total = total + jnp.dot(
            attended, out_w[0, h * HD : (h + 1) * HD, :], preferred_element_type=jnp.float32
        )
    update[...] = total


def linear_layer(ids, pieces, gain, feature_w, value_w, out_w, conv_w, conv_state, state, norm):
    rows = pieces[0].shape[0]
    return kernel_call(
        linear_kernel,
        0,
        "linear_layer",
        jax.ShapeDtypeStruct((rows, out_w.shape[2]), jnp.float32),
        [VMEM] * 11 + [HBM],
        [pltpu.VMEM(state.shape, jnp.bfloat16), pltpu.SemaphoreType.DMA],
        (ids, *pieces, gain, conv_w, conv_state, norm, feature_w, value_w, out_w, state),
    )


def project_kernel(
    ids, table, lengths, p0, p1, p2, p3, gain, qk_w, v_w, one, asked, key_new, value_new
):
    rows, share = one.shape
    heads = share // HD
    layer_one = (p0[...] + p1[...] + p2[...] + p3[...]).astype(jnp.bfloat16)
    rounded = layer_one.astype(jnp.float32)
    mine = rounded[:, :share]
    for h in range(1, heads):
        mine = jnp.where(ids[2] == h, rounded[:, h * share : (h + 1) * share], mine)
    one[...] = mine.astype(jnp.bfloat16)
    normed = normed_rows(rounded, gain[...])
    query_key = jnp.dot(normed, qk_w[...], preferred_element_type=jnp.float32)
    width = query_key.shape[1]
    lane = lanes_of((rows, LANES))
    query = jnp.where(in_head(lane, 0), query_key[:, :LANES], 0.0)
    key = query
    for h in range(heads):
        if h:
            moved = pltpu.roll(query_key, width - h * HD, 1)[:, :LANES]
            query = jnp.where(in_head(lane, h), moved, query)
        moved = pltpu.roll(query_key, width - (h + 1) * HD, 1)[:, :LANES]
        key = jnp.where(in_head(lane, h), moved, key)
    row = lax.broadcasted_iota(jnp.int32, (rows, LANES), 0)
    for r in range(rows):
        group = table[r, 0].astype(jnp.float32)
        start = jnp.minimum(lengths[r] - WINDOW, PAGE).astype(jnp.float32)
        query = jnp.where((row == r) & (lane == share), group, query)
        query = jnp.where((row == r) & (lane == share + 1), start, query)
    asked[...] = query.astype(jnp.bfloat16)
    key_new[...] = key[:, :share].astype(jnp.bfloat16)
    value_new[...] = lax.dot_general(
        normed, v_w[0], FLAT, preferred_element_type=jnp.float32
    ).astype(jnp.bfloat16)


def project(ids, table, lengths, pieces, gain, query_key_w, value_w):
    rows = pieces[0].shape[0]
    share = value_w.shape[1]
    return kernel_call(
        project_kernel,
        1,
        "project",
        [
            jax.ShapeDtypeStruct((rows, share), jnp.bfloat16),
            jax.ShapeDtypeStruct((rows, LANES), jnp.bfloat16),
            jax.ShapeDtypeStruct((rows, share), jnp.bfloat16),
            jax.ShapeDtypeStruct((rows, share), jnp.bfloat16),
        ],
        [SMEM] * 2 + [VMEM] * 7,
        [],
        (ids, table, lengths, *pieces, gain, query_key_w, value_w),
    )


def own_kernel(
    ids,
    table,
    lengths,
    asked,
    key_new,
    value_new,
    own_pages,
    summed_out,
    highest_out,
    total_out,
    pages,
    sems,
):
    rows, share = key_new.shape
    count = own_pages.shape[0]
    bounds = []
    copies = []
    for r in range(rows):
        length = lengths[r]
        first = jnp.maximum((length - WINDOW) // PAGE, 1)
        last = jnp.maximum((length - 2) // PAGE, 1)
        bounds.append((length, first, last))
        for slot, logical in enumerate((first, last)):
            page = jnp.clip(table[r, logical] - GROUPS - ids[1] * count, 0, count - 1)
            copies.append(
                pltpu.make_async_copy(own_pages.at[page], pages.at[r, slot], sems.at[r, slot])
            )
            copies[-1].start()
    head = lax.broadcasted_iota(jnp.int32, (8, share), 0)
    lane = lanes_of((8, share))
    mine = (lane >= head * HD) & (lane < (head + 1) * HD)
    token = lanes_of((8, 2 * PAGE))
    scale = HD ** (-0.5)
    query = asked[:, :share].astype(jnp.float32)
    new_key = key_new[...].astype(jnp.float32)
    new_value = value_new[...].astype(jnp.float32)
    for r in range(rows):
        query_here = jnp.where(mine, query[r : r + 1], 0.0)
        new_score = jnp.sum(query_here * new_key[r : r + 1], axis=-1, keepdims=True) * scale
        low = query_here.astype(jnp.bfloat16)
        copies[2 * r].wait()
        copies[2 * r + 1].wait()
        scores = (
            jnp.concatenate(
                [
                    jnp.dot(low, pages[r, slot, 0], preferred_element_type=jnp.float32)
                    for slot in range(2)
                ],
                axis=1,
            )
            * scale
        )
        length, first, last = bounds[r]
        position = jnp.where(
            token < PAGE,
            first * PAGE + token,
            jnp.where(last != first, last * PAGE + token - PAGE, -1),
        )
        usable = (position >= length - WINDOW) & (position <= length - 2)
        scores = jnp.where(usable, scores, MASKED)
        highest = jnp.maximum(jnp.max(scores, axis=-1, keepdims=True), new_score)
        exps = jnp.where(usable, jnp.exp(scores - highest), 0.0)
        exp_new = jnp.exp(new_score - highest)
        total = jnp.sum(exps, axis=-1, keepdims=True) + exp_new
        exps = exps.astype(jnp.bfloat16)
        found = exp_new * new_value[r : r + 1]
        for slot in range(2):
            found = found + lax.dot_general(
                exps[:, slot * PAGE : (slot + 1) * PAGE],
                pages[r, slot, 1],
                FLAT,
                preferred_element_type=jnp.float32,
            )
        for ref, value in ((summed_out, found), (highest_out, highest), (total_out, total)):
            ref[r : r + 1, :] = jnp.sum(jnp.where(mine, value, 0.0), axis=0, keepdims=True)


def own_attention(ids, table, lengths, asked, key_new, value_new, own_pages):
    rows, share = key_new.shape
    return kernel_call(
        own_kernel,
        1,
        "own_attention",
        [jax.ShapeDtypeStruct((rows, share), jnp.float32)] * 3,
        [SMEM] * 2 + [VMEM] * 3 + [HBM],
        [
            pltpu.VMEM((rows, 2) + own_pages.shape[1:], jnp.bfloat16),
            pltpu.SemaphoreType.DMA((rows, 2)),
        ],
        (ids, table, lengths, asked, key_new, value_new, own_pages),
    )


def prompt_kernel(ids, a0, a1, a2, a3, near_pages, above, below, o0, o1, o2, o3):
    rows = a0.shape[0]
    share = near_pages.shape[1]
    heads = share // HD
    pages = jnp.concatenate(
        [near_pages[i] for i in range(3)]
        + [above[i] for i in range(3)]
        + [below[i] for i in range(2)],
        axis=1,
    )
    asked = jnp.concatenate([ref[...].astype(jnp.float32) for ref in (a0, a1, a2, a3)], axis=0)
    count = asked.shape[0]
    lane = lanes_of(asked.shape)
    group = jnp.sum(jnp.where(lane == share, asked, 0.0), axis=-1, keepdims=True)
    start = jnp.sum(jnp.where(lane == share + 1, asked, 0.0), axis=-1, keepdims=True)
    group, start = group.astype(jnp.int32), start.astype(jnp.int32)
    query = jnp.concatenate(
        [jnp.where(in_head(lane, h), asked, 0.0)[:, :share] for h in range(heads)], axis=0
    ).astype(jnp.bfloat16)
    scores = jnp.dot(query, pages, preferred_element_type=jnp.float32) * HD ** (-0.5)
    token = lanes_of((count, ZN * PAGE))
    z, x = ids[1] // XN, ids[1] % XN
    slot_group = (((token >> 7) + (z + ZN - 1)) & (ZN - 1)) * XN + x
    offset = token & (PAGE - 1)
    usable = (slot_group == group) & (offset < HALF) & (offset + HALF >= start)
    lane = lanes_of((count, share))
    stat_lane = lanes_of((count, 128))
    weights = []
    stats = jnp.zeros((count, 128), jnp.float32)
    for h in range(heads):
        here = jnp.where(usable, scores[h * count : (h + 1) * count], MASKED)
        highest = jnp.max(here, axis=-1, keepdims=True)
        exps = jnp.where(usable, jnp.exp(here - highest), 0.0)
        total = jnp.sum(exps, axis=-1, keepdims=True)
        stats = jnp.where(stat_lane == h, highest, stats)
        stats = jnp.where(stat_lane == heads + h, total, stats)
        weights.append(pltpu.roll(exps, HALF, 1))
    found = lax.dot_general(
        jnp.concatenate(weights, axis=0).astype(jnp.bfloat16),
        pages,
        FLAT,
        preferred_element_type=jnp.float32,
    )
    summed = jnp.zeros((count, share), jnp.float32)
    for h in range(heads):
        summed = jnp.where(in_head(lane, h), found[h * count : (h + 1) * count], summed)
    for at, ref in enumerate((o0, o1, o2, o3)):
        ref[:, :share] = summed[at * rows : (at + 1) * rows]
        ref[:, share:LANES] = jnp.zeros((rows, LANES - share), jnp.float32)
        ref[:, LANES:] = stats[at * rows : (at + 1) * rows]


def prompt_attention(ids, asked, near_pages, above, below):
    rows = asked[0].shape[0]
    return kernel_call(
        prompt_kernel,
        1,
        "prompt_attention",
        [jax.ShapeDtypeStruct((rows, LANES + 128), jnp.float32)] * 4,
        [VMEM] * 7,
        [],
        (ids, *asked, near_pages, above, below),
    )


def combine_kernel(ids, summed, highest, total, r0, r1, r2, r3, out_w, s0, s1, s2, s3):
    rows, share = summed.shape
    heads = share // HD
    refs = (r0, r1, r2, r3)
    prompt_summed = sum(ref[:, :share] for ref in refs)
    stats = [ref[:, LANES:] for ref in refs]
    top = jnp.maximum(jnp.maximum(stats[0], stats[1]), jnp.maximum(stats[2], stats[3]))
    added = stats[0] + stats[1] + stats[2] + stats[3]
    lane = lanes_of((rows, share))
    prompt_highest = jnp.zeros((rows, share), jnp.float32)
    prompt_total = jnp.zeros((rows, share), jnp.float32)
    for h in range(heads):
        here = in_head(lane, h)
        prompt_highest = jnp.where(here, top[:, h : h + 1], prompt_highest)
        prompt_total = jnp.where(here, added[:, heads + h : heads + h + 1], prompt_total)
    peak = jnp.maximum(highest[...], prompt_highest)
    own_factor = jnp.exp(highest[...] - peak)
    prompt_factor = jnp.exp(prompt_highest - peak)
    whole = total[...] * own_factor + prompt_total * prompt_factor
    attended = (summed[...] * own_factor + prompt_summed * prompt_factor) / whole
    second = jnp.dot(attended.astype(jnp.bfloat16), out_w[0], preferred_element_type=jnp.float32)
    for steps, ref in enumerate((s0, s1, s2, s3)):
        slab = second[:, :share]
        for h in range(1, heads):
            slab = jnp.where(
                ((ids[2] + steps) & (heads - 1)) == h, second[:, h * share : (h + 1) * share], slab
            )
        ref[...] = slab


def combine(ids, own, parts, out_w):
    return kernel_call(
        combine_kernel,
        1,
        "combine",
        [jax.ShapeDtypeStruct(own[0].shape, jnp.float32)] * 4,
        [VMEM] * 8,
        [],
        (ids, *own, *parts, out_w),
    )


def body(
    tokens,
    norm_gain,
    feature_w,
    query_key_w,
    value_w,
    out_w,
    conv_w,
    conv_state,
    lin_state,
    lin_norm,
    own_pages,
    prompt_pages,
    page_table,
    lengths,
):
    section_index = lax.axis_index("section")
    ids = jnp.stack([section_index, lax.axis_index("req"), lax.axis_index("head")])
    value_w = value_w.transpose(0, 2, 1)
    lin_state = lin_state.transpose(0, 2, 1, 3).reshape(-1, HD)
    own_pages = own_pages.transpose(0, 1, 3, 2)
    prompt_pages = prompt_pages.transpose(0, 1, 3, 2)

    received = [head_shift(tokens, k) for k in (1, 3, 2)]
    page = jnp.concatenate([prompt_pages[0, 0, :, HALF:], prompt_pages[0, 1, :, HALF:]], axis=1)
    near_pages = jnp.stack([z_shift(page, 1), page, z_shift(page, -1)])
    near_pages, received = lax.optimization_barrier((near_pages, received))
    above = z_shift(near_pages, -3)
    below = z_shift(near_pages[1:], 3)

    update = linear_layer(
        ids,
        [tokens] + received,
        norm_gain,
        feature_w,
        value_w,
        out_w,
        conv_w,
        conv_state,
        lin_state,
        lin_norm,
    )
    swapped = [section_swap(update, k) for k in (0, 1, 3, 2)]
    one_share, packed, key_new, value_new = project(
        ids, page_table, lengths, swapped, norm_gain, query_key_w, value_w
    )
    asked = [packed] + [x_shift(packed, k) for k in (1, 3, 2)]
    own = own_attention(ids, page_table, lengths, packed, key_new, value_new, own_pages)
    answers = prompt_attention(ids, asked, near_pages, above, below)
    parts = [answers[0]] + [x_shift(answers[at], -k) for at, k in ((1, 1), (2, 3), (3, 2))]
    slabs = combine(ids, own, parts, out_w)
    one_back = lax.ppermute(one_share, "section", [(1, 0)])
    total = one_share.astype(jnp.float32) + slabs[0]
    for piece in [head_shift(slabs[k], k) for k in (1, 3, 2)]:
        total = total + piece
    output = jnp.where(section_index == 0, one_back, total.astype(jnp.bfloat16))
    return output[None]


def solution(mesh):
    placed = (
        P("req", "head"),
        P("section", None),
        P(None, "head"),
        P(None, "head"),
        P("section", None, "head"),
        P("section", "head", None),
        P(None, "head"),
        P("req", None, "head"),
        P("req", "head", None, None),
        P("req", "head", None),
        P("req", None, None, "head"),
        P("req", None, None, "head"),
        P("req", None),
        P("req"),
    )
    return jax.shard_map(
        body, mesh=mesh, in_specs=placed, out_specs=P("section", "req", "head"), check_vma=False
    )
```

time: 345 us -> 68.8 us (0.20)
  waiting for transfers between devices: 161 us -> 10.7 us
  local copies, waits for them, and re-layouts: 99.9 us -> 4.33 us
  starting transfers between devices: 2.7 us -> 37.8 us
  blocking collectives: 28.6 us -> 0 us
  other arithmetic: 18.5 us -> 0.94 us
  matrix products: 17.3 us -> 0 us
  Pallas kernels: 0 us -> 14.4 us
  between operations: 13.3 us -> 0.3 us
    all_gather x1 -> x0, waiting for transfers between devices: 87.2 us -> none  [body(): prompt_source = lax.all_gather(prompt_pages, 'req', axis=0, tiled=True)]
    unnamed x7 -> x0, waiting for transfers between devices: 68 us -> none
    gather x24 -> x0, local copies, waits for them, and re-layouts: 42.9 us -> none  [the longest x6 27.5 us: window_local(): own_rows = jnp.take(own_pages, own_ids, axis=0)]
    ppermute x2 -> x21, starting transfers between devices: 2.57 us -> 37.8 us  [the longest x4 17.3 us: z_shift(): lax.ppermute(value, ('section', 'req'), [(base + z * XN + i, base + (z +...]
    all_gather x3 -> x0, blocking collectives: 28.6 us -> none  [body(): whole = lax.all_gather(rows_in, 'head', axis=1, tiled=True)]
    another operation x6 -> x0, local copies, waits for them, and re-layouts: 19.6 us -> none
    squeeze x6 -> x1, local copies, waits for them, and re-layouts: 19.1 us -> 1.22 us  [body(): prompt_pages[0, 0, :, HALF:]]
    dot_general x21 -> x0, matrix products: 17.3 us -> none  [the longest x3 5.46 us: window_local(): jnp.dot(normed, query_key_w, preferred_element_type=jnp.float32)]
  transfers between devices with their start and end apart: 6 -> 21, of which waited for: 6 -> 7; matrix products, arithmetic and copies ran while one was open for 1% -> 0% of each run, Pallas kernels for 0% -> 17%
where the time goes in v2:
time: 68.8 us; the launch traced here: 68.6 us
  starting transfers between devices  37.8 us (55%)
  Pallas kernels  14.4 us (21%)
  waiting for transfers between devices  10.7 us (16%)
  local copies, waits for them, and re-layouts  4.33 us (6%)
  other arithmetic  0.94 us (1%)
    ppermute x4, starting transfers between devices, z_shift(): lax.ppermute(value, ('section', 'req'), [(base + z * XN + i, base + (z +...  17.3 us
    pallas_call x5, Pallas kernels, kernel_call(): pl.pallas_call(run, out_shape=out_shape, in_specs=[SMEM] + in_specs, out_...  14.4 us
    ppermute x6, starting transfers between devices, head_shift(): lax.ppermute(value, 'head', [(i, (i + steps) % count) for i in range(coun...  7.91 us
    ppermute x6, starting transfers between devices, x_shift(): lax.ppermute(value, 'req', [(z * XN + i, z * XN + (i + steps) % XN) for z...  7.31 us
    ppermute x4, starting transfers between devices, section_swap(): lax.ppermute(value, ('section', 'head'), there + [(b, a) for a, b in there])  4.01 us
    ppermute x6, waiting for transfers between devices, head_shift(): lax.ppermute(value, 'head', [(i, (i + steps) % count) for i in range(coun...  3.76 us
    ppermute x4, waiting for transfers between devices, section_swap(): lax.ppermute(value, ('section', 'head'), there + [(b, a) for a, b in there])  3.69 us
    unnamed x28, local copies, waits for them, and re-layouts  3.09 us
  transfers between devices with their start and end apart: 21, of which 7 were waited for; matrix products, arithmetic and copies ran while one was open for 0% of the time, Pallas kernels for 17%

profile of v2, /device:TPU:1, one launch (start us, length us, event | category | flops | bytes accessed | tf_op | source)
XLA Modules:
  0.0 68.6 jit_solution(7538220180636733419)
XLA Ops:
  0.0 1.2 %slice_bitcast_fusion.1 = (bf16[448,64]{1,0:T(8,128)(2,1)S(1)}, bf16[448,64]{1,0:T(8,128)(2,1)S(1)}) fusion(bf16[1,2,448,128]{3,2,1,0:T(8,128)(2,1)} %bitcast.23), kind=kLoop, calls=%fused_computation.2 | loop fusion | bytes 229376 | tf_op jit(solution)/shard_map/squeeze | solution.py:508
  1.3 0.1 pad_maximum_fusion.1
  1.4 4.4 %collective-permute-start = (bf16[448,128]{1,0:T(8,128)(2,1)S(1)}, bf16[448,128]{1,0:T(8,128)(2,1)S(1)}, u32[]{:S(2)}, u32[]{:S(2)}) collective-permute-start(bf16[448,128]{1,0:T(8,128)(2,1)S(1)} %pad_maximum_fusion.1), channel_id=1, source_target_pairs={{128,144},{132,148},{136,152},{140,156},{144,160},{148,164},{152,1... | collective-permute-start | bytes 344072 | tf_op jit(solution)/shard_map/ppermute | solution.py:40
  5.8 5.9 %collective-permute-start.1 = (bf16[448,128]{1,0:T(8,128)(2,1)S(1)}, bf16[448,128]{1,0:T(8,128)(2,1)S(1)}, u32[]{:S(2)}, u32[]{:S(2)}) collective-permute-start(bf16[448,128]{1,0:T(8,128)(2,1)S(1)} %pad_maximum_fusion.1), channel_id=1, source_target_pairs={{128,240},{132,244},{136,248},{140,252},{144,128},{148,132},{152,1... | collective-permute-start | bytes 344072 | tf_op jit(solution)/shard_map/ppermute | solution.py:40
  11.6 1.4 %collective-permute-start.2 = (bf16[8,448]{1,0:T(8,128)(2,1)}, bf16[8,448]{1,0:T(8,128)(2,1)S(1)}, u32[]{:S(2)}, u32[]{:S(2)}) collective-permute-start(bf16[8,448]{1,0:T(8,128)(2,1)} %refs_0_.3), channel_id=1, source_target_pairs={{0,1},{1,2},{2,3},{3,0},{4,5},{5,6},{6,7},{7,4},{8,9},{9,10},{10,1... | collective-permute-start | bytes 21512 | tf_op jit(solution)/shard_map/ppermute | solution.py:27
  13.0 1.5 %collective-permute-start.3 = (bf16[8,448]{1,0:T(8,128)(2,1)}, bf16[8,448]{1,0:T(8,128)(2,1)S(1)}, u32[]{:S(2)}, u32[]{:S(2)}) collective-permute-start(bf16[8,448]{1,0:T(8,128)(2,1)} %refs_0_.3), channel_id=1, source_target_pairs={{0,3},{1,0},{2,1},{3,2},{4,7},{5,4},{6,5},{7,6},{8,11},{9,8},{10,9... | collective-permute-start | bytes 21512 | tf_op jit(solution)/shard_map/ppermute | solution.py:27
  14.5 1.6 %collective-permute-start.4 = (bf16[8,448]{1,0:T(8,128)(2,1)}, bf16[8,448]{1,0:T(8,128)(2,1)S(1)}, u32[]{:S(2)}, u32[]{:S(2)}) collective-permute-start(bf16[8,448]{1,0:T(8,128)(2,1)} %refs_0_.3), channel_id=1, source_target_pairs={{0,2},{1,3},{2,0},{3,1},{4,6},{5,7},{6,4},{7,5},{8,10},{9,11},{10,... | collective-permute-start | bytes 21512 | tf_op jit(solution)/shard_map/ppermute | solution.py:27
  16.1 0.1 fusion.2
  16.2 0.0 collective-permute-done
  16.2 0.0 collective-permute-done.1
  16.3 0.0 collective-permute-done.3.refs_2_
  16.3 2.5 %collective-permute-done.4.refs_3_ = bf16[8,448]{1,0:T(8,128)(2,1)S(1)} collective-permute-done((bf16[8,448]{1,0:T(8,128)(2,1)}, bf16[8,448]{1,0:T(8,128)(2,1)S(1)}, u32[]{:S(2)}, u32[]{:S(2)}) %collective-permute-start.4) | collective-permute-done | bytes 7200 | tf_op jit(solution)/shard_map/ppermute | solution.py:27
  18.8 4.2 %collective-permute-start.13 = (bf16[3,448,128]{2,1,0:T(8,128)(2,1)S(1)}, bf16[3,448,128]{2,1,0:T(8,128)(2,1)S(1)}, u32[]{:S(2)}, u32[]{:S(2)}) collective-permute-start(bf16[3,448,128]{2,1,0:T(8,128)(2,1)S(1)} %pad_maximum_fusion.refs_4_), channel_id=1, source_target_pairs={{128,208},{132,212},{136,216},{140,220},{144,224},{148,228},{152,2... | collective-permute-start | bytes 1032200 | tf_op jit(solution)/shard_map/ppermute | solution.py:40
  23.0 2.8 %collective-permute-start.14 = (bf16[2,448,128]{2,1,0:T(8,128)(2,1)S(1)}, bf16[2,448,128]{2,1,0:T(8,128)(2,1)S(1)}, u32[]{:S(2)}, u32[]{:S(2)}) collective-permute-start(bf16[2,448,128]{2,1,0:T(8,128)(2,1)S(1)} %slice.11), channel_id=1, source_target_pairs={{128,176},{132,180},{136,184},{140,188},{144,192},{148,196},{152,2... | collective-permute-start | bytes 688136 | tf_op jit(solution)/shard_map/ppermute | solution.py:40
  25.9 0.1 pad_add_fusion.ids
  26.0 0.0 copy-start.1
  26.0 1.4 %copy-done.1 = bf16[1,448,1792]{2,1,0:T(8,128)(2,1)S(1)} copy-done((bf16[1,448,1792]{2,1,0:T(8,128)(2,1)S(1)}, bf16[1,448,1792]{2,1,0:T(8,128)(2,1)}, u32[]{:S(2)}) %copy-start.1) | copy-done | bytes 1605656
  27.4 1.6 %copy-done.5 = bf16[8,4,273,112]{3,1,2,0:T(4,128)(2,1)S(1)} copy-done((bf16[8,4,273,112]{3,1,2,0:T(4,128)(2,1)S(1)}, bf16[8,4,273,112]{3,1,2,0:T(4,128)(2,1)}, u32[]{:S(2)}) %copy-start.5) | copy-done | bytes 1956888
  29.1 0.6 linear_layer.1
  29.6 0.0 copy-start.3
  29.6 0.1 collective-permute-start.5
  29.7 1.8 %collective-permute-start.6 = (f32[8,1792]{1,0:T(8,128)S(1)}, f32[8,1792]{1,0:T(8,128)S(1)}, u32[]{:S(2)}, u32[]{:S(2)}) collective-permute-start(f32[8,1792]{1,0:T(8,128)S(1)} %linear_layer.1), channel_id=1, source_target_pairs={{0,129},{1,130},{2,131},{3,128},{129,0},{130,1},{131,2},{128,3},{4... | collective-permute-start | bytes 172040 | tf_op jit(solution)/shard_map/ppermute | solution.py:54
  31.5 2.2 %collective-permute-start.8 = (f32[8,1792]{1,0:T(8,128)S(1)}, f32[8,1792]{1,0:T(8,128)S(1)}, u32[]{:S(2)}, u32[]{:S(2)}) collective-permute-start(f32[8,1792]{1,0:T(8,128)S(1)} %linear_layer.1), channel_id=1, source_target_pairs={{0,130},{1,131},{2,128},{3,129},{130,0},{131,1},{128,2},{129,3},{4... | collective-permute-start | bytes 172040 | tf_op jit(solution)/shard_map/ppermute | solution.py:54
  33.7 1.3 %collective-permute-done.6.refs_3_ = f32[8,1792]{1,0:T(8,128)S(1)} collective-permute-done((f32[8,1792]{1,0:T(8,128)S(1)}, f32[8,1792]{1,0:T(8,128)S(1)}, u32[]{:S(2)}, u32[]{:S(2)}) %collective-permute-start.6) | collective-permute-done | bytes 57376 | tf_op jit(solution)/shard_map/ppermute | solution.py:54
  35.0 0.6 collective-permute-done.7.refs_4_
  35.6 1.8 %collective-permute-done.8.refs_5_ = f32[8,1792]{1,0:T(8,128)S(1)} collective-permute-done((f32[8,1792]{1,0:T(8,128)S(1)}, f32[8,1792]{1,0:T(8,128)S(1)}, u32[]{:S(2)}, u32[]{:S(2)}) %collective-permute-start.8) | collective-permute-done | bytes 57376 | tf_op jit(solution)/shard_map/ppermute | solution.py:54
  37.4 1.7 %project.1 = (bf16[8,448]{1,0:T(8,128)(2,1)S(1)}, bf16[8,512]{1,0:T(8,128)(2,1)S(1)}, bf16[8,448]{1,0:T(8,128)(2,1)S(1)}, bf16[8,448]{1,0:T(8,128)(2,1)S(1)}) custom-call(s32[3]{0:T(128)S(1)} %pad_add_fusion.ids, s32[8,256]{1,0:T(8,128)S(1)} %copy-done.8, s32[8]{0:T(128)S(1)} %copy-done.13, f32[8,1792]{1,0:T(8,128)S(1)} %collective-permute-done.5.refs_2_, ...), custom_call_target="tpu_custom_call" | custom-call | tf_op jit(solution)/shard_map/project/pallas_call | solution.py:82
  39.1 1.2 %collective-permute-start.10 = (bf16[8,512]{1,0:T(8,128)(2,1)S(1)}, bf16[8,512]{1,0:T(8,128)(2,1)S(1)}, u32[]{:S(2)}, u32[]{:S(2)}) collective-permute-start(bf16[8,512]{1,0:T(8,128)(2,1)S(1)} %get-tuple-element.28.refs_2_.refs_0_), channel_id=1, source_target_pairs={{0,4},{4,8},{8,12},{12,0},{16,20},{20,24},{24,28},{28,16},{32,36},... | collective-permute-start | bytes 24584 | tf_op jit(solution)/shard_map/ppermute | solution.py:31
  40.3 1.5 %collective-permute-start.11 = (bf16[8,512]{1,0:T(8,128)(2,1)S(1)}, bf16[8,512]{1,0:T(8,128)(2,1)S(1)}, u32[]{:S(2)}, u32[]{:S(2)}) collective-permute-start(bf16[8,512]{1,0:T(8,128)(2,1)S(1)} %get-tuple-element.28.refs_2_.refs_0_), channel_id=1, source_target_pairs={{0,12},{4,0},{8,4},{12,8},{16,28},{20,16},{24,20},{28,24},{32,44},... | collective-permute-start | bytes 24584 | tf_op jit(solution)/shard_map/ppermute | solution.py:31
  41.8 1.5 %collective-permute-start.12 = (bf16[8,512]{1,0:T(8,128)(2,1)S(1)}, bf16[8,512]{1,0:T(8,128)(2,1)S(1)}, u32[]{:S(2)}, u32[]{:S(2)}) collective-permute-start(bf16[8,512]{1,0:T(8,128)(2,1)S(1)} %get-tuple-element.28.refs_2_.refs_0_), channel_id=1, source_target_pairs={{0,8},{4,12},{8,0},{12,4},{16,24},{20,28},{24,16},{28,20},{32,40},... | collective-permute-start | bytes 24584 | tf_op jit(solution)/shard_map/ppermute | solution.py:31
  43.3 2.5 %collective-permute-done.12.refs_3_ = bf16[8,512]{1,0:T(8,128)(2,1)S(1)} collective-permute-done((bf16[8,512]{1,0:T(8,128)(2,1)S(1)}, bf16[8,512]{1,0:T(8,128)(2,1)S(1)}, u32[]{:S(2)}, u32[]{:S(2)}) %collective-permute-start.12) | collective-permute-done | bytes 8224 | tf_op jit(solution)/shard_map/ppermute | solution.py:31
  45.8 0.0 collective-permute-done.14.refs_6_
  45.8 0.0 collective-permute-done.13.refs_5_
  45.8 1.5 %prompt_attention.1 = (f32[8,640]{1,0:T(8,128)S(1)}, f32[8,640]{1,0:T(8,128)S(1)}, f32[8,640]{1,0:T(8,128)S(1)}, f32[8,640]{1,0:T(8,128)S(1)}) custom-call(s32[3]{0:T(128)S(1)} %pad_add_fusion.ids, bf16[8,512]{1,0:T(8,128)(2,1)S(1)} %get-tuple-element.28.refs_2_.refs_0_, bf16[8,512]{1,0:T(8,128)(2,1)S(1)} %collective-permute-done.10.refs_1_, ...), custom_call_target="tpu_custom_call" | custom-call | tf_op jit(solution)/shard_map/prompt_attention/pallas_call | solution.py:82
  47.3 1.3 %collective-permute-start.15 = (f32[8,640]{1,0:T(8,128)S(1)}, f32[8,640]{1,0:T(8,128)S(1)}, u32[]{:S(2)}, u32[]{:S(2)}) collective-permute-start(f32[8,640]{1,0:T(8,128)S(1)} %get-tuple-element.36), channel_id=1, source_target_pairs={{0,12},{4,0},{8,4},{12,8},{16,28},{20,16},{24,20},{28,24},{32,44},... | collective-permute-start | bytes 61448 | tf_op jit(solution)/shard_map/ppermute | solution.py:31
  48.6 0.2 collective-permute-start.16
  48.8 1.5 %collective-permute-start.17 = (f32[8,640]{1,0:T(8,128)S(1)}, f32[8,640]{1,0:T(8,128)S(1)}, u32[]{:S(2)}, u32[]{:S(2)}) collective-permute-start(f32[8,640]{1,0:T(8,128)S(1)} %get-tuple-element.38), channel_id=1, source_target_pairs={{0,8},{4,12},{8,0},{12,4},{16,24},{20,28},{24,16},{28,20},{32,40},... | collective-permute-start | bytes 61448 | tf_op jit(solution)/shard_map/ppermute | solution.py:31
  50.3 9.6 %own_attention.1 = (f32[8,448]{1,0:T(8,128)S(1)}, f32[8,448]{1,0:T(8,128)S(1)}, f32[8,448]{1,0:T(8,128)S(1)}) custom-call(s32[3]{0:T(128)S(1)} %pad_add_fusion.ids, s32[8,256]{1,0:T(8,128)S(1)} %copy-done.8, s32[8]{0:T(128)S(1)} %copy-done.13, bf16[8,512]{1,0:T(8,128)(2,1)S(1)} %get-tuple-element.28.refs_2_.refs_0_, ...), custom_call_target="tpu_custom_call" | custom-call | tf_op jit(solution)/shard_map/own_attention/pallas_call | solution.py:82
  59.9 0.0 collective-permute-done.15.refs_4_
  60.0 0.0 collective-permute-done.16.refs_5_
  60.0 1.1 %combine.1 = (f32[8,448]{1,0:T(8,128)S(1)}, f32[8,448]{1,0:T(8,128)S(1)}, f32[8,448]{1,0:T(8,128)S(1)}, f32[8,448]{1,0:T(8,128)S(1)}) custom-call(s32[3]{0:T(128)S(1)} %pad_add_fusion.ids, f32[8,448]{1,0:T(8,128)S(1)} %get-tuple-element.31.refs_0_, f32[8,448]{1,0:T(8,128)S(1)} %get-tuple-element.32.refs_1_, f32[8,448]{1,0:T(8,128)S(1)} %get-tuple-element.33.refs_2_, ...), custom_call_target="tpu_custom_call" | custom-call | tf_op jit(solution)/shard_map/combine/pallas_call | solution.py:82
  61.1 0.8 %collective-permute-start.18 = (f32[8,448]{1,0:T(8,128)S(1)}, f32[8,448]{1,0:T(8,128)S(1)}, u32[]{:S(2)}, u32[]{:S(2)}) collective-permute-start(f32[8,448]{1,0:T(8,128)S(1)} %get-tuple-element.40), channel_id=1, source_target_pairs={{0,1},{1,2},{2,3},{3,0},{4,5},{5,6},{6,7},{7,4},{8,9},{9,10},{10,1... | collective-permute-start | bytes 43016 | tf_op jit(solution)/shard_map/ppermute | solution.py:27
  61.9 2.0 %collective-permute-start.19 = (f32[8,448]{1,0:T(8,128)S(1)}, f32[8,448]{1,0:T(8,128)S(1)}, u32[]{:S(2)}, u32[]{:S(2)}) collective-permute-start(f32[8,448]{1,0:T(8,128)S(1)} %get-tuple-element.41), channel_id=1, source_target_pairs={{0,3},{1,0},{2,1},{3,2},{4,7},{5,4},{6,5},{7,6},{8,11},{9,8},{10,9... | collective-permute-start | bytes 43016 | tf_op jit(solution)/shard_map/ppermute | solution.py:27
  63.9 0.7 %collective-permute-start.20 = (f32[8,448]{1,0:T(8,128)S(1)}, f32[8,448]{1,0:T(8,128)S(1)}, u32[]{:S(2)}, u32[]{:S(2)}) collective-permute-start(f32[8,448]{1,0:T(8,128)S(1)} %get-tuple-element.42), channel_id=1, source_target_pairs={{0,2},{1,3},{2,0},{3,1},{4,6},{5,7},{6,4},{7,5},{8,10},{9,11},{10,... | collective-permute-start | bytes 43016 | tf_op jit(solution)/shard_map/ppermute | solution.py:27
  64.6 1.3 %collective-permute-start.9 = (bf16[8,448]{1,0:T(8,128)(2,1)S(1)}, bf16[8,448]{1,0:T(8,128)(2,1)S(1)}, u32[]{:S(2)}, u32[]{:S(2)}) collective-permute-start(bf16[8,448]{1,0:T(8,128)(2,1)S(1)} %get-tuple-element.27), channel_id=1, source_target_pairs={{128,0},{129,1},{130,2},{131,3},{132,4},{133,5},{134,6},{135,7},{1... | collective-permute-start | bytes 21512 | tf_op jit(solution)/shard_map/ppermute | solution.py:535
  65.8 0.8 %collective-permute-done.9 = bf16[8,448]{1,0:T(8,128)(2,1)S(1)} collective-permute-done((bf16[8,448]{1,0:T(8,128)(2,1)S(1)}, bf16[8,448]{1,0:T(8,128)(2,1)S(1)}, u32[]{:S(2)}, u32[]{:S(2)}) %collective-permute-start.9) | collective-permute-done | bytes 7200 | tf_op jit(solution)/shard_map/ppermute | solution.py:535
  66.7 1.3 %collective-permute-done.20 = f32[8,448]{1,0:T(8,128)S(1)} collective-permute-done((f32[8,448]{1,0:T(8,128)S(1)}, f32[8,448]{1,0:T(8,128)S(1)}, u32[]{:S(2)}, u32[]{:S(2)}) %collective-permute-start.20) | collective-permute-done | bytes 14368 | tf_op jit(solution)/shard_map/ppermute | solution.py:27
  67.9 0.6 fusion.1
  (34 shorter events, 0.1 us)
Async XLA Ops:
  0.0 26.0 %copy-start.11 = (bf16[8,448]{1,0:T(8,128)(2,1)S(1)}, bf16[8,448]{1,0:T(8,128)(2,1)}, u32[]{:S(2)}) copy-start(bf16[8,448]{1,0:T(8,128)(2,1)} %refs_0_.3) | copy-start | bytes 21508
  0.0 26.0 %copy-start = (bf16[1,1792,448]{1,2,0:T(8,128)(2,1)S(1)}, bf16[1,1792,448]{1,2,0:T(8,128)(2,1)}, u32[]{:S(2)}) copy-start(bf16[1,1792,448]{1,2,0:T(8,128)(2,1)} %param.18) | copy-start | bytes 4816900
  0.0 26.0 %copy-start.9 = (f32[1,1792]{1,0:T(1,128)S(1)}, f32[1,1792]{1,0:T(1,128)}, u32[]{:S(2)}) copy-start(f32[1,1792]{1,0:T(1,128)} %refs_6_.3) | copy-start | bytes 21508
  0.0 26.0 %copy-start.6 = (bf16[1792,128]{1,0:T(8,128)(2,1)S(1)}, bf16[1792,128]{1,0:T(8,128)(2,1)}, u32[]{:S(2)}) copy-start(bf16[1792,128]{1,0:T(8,128)(2,1)} %refs_8_.1) | copy-start | bytes 1376260
  0.0 26.0 %copy-start.12 = (f32[3,448]{1,0:T(4,128)S(1)}, f32[3,448]{1,0:T(4,128)}, u32[]{:S(2)}) copy-start(f32[3,448]{1,0:T(4,128)} %refs_5_.1) | copy-start | bytes 16132
  0.0 26.0 %copy-start.10 = (bf16[8,2,448]{2,1,0:T(2,128)(2,1)S(1)}, bf16[8,2,448]{2,1,0:T(2,128)(2,1)}, u32[]{:S(2)}) copy-start(bf16[8,2,448]{2,1,0:T(2,128)(2,1)} %refs_6_.2) | copy-start | bytes 43012
  0.0 26.0 %copy-start.7 = (f32[8,4,273]{2,1,0:T(4,128)S(1)}, f32[8,4,273]{2,1,0:T(4,128)}, u32[]{:S(2)}) copy-start(f32[8,4,273]{2,1,0:T(4,128)} %refs_7_.3) | copy-start | bytes 104836
  1.4 14.8 %collective-permute-start = (bf16[448,128]{1,0:T(8,128)(2,1)S(1)}, bf16[448,128]{1,0:T(8,128)(2,1)S(1)}, u32[]{:S(2)}, u32[]{:S(2)}) collective-permute-start(bf16[448,128]{1,0:T(8,128)(2,1)S(1)} %pad_maximum_fusion.1), channel_id=1, source_target_pairs={{128,144},{132,148},{136,152},{140,156},{144,160},{148,164},{152,1... | collective-permute-start | bytes 344072 | tf_op jit(solution)/shard_map/ppermute | solution.py:40
  5.8 10.4 %collective-permute-start.1 = (bf16[448,128]{1,0:T(8,128)(2,1)S(1)}, bf16[448,128]{1,0:T(8,128)(2,1)S(1)}, u32[]{:S(2)}, u32[]{:S(2)}) collective-permute-start(bf16[448,128]{1,0:T(8,128)(2,1)S(1)} %pad_maximum_fusion.1), channel_id=1, source_target_pairs={{128,240},{132,244},{136,248},{140,252},{144,128},{148,132},{152,1... | collective-permute-start | bytes 344072 | tf_op jit(solution)/shard_map/ppermute | solution.py:40
  11.6 4.6 %collective-permute-start.2 = (bf16[8,448]{1,0:T(8,128)(2,1)}, bf16[8,448]{1,0:T(8,128)(2,1)S(1)}, u32[]{:S(2)}, u32[]{:S(2)}) collective-permute-start(bf16[8,448]{1,0:T(8,128)(2,1)} %refs_0_.3), channel_id=1, source_target_pairs={{0,1},{1,2},{2,3},{3,0},{4,5},{5,6},{6,7},{7,4},{8,9},{9,10},{10,1... | collective-permute-start | bytes 21512 | tf_op jit(solution)/shard_map/ppermute | solution.py:27
  13.0 3.3 %collective-permute-start.3 = (bf16[8,448]{1,0:T(8,128)(2,1)}, bf16[8,448]{1,0:T(8,128)(2,1)S(1)}, u32[]{:S(2)}, u32[]{:S(2)}) collective-permute-start(bf16[8,448]{1,0:T(8,128)(2,1)} %refs_0_.3), channel_id=1, source_target_pairs={{0,3},{1,0},{2,1},{3,2},{4,7},{5,4},{6,5},{7,6},{8,11},{9,8},{10,9... | collective-permute-start | bytes 21512 | tf_op jit(solution)/shard_map/ppermute | solution.py:27
  14.5 4.2 %collective-permute-start.4 = (bf16[8,448]{1,0:T(8,128)(2,1)}, bf16[8,448]{1,0:T(8,128)(2,1)S(1)}, u32[]{:S(2)}, u32[]{:S(2)}) collective-permute-start(bf16[8,448]{1,0:T(8,128)(2,1)} %refs_0_.3), channel_id=1, source_target_pairs={{0,2},{1,3},{2,0},{3,1},{4,6},{5,7},{6,4},{7,5},{8,10},{9,11},{10,... | collective-permute-start | bytes 21512 | tf_op jit(solution)/shard_map/ppermute | solution.py:27
  18.8 27.0 %collective-permute-start.13 = (bf16[3,448,128]{2,1,0:T(8,128)(2,1)S(1)}, bf16[3,448,128]{2,1,0:T(8,128)(2,1)S(1)}, u32[]{:S(2)}, u32[]{:S(2)}) collective-permute-start(bf16[3,448,128]{2,1,0:T(8,128)(2,1)S(1)} %pad_maximum_fusion.refs_4_), channel_id=1, source_target_pairs={{128,208},{132,212},{136,216},{140,220},{144,224},{148,228},{152,2... | collective-permute-start | bytes 1032200 | tf_op jit(solution)/shard_map/ppermute | solution.py:40
  23.0 22.7 %collective-permute-start.14 = (bf16[2,448,128]{2,1,0:T(8,128)(2,1)S(1)}, bf16[2,448,128]{2,1,0:T(8,128)(2,1)S(1)}, u32[]{:S(2)}, u32[]{:S(2)}) collective-permute-start(bf16[2,448,128]{2,1,0:T(8,128)(2,1)S(1)} %slice.11), channel_id=1, source_target_pairs={{128,176},{132,180},{136,184},{140,188},{144,192},{148,196},{152,2... | collective-permute-start | bytes 688136 | tf_op jit(solution)/shard_map/ppermute | solution.py:40
  26.0 1.4 %copy-start.1 = (bf16[1,448,1792]{2,1,0:T(8,128)(2,1)S(1)}, bf16[1,448,1792]{2,1,0:T(8,128)(2,1)}, u32[]{:S(2)}) copy-start(bf16[1,448,1792]{2,1,0:T(8,128)(2,1)} %refs_7_.5) | copy-start | bytes 4816900
  27.4 1.6 %copy-start.5 = (bf16[8,4,273,112]{3,1,2,0:T(4,128)(2,1)S(1)}, bf16[8,4,273,112]{3,1,2,0:T(4,128)(2,1)}, u32[]{:S(2)}) copy-start(bf16[8,4,273,112]{3,1,2,0:T(4,128)(2,1)} %param.22) | copy-start | bytes 5870596
  29.1 8.3 %copy-start.4 = (bf16[1792,896]{1,0:T(8,128)(2,1)S(1)}, bf16[1792,896]{1,0:T(8,128)(2,1)}, u32[]{:S(2)}) copy-start(bf16[1792,896]{1,0:T(8,128)(2,1)} %refs_7_.4) | copy-start | bytes 9633796
  29.1 8.3 %copy-start.8 = (s32[8,256]{1,0:T(8,128)S(1)}, s32[8,256]{1,0:T(8,128)}, u32[]{:S(2)}) copy-start(s32[8,256]{1,0:T(8,128)} %refs_0_.5) | copy-start | bytes 24580
  29.1 8.3 %copy-start.13 = (s32[8]{0:T(128)S(1)}, s32[8]{0:T(128)}, u32[]{:S(2)}) copy-start(s32[8]{0:T(128)} %refs_1_.3) | copy-start | bytes 100
  29.6 20.7 %copy-start.3 = (bf16[16,2,128,448]{2,3,1,0:T(8,128)(2,1)S(1)}, bf16[16,2,128,448]{2,3,1,0:T(8,128)(2,1)}, u32[]{:S(2)}) copy-start(bf16[16,2,128,448]{2,3,1,0:T(8,128)(2,1)} %param.24) | copy-start | bytes 11010052
  29.6 1.9 %collective-permute-start.5 = (f32[8,1792]{1,0:T(8,128)S(1)}, f32[8,1792]{1,0:T(8,128)S(1)}, u32[]{:S(2)}, u32[]{:S(2)}) collective-permute-start(f32[8,1792]{1,0:T(8,128)S(1)} %linear_layer.1), channel_id=1, source_target_pairs={{0,128},{1,129},{2,130},{3,131},{128,0},{129,1},{130,2},{131,3},{4... | collective-permute-start | bytes 172040 | tf_op jit(solution)/shard_map/ppermute | solution.py:54
  29.7 5.3 %collective-permute-start.6 = (f32[8,1792]{1,0:T(8,128)S(1)}, f32[8,1792]{1,0:T(8,128)S(1)}, u32[]{:S(2)}, u32[]{:S(2)}) collective-permute-start(f32[8,1792]{1,0:T(8,128)S(1)} %linear_layer.1), channel_id=1, source_target_pairs={{0,129},{1,130},{2,131},{3,128},{129,0},{130,1},{131,2},{128,3},{4... | collective-permute-start | bytes 172040 | tf_op jit(solution)/shard_map/ppermute | solution.py:54
  31.5 4.0 %collective-permute-start.7 = (f32[8,1792]{1,0:T(8,128)S(1)}, f32[8,1792]{1,0:T(8,128)S(1)}, u32[]{:S(2)}, u32[]{:S(2)}) collective-permute-start(f32[8,1792]{1,0:T(8,128)S(1)} %linear_layer.1), channel_id=1, source_target_pairs={{0,131},{1,128},{2,129},{3,130},{131,0},{128,1},{129,2},{130,3},{4... | collective-permute-start | bytes 172040 | tf_op jit(solution)/shard_map/ppermute | solution.py:54
  31.5 5.8 %collective-permute-start.8 = (f32[8,1792]{1,0:T(8,128)S(1)}, f32[8,1792]{1,0:T(8,128)S(1)}, u32[]{:S(2)}, u32[]{:S(2)}) collective-permute-start(f32[8,1792]{1,0:T(8,128)S(1)} %linear_layer.1), channel_id=1, source_target_pairs={{0,130},{1,131},{2,128},{3,129},{130,0},{131,1},{128,2},{129,3},{4... | collective-permute-start | bytes 172040 | tf_op jit(solution)/shard_map/ppermute | solution.py:54
  39.1 20.9 %copy-start.2 = (bf16[1,448,1792]{2,1,0:T(8,128)(2,1)S(1)}, bf16[1,448,1792]{2,1,0:T(8,128)(2,1)}, u32[]{:S(2)}) copy-start(bf16[1,448,1792]{2,1,0:T(8,128)(2,1)} %refs_7_.5) | copy-start | bytes 4816900
  39.1 4.2 %collective-permute-start.10 = (bf16[8,512]{1,0:T(8,128)(2,1)S(1)}, bf16[8,512]{1,0:T(8,128)(2,1)S(1)}, u32[]{:S(2)}, u32[]{:S(2)}) collective-permute-start(bf16[8,512]{1,0:T(8,128)(2,1)S(1)} %get-tuple-element.28.refs_2_.refs_0_), channel_id=1, source_target_pairs={{0,4},{4,8},{8,12},{12,0},{16,20},{20,24},{24,28},{28,16},{32,36},... | collective-permute-start | bytes 24584 | tf_op jit(solution)/shard_map/ppermute | solution.py:31
  40.3 3.0 %collective-permute-start.11 = (bf16[8,512]{1,0:T(8,128)(2,1)S(1)}, bf16[8,512]{1,0:T(8,128)(2,1)S(1)}, u32[]{:S(2)}, u32[]{:S(2)}) collective-permute-start(bf16[8,512]{1,0:T(8,128)(2,1)S(1)} %get-tuple-element.28.refs_2_.refs_0_), channel_id=1, source_target_pairs={{0,12},{4,0},{8,4},{12,8},{16,28},{20,16},{24,20},{28,24},{32,44},... | collective-permute-start | bytes 24584 | tf_op jit(solution)/shard_map/ppermute | solution.py:31
  41.8 4.0 %collective-permute-start.12 = (bf16[8,512]{1,0:T(8,128)(2,1)S(1)}, bf16[8,512]{1,0:T(8,128)(2,1)S(1)}, u32[]{:S(2)}, u32[]{:S(2)}) collective-permute-start(bf16[8,512]{1,0:T(8,128)(2,1)S(1)} %get-tuple-element.28.refs_2_.refs_0_), channel_id=1, source_target_pairs={{0,8},{4,12},{8,0},{12,4},{16,24},{20,28},{24,16},{28,20},{32,40},... | collective-permute-start | bytes 24584 | tf_op jit(solution)/shard_map/ppermute | solution.py:31
  47.3 12.7 %collective-permute-start.15 = (f32[8,640]{1,0:T(8,128)S(1)}, f32[8,640]{1,0:T(8,128)S(1)}, u32[]{:S(2)}, u32[]{:S(2)}) collective-permute-start(f32[8,640]{1,0:T(8,128)S(1)} %get-tuple-element.36), channel_id=1, source_target_pairs={{0,12},{4,0},{8,4},{12,8},{16,28},{20,16},{24,20},{28,24},{32,44},... | collective-permute-start | bytes 61448 | tf_op jit(solution)/shard_map/ppermute | solution.py:31
  48.6 11.4 %collective-permute-start.16 = (f32[8,640]{1,0:T(8,128)S(1)}, f32[8,640]{1,0:T(8,128)S(1)}, u32[]{:S(2)}, u32[]{:S(2)}) collective-permute-start(f32[8,640]{1,0:T(8,128)S(1)} %get-tuple-element.37), channel_id=1, source_target_pairs={{0,4},{4,8},{8,12},{12,0},{16,20},{20,24},{24,28},{28,16},{32,36},... | collective-permute-start | bytes 61448 | tf_op jit(solution)/shard_map/ppermute | solution.py:31
  48.8 11.2 %collective-permute-start.17 = (f32[8,640]{1,0:T(8,128)S(1)}, f32[8,640]{1,0:T(8,128)S(1)}, u32[]{:S(2)}, u32[]{:S(2)}) collective-permute-start(f32[8,640]{1,0:T(8,128)S(1)} %get-tuple-element.38), channel_id=1, source_target_pairs={{0,8},{4,12},{8,0},{12,4},{16,24},{20,28},{24,16},{28,20},{32,40},... | collective-permute-start | bytes 61448 | tf_op jit(solution)/shard_map/ppermute | solution.py:31
  61.1 5.6 %collective-permute-start.18 = (f32[8,448]{1,0:T(8,128)S(1)}, f32[8,448]{1,0:T(8,128)S(1)}, u32[]{:S(2)}, u32[]{:S(2)}) collective-permute-start(f32[8,448]{1,0:T(8,128)S(1)} %get-tuple-element.40), channel_id=1, source_target_pairs={{0,1},{1,2},{2,3},{3,0},{4,5},{5,6},{6,7},{7,4},{8,9},{9,10},{10,1... | collective-permute-start | bytes 43016 | tf_op jit(solution)/shard_map/ppermute | solution.py:27
  61.9 4.8 %collective-permute-start.19 = (f32[8,448]{1,0:T(8,128)S(1)}, f32[8,448]{1,0:T(8,128)S(1)}, u32[]{:S(2)}, u32[]{:S(2)}) collective-permute-start(f32[8,448]{1,0:T(8,128)S(1)} %get-tuple-element.41), channel_id=1, source_target_pairs={{0,3},{1,0},{2,1},{3,2},{4,7},{5,4},{6,5},{7,6},{8,11},{9,8},{10,9... | collective-permute-start | bytes 43016 | tf_op jit(solution)/shard_map/ppermute | solution.py:27
  63.9 4.1 %collective-permute-start.20 = (f32[8,448]{1,0:T(8,128)S(1)}, f32[8,448]{1,0:T(8,128)S(1)}, u32[]{:S(2)}, u32[]{:S(2)}) collective-permute-start(f32[8,448]{1,0:T(8,128)S(1)} %get-tuple-element.42), channel_id=1, source_target_pairs={{0,2},{1,3},{2,0},{3,1},{4,6},{5,7},{6,4},{7,5},{8,10},{9,11},{10,... | collective-permute-start | bytes 43016 | tf_op jit(solution)/shard_map/ppermute | solution.py:27
  64.6 2.1 %collective-permute-start.9 = (bf16[8,448]{1,0:T(8,128)(2,1)S(1)}, bf16[8,448]{1,0:T(8,128)(2,1)S(1)}, u32[]{:S(2)}, u32[]{:S(2)}) collective-permute-start(bf16[8,448]{1,0:T(8,128)(2,1)S(1)} %get-tuple-element.27), channel_id=1, source_target_pairs={{128,0},{129,1},{130,2},{131,3},{132,4},{133,5},{134,6},{135,7},{1... | collective-permute-start | bytes 21512 | tf_op jit(solution)/shard_map/ppermute | solution.py:535

commit v3 on v2

--- a/solution.py
+++ b/solution.py
@@ -10,10 +10,11 @@
 WINDOW = 64
 PAGE = 128
 HALF = 64
+MAXP = 256
+GROUPS = 32
 XN = 4
 ZN = 8
 LANES = 512
-GROUPS = 32
 TAYLOR = 273
 TAYLOR_LANES = 384
 SPREAD = 1152
@@ -27,21 +28,28 @@
     return lax.ppermute(value, "head", [(i, (i + steps) % count) for i in range(count)])
 
 
-def x_shift(value, steps):
+def token_shift(value, steps):
+    count = lax.axis_size("head")
+    return lax.ppermute(
+        value, ("section", "head"), [(i, (i + steps) % count) for i in range(count)]
+    )
+
+
+def z_shift(value, steps):
     return lax.ppermute(
         value,
         "req",
-        [(z * XN + i, z * XN + (i + steps) % XN) for z in range(ZN) for i in range(XN)],
-    )
-
-
-def z_shift(value, steps):
+        [(z * XN + i, (z + steps) % ZN * XN + i) for z in range(ZN) for i in range(XN)],
+    )
+
+
+def page_shift(value, z_steps, x_steps):
     base = XN * ZN
     return lax.ppermute(
         value,
         ("section", "req"),
         [
-            (base + z * XN + i, base + ((z + steps) % ZN) * XN + i)
+            (base + z * XN + i, base + (z + z_steps) % ZN * XN + (i + x_steps) % XN)
             for z in range(ZN)
             for i in range(XN)
         ],
@@ -56,7 +64,7 @@
 
 VMEM = pl.BlockSpec(memory_space=pltpu.VMEM)
 SMEM = pl.BlockSpec(memory_space=pltpu.SMEM)
-HBM = pl.BlockSpec(memory_space=pl.ANY)
+HBM = pl.BlockSpec(memory_space=pltpu.HBM)
 FLAT = (((1,), (1,)), ((), ()))
 
 
@@ -73,19 +81,32 @@
     return (lane >= h * HD) & (lane < (h + 1) * HD)
 
 
-def kernel_call(kernel, section, name, out_shape, in_specs, scratch_shapes, args, vmem=24 << 20):
-    def run(ids, *refs):
+def place():
+    return lax.axis_index("section"), lax.axis_index("req"), lax.axis_index("head")
+
+
+def kernel_call(
+    kernel, section, name, out_shape, in_specs, scratch_shapes, args, vmem=24 << 20, cost=None
+):
+    def run(*refs):
+        ids = place()
+
         @pl.when(ids[0] == section)
         def _():
             kernel(ids, *refs)
 
+    args = [
+        pltpu.with_memory_space_constraint(arg, pltpu.HBM) if spec is HBM else arg
+        for arg, spec in zip(args, in_specs, strict=True)
+    ]
     return pl.pallas_call(
         run,
         out_shape=out_shape,
-        in_specs=[SMEM] + in_specs,
+        in_specs=in_specs,
         out_specs=jax.tree.map(lambda _: VMEM, out_shape),
         scratch_shapes=scratch_shapes,
         compiler_params=pltpu.CompilerParams(vmem_limit_bytes=vmem),
+        cost_estimate=cost,
         name=name,
     )(*args)
 
@@ -112,31 +133,57 @@
 
 def linear_kernel(
     ids,
-    t0,
     t1,
     t2,
     t3,
+    t0_hbm,
+    gain_hbm,
+    feature_hbm,
+    state_hbm,
+    norm_hbm,
+    conv_w_hbm,
+    conv_state_hbm,
+    value_hbm,
+    out_hbm,
+    update,
+    t0,
     gain,
+    feature_w,
+    state,
+    lin_norm,
     conv_w,
     conv_state,
-    lin_norm,
-    feature_w,
     value_w,
     out_w,
-    state_hbm,
-    update,
-    state,
-    sem,
+    sems,
 ):
     rows, share = t0.shape
     heads = share // HD
     span = TAYLOR * heads
-    copy = pltpu.make_async_copy(state_hbm, state, sem)
-    copy.start()
+    copies = [
+        pltpu.make_async_copy(source, target, sems.at[at])
+        for at, (source, target) in enumerate(
+            [
+                (t0_hbm, t0),
+                (gain_hbm, gain),
+                (feature_hbm, feature_w),
+                (state_hbm, state),
+                (norm_hbm, lin_norm),
+                (conv_w_hbm, conv_w),
+                (conv_state_hbm, conv_state),
+                (value_hbm.at[0], value_w),
+                (out_hbm.at[0], out_w),
+            ]
+        )
+    ]
+    for copy in copies:
+        copy.start()
     by_state = expansion(128, SPREAD, heads)
     by_norm = expansion(128, TAYLOR_LANES, 1)
     expand = jnp.concatenate([by_state, by_norm], axis=1)
 
+    for copy in copies[:3]:
+        copy.wait()
     own = ids[2]
     got = [ref[...].astype(jnp.float32) for ref in (t0, t1, t3, t2)]
     whole = []
@@ -175,10 +222,6 @@
     ) * FEAT ** (-0.5)
     intersection = 1.0 + near + 0.5 * near * near
 
-    fresh = lax.dot_general(normed, value_w[0], FLAT, preferred_element_type=jnp.float32)
-    older = conv_state[...].astype(jnp.float32)
-    mixed = conv_w[0:1] * older[:, 0] + conv_w[1:2] * older[:, 1] + conv_w[2:3] * fresh
-
     length = span + 12
     queries = []
     for shift in range(0, 16, 4):
@@ -186,7 +229,7 @@
         queries.append(moved[:, :length].astype(jnp.bfloat16))
     row = lax.broadcasted_iota(jnp.int32, (count, HD), 0) & (rows - 1)
     found = jnp.zeros((count, HD), jnp.float32)
-    copy.wait()
+    copies[3].wait()
     for r in range(rows):
         first = span * r
         shift = first % 16
@@ -196,7 +239,13 @@
             preferred_element_type=jnp.float32,
         )
         found = jnp.where(row == r, product, found)
+    for copy in copies[4:8]:
+        copy.wait()
+    fresh = lax.dot_general(normed, value_w[...], FLAT, preferred_element_type=jnp.float32)
+    older = conv_state[...].astype(jnp.float32)
+    mixed = conv_w[0:1] * older[:, 0] + conv_w[1:2] * older[:, 1] + conv_w[2:3] * fresh
     total = tokens * 0.25
+    copies[8].wait()
     for h in range(heads):
         here = slice(h * rows, (h + 1) * rows)
         denominator = (
@@ -207,28 +256,53 @@
             (found[here] + intersection[here] * mixed[:, h * HD : (h + 1) * HD]) / denominator
         ).astype(jnp.bfloat16)
         total = total + jnp.dot(
-            attended, out_w[0, h * HD : (h + 1) * HD, :], preferred_element_type=jnp.float32
+            attended, out_w[h * HD : (h + 1) * HD, :], preferred_element_type=jnp.float32
         )
     update[...] = total
 
 
-def linear_layer(ids, pieces, gain, feature_w, value_w, out_w, conv_w, conv_state, state, norm):
+def linear_layer(pieces, gain, feature_w, value_w, out_w, conv_w, conv_state, state, norm):
     rows = pieces[0].shape[0]
+    near = (pieces[0], gain, feature_w, state, norm, conv_w, conv_state, value_w, out_w)
     return kernel_call(
         linear_kernel,
         0,
         "linear_layer",
         jax.ShapeDtypeStruct((rows, out_w.shape[2]), jnp.float32),
-        [VMEM] * 11 + [HBM],
-        [pltpu.VMEM(state.shape, jnp.bfloat16), pltpu.SemaphoreType.DMA],
-        (ids, *pieces, gain, conv_w, conv_state, norm, feature_w, value_w, out_w, state),
+        [VMEM] * 3 + [HBM] * len(near),
+        [
+            *(pltpu.VMEM(array.shape, array.dtype) for array in near[:-2]),
+            pltpu.VMEM(value_w.shape[1:], jnp.bfloat16),
+            pltpu.VMEM(out_w.shape[1:], jnp.bfloat16),
+            pltpu.SemaphoreType.DMA((len(near),)),
+        ],
+        (*pieces[1:], *near),
     )
 
 
 def project_kernel(
-    ids, table, lengths, p0, p1, p2, p3, gain, qk_w, v_w, one, asked, key_new, value_new
+    ids,
+    tags,
+    p0,
+    p1,
+    p2,
+    p3,
+    gain,
+    qk_hbm,
+    v_hbm,
+    one,
+    asked,
+    key_new,
+    value_new,
+    v_w,
+    qk_w,
+    sems,
 ):
     rows, share = one.shape
+    copy_value = pltpu.make_async_copy(v_hbm.at[0], v_w, sems.at[0])
+    copy_query = pltpu.make_async_copy(qk_hbm, qk_w, sems.at[1])
+    copy_value.start()
+    copy_query.start()
     heads = share // HD
     layer_one = (p0[...] + p1[...] + p2[...] + p3[...]).astype(jnp.bfloat16)
     rounded = layer_one.astype(jnp.float32)
@@ -237,6 +311,11 @@
         mine = jnp.where(ids[2] == h, rounded[:, h * share : (h + 1) * share], mine)
     one[...] = mine.astype(jnp.bfloat16)
     normed = normed_rows(rounded, gain[...])
+    copy_value.wait()
+    value_new[...] = lax.dot_general(
+        normed, v_w[...], FLAT, preferred_element_type=jnp.float32
+    ).astype(jnp.bfloat16)
+    copy_query.wait()
     query_key = jnp.dot(normed, qk_w[...], preferred_element_type=jnp.float32)
     width = query_key.shape[1]
     lane = lanes_of((rows, LANES))
@@ -248,20 +327,15 @@
             query = jnp.where(in_head(lane, h), moved, query)
         moved = pltpu.roll(query_key, width - (h + 1) * HD, 1)[:, :LANES]
         key = jnp.where(in_head(lane, h), moved, key)
-    row = lax.broadcasted_iota(jnp.int32, (rows, LANES), 0)
-    for r in range(rows):
-        group = table[r, 0].astype(jnp.float32)
-        start = jnp.minimum(lengths[r] - WINDOW, PAGE).astype(jnp.float32)
-        query = jnp.where((row == r) & (lane == share), group, query)
-        query = jnp.where((row == r) & (lane == share + 1), start, query)
+    group = tags[:, 0:1].astype(jnp.float32)
+    start = jnp.minimum(tags[:, 1:2] - WINDOW, PAGE).astype(jnp.float32)
+    query = jnp.where(lane == share, group, query)
+    query = jnp.where(lane == share + 1, start, query)
     asked[...] = query.astype(jnp.bfloat16)
     key_new[...] = key[:, :share].astype(jnp.bfloat16)
-    value_new[...] = lax.dot_general(
-        normed, v_w[0], FLAT, preferred_element_type=jnp.float32
-    ).astype(jnp.bfloat16)
-
-
-def project(ids, table, lengths, pieces, gain, query_key_w, value_w):
+
+
+def project(tags, pieces, gain, query_key_w, value_w):
     rows = pieces[0].shape[0]
     share = value_w.shape[1]
     return kernel_call(
@@ -274,9 +348,13 @@
             jax.ShapeDtypeStruct((rows, share), jnp.bfloat16),
             jax.ShapeDtypeStruct((rows, share), jnp.bfloat16),
         ],
-        [SMEM] * 2 + [VMEM] * 7,
-        [],
-        (ids, table, lengths, *pieces, gain, query_key_w, value_w),
+        [VMEM] * 6 + [HBM] * 2,
+        [
+            pltpu.VMEM(value_w.shape[1:], jnp.bfloat16),
+            pltpu.VMEM(query_key_w.shape, jnp.bfloat16),
+            pltpu.SemaphoreType.DMA((2,)),
+        ],
+        (tags, *pieces, gain, query_key_w, value_w),
     )
 
 
@@ -312,18 +390,31 @@
     head = lax.broadcasted_iota(jnp.int32, (8, share), 0)
     lane = lanes_of((8, share))
     mine = (lane >= head * HD) & (lane < (head + 1) * HD)
-    token = lanes_of((8, 2 * PAGE))
     scale = HD ** (-0.5)
     query = asked[:, :share].astype(jnp.float32)
     new_key = key_new[...].astype(jnp.float32)
     new_value = value_new[...].astype(jnp.float32)
+    wide = jnp.concatenate([jnp.where(mine, query[r : r + 1], 0.0) for r in range(rows)], axis=0)
+    keys = jnp.concatenate(
+        [jnp.broadcast_to(new_key[r : r + 1], (8, share)) for r in range(rows)], axis=0
+    )
+    new_score = jnp.sum(wide * keys, axis=-1, keepdims=True) * scale
+    token = lanes_of((8 * rows, 2 * PAGE))
+    request = lax.broadcasted_iota(jnp.int32, (8 * rows, 2 * PAGE), 0) >> 3
+    length = jnp.zeros(token.shape, jnp.int32)
+    base = jnp.zeros(token.shape, jnp.int32)
     for r in range(rows):
-        query_here = jnp.where(mine, query[r : r + 1], 0.0)
-        new_score = jnp.sum(query_here * new_key[r : r + 1], axis=-1, keepdims=True) * scale
-        low = query_here.astype(jnp.bfloat16)
+        length = jnp.where(request == r, bounds[r][0], length)
+        second = jnp.where(bounds[r][1] != bounds[r][2], bounds[r][2] - 1, -MAXP) * PAGE
+        base = jnp.where(request == r, jnp.where(token < PAGE, bounds[r][1] * PAGE, second), base)
+    position = base + token
+    usable = (position >= length - WINDOW) & (position <= length - 2)
+    scores = []
+    for r in range(rows):
+        low = wide[8 * r : 8 * r + 8].astype(jnp.bfloat16)
         copies[2 * r].wait()
         copies[2 * r + 1].wait()
-        scores = (
+        scores.append(
             jnp.concatenate(
                 [
                     jnp.dot(low, pages[r, slot, 0], preferred_element_type=jnp.float32)
@@ -331,34 +422,32 @@
                 ],
                 axis=1,
             )
-            * scale
         )
-        length, first, last = bounds[r]
-        position = jnp.where(
-            token < PAGE,
-            first * PAGE + token,
-            jnp.where(last != first, last * PAGE + token - PAGE, -1),
-        )
-        usable = (position >= length - WINDOW) & (position <= length - 2)
-        scores = jnp.where(usable, scores, MASKED)
-        highest = jnp.maximum(jnp.max(scores, axis=-1, keepdims=True), new_score)
-        exps = jnp.where(usable, jnp.exp(scores - highest), 0.0)
-        exp_new = jnp.exp(new_score - highest)
-        total = jnp.sum(exps, axis=-1, keepdims=True) + exp_new
-        exps = exps.astype(jnp.bfloat16)
-        found = exp_new * new_value[r : r + 1]
+    scores = jnp.where(usable, jnp.concatenate(scores, axis=0) * scale, MASKED)
+    highest = jnp.maximum(jnp.max(scores, axis=-1, keepdims=True), new_score)
+    exps = jnp.where(usable, jnp.exp(scores - highest), 0.0)
+    exp_new = jnp.exp(new_score - highest)
+    total = jnp.sum(exps, axis=-1, keepdims=True) + exp_new
+    for r in range(rows):
+        here = slice(8 * r, 8 * r + 8)
+        low = exps[here].astype(jnp.bfloat16)
+        found = exp_new[here] * new_value[r : r + 1]
         for slot in range(2):
             found = found + lax.dot_general(
-                exps[:, slot * PAGE : (slot + 1) * PAGE],
+                low[:, slot * PAGE : (slot + 1) * PAGE],
                 pages[r, slot, 1],
                 FLAT,
                 preferred_element_type=jnp.float32,
             )
-        for ref, value in ((summed_out, found), (highest_out, highest), (total_out, total)):
+        for ref, value in (
+            (summed_out, found),
+            (highest_out, highest[here]),
+            (total_out, total[here]),
+        ):
             ref[r : r + 1, :] = jnp.sum(jnp.where(mine, value, 0.0), axis=0, keepdims=True)
 
 
-def own_attention(ids, table, lengths, asked, key_new, value_new, own_pages):
+def own_attention(table, lengths, asked, key_new, value_new, own_pages):
     rows, share = key_new.shape
     return kernel_call(
         own_kernel,
@@ -370,19 +459,16 @@
             pltpu.VMEM((rows, 2) + own_pages.shape[1:], jnp.bfloat16),
             pltpu.SemaphoreType.DMA((rows, 2)),
         ],
-        (ids, table, lengths, asked, key_new, value_new, own_pages),
-    )
-
-
-def prompt_kernel(ids, a0, a1, a2, a3, near_pages, above, below, o0, o1, o2, o3):
+        (table, lengths, asked, key_new, value_new, own_pages),
+    )
+
+
+def prompt_kernel(ids, a0, a1, a2, a3, near_pages, far_pages, o0, o1, o2, o3):
     rows = a0.shape[0]
     share = near_pages.shape[1]
     heads = share // HD
     pages = jnp.concatenate(
-        [near_pages[i] for i in range(3)]
-        + [above[i] for i in range(3)]
-        + [below[i] for i in range(2)],
-        axis=1,
+        [near_pages[i] for i in range(XN)] + [far_pages[i] for i in range(XN)], axis=1
     )
     asked = jnp.concatenate([ref[...].astype(jnp.float32) for ref in (a0, a1, a2, a3)], axis=0)
     count = asked.shape[0]
@@ -394,9 +480,11 @@
         [jnp.where(in_head(lane, h), asked, 0.0)[:, :share] for h in range(heads)], axis=0
     ).astype(jnp.bfloat16)
     scores = jnp.dot(query, pages, preferred_element_type=jnp.float32) * HD ** (-0.5)
-    token = lanes_of((count, ZN * PAGE))
+    token = lanes_of((count, 2 * XN * PAGE))
     z, x = ids[1] // XN, ids[1] % XN
-    slot_group = (((token >> 7) + (z + ZN - 1)) & (ZN - 1)) * XN + x
+    slot = token >> 7
+    slot_group = jnp.where(slot < XN, z, (z + ZN // 2) & (ZN - 1)) * XN
+    slot_group = slot_group + ((slot + x + XN - 1) & (XN - 1))
     offset = token & (PAGE - 1)
     usable = (slot_group == group) & (offset < HALF) & (offset + HALF >= start)
     lane = lanes_of((count, share))
@@ -426,16 +514,16 @@
         ref[:, LANES:] = stats[at * rows : (at + 1) * rows]
 
 
-def prompt_attention(ids, asked, near_pages, above, below):
+def prompt_attention(asked, near_pages, far_pages):
     rows = asked[0].shape[0]
     return kernel_call(
         prompt_kernel,
         1,
         "prompt_attention",
         [jax.ShapeDtypeStruct((rows, LANES + 128), jnp.float32)] * 4,
-        [VMEM] * 7,
+        [VMEM] * 6,
         [],
-        (ids, *asked, near_pages, above, below),
+        (*asked, near_pages, far_pages),
     )
 
 
@@ -469,7 +557,7 @@
         ref[...] = slab
 
 
-def combine(ids, own, parts, out_w):
+def combine(own, parts, out_w):
     return kernel_call(
         combine_kernel,
         1,
@@ -477,7 +565,30 @@
         [jax.ShapeDtypeStruct(own[0].shape, jnp.float32)] * 4,
         [VMEM] * 8,
         [],
-        (ids, *own, *parts, out_w),
+        (*own, *parts, out_w),
+    )
+
+
+def page_kernel(ids, pages_hbm, page, pages, sem):
+    copy = pltpu.make_async_copy(pages_hbm.at[0], pages, sem)
+    copy.start()
+    copy.wait()
+    lane = lanes_of(page.shape)
+    keys = pltpu.roll(pages[0].astype(jnp.float32), HALF, 1)
+    page[...] = jnp.where(lane < HALF, keys, pages[1].astype(jnp.float32)).astype(jnp.bfloat16)
+
+
+def window_page(prompt_pages):
+    shape = prompt_pages.shape[1:]
+    return kernel_call(
+        page_kernel,
+        1,
+        "window_page",
+        jax.ShapeDtypeStruct(shape[1:], jnp.bfloat16),
+        [HBM],
+        [pltpu.VMEM(shape, jnp.bfloat16), pltpu.SemaphoreType.DMA],
+        (prompt_pages,),
+        cost=pl.CostEstimate(flops=0, bytes_accessed=16 << 20, transcendentals=0),
     )
 
 
@@ -497,22 +608,19 @@
     page_table,
     lengths,
 ):
-    section_index = lax.axis_index("section")
-    ids = jnp.stack([section_index, lax.axis_index("req"), lax.axis_index("head")])
     value_w = value_w.transpose(0, 2, 1)
     lin_state = lin_state.transpose(0, 2, 1, 3).reshape(-1, HD)
     own_pages = own_pages.transpose(0, 1, 3, 2)
     prompt_pages = prompt_pages.transpose(0, 1, 3, 2)
 
-    received = [head_shift(tokens, k) for k in (1, 3, 2)]
-    page = jnp.concatenate([prompt_pages[0, 0, :, HALF:], prompt_pages[0, 1, :, HALF:]], axis=1)
-    near_pages = jnp.stack([z_shift(page, 1), page, z_shift(page, -1)])
+    received = [token_shift(tokens, k) for k in (1, 3, 2)]
+    page = window_page(prompt_pages)
+    row_pages = [page_shift(page, 0, k) for k in (1, 3, 2)]
+    near_pages = jnp.stack([row_pages[0], page, row_pages[1], row_pages[2]])
     near_pages, received = lax.optimization_barrier((near_pages, received))
-    above = z_shift(near_pages, -3)
-    below = z_shift(near_pages[1:], 3)
+    far_pages = page_shift(near_pages, ZN // 2, 0)
 
     update = linear_layer(
-        ids,
         [tokens] + received,
         norm_gain,
         feature_w,
@@ -523,16 +631,21 @@
         lin_state,
         lin_norm,
     )
+    table, ends, update = lax.optimization_barrier((page_table, lengths, update))
+    tags = jnp.concatenate([table[:, :1], ends[:, None]], axis=1)
     swapped = [section_swap(update, k) for k in (0, 1, 3, 2)]
     one_share, packed, key_new, value_new = project(
-        ids, page_table, lengths, swapped, norm_gain, query_key_w, value_w
-    )
-    asked = [packed] + [x_shift(packed, k) for k in (1, 3, 2)]
-    own = own_attention(ids, page_table, lengths, packed, key_new, value_new, own_pages)
-    answers = prompt_attention(ids, asked, near_pages, above, below)
-    parts = [answers[0]] + [x_shift(answers[at], -k) for at, k in ((1, 1), (2, 3), (3, 2))]
-    slabs = combine(ids, own, parts, out_w)
+        tags, swapped, norm_gain, query_key_w, value_w
+    )
+    asked = [packed] + [z_shift(packed, k) for k in (1, 7, 2)]
     one_back = lax.ppermute(one_share, "section", [(1, 0)])
+    own_query, one_back = lax.optimization_barrier((packed, one_back))
+    own = own_attention(page_table, lengths, own_query, key_new, value_new, own_pages)
+    asked, own = lax.optimization_barrier((asked, own))
+    answers = prompt_attention(asked, near_pages, far_pages)
+    parts = [answers[0]] + [z_shift(answers[at], -k) for at, k in ((1, 1), (2, 7), (3, 2))]
+    slabs = combine(own, parts, out_w)
+    section_index = lax.axis_index("section")
     total = one_share.astype(jnp.float32) + slabs[0]
     for piece in [head_shift(slabs[k], k) for k in (1, 3, 2)]:
         total = total + piece

time: 68.8 us -> 62.1 us (0.903)
  Pallas kernels: 14.4 us -> 9.84 us
  local copies, waits for them, and re-layouts: 4.33 us -> 0.23 us
  waiting for transfers between devices: 10.7 us -> 12.2 us
  starting transfers between devices: 37.8 us -> 38.6 us
    ppermute x10 -> x13, starting transfers between devices: 24.6 us -> 29.5 us  [the longest x4 19.6 us: page_shift(): lax.ppermute(value, ('section', 'req'), [(base + z * XN + i, base + (z +...]
    ppermute x6 -> x3, starting transfers between devices: 7.91 us -> 3.16 us  [head_shift(): lax.ppermute(value, 'head', [(i, (i + steps) % count) for i in range(coun...]
    pallas_call x5 -> x6, Pallas kernels: 14.4 us -> 9.84 us  [kernel_call(): pl.pallas_call(run, out_shape=out_shape, in_specs=in_specs, out_specs=jax...]
    unnamed x28 -> x8, local copies, waits for them, and re-layouts: 3.09 us -> 0.02 us
    squeeze x1 -> x0, local copies, waits for them, and re-layouts: 1.22 us -> none  [body(): prompt_pages[0, 0, :, HALF:]]
    ppermute x4, waiting for transfers between devices: 3.69 us -> 4.52 us  [section_swap(): lax.ppermute(value, ('section', 'head'), there + [(b, a) for a, b in there])]
    ppermute x10 -> x13, waiting for transfers between devices: 2.49 us -> 3.13 us  [the longest x4 2.2 us: page_shift(): lax.ppermute(value, ('section', 'req'), [(base + z * XN + i, base + (z +...]
    ppermute x6 -> x3, waiting for transfers between devices: 3.76 us -> 3.8 us  [head_shift(): lax.ppermute(value, 'head', [(i, (i + steps) % count) for i in range(coun...]
  transfers between devices with their start and end apart: 21 -> 21, of which waited for: 7 -> 9; matrix products, arithmetic and copies ran while one was open for 0% -> 0% of each run, Pallas kernels for 17% -> 12%
where the time goes in v3:
time: 62.1 us; the launch traced here: 61.8 us
  starting transfers between devices  38.6 us (62%)
  waiting for transfers between devices  12.2 us (20%)
  Pallas kernels  9.84 us (16%)
  other arithmetic  0.68 us (1%)
    ppermute x4, starting transfers between devices, page_shift(): lax.ppermute(value, ('section', 'req'), [(base + z * XN + i, base + (z +...  19.6 us
    pallas_call x6, Pallas kernels, kernel_call(): pl.pallas_call(run, out_shape=out_shape, in_specs=in_specs, out_specs=jax...  9.84 us
    ppermute x6, starting transfers between devices, z_shift(): lax.ppermute(value, 'req', [(z * XN + i, (z + steps) % ZN * XN + i) for z...  7.96 us
    ppermute x4, starting transfers between devices, section_swap(): lax.ppermute(value, ('section', 'head'), there + [(b, a) for a, b in there])  4.6 us
    ppermute x4, waiting for transfers between devices, section_swap(): lax.ppermute(value, ('section', 'head'), there + [(b, a) for a, b in there])  4.52 us
    ppermute x3, waiting for transfers between devices, head_shift(): lax.ppermute(value, 'head', [(i, (i + steps) % count) for i in range(coun...  3.8 us
    ppermute x3, starting transfers between devices, head_shift(): lax.ppermute(value, 'head', [(i, (i + steps) % count) for i in range(coun...  3.16 us
    ppermute x4, waiting for transfers between devices, page_shift(): lax.ppermute(value, ('section', 'req'), [(base + z * XN + i, base + (z +...  2.2 us
  transfers between devices with their start and end apart: 21, of which 9 were waited for; matrix products, arithmetic and copies ran while one was open for 0% of the time, Pallas kernels for 12%

profile of v3, /device:TPU:1, one launch (start us, length us, event | category | flops | bytes accessed | tf_op | source)
XLA Modules:
  0.0 61.8 jit_solution(3230316956239929651)
XLA Ops:
  0.0 1.0 %window_page.1 = bf16[448,128]{1,0:T(8,128)(2,1)S(1)} custom-call(bf16[1,2,448,128]{3,2,1,0:T(8,128)(2,1)} %bitcast.19), custom_call_target="tpu_custom_call" | custom-call | bytes 16777216 | tf_op jit(solution)/shard_map/window_page/pallas_call | solution.py:102
  1.1 5.5 %collective-permute-start.2 = (bf16[448,128]{1,0:T(8,128)(2,1)S(1)}, bf16[448,128]{1,0:T(8,128)(2,1)S(1)}, u32[]{:S(2)}, u32[]{:S(2)}) collective-permute-start(bf16[448,128]{1,0:T(8,128)(2,1)S(1)} %window_page.1), channel_id=1, source_target_pairs={{128,136},{132,140},{136,128},{140,132},{144,152},{148,156},{152,1... | collective-permute-start | bytes 344072 | tf_op jit(solution)/shard_map/ppermute | solution.py:48
  6.5 2.8 %collective-permute-start.1 = (bf16[448,128]{1,0:T(8,128)(2,1)S(1)}, bf16[448,128]{1,0:T(8,128)(2,1)S(1)}, u32[]{:S(2)}, u32[]{:S(2)}) collective-permute-start(bf16[448,128]{1,0:T(8,128)(2,1)S(1)} %window_page.1), channel_id=1, source_target_pairs={{128,140},{132,128},{136,132},{140,136},{144,156},{148,144},{152,1... | collective-permute-start | bytes 344072 | tf_op jit(solution)/shard_map/ppermute | solution.py:48
  9.3 2.5 %collective-permute-start = (bf16[448,128]{1,0:T(8,128)(2,1)S(1)}, bf16[448,128]{1,0:T(8,128)(2,1)S(1)}, u32[]{:S(2)}, u32[]{:S(2)}) collective-permute-start(bf16[448,128]{1,0:T(8,128)(2,1)S(1)} %window_page.1), channel_id=1, source_target_pairs={{128,132},{132,136},{136,140},{140,128},{144,148},{148,152},{152,1... | collective-permute-start | bytes 344072 | tf_op jit(solution)/shard_map/ppermute | solution.py:48
  11.8 0.7 %collective-permute-start.3 = (bf16[8,448]{1,0:T(8,128)(2,1)}, bf16[8,448]{1,0:T(8,128)(2,1)S(1)}, u32[]{:S(2)}, u32[]{:S(2)}) collective-permute-start(bf16[8,448]{1,0:T(8,128)(2,1)} %refs_3_.1), channel_id=1, source_target_pairs={{0,1},{1,2},{2,3},{3,0},{4,5},{5,6},{6,7},{7,4},{8,9},{9,10},{10,1... | collective-permute-start | bytes 21512 | tf_op jit(solution)/shard_map/ppermute | solution.py:33
  12.5 0.7 %collective-permute-start.4 = (bf16[8,448]{1,0:T(8,128)(2,1)}, bf16[8,448]{1,0:T(8,128)(2,1)S(1)}, u32[]{:S(2)}, u32[]{:S(2)}) collective-permute-start(bf16[8,448]{1,0:T(8,128)(2,1)} %refs_3_.1), channel_id=1, source_target_pairs={{0,3},{1,0},{2,1},{3,2},{4,7},{5,4},{6,5},{7,6},{8,11},{9,8},{10,9... | collective-permute-start | bytes 21512 | tf_op jit(solution)/shard_map/ppermute | solution.py:33
  13.2 0.0 collective-permute-done.2
  13.2 0.7 %collective-permute-start.5 = (bf16[8,448]{1,0:T(8,128)(2,1)}, bf16[8,448]{1,0:T(8,128)(2,1)S(1)}, u32[]{:S(2)}, u32[]{:S(2)}) collective-permute-start(bf16[8,448]{1,0:T(8,128)(2,1)} %refs_3_.1), channel_id=1, source_target_pairs={{0,2},{1,3},{2,0},{3,1},{4,6},{5,7},{6,4},{7,5},{8,10},{9,11},{10,... | collective-permute-start | bytes 21512 | tf_op jit(solution)/shard_map/ppermute | solution.py:33
  13.9 0.0 collective-permute-done.1
  13.9 2.2 %collective-permute-done = bf16[448,128]{1,0:T(8,128)(2,1)S(1)} collective-permute-done((bf16[448,128]{1,0:T(8,128)(2,1)S(1)}, bf16[448,128]{1,0:T(8,128)(2,1)S(1)}, u32[]{:S(2)}, u32[]{:S(2)}) %collective-permute-start) | collective-permute-done | bytes 114720 | tf_op jit(solution)/shard_map/ppermute | solution.py:48
  16.1 0.1 pad_maximum_fusion.refs_4_
  16.1 0.0 collective-permute-done.3.refs_0_
  16.1 0.0 collective-permute-done.4.refs_1_
  16.2 8.8 %collective-permute-start.14 = (bf16[4,448,128]{2,1,0:T(8,128)(2,1)S(1)}, bf16[4,448,128]{2,1,0:T(8,128)(2,1)S(1)}, u32[]{:S(2)}, u32[]{:S(2)}) collective-permute-start(bf16[4,448,128]{2,1,0:T(8,128)(2,1)S(1)} %pad_maximum_fusion.refs_4_), channel_id=1, source_target_pairs={{128,192},{132,196},{136,200},{140,204},{144,208},{148,212},{152,2... | collective-permute-start | bytes 1376264 | tf_op jit(solution)/shard_map/ppermute | solution.py:48
  25.0 0.0 copy-start.1
  25.0 0.0 copy-start.3
  25.0 0.0 copy-start.2
  25.0 0.1 linear_layer.1
  25.1 0.1 collective-permute-start.6
  25.2 3.3 %collective-permute-start.7 = (f32[8,1792]{1,0:T(8,128)S(1)}, f32[8,1792]{1,0:T(8,128)S(1)}, u32[]{:S(2)}, u32[]{:S(2)}) collective-permute-start(f32[8,1792]{1,0:T(8,128)S(1)} %linear_layer.1), channel_id=1, source_target_pairs={{0,129},{1,130},{2,131},{3,128},{129,0},{130,1},{131,2},{128,3},{4... | collective-permute-start | bytes 172040 | tf_op jit(solution)/shard_map/ppermute | solution.py:62
  28.6 0.0 collective-permute-start.8
  28.6 1.2 %collective-permute-start.9 = (f32[8,1792]{1,0:T(8,128)S(1)}, f32[8,1792]{1,0:T(8,128)S(1)}, u32[]{:S(2)}, u32[]{:S(2)}) collective-permute-start(f32[8,1792]{1,0:T(8,128)S(1)} %linear_layer.1), channel_id=1, source_target_pairs={{0,130},{1,131},{2,128},{3,129},{130,0},{131,1},{128,2},{129,3},{4... | collective-permute-start | bytes 172040 | tf_op jit(solution)/shard_map/ppermute | solution.py:62
  29.7 0.1 copy.16
  29.9 0.1 copy.17.refs_0_
  30.0 0.4 collective-permute-done.7.refs_2_
  30.4 1.7 %collective-permute-done.8.refs_3_ = f32[8,1792]{1,0:T(8,128)S(1)} collective-permute-done((f32[8,1792]{1,0:T(8,128)S(1)}, f32[8,1792]{1,0:T(8,128)S(1)}, u32[]{:S(2)}, u32[]{:S(2)}) %collective-permute-start.8) | collective-permute-done | bytes 57376 | tf_op jit(solution)/shard_map/ppermute | solution.py:62
  32.2 2.3 %collective-permute-done.9.refs_4_ = f32[8,1792]{1,0:T(8,128)S(1)} collective-permute-done((f32[8,1792]{1,0:T(8,128)S(1)}, f32[8,1792]{1,0:T(8,128)S(1)}, u32[]{:S(2)}, u32[]{:S(2)}) %collective-permute-start.9) | collective-permute-done | bytes 57376 | tf_op jit(solution)/shard_map/ppermute | solution.py:62
  34.5 3.1 %project.1 = (bf16[8,448]{1,0:T(8,128)(2,1)S(1)}, bf16[8,512]{1,0:T(8,128)(2,1)S(1)}, bf16[8,448]{1,0:T(8,128)(2,1)S(1)}, bf16[8,448]{1,0:T(8,128)(2,1)S(1)}) custom-call(s32[8,2]{1,0:T(8,128)S(1)} %copy.17.refs_0_, f32[8,1792]{1,0:T(8,128)S(1)} %collective-permute-done.6.refs_1_, f32[8,1792]{1,0:T(8,128)S(1)} %collective-permute-done.7.refs_2_, ...), custom_call_target="tpu_custom_call" | custom-call | tf_op jit(solution)/shard_map/project/pallas_call | solution.py:102
  37.6 0.8 %collective-permute-start.11 = (bf16[8,512]{1,0:T(8,128)(2,1)S(1)}, bf16[8,512]{1,0:T(8,128)(2,1)S(1)}, u32[]{:S(2)}, u32[]{:S(2)}) collective-permute-start(bf16[8,512]{1,0:T(8,128)(2,1)S(1)} %get-tuple-element.54.refs_2_.refs_0_), channel_id=1, source_target_pairs={{0,16},{4,20},{8,24},{12,28},{16,32},{20,36},{24,40},{28,44},{32,4... | collective-permute-start | bytes 24584 | tf_op jit(solution)/shard_map/ppermute | solution.py:39
  38.4 1.9 %collective-permute-start.12 = (bf16[8,512]{1,0:T(8,128)(2,1)S(1)}, bf16[8,512]{1,0:T(8,128)(2,1)S(1)}, u32[]{:S(2)}, u32[]{:S(2)}) collective-permute-start(bf16[8,512]{1,0:T(8,128)(2,1)S(1)} %get-tuple-element.54.refs_2_.refs_0_), channel_id=1, source_target_pairs={{0,112},{4,116},{8,120},{12,124},{16,0},{20,4},{24,8},{28,12},{32,... | collective-permute-start | bytes 24584 | tf_op jit(solution)/shard_map/ppermute | solution.py:39
  40.4 0.0 collective-permute-start.13
  40.4 1.3 %collective-permute-start.10 = (bf16[8,448]{1,0:T(8,128)(2,1)S(1)}, bf16[8,448]{1,0:T(8,128)(2,1)S(1)}, u32[]{:S(2)}, u32[]{:S(2)}) collective-permute-start(bf16[8,448]{1,0:T(8,128)(2,1)S(1)} %get-tuple-element.43), channel_id=1, source_target_pairs={{128,0},{129,1},{130,2},{131,3},{132,4},{133,5},{134,6},{135,7},{1... | collective-permute-start | bytes 21512 | tf_op jit(solution)/shard_map/ppermute | solution.py:641
  41.7 0.8 %collective-permute-done.10 = bf16[8,448]{1,0:T(8,128)(2,1)S(1)} collective-permute-done((bf16[8,448]{1,0:T(8,128)(2,1)S(1)}, bf16[8,448]{1,0:T(8,128)(2,1)S(1)}, u32[]{:S(2)}, u32[]{:S(2)}) %collective-permute-start.10) | collective-permute-done | bytes 7200 | tf_op jit(solution)/shard_map/ppermute | solution.py:641
  42.5 4.1 %own_attention.1 = (f32[8,448]{1,0:T(8,128)S(1)}, f32[8,448]{1,0:T(8,128)S(1)}, f32[8,448]{1,0:T(8,128)S(1)}) custom-call(s32[8,256]{1,0:T(8,128)S(1)} %copy-done.1, s32[8]{0:T(128)S(1)} %copy-done.3, bf16[8,512]{1,0:T(8,128)(2,1)S(1)} %get-tuple-element.54.refs_2_.refs_0_, bf16[8,448]{1,0:T(8,128)(2,1)S(1)} %get-tuple-element.46.refs_3_, ...), custom_call_target="tpu_custom_call" | custom-call | tf_op jit(solution)/shard_map/own_attention/pallas_call | solution.py:102
  46.6 0.0 collective-permute-done.11.refs_1_
  46.6 0.0 collective-permute-done.12.refs_2_
  46.6 0.9 %prompt_attention.1 = (f32[8,640]{1,0:T(8,128)S(1)}, f32[8,640]{1,0:T(8,128)S(1)}, f32[8,640]{1,0:T(8,128)S(1)}, f32[8,640]{1,0:T(8,128)S(1)}) custom-call(bf16[8,512]{1,0:T(8,128)(2,1)S(1)} %get-tuple-element.54.refs_2_.refs_0_, bf16[8,512]{1,0:T(8,128)(2,1)S(1)} %collective-permute-done.11.refs_1_, bf16[8,512]{1,0:T(8,128)(2,1)S(1)} %collective-permute-done.12.refs_2_, ...), custom_call_target="tpu_custom_call" | custom-call | tf_op jit(solution)/shard_map/prompt_attention/pallas_call | solution.py:102
  47.6 2.1 %collective-permute-start.15 = (f32[8,640]{1,0:T(8,128)S(1)}, f32[8,640]{1,0:T(8,128)S(1)}, u32[]{:S(2)}, u32[]{:S(2)}) collective-permute-start(f32[8,640]{1,0:T(8,128)S(1)} %get-tuple-element.60), channel_id=1, source_target_pairs={{0,112},{4,116},{8,120},{12,124},{16,0},{20,4},{24,8},{28,12},{32,... | collective-permute-start | bytes 61448 | tf_op jit(solution)/shard_map/ppermute | solution.py:39
  49.7 3.1 %collective-permute-start.17 = (f32[8,640]{1,0:T(8,128)S(1)}, f32[8,640]{1,0:T(8,128)S(1)}, u32[]{:S(2)}, u32[]{:S(2)}) collective-permute-start(f32[8,640]{1,0:T(8,128)S(1)} %get-tuple-element.62), channel_id=1, source_target_pairs={{0,96},{4,100},{8,104},{12,108},{16,112},{20,116},{24,120},{28,124... | collective-permute-start | bytes 61448 | tf_op jit(solution)/shard_map/ppermute | solution.py:39
  52.8 0.0 collective-permute-done.15.refs_4_
  52.8 0.7 %collective-permute-done.16.refs_5_ = f32[8,640]{1,0:T(8,128)S(1)} collective-permute-done((f32[8,640]{1,0:T(8,128)S(1)}, f32[8,640]{1,0:T(8,128)S(1)}, u32[]{:S(2)}, u32[]{:S(2)}) %collective-permute-start.16) | collective-permute-done | bytes 20512 | tf_op jit(solution)/shard_map/ppermute | solution.py:39
  53.5 0.2 collective-permute-done.17.refs_6_
  53.7 0.6 combine.1
  54.2 1.3 %collective-permute-start.20 = (f32[8,448]{1,0:T(8,128)S(1)}, f32[8,448]{1,0:T(8,128)S(1)}, u32[]{:S(2)}, u32[]{:S(2)}) collective-permute-start(f32[8,448]{1,0:T(8,128)S(1)} %get-tuple-element.66), channel_id=1, source_target_pairs={{0,2},{1,3},{2,0},{3,1},{4,6},{5,7},{6,4},{7,5},{8,10},{9,11},{10,... | collective-permute-start | bytes 43016 | tf_op jit(solution)/shard_map/ppermute | solution.py:28
  55.6 1.8 %collective-permute-start.19 = (f32[8,448]{1,0:T(8,128)S(1)}, f32[8,448]{1,0:T(8,128)S(1)}, u32[]{:S(2)}, u32[]{:S(2)}) collective-permute-start(f32[8,448]{1,0:T(8,128)S(1)} %get-tuple-element.65), channel_id=1, source_target_pairs={{0,3},{1,0},{2,1},{3,2},{4,7},{5,4},{6,5},{7,6},{8,11},{9,8},{10,9... | collective-permute-start | bytes 43016 | tf_op jit(solution)/shard_map/ppermute | solution.py:28
  57.4 1.0 %collective-permute-done.20 = f32[8,448]{1,0:T(8,128)S(1)} collective-permute-done((f32[8,448]{1,0:T(8,128)S(1)}, f32[8,448]{1,0:T(8,128)S(1)}, u32[]{:S(2)}, u32[]{:S(2)}) %collective-permute-start.20) | collective-permute-done | bytes 14368 | tf_op jit(solution)/shard_map/ppermute | solution.py:28
  58.4 2.8 %collective-permute-done.18 = f32[8,448]{1,0:T(8,128)S(1)} collective-permute-done((f32[8,448]{1,0:T(8,128)S(1)}, f32[8,448]{1,0:T(8,128)S(1)}, u32[]{:S(2)}, u32[]{:S(2)}) %collective-permute-start.18) | collective-permute-done | bytes 14368 | tf_op jit(solution)/shard_map/ppermute | solution.py:28
  61.2 0.6 fusion.1
  (14 shorter events, 0.0 us)
Async XLA Ops:
  1.1 12.1 %collective-permute-start.2 = (bf16[448,128]{1,0:T(8,128)(2,1)S(1)}, bf16[448,128]{1,0:T(8,128)(2,1)S(1)}, u32[]{:S(2)}, u32[]{:S(2)}) collective-permute-start(bf16[448,128]{1,0:T(8,128)(2,1)S(1)} %window_page.1), channel_id=1, source_target_pairs={{128,136},{132,140},{136,128},{140,132},{144,152},{148,156},{152,1... | collective-permute-start | bytes 344072 | tf_op jit(solution)/shard_map/ppermute | solution.py:48
  6.5 7.3 %collective-permute-start.1 = (bf16[448,128]{1,0:T(8,128)(2,1)S(1)}, bf16[448,128]{1,0:T(8,128)(2,1)S(1)}, u32[]{:S(2)}, u32[]{:S(2)}) collective-permute-start(bf16[448,128]{1,0:T(8,128)(2,1)S(1)} %window_page.1), channel_id=1, source_target_pairs={{128,140},{132,128},{136,132},{140,136},{144,156},{148,144},{152,1... | collective-permute-start | bytes 344072 | tf_op jit(solution)/shard_map/ppermute | solution.py:48
  9.3 6.7 %collective-permute-start = (bf16[448,128]{1,0:T(8,128)(2,1)S(1)}, bf16[448,128]{1,0:T(8,128)(2,1)S(1)}, u32[]{:S(2)}, u32[]{:S(2)}) collective-permute-start(bf16[448,128]{1,0:T(8,128)(2,1)S(1)} %window_page.1), channel_id=1, source_target_pairs={{128,132},{132,136},{136,140},{140,128},{144,148},{148,152},{152,1... | collective-permute-start | bytes 344072 | tf_op jit(solution)/shard_map/ppermute | solution.py:48
  11.8 4.3 %collective-permute-start.3 = (bf16[8,448]{1,0:T(8,128)(2,1)}, bf16[8,448]{1,0:T(8,128)(2,1)S(1)}, u32[]{:S(2)}, u32[]{:S(2)}) collective-permute-start(bf16[8,448]{1,0:T(8,128)(2,1)} %refs_3_.1), channel_id=1, source_target_pairs={{0,1},{1,2},{2,3},{3,0},{4,5},{5,6},{6,7},{7,4},{8,9},{9,10},{10,1... | collective-permute-start | bytes 21512 | tf_op jit(solution)/shard_map/ppermute | solution.py:33
  12.5 3.6 %collective-permute-start.4 = (bf16[8,448]{1,0:T(8,128)(2,1)}, bf16[8,448]{1,0:T(8,128)(2,1)S(1)}, u32[]{:S(2)}, u32[]{:S(2)}) collective-permute-start(bf16[8,448]{1,0:T(8,128)(2,1)} %refs_3_.1), channel_id=1, source_target_pairs={{0,3},{1,0},{2,1},{3,2},{4,7},{5,4},{6,5},{7,6},{8,11},{9,8},{10,9... | collective-permute-start | bytes 21512 | tf_op jit(solution)/shard_map/ppermute | solution.py:33
  13.2 3.0 %collective-permute-start.5 = (bf16[8,448]{1,0:T(8,128)(2,1)}, bf16[8,448]{1,0:T(8,128)(2,1)S(1)}, u32[]{:S(2)}, u32[]{:S(2)}) collective-permute-start(bf16[8,448]{1,0:T(8,128)(2,1)} %refs_3_.1), channel_id=1, source_target_pairs={{0,2},{1,3},{2,0},{3,1},{4,6},{5,7},{6,4},{7,5},{8,10},{9,11},{10,... | collective-permute-start | bytes 21512 | tf_op jit(solution)/shard_map/ppermute | solution.py:33
  16.2 30.5 %collective-permute-start.14 = (bf16[4,448,128]{2,1,0:T(8,128)(2,1)S(1)}, bf16[4,448,128]{2,1,0:T(8,128)(2,1)S(1)}, u32[]{:S(2)}, u32[]{:S(2)}) collective-permute-start(bf16[4,448,128]{2,1,0:T(8,128)(2,1)S(1)} %pad_maximum_fusion.refs_4_), channel_id=1, source_target_pairs={{128,192},{132,196},{136,200},{140,204},{144,208},{148,212},{152,2... | collective-permute-start | bytes 1376264 | tf_op jit(solution)/shard_map/ppermute | solution.py:48
  25.0 4.8 %copy-start.1 = (s32[8,256]{1,0:T(8,128)S(1)}, s32[8,256]{1,0:T(8,128)}, u32[]{:S(2)}) copy-start(s32[8,256]{1,0:T(8,128)} %refs_0_.1) | copy-start | bytes 24580
  25.0 4.9 %copy-start.3 = (s32[8]{0:T(128)S(1)}, s32[8]{0:T(128)}, u32[]{:S(2)}) copy-start(s32[8]{0:T(128)} %refs_1_.1) | copy-start | bytes 100
  25.0 9.5 %copy-start.2 = (f32[1,1792]{1,0:T(1,128)S(1)}, f32[1,1792]{1,0:T(1,128)}, u32[]{:S(2)}) copy-start(f32[1,1792]{1,0:T(1,128)} %refs_5_.3) | copy-start | bytes 21508
  25.1 4.9 %collective-permute-start.6 = (f32[8,1792]{1,0:T(8,128)S(1)}, f32[8,1792]{1,0:T(8,128)S(1)}, u32[]{:S(2)}, u32[]{:S(2)}) collective-permute-start(f32[8,1792]{1,0:T(8,128)S(1)} %linear_layer.1), channel_id=1, source_target_pairs={{0,128},{1,129},{2,130},{3,131},{128,0},{129,1},{130,2},{131,3},{4... | collective-permute-start | bytes 172040 | tf_op jit(solution)/shard_map/ppermute | solution.py:62
  25.2 5.2 %collective-permute-start.7 = (f32[8,1792]{1,0:T(8,128)S(1)}, f32[8,1792]{1,0:T(8,128)S(1)}, u32[]{:S(2)}, u32[]{:S(2)}) collective-permute-start(f32[8,1792]{1,0:T(8,128)S(1)} %linear_layer.1), channel_id=1, source_target_pairs={{0,129},{1,130},{2,131},{3,128},{129,0},{130,1},{131,2},{128,3},{4... | collective-permute-start | bytes 172040 | tf_op jit(solution)/shard_map/ppermute | solution.py:62
  28.6 3.6 %collective-permute-start.8 = (f32[8,1792]{1,0:T(8,128)S(1)}, f32[8,1792]{1,0:T(8,128)S(1)}, u32[]{:S(2)}, u32[]{:S(2)}) collective-permute-start(f32[8,1792]{1,0:T(8,128)S(1)} %linear_layer.1), channel_id=1, source_target_pairs={{0,131},{1,128},{2,129},{3,130},{131,0},{128,1},{129,2},{130,3},{4... | collective-permute-start | bytes 172040 | tf_op jit(solution)/shard_map/ppermute | solution.py:62
  28.6 5.9 %collective-permute-start.9 = (f32[8,1792]{1,0:T(8,128)S(1)}, f32[8,1792]{1,0:T(8,128)S(1)}, u32[]{:S(2)}, u32[]{:S(2)}) collective-permute-start(f32[8,1792]{1,0:T(8,128)S(1)} %linear_layer.1), channel_id=1, source_target_pairs={{0,130},{1,131},{2,128},{3,129},{130,0},{131,1},{128,2},{129,3},{4... | collective-permute-start | bytes 172040 | tf_op jit(solution)/shard_map/ppermute | solution.py:62
  37.6 9.0 %collective-permute-start.11 = (bf16[8,512]{1,0:T(8,128)(2,1)S(1)}, bf16[8,512]{1,0:T(8,128)(2,1)S(1)}, u32[]{:S(2)}, u32[]{:S(2)}) collective-permute-start(bf16[8,512]{1,0:T(8,128)(2,1)S(1)} %get-tuple-element.54.refs_2_.refs_0_), channel_id=1, source_target_pairs={{0,16},{4,20},{8,24},{12,28},{16,32},{20,36},{24,40},{28,44},{32,4... | collective-permute-start | bytes 24584 | tf_op jit(solution)/shard_map/ppermute | solution.py:39
  38.4 8.2 %collective-permute-start.12 = (bf16[8,512]{1,0:T(8,128)(2,1)S(1)}, bf16[8,512]{1,0:T(8,128)(2,1)S(1)}, u32[]{:S(2)}, u32[]{:S(2)}) collective-permute-start(bf16[8,512]{1,0:T(8,128)(2,1)S(1)} %get-tuple-element.54.refs_2_.refs_0_), channel_id=1, source_target_pairs={{0,112},{4,116},{8,120},{12,124},{16,0},{20,4},{24,8},{28,12},{32,... | collective-permute-start | bytes 24584 | tf_op jit(solution)/shard_map/ppermute | solution.py:39
  40.4 6.2 %collective-permute-start.13 = (bf16[8,512]{1,0:T(8,128)(2,1)S(1)}, bf16[8,512]{1,0:T(8,128)(2,1)S(1)}, u32[]{:S(2)}, u32[]{:S(2)}) collective-permute-start(bf16[8,512]{1,0:T(8,128)(2,1)S(1)} %get-tuple-element.54.refs_2_.refs_0_), channel_id=1, source_target_pairs={{0,32},{4,36},{8,40},{12,44},{16,48},{20,52},{24,56},{28,60},{32,6... | collective-permute-start | bytes 24584 | tf_op jit(solution)/shard_map/ppermute | solution.py:39
  40.4 2.1 %collective-permute-start.10 = (bf16[8,448]{1,0:T(8,128)(2,1)S(1)}, bf16[8,448]{1,0:T(8,128)(2,1)S(1)}, u32[]{:S(2)}, u32[]{:S(2)}) collective-permute-start(bf16[8,448]{1,0:T(8,128)(2,1)S(1)} %get-tuple-element.43), channel_id=1, source_target_pairs={{128,0},{129,1},{130,2},{131,3},{132,4},{133,5},{134,6},{135,7},{1... | collective-permute-start | bytes 21512 | tf_op jit(solution)/shard_map/ppermute | solution.py:641
  42.5 11.2 %copy-start = (bf16[1,448,1792]{2,1,0:T(8,128)(2,1)S(1)}, bf16[1,448,1792]{2,1,0:T(8,128)(2,1)}, u32[]{:S(2)}) copy-start(bf16[1,448,1792]{2,1,0:T(8,128)(2,1)} %refs_7_.3) | copy-start | bytes 4816900
  47.6 5.2 %collective-permute-start.15 = (f32[8,640]{1,0:T(8,128)S(1)}, f32[8,640]{1,0:T(8,128)S(1)}, u32[]{:S(2)}, u32[]{:S(2)}) collective-permute-start(f32[8,640]{1,0:T(8,128)S(1)} %get-tuple-element.60), channel_id=1, source_target_pairs={{0,112},{4,116},{8,120},{12,124},{16,0},{20,4},{24,8},{28,12},{32,... | collective-permute-start | bytes 61448 | tf_op jit(solution)/shard_map/ppermute | solution.py:39
  49.7 3.8 %collective-permute-start.16 = (f32[8,640]{1,0:T(8,128)S(1)}, f32[8,640]{1,0:T(8,128)S(1)}, u32[]{:S(2)}, u32[]{:S(2)}) collective-permute-start(f32[8,640]{1,0:T(8,128)S(1)} %get-tuple-element.61), channel_id=1, source_target_pairs={{0,16},{4,20},{8,24},{12,28},{16,32},{20,36},{24,40},{28,44},{32,4... | collective-permute-start | bytes 61448 | tf_op jit(solution)/shard_map/ppermute | solution.py:39
  49.7 4.0 %collective-permute-start.17 = (f32[8,640]{1,0:T(8,128)S(1)}, f32[8,640]{1,0:T(8,128)S(1)}, u32[]{:S(2)}, u32[]{:S(2)}) collective-permute-start(f32[8,640]{1,0:T(8,128)S(1)} %get-tuple-element.62), channel_id=1, source_target_pairs={{0,96},{4,100},{8,104},{12,108},{16,112},{20,116},{24,120},{28,124... | collective-permute-start | bytes 61448 | tf_op jit(solution)/shard_map/ppermute | solution.py:39
  54.2 4.2 %collective-permute-start.20 = (f32[8,448]{1,0:T(8,128)S(1)}, f32[8,448]{1,0:T(8,128)S(1)}, u32[]{:S(2)}, u32[]{:S(2)}) collective-permute-start(f32[8,448]{1,0:T(8,128)S(1)} %get-tuple-element.66), channel_id=1, source_target_pairs={{0,2},{1,3},{2,0},{3,1},{4,6},{5,7},{6,4},{7,5},{8,10},{9,11},{10,... | collective-permute-start | bytes 43016 | tf_op jit(solution)/shard_map/ppermute | solution.py:28
  55.6 2.8 %collective-permute-start.19 = (f32[8,448]{1,0:T(8,128)S(1)}, f32[8,448]{1,0:T(8,128)S(1)}, u32[]{:S(2)}, u32[]{:S(2)}) collective-permute-start(f32[8,448]{1,0:T(8,128)S(1)} %get-tuple-element.65), channel_id=1, source_target_pairs={{0,3},{1,0},{2,1},{3,2},{4,7},{5,4},{6,5},{7,6},{8,11},{9,8},{10,9... | collective-permute-start | bytes 43016 | tf_op jit(solution)/shard_map/ppermute | solution.py:28
  57.4 3.8 %collective-permute-start.18 = (f32[8,448]{1,0:T(8,128)S(1)}, f32[8,448]{1,0:T(8,128)S(1)}, u32[]{:S(2)}, u32[]{:S(2)}) collective-permute-start(f32[8,448]{1,0:T(8,128)S(1)} %get-tuple-element.64), channel_id=1, source_target_pairs={{0,1},{1,2},{2,3},{3,0},{4,5},{5,6},{6,7},{7,4},{8,9},{9,10},{10,1... | collective-permute-start | bytes 43016 | tf_op jit(solution)/shard_map/ppermute | solution.py:28

commit v4 on v3

--- a/solution.py
+++ b/solution.py
@@ -28,13 +28,6 @@
     return lax.ppermute(value, "head", [(i, (i + steps) % count) for i in range(count)])
 
 
-def token_shift(value, steps):
-    count = lax.axis_size("head")
-    return lax.ppermute(
-        value, ("section", "head"), [(i, (i + steps) % count) for i in range(count)]
-    )
-
-
 def z_shift(value, steps):
     return lax.ppermute(
         value,
@@ -43,16 +36,11 @@
     )
 
 
-def page_shift(value, z_steps, x_steps):
-    base = XN * ZN
+def x_shift(value, steps):
     return lax.ppermute(
         value,
-        ("section", "req"),
-        [
-            (base + z * XN + i, base + (z + z_steps) % ZN * XN + (i + x_steps) % XN)
-            for z in range(ZN)
-            for i in range(XN)
-        ],
+        "req",
+        [(z * XN + i, z * XN + (i + steps) % XN) for z in range(ZN) for i in range(XN)],
     )
 
 
@@ -86,7 +74,16 @@
 
 
 def kernel_call(
-    kernel, section, name, out_shape, in_specs, scratch_shapes, args, vmem=24 << 20, cost=None
+    kernel,
+    section,
+    name,
+    out_shape,
+    in_specs,
+    scratch_shapes,
+    args,
+    vmem=10 << 20,
+    cost=None,
+    elsewhere=None,
 ):
     def run(*refs):
         ids = place()
@@ -94,6 +91,12 @@
         @pl.when(ids[0] == section)
         def _():
             kernel(ids, *refs)
+
+        if elsewhere is not None:
+
+            @pl.when(ids[0] != section)
+            def _():
+                elsewhere(ids, *refs)
 
     args = [
         pltpu.with_memory_space_constraint(arg, pltpu.HBM) if spec is HBM else arg
@@ -133,20 +136,10 @@
 
 def linear_kernel(
     ids,
+    t0,
     t1,
     t2,
     t3,
-    t0_hbm,
-    gain_hbm,
-    feature_hbm,
-    state_hbm,
-    norm_hbm,
-    conv_w_hbm,
-    conv_state_hbm,
-    value_hbm,
-    out_hbm,
-    update,
-    t0,
     gain,
     feature_w,
     state,
@@ -155,35 +148,15 @@
     conv_state,
     value_w,
     out_w,
-    sems,
+    update,
 ):
     rows, share = t0.shape
     heads = share // HD
     span = TAYLOR * heads
-    copies = [
-        pltpu.make_async_copy(source, target, sems.at[at])
-        for at, (source, target) in enumerate(
-            [
-                (t0_hbm, t0),
-                (gain_hbm, gain),
-                (feature_hbm, feature_w),
-                (state_hbm, state),
-                (norm_hbm, lin_norm),
-                (conv_w_hbm, conv_w),
-                (conv_state_hbm, conv_state),
-                (value_hbm.at[0], value_w),
-                (out_hbm.at[0], out_w),
-            ]
-        )
-    ]
-    for copy in copies:
-        copy.start()
     by_state = expansion(128, SPREAD, heads)
     by_norm = expansion(128, TAYLOR_LANES, 1)
     expand = jnp.concatenate([by_state, by_norm], axis=1)
 
-    for copy in copies[:3]:
-        copy.wait()
     own = ids[2]
     got = [ref[...].astype(jnp.float32) for ref in (t0, t1, t3, t2)]
     whole = []
@@ -229,7 +202,6 @@
         queries.append(moved[:, :length].astype(jnp.bfloat16))
     row = lax.broadcasted_iota(jnp.int32, (count, HD), 0) & (rows - 1)
     found = jnp.zeros((count, HD), jnp.float32)
-    copies[3].wait()
     for r in range(rows):
         first = span * r
         shift = first % 16
@@ -239,13 +211,10 @@
             preferred_element_type=jnp.float32,
         )
         found = jnp.where(row == r, product, found)
-    for copy in copies[4:8]:
-        copy.wait()
     fresh = lax.dot_general(normed, value_w[...], FLAT, preferred_element_type=jnp.float32)
     older = conv_state[...].astype(jnp.float32)
     mixed = conv_w[0:1] * older[:, 0] + conv_w[1:2] * older[:, 1] + conv_w[2:3] * fresh
     total = tokens * 0.25
-    copies[8].wait()
     for h in range(heads):
         here = slice(h * rows, (h + 1) * rows)
         denominator = (
@@ -261,22 +230,15 @@
     update[...] = total
 
 
-def linear_layer(pieces, gain, feature_w, value_w, out_w, conv_w, conv_state, state, norm):
-    rows = pieces[0].shape[0]
-    near = (pieces[0], gain, feature_w, state, norm, conv_w, conv_state, value_w, out_w)
+def linear_layer(pieces, near):
     return kernel_call(
         linear_kernel,
         0,
         "linear_layer",
-        jax.ShapeDtypeStruct((rows, out_w.shape[2]), jnp.float32),
-        [VMEM] * 3 + [HBM] * len(near),
-        [
-            *(pltpu.VMEM(array.shape, array.dtype) for array in near[:-2]),
-            pltpu.VMEM(value_w.shape[1:], jnp.bfloat16),
-            pltpu.VMEM(out_w.shape[1:], jnp.bfloat16),
-            pltpu.SemaphoreType.DMA((len(near),)),
-        ],
-        (*pieces[1:], *near),
+        jax.ShapeDtypeStruct((pieces[0].shape[0], near["out_w"].shape[1]), jnp.float32),
+        [VMEM] * 12,
+        [],
+        (*pieces, *(near[name] for name in LINEAR_NEAR)),
     )
 
 
@@ -288,21 +250,14 @@
     p2,
     p3,
     gain,
-    qk_hbm,
-    v_hbm,
+    v_w,
+    qk_w,
     one,
     asked,
     key_new,
     value_new,
-    v_w,
-    qk_w,
-    sems,
 ):
     rows, share = one.shape
-    copy_value = pltpu.make_async_copy(v_hbm.at[0], v_w, sems.at[0])
-    copy_query = pltpu.make_async_copy(qk_hbm, qk_w, sems.at[1])
-    copy_value.start()
-    copy_query.start()
     heads = share // HD
     layer_one = (p0[...] + p1[...] + p2[...] + p3[...]).astype(jnp.bfloat16)
     rounded = layer_one.astype(jnp.float32)
@@ -311,11 +266,9 @@
         mine = jnp.where(ids[2] == h, rounded[:, h * share : (h + 1) * share], mine)
     one[...] = mine.astype(jnp.bfloat16)
     normed = normed_rows(rounded, gain[...])
-    copy_value.wait()
     value_new[...] = lax.dot_general(
         normed, v_w[...], FLAT, preferred_element_type=jnp.float32
     ).astype(jnp.bfloat16)
-    copy_query.wait()
     query_key = jnp.dot(normed, qk_w[...], preferred_element_type=jnp.float32)
     width = query_key.shape[1]
     lane = lanes_of((rows, LANES))
@@ -335,9 +288,9 @@
     key_new[...] = key[:, :share].astype(jnp.bfloat16)
 
 
-def project(tags, pieces, gain, query_key_w, value_w):
+def project(tags, pieces, near):
     rows = pieces[0].shape[0]
-    share = value_w.shape[1]
+    share = near["value_w"].shape[0]
     return kernel_call(
         project_kernel,
         1,
@@ -348,45 +301,22 @@
             jax.ShapeDtypeStruct((rows, share), jnp.bfloat16),
             jax.ShapeDtypeStruct((rows, share), jnp.bfloat16),
         ],
-        [VMEM] * 6 + [HBM] * 2,
-        [
-            pltpu.VMEM(value_w.shape[1:], jnp.bfloat16),
-            pltpu.VMEM(query_key_w.shape, jnp.bfloat16),
-            pltpu.SemaphoreType.DMA((2,)),
-        ],
-        (tags, *pieces, gain, query_key_w, value_w),
-    )
+        [VMEM] * 8,
+        [],
+        (tags, *pieces, near["gain"], near["value_w"], near["query_key_w"]),
+    )
+
+
+def window_pages(lengths, r):
+    length = lengths[r]
+    return jnp.maximum((length - WINDOW) // PAGE, 1), jnp.maximum((length - 2) // PAGE, 1)
 
 
 def own_kernel(
-    ids,
-    table,
-    lengths,
-    asked,
-    key_new,
-    value_new,
-    own_pages,
-    summed_out,
-    highest_out,
-    total_out,
-    pages,
-    sems,
+    ids, lengths, asked, key_new, value_new, pages, summed_out, highest_out, total_out
 ):
     rows, share = key_new.shape
-    count = own_pages.shape[0]
-    bounds = []
-    copies = []
-    for r in range(rows):
-        length = lengths[r]
-        first = jnp.maximum((length - WINDOW) // PAGE, 1)
-        last = jnp.maximum((length - 2) // PAGE, 1)
-        bounds.append((length, first, last))
-        for slot, logical in enumerate((first, last)):
-            page = jnp.clip(table[r, logical] - GROUPS - ids[1] * count, 0, count - 1)
-            copies.append(
-                pltpu.make_async_copy(own_pages.at[page], pages.at[r, slot], sems.at[r, slot])
-            )
-            copies[-1].start()
+    bounds = [(lengths[r], *window_pages(lengths, r)) for r in range(rows)]
     head = lax.broadcasted_iota(jnp.int32, (8, share), 0)
     lane = lanes_of((8, share))
     mine = (lane >= head * HD) & (lane < (head + 1) * HD)
@@ -412,8 +342,6 @@
     scores = []
     for r in range(rows):
         low = wide[8 * r : 8 * r + 8].astype(jnp.bfloat16)
-        copies[2 * r].wait()
-        copies[2 * r + 1].wait()
         scores.append(
             jnp.concatenate(
                 [
@@ -447,19 +375,16 @@
             ref[r : r + 1, :] = jnp.sum(jnp.where(mine, value, 0.0), axis=0, keepdims=True)
 
 
-def own_attention(table, lengths, asked, key_new, value_new, own_pages):
+def own_attention(lengths, asked, key_new, value_new, near):
     rows, share = key_new.shape
     return kernel_call(
         own_kernel,
         1,
         "own_attention",
         [jax.ShapeDtypeStruct((rows, share), jnp.float32)] * 3,
-        [SMEM] * 2 + [VMEM] * 3 + [HBM],
-        [
-            pltpu.VMEM((rows, 2) + own_pages.shape[1:], jnp.bfloat16),
-            pltpu.SemaphoreType.DMA((rows, 2)),
-        ],
-        (table, lengths, asked, key_new, value_new, own_pages),
+        [SMEM] + [VMEM] * 4,
+        [],
+        (lengths, asked, key_new, value_new, near["own_pages"]),
     )
 
 
@@ -547,7 +472,7 @@
     prompt_factor = jnp.exp(prompt_highest - peak)
     whole = total[...] * own_factor + prompt_total * prompt_factor
     attended = (summed[...] * own_factor + prompt_summed * prompt_factor) / whole
-    second = jnp.dot(attended.astype(jnp.bfloat16), out_w[0], preferred_element_type=jnp.float32)
+    second = jnp.dot(attended.astype(jnp.bfloat16), out_w[...], preferred_element_type=jnp.float32)
     for steps, ref in enumerate((s0, s1, s2, s3)):
         slab = second[:, :share]
         for h in range(1, heads):
@@ -557,7 +482,7 @@
         ref[...] = slab
 
 
-def combine(own, parts, out_w):
+def combine(own, parts, near):
     return kernel_call(
         combine_kernel,
         1,
@@ -565,7 +490,89 @@
         [jax.ShapeDtypeStruct(own[0].shape, jnp.float32)] * 4,
         [VMEM] * 8,
         [],
-        (*own, *parts, out_w),
+        (*own, *parts, near["out_w"]),
+    )
+
+
+LINEAR_NEAR = (
+    "gain",
+    "feature_w",
+    "state",
+    "lin_norm",
+    "conv_w",
+    "conv_state",
+    "value_w",
+    "out_w",
+)
+SHARED_NEAR = ("gain", "value_w", "out_w")
+
+
+def bring_near(arrays):
+    names = list(arrays)
+    count = len(names)
+    both = [at for at, name in enumerate(names) if name in SHARED_NEAR]
+
+    def copy_some(chosen, refs):
+        sems = refs[-1]
+        copies = [
+            pltpu.make_async_copy(refs[at], refs[count + at], sems.at[at]) for at in chosen
+        ]
+        for copy in copies:
+            copy.start()
+        for copy in copies:
+            copy.wait()
+
+    near = kernel_call(
+        lambda ids, *refs: copy_some(range(count), refs),
+        0,
+        "bring_near",
+        [jax.ShapeDtypeStruct(array.shape, array.dtype) for array in arrays.values()],
+        [HBM] * count,
+        [pltpu.SemaphoreType.DMA((count,))],
+        tuple(arrays.values()),
+        4 << 20,
+        bytes_only(arrays.values()),
+        lambda ids, *refs: copy_some(both, refs),
+    )
+    return dict(zip(names, near))
+
+
+def bytes_only(arrays):
+    moved = sum(array.size * array.dtype.itemsize for array in arrays)
+    return pl.CostEstimate(flops=0, bytes_accessed=2 * moved, transcendentals=0)
+
+
+def window_kernel(
+    ids, table, lengths, query_key_hbm, own_hbm, query_key_near, own_near, key_sem, sems
+):
+    rows = lengths.shape[0]
+    total = own_hbm.shape[0]
+    copies = [pltpu.make_async_copy(query_key_hbm, query_key_near, key_sem)]
+    for r in range(rows):
+        for slot, logical in enumerate(window_pages(lengths, r)):
+            page = jnp.clip(table[r, logical] - GROUPS - ids[1] * total, 0, total - 1)
+            copies.append(
+                pltpu.make_async_copy(own_hbm.at[page], own_near.at[r, slot], sems.at[r, slot])
+            )
+    for copy in copies:
+        copy.start()
+    for copy in copies:
+        copy.wait()
+
+
+def bring_windows(table, lengths, query_key_w, own_pages):
+    rows = lengths.shape[0]
+    windows = jax.ShapeDtypeStruct((rows, 2) + own_pages.shape[1:], own_pages.dtype)
+    return kernel_call(
+        window_kernel,
+        1,
+        "bring_windows",
+        [jax.ShapeDtypeStruct(query_key_w.shape, query_key_w.dtype), windows],
+        [SMEM] * 2 + [HBM] * 2,
+        [pltpu.SemaphoreType.DMA, pltpu.SemaphoreType.DMA((rows, 2))],
+        (table, lengths, query_key_w, own_pages),
+        4 << 20,
+        bytes_only([query_key_w, windows]),
     )
 
 
@@ -608,43 +615,48 @@
     page_table,
     lengths,
 ):
-    value_w = value_w.transpose(0, 2, 1)
-    lin_state = lin_state.transpose(0, 2, 1, 3).reshape(-1, HD)
+    pages_first = prompt_pages.transpose(0, 1, 3, 2)
+    near = bring_near(
+        {
+            "gain": norm_gain,
+            "feature_w": feature_w,
+            "state": lin_state.transpose(0, 2, 1, 3).reshape(-1, HD),
+            "lin_norm": lin_norm,
+            "conv_w": conv_w,
+            "conv_state": conv_state,
+            "value_w": value_w.transpose(0, 2, 1)[0],
+            "out_w": out_w[0],
+        }
+    )
+
+    received = [head_shift(tokens, k) for k in (1, 3, 2)]
+    page = window_page(pages_first)
+    near, received = lax.optimization_barrier((near, received))
+    page, received = lax.optimization_barrier((page, received))
+    row_pages = [x_shift(page, k) for k in (1, 3, 2)]
+    update = linear_layer([tokens] + received, near)
+    row_pages, update = lax.optimization_barrier((row_pages, update))
+    near_pages = jnp.stack([row_pages[0], page, row_pages[1], row_pages[2]])
+    far_pages = z_shift(near_pages, ZN // 2)
     own_pages = own_pages.transpose(0, 1, 3, 2)
-    prompt_pages = prompt_pages.transpose(0, 1, 3, 2)
-
-    received = [token_shift(tokens, k) for k in (1, 3, 2)]
-    page = window_page(prompt_pages)
-    row_pages = [page_shift(page, 0, k) for k in (1, 3, 2)]
-    near_pages = jnp.stack([row_pages[0], page, row_pages[1], row_pages[2]])
-    near_pages, received = lax.optimization_barrier((near_pages, received))
-    far_pages = page_shift(near_pages, ZN // 2, 0)
-
-    update = linear_layer(
-        [tokens] + received,
-        norm_gain,
-        feature_w,
-        value_w,
-        out_w,
-        conv_w,
-        conv_state,
-        lin_state,
-        lin_norm,
-    )
-    table, ends, update = lax.optimization_barrier((page_table, lengths, update))
-    tags = jnp.concatenate([table[:, :1], ends[:, None]], axis=1)
+    query_key_w, own_pages, page_table, ends, update = lax.optimization_barrier(
+        (query_key_w, own_pages, page_table, lengths, update)
+    )
+    near["query_key_w"], near["own_pages"] = bring_windows(
+        page_table, ends, query_key_w, own_pages
+    )
+    tags = jnp.concatenate([page_table[:, :1], ends[:, None]], axis=1)
     swapped = [section_swap(update, k) for k in (0, 1, 3, 2)]
-    one_share, packed, key_new, value_new = project(
-        tags, swapped, norm_gain, query_key_w, value_w
-    )
+    one_share, packed, key_new, value_new = project(tags, swapped, near)
     asked = [packed] + [z_shift(packed, k) for k in (1, 7, 2)]
-    one_back = lax.ppermute(one_share, "section", [(1, 0)])
-    own_query, one_back = lax.optimization_barrier((packed, one_back))
-    own = own_attention(page_table, lengths, own_query, key_new, value_new, own_pages)
+    own = own_attention(lengths, packed, key_new, value_new, near)
     asked, own = lax.optimization_barrier((asked, own))
     answers = prompt_attention(asked, near_pages, far_pages)
+    answers, one_share = lax.optimization_barrier((answers, one_share))
     parts = [answers[0]] + [z_shift(answers[at], -k) for at, k in ((1, 1), (2, 7), (3, 2))]
-    slabs = combine(own, parts, out_w)
+    one_back = lax.ppermute(one_share, "section", [(1, 0), (0, 1)])
+    parts, one_back = lax.optimization_barrier((parts, one_back))
+    slabs = combine(own, parts, near)
     section_index = lax.axis_index("section")
     total = one_share.astype(jnp.float32) + slabs[0]
     for piece in [head_shift(slabs[k], k) for k in (1, 3, 2)]:

time: 62.1 us -> 63.7 us (1.026)
  starting transfers between devices: 38.6 us -> 35.4 us
  Pallas kernels: 9.84 us -> 12.6 us
  local copies, waits for them, and re-layouts: 0.23 us -> 1.57 us
  other arithmetic: 0.68 us -> 1.45 us
    ppermute x8 -> x4, starting transfers between devices: 22.8 us -> 5.39 us  [the longest x3 4.29 us: x_shift(): lax.ppermute(value, 'req', [(z * XN + i, z * XN + (i + steps) % XN) for z...]
    ppermute x6 -> x7, starting transfers between devices: 7.96 us -> 16 us  [z_shift(): lax.ppermute(value, 'req', [(z * XN + i, (z + steps) % ZN * XN + i) for z...]
    ppermute x3 -> x6, starting transfers between devices: 3.16 us -> 8.05 us  [head_shift(): lax.ppermute(value, 'head', [(i, (i + steps) % count) for i in range(coun...]
    ppermute x4, waiting for transfers between devices: 4.52 us -> 0.01 us  [section_swap(): lax.ppermute(value, ('section', 'head'), there + [(b, a) for a, b in there])]
    pallas_call x6 -> x8, Pallas kernels: 9.84 us -> 12.6 us  [kernel_call(): pl.pallas_call(run, out_shape=out_shape, in_specs=in_specs, out_specs=jax...]
    ppermute x8 -> x4, waiting for transfers between devices: 3.02 us -> 5.51 us  [the longest x3 4.68 us: x_shift(): lax.ppermute(value, 'req', [(z * XN + i, z * XN + (i + steps) % XN) for z...]
    ppermute x6 -> x7, waiting for transfers between devices: 0.92 us -> 2.99 us  [z_shift(): lax.ppermute(value, 'req', [(z * XN + i, (z + steps) % ZN * XN + i) for z...]
    ppermute x4, starting transfers between devices: 4.6 us -> 6.01 us  [section_swap(): lax.ppermute(value, ('section', 'head'), there + [(b, a) for a, b in there])]
  transfers between devices with their start and end apart: 21 -> 21, of which waited for: 9 -> 7; matrix products, arithmetic and copies ran while one was open for 0% -> 2% of each run, Pallas kernels for 12% -> 16%
where the time goes in v4:
time: 63.7 us; the launch traced here: 63.5 us
  starting transfers between devices  35.4 us (56%)
  Pallas kernels  12.6 us (20%)
  waiting for transfers between devices  12.3 us (19%)
  local copies, waits for them, and re-layouts  1.57 us (2%)
  other arithmetic  1.45 us (2%)
    ppermute x7, starting transfers between devices, z_shift(): lax.ppermute(value, 'req', [(z * XN + i, (z + steps) % ZN * XN + i) for z...  16 us
    pallas_call x8, Pallas kernels, kernel_call(): pl.pallas_call(run, out_shape=out_shape, in_specs=in_specs, out_specs=jax...  12.6 us
    ppermute x6, starting transfers between devices, head_shift(): lax.ppermute(value, 'head', [(i, (i + steps) % count) for i in range(coun...  8.05 us
    ppermute x4, starting transfers between devices, section_swap(): lax.ppermute(value, ('section', 'head'), there + [(b, a) for a, b in there])  6.01 us
    ppermute x3, waiting for transfers between devices, x_shift(): lax.ppermute(value, 'req', [(z * XN + i, z * XN + (i + steps) % XN) for z...  4.68 us
    ppermute x3, starting transfers between devices, x_shift(): lax.ppermute(value, 'req', [(z * XN + i, z * XN + (i + steps) % XN) for z...  4.29 us
    ppermute x6, waiting for transfers between devices, head_shift(): lax.ppermute(value, 'head', [(i, (i + steps) % count) for i in range(coun...  3.8 us
    ppermute x7, waiting for transfers between devices, z_shift(): lax.ppermute(value, 'req', [(z * XN + i, (z + steps) % ZN * XN + i) for z...  2.99 us
  transfers between devices with their start and end apart: 21, of which 7 were waited for; matrix products, arithmetic and copies ran while one was open for 2% of the time, Pallas kernels for 16%

profile of v4, /device:TPU:1, one launch (start us, length us, event | category | flops | bytes accessed | tf_op | source)
XLA Modules:
  0.0 63.5 jit_solution(5201792064722739407)
XLA Ops:
  0.0 2.1 %collective-permute-start = (bf16[8,448]{1,0:T(8,128)(2,1)}, bf16[8,448]{1,0:T(8,128)(2,1)S(1)}, u32[]{:S(2)}, u32[]{:S(2)}) collective-permute-start(bf16[8,448]{1,0:T(8,128)(2,1)} %refs_0_.4), channel_id=1, source_target_pairs={{0,1},{1,2},{2,3},{3,0},{4,5},{5,6},{6,7},{7,4},{8,9},{9,10},{10,1... | collective-permute-start | bytes 21512 | tf_op jit(solution)/shard_map/ppermute | solution.py:28
  2.1 1.4 %collective-permute-start.1 = (bf16[8,448]{1,0:T(8,128)(2,1)}, bf16[8,448]{1,0:T(8,128)(2,1)S(1)}, u32[]{:S(2)}, u32[]{:S(2)}) collective-permute-start(bf16[8,448]{1,0:T(8,128)(2,1)} %refs_0_.4), channel_id=1, source_target_pairs={{0,3},{1,0},{2,1},{3,2},{4,7},{5,4},{6,5},{7,6},{8,11},{9,8},{10,9... | collective-permute-start | bytes 21512 | tf_op jit(solution)/shard_map/ppermute | solution.py:28
  3.6 1.6 %collective-permute-start.2 = (bf16[8,448]{1,0:T(8,128)(2,1)}, bf16[8,448]{1,0:T(8,128)(2,1)S(1)}, u32[]{:S(2)}, u32[]{:S(2)}) collective-permute-start(bf16[8,448]{1,0:T(8,128)(2,1)} %refs_0_.4), channel_id=1, source_target_pairs={{0,2},{1,3},{2,0},{3,1},{4,6},{5,7},{6,4},{7,5},{8,10},{9,11},{10,... | collective-permute-start | bytes 21512 | tf_op jit(solution)/shard_map/ppermute | solution.py:28
  5.2 1.0 %window_page.1 = bf16[448,128]{1,0:T(8,128)(2,1)S(1)} custom-call(bf16[1,2,448,128]{3,2,1,0:T(8,128)(2,1)} %bitcast.22), custom_call_target="tpu_custom_call" | custom-call | bytes 16777216 | tf_op jit(solution)/shard_map/window_page/pallas_call | solution.py:105
  6.3 0.0 copy-start.1
  6.3 2.0 %bring_near.1 = (f32[1,1792]{1,0:T(1,128)S(1)}, bf16[1792,128]{1,0:T(8,128)(2,1)S(1)}, bf16[8736,112]{1,0:T(8,128)(2,1)S(1)}, f32[8,4,273]{2,1,0:T(4,128)S(1)}, ...) custom-call(f32[1,1792]{1,0:T(1,128)} %refs_0_.3, ...), custom_call_target="tpu_custom_call" | custom-call | bytes 11377408 | tf_op jit(solution)/shard_map/bring_near/pallas_call | solution.py:105
  8.3 0.0 collective-permute-done.refs_1_
  8.3 0.0 collective-permute-done.2.refs_3_
  8.3 0.0 copy-start
  8.3 0.0 copy-start.2
  8.4 1.3 %collective-permute-start.3 = (bf16[448,128]{1,0:T(8,128)(2,1)S(1)}, bf16[448,128]{1,0:T(8,128)(2,1)S(1)}, u32[]{:S(2)}, u32[]{:S(2)}) collective-permute-start(bf16[448,128]{1,0:T(8,128)(2,1)S(1)} %window_page.1), channel_id=1, source_target_pairs={{0,4},{4,8},{8,12},{12,0},{16,20},{20,24},{24,28},{28,16},{32,36},... | collective-permute-start | bytes 344072 | tf_op jit(solution)/shard_map/ppermute | solution.py:40
  9.6 1.5 %collective-permute-start.4 = (bf16[448,128]{1,0:T(8,128)(2,1)S(1)}, bf16[448,128]{1,0:T(8,128)(2,1)S(1)}, u32[]{:S(2)}, u32[]{:S(2)}) collective-permute-start(bf16[448,128]{1,0:T(8,128)(2,1)S(1)} %window_page.1), channel_id=1, source_target_pairs={{0,12},{4,0},{8,4},{12,8},{16,28},{20,16},{24,20},{28,24},{32,44},... | collective-permute-start | bytes 344072 | tf_op jit(solution)/shard_map/ppermute | solution.py:40
  11.1 1.5 %collective-permute-start.5 = (bf16[448,128]{1,0:T(8,128)(2,1)S(1)}, bf16[448,128]{1,0:T(8,128)(2,1)S(1)}, u32[]{:S(2)}, u32[]{:S(2)}) collective-permute-start(bf16[448,128]{1,0:T(8,128)(2,1)S(1)} %window_page.1), channel_id=1, source_target_pairs={{0,8},{4,12},{8,0},{12,4},{16,24},{20,28},{24,16},{28,20},{32,40},... | collective-permute-start | bytes 344072 | tf_op jit(solution)/shard_map/ppermute | solution.py:40
  12.7 0.6 %collective-permute-done.3 = bf16[448,128]{1,0:T(8,128)(2,1)S(1)} collective-permute-done((bf16[448,128]{1,0:T(8,128)(2,1)S(1)}, bf16[448,128]{1,0:T(8,128)(2,1)S(1)}, u32[]{:S(2)}, u32[]{:S(2)}) %collective-permute-start.3) | collective-permute-done | bytes 114720 | tf_op jit(solution)/shard_map/ppermute | solution.py:40
  13.3 4.0 %collective-permute-done.5 = bf16[448,128]{1,0:T(8,128)(2,1)S(1)} collective-permute-done((bf16[448,128]{1,0:T(8,128)(2,1)S(1)}, bf16[448,128]{1,0:T(8,128)(2,1)S(1)}, u32[]{:S(2)}, u32[]{:S(2)}) %collective-permute-start.5) | collective-permute-done | bytes 114720 | tf_op jit(solution)/shard_map/ppermute | solution.py:40
  17.3 0.8 %pad_maximum_fusion.refs_4_ = bf16[4,448,128]{2,1,0:T(8,128)(2,1)} fusion(bf16[1,448,128]{2,1,0:T(8,128)(2,1)S(1)} %bitcast.25, bf16[1,448,128]{2,1,0:T(8,128)(2,1)S(1)} %bitcast.24, bf16[1,448,128]{2,1,0:T(8,128)(2,1)S(1)} %bitcast.16, bf16[1,448,128]{2,1,0:T(8,128)(2,1)S(1)} %bitcast.23), kind=kLoop, calls=%fused_computation | loop fusion | flops 688128 | bytes 917504 | tf_op jit(solution)/shard_map/stack | solution.py:639
  18.2 6.9 %collective-permute-start.13 = (bf16[4,448,128]{2,1,0:T(8,128)(2,1)}, bf16[4,448,128]{2,1,0:T(8,128)(2,1)}, u32[]{:S(2)}, u32[]{:S(2)}) collective-permute-start(bf16[4,448,128]{2,1,0:T(8,128)(2,1)} %pad_maximum_fusion.refs_4_), channel_id=1, source_target_pairs={{0,64},{4,68},{8,72},{12,76},{16,80},{20,84},{24,88},{28,92},{32,9... | collective-permute-start | bytes 1376264 | tf_op jit(solution)/shard_map/ppermute | solution.py:32
  25.1 2.6 %collective-permute-start.6 = (f32[8,1792]{1,0:T(8,128)S(1)}, f32[8,1792]{1,0:T(8,128)S(1)}, u32[]{:S(2)}, u32[]{:S(2)}) collective-permute-start(f32[8,1792]{1,0:T(8,128)S(1)} %linear_layer.1), channel_id=1, source_target_pairs={{0,128},{1,129},{2,130},{3,131},{128,0},{129,1},{130,2},{131,3},{4... | collective-permute-start | bytes 172040 | tf_op jit(solution)/shard_map/ppermute | solution.py:50
  27.7 1.4 %collective-permute-start.7 = (f32[8,1792]{1,0:T(8,128)S(1)}, f32[8,1792]{1,0:T(8,128)S(1)}, u32[]{:S(2)}, u32[]{:S(2)}) collective-permute-start(f32[8,1792]{1,0:T(8,128)S(1)} %linear_layer.1), channel_id=1, source_target_pairs={{0,129},{1,130},{2,131},{3,128},{129,0},{130,1},{131,2},{128,3},{4... | collective-permute-start | bytes 172040 | tf_op jit(solution)/shard_map/ppermute | solution.py:50
  29.1 0.3 collective-permute-start.8
  29.3 1.8 %collective-permute-start.9 = (f32[8,1792]{1,0:T(8,128)S(1)}, f32[8,1792]{1,0:T(8,128)S(1)}, u32[]{:S(2)}, u32[]{:S(2)}) collective-permute-start(f32[8,1792]{1,0:T(8,128)S(1)} %linear_layer.1), channel_id=1, source_target_pairs={{0,130},{1,131},{2,128},{3,129},{130,0},{131,1},{128,2},{129,3},{4... | collective-permute-start | bytes 172040 | tf_op jit(solution)/shard_map/ppermute | solution.py:50
  31.1 0.8 %copy.16 = s32[8,256]{0,1:T(8,128)} copy(s32[8,256]{1,0:T(8,128)S(1)} %copy-done) | data formatting | bytes 16384 | tf_op jit(solution)/shard_map/optimization_barrier | solution.py:642
  31.9 0.7 %slice.4 = s32[8,1]{0,1:T(1,128)S(1)} slice(s32[8,256]{0,1:T(8,128)} %copy.16), slice={[0:8], [0:1]} | slice | bytes 64 | tf_op jit(solution)/shard_map/slice | solution.py:648
  32.6 0.1 copy.17.refs_0_
  32.7 3.9 %bring_windows.1 = (bf16[1792,896]{1,0:T(8,128)(2,1)S(1)}, bf16[8,2,2,448,128]{4,3,2,1,0:T(8,128)(2,1)S(1)}) custom-call(s32[8,256]{1,0:T(8,128)S(1)} %copy-done, s32[8]{0:T(128)S(1)} %copy-done.2, bf16[1792,896]{1,0:T(8,128)(2,1)} %refs_2_, bf16[16,2,448,128]{3,2,1,0:T(8,128)(2,1)} %bitcast.18), custom_call_target="tpu_custom_call" | custom-call | bytes 13762560 | tf_op jit(solution)/shard_map/bring_windows/pallas_call | solution.py:105
  36.6 0.0 collective-permute-done.6.refs_1_
  36.6 0.0 collective-permute-done.7.refs_2_
  36.7 1.1 %project.1 = (bf16[8,448]{1,0:T(8,128)(2,1)S(1)}, bf16[8,512]{1,0:T(8,128)(2,1)S(1)}, bf16[8,448]{1,0:T(8,128)(2,1)S(1)}, bf16[8,448]{1,0:T(8,128)(2,1)S(1)}) custom-call(s32[8,2]{1,0:T(8,128)S(1)} %copy.17.refs_0_, f32[8,1792]{1,0:T(8,128)S(1)} %collective-permute-done.6.refs_1_, f32[8,1792]{1,0:T(8,128)S(1)} %collective-permute-done.7.refs_2_, ...), custom_call_target="tpu_custom_call" | custom-call | tf_op jit(solution)/shard_map/project/pallas_call | solution.py:105
  37.7 0.8 %collective-permute-start.10 = (bf16[8,512]{1,0:T(8,128)(2,1)S(1)}, bf16[8,512]{1,0:T(8,128)(2,1)S(1)}, u32[]{:S(2)}, u32[]{:S(2)}) collective-permute-start(bf16[8,512]{1,0:T(8,128)(2,1)S(1)} %get-tuple-element.108.refs_1_.refs_0_), channel_id=1, source_target_pairs={{0,16},{4,20},{8,24},{12,28},{16,32},{20,36},{24,40},{28,44},{32,4... | collective-permute-start | bytes 24584 | tf_op jit(solution)/shard_map/ppermute | solution.py:32
  38.5 2.0 %collective-permute-start.11 = (bf16[8,512]{1,0:T(8,128)(2,1)S(1)}, bf16[8,512]{1,0:T(8,128)(2,1)S(1)}, u32[]{:S(2)}, u32[]{:S(2)}) collective-permute-start(bf16[8,512]{1,0:T(8,128)(2,1)S(1)} %get-tuple-element.108.refs_1_.refs_0_), channel_id=1, source_target_pairs={{0,112},{4,116},{8,120},{12,124},{16,0},{20,4},{24,8},{28,12},{32,... | collective-permute-start | bytes 24584 | tf_op jit(solution)/shard_map/ppermute | solution.py:32
  40.4 0.0 collective-permute-start.12
  40.4 1.9 %own_attention.1 = (f32[8,448]{1,0:T(8,128)S(1)}, f32[8,448]{1,0:T(8,128)S(1)}, f32[8,448]{1,0:T(8,128)S(1)}) custom-call(s32[8]{0:T(128)S(1)} %copy-done.2, bf16[8,512]{1,0:T(8,128)(2,1)S(1)} %get-tuple-element.108.refs_1_.refs_0_, bf16[8,448]{1,0:T(8,128)(2,1)S(1)} %get-tuple-element.102.refs_2_, bf16[8,448]{1,0:T(8,128)(2,1)S(1)} %get-tuple-element.103.refs_3_, ...), custom_call_target="tpu_custom_call" | custom-call | tf_op jit(solution)/shard_map/own_attention/pallas_call | solution.py:105
  42.4 2.9 %collective-permute-done.10.refs_1_ = bf16[8,512]{1,0:T(8,128)(2,1)S(1)} collective-permute-done((bf16[8,512]{1,0:T(8,128)(2,1)S(1)}, bf16[8,512]{1,0:T(8,128)(2,1)S(1)}, u32[]{:S(2)}, u32[]{:S(2)}) %collective-permute-start.10) | collective-permute-done | bytes 8224 | tf_op jit(solution)/shard_map/ppermute | solution.py:32
  45.3 0.1 collective-permute-done.12.refs_3_
  45.3 0.0 collective-permute-done.13.refs_5_
  45.3 2.1 %prompt_attention.1 = (f32[8,640]{1,0:T(8,128)S(1)}, f32[8,640]{1,0:T(8,128)S(1)}, f32[8,640]{1,0:T(8,128)S(1)}, f32[8,640]{1,0:T(8,128)S(1)}) custom-call(bf16[8,512]{1,0:T(8,128)(2,1)S(1)} %get-tuple-element.108.refs_1_.refs_0_, bf16[8,512]{1,0:T(8,128)(2,1)S(1)} %collective-permute-done.10.refs_1_, bf16[8,512]{1,0:T(8,128)(2,1)S(1)} %collective-permute-done.11.refs_2_, ...), custom_call_target="tpu_custom_call" | custom-call | tf_op jit(solution)/shard_map/prompt_attention/pallas_call | solution.py:105
  47.4 2.3 %collective-permute-start.14 = (f32[8,640]{1,0:T(8,128)S(1)}, f32[8,640]{1,0:T(8,128)S(1)}, u32[]{:S(2)}, u32[]{:S(2)}) collective-permute-start(f32[8,640]{1,0:T(8,128)S(1)} %get-tuple-element.121), channel_id=1, source_target_pairs={{0,112},{4,116},{8,120},{12,124},{16,0},{20,4},{24,8},{28,12},{32,... | collective-permute-start | bytes 61448 | tf_op jit(solution)/shard_map/ppermute | solution.py:32
  49.7 0.0 collective-permute-start.15
  49.7 4.0 %collective-permute-start.16 = (f32[8,640]{1,0:T(8,128)S(1)}, f32[8,640]{1,0:T(8,128)S(1)}, u32[]{:S(2)}, u32[]{:S(2)}) collective-permute-start(f32[8,640]{1,0:T(8,128)S(1)} %get-tuple-element.123), channel_id=1, source_target_pairs={{0,96},{4,100},{8,104},{12,108},{16,112},{20,116},{24,120},{28,124... | collective-permute-start | bytes 61448 | tf_op jit(solution)/shard_map/ppermute | solution.py:32
  53.8 1.1 %collective-permute-start.17 = (bf16[8,448]{1,0:T(8,128)(2,1)S(1)}, bf16[8,448]{1,0:T(8,128)(2,1)S(1)}, u32[]{:S(2)}, u32[]{:S(2)}) collective-permute-start(bf16[8,448]{1,0:T(8,128)(2,1)S(1)} %get-tuple-element.124), channel_id=1, source_target_pairs={{128,0},{0,128},{129,1},{1,129},{130,2},{2,130},{131,3},{3,131},{1... | collective-permute-start | bytes 21512 | tf_op jit(solution)/shard_map/ppermute | solution.py:657
  54.9 0.8 %collective-permute-done.17 = bf16[8,448]{1,0:T(8,128)(2,1)S(1)} collective-permute-done((bf16[8,448]{1,0:T(8,128)(2,1)S(1)}, bf16[8,448]{1,0:T(8,128)(2,1)S(1)}, u32[]{:S(2)}, u32[]{:S(2)}) %collective-permute-start.17) | collective-permute-done | bytes 7200 | tf_op jit(solution)/shard_map/ppermute | solution.py:657
  55.7 0.6 combine.1
  56.3 1.1 %collective-permute-start.20 = (f32[8,448]{1,0:T(8,128)S(1)}, f32[8,448]{1,0:T(8,128)S(1)}, u32[]{:S(2)}, u32[]{:S(2)}) collective-permute-start(f32[8,448]{1,0:T(8,128)S(1)} %get-tuple-element.136), channel_id=1, source_target_pairs={{0,2},{1,3},{2,0},{3,1},{4,6},{5,7},{6,4},{7,5},{8,10},{9,11},{10,... | collective-permute-start | bytes 43016 | tf_op jit(solution)/shard_map/ppermute | solution.py:28
  57.4 1.8 %collective-permute-start.19 = (f32[8,448]{1,0:T(8,128)S(1)}, f32[8,448]{1,0:T(8,128)S(1)}, u32[]{:S(2)}, u32[]{:S(2)}) collective-permute-start(f32[8,448]{1,0:T(8,128)S(1)} %get-tuple-element.135), channel_id=1, source_target_pairs={{0,3},{1,0},{2,1},{3,2},{4,7},{5,4},{6,5},{7,6},{8,11},{9,8},{10,9... | collective-permute-start | bytes 43016 | tf_op jit(solution)/shard_map/ppermute | solution.py:28
  59.1 1.3 %collective-permute-done.20 = f32[8,448]{1,0:T(8,128)S(1)} collective-permute-done((f32[8,448]{1,0:T(8,128)S(1)}, f32[8,448]{1,0:T(8,128)S(1)}, u32[]{:S(2)}, u32[]{:S(2)}) %collective-permute-start.20) | collective-permute-done | bytes 14368 | tf_op jit(solution)/shard_map/ppermute | solution.py:28
  60.5 0.0 collective-permute-done.19
  60.5 2.5 %collective-permute-done.18 = f32[8,448]{1,0:T(8,128)S(1)} collective-permute-done((f32[8,448]{1,0:T(8,128)S(1)}, f32[8,448]{1,0:T(8,128)S(1)}, u32[]{:S(2)}, u32[]{:S(2)}) %collective-permute-start.18) | collective-permute-done | bytes 14368 | tf_op jit(solution)/shard_map/ppermute | solution.py:28
  62.9 0.6 fusion.1
  (14 shorter events, 0.0 us)
Async XLA Ops:
  0.0 8.3 %collective-permute-start = (bf16[8,448]{1,0:T(8,128)(2,1)}, bf16[8,448]{1,0:T(8,128)(2,1)S(1)}, u32[]{:S(2)}, u32[]{:S(2)}) collective-permute-start(bf16[8,448]{1,0:T(8,128)(2,1)} %refs_0_.4), channel_id=1, source_target_pairs={{0,1},{1,2},{2,3},{3,0},{4,5},{5,6},{6,7},{7,4},{8,9},{9,10},{10,1... | collective-permute-start | bytes 21512 | tf_op jit(solution)/shard_map/ppermute | solution.py:28
  2.1 6.2 %collective-permute-start.1 = (bf16[8,448]{1,0:T(8,128)(2,1)}, bf16[8,448]{1,0:T(8,128)(2,1)S(1)}, u32[]{:S(2)}, u32[]{:S(2)}) collective-permute-start(bf16[8,448]{1,0:T(8,128)(2,1)} %refs_0_.4), channel_id=1, source_target_pairs={{0,3},{1,0},{2,1},{3,2},{4,7},{5,4},{6,5},{7,6},{8,11},{9,8},{10,9... | collective-permute-start | bytes 21512 | tf_op jit(solution)/shard_map/ppermute | solution.py:28
  3.6 4.8 %collective-permute-start.2 = (bf16[8,448]{1,0:T(8,128)(2,1)}, bf16[8,448]{1,0:T(8,128)(2,1)S(1)}, u32[]{:S(2)}, u32[]{:S(2)}) collective-permute-start(bf16[8,448]{1,0:T(8,128)(2,1)} %refs_0_.4), channel_id=1, source_target_pairs={{0,2},{1,3},{2,0},{3,1},{4,6},{5,7},{6,4},{7,5},{8,10},{9,11},{10,... | collective-permute-start | bytes 21512 | tf_op jit(solution)/shard_map/ppermute | solution.py:28
  6.3 6.4 %copy-start.1 = (bf16[8,448]{1,0:T(8,128)(2,1)S(1)}, bf16[8,448]{1,0:T(8,128)(2,1)}, u32[]{:S(2)}) copy-start(bf16[8,448]{1,0:T(8,128)(2,1)} %refs_0_.4) | copy-start | bytes 21508
  8.3 22.8 %copy-start = (s32[8,256]{1,0:T(8,128)S(1)}, s32[8,256]{1,0:T(8,128)}, u32[]{:S(2)}) copy-start(s32[8,256]{1,0:T(8,128)} %refs_0_.5) | copy-start | bytes 24580
  8.3 24.2 %copy-start.2 = (s32[8]{0:T(128)S(1)}, s32[8]{0:T(128)}, u32[]{:S(2)}) copy-start(s32[8]{0:T(128)} %refs_0_.6) | copy-start | bytes 100
  8.4 4.9 %collective-permute-start.3 = (bf16[448,128]{1,0:T(8,128)(2,1)S(1)}, bf16[448,128]{1,0:T(8,128)(2,1)S(1)}, u32[]{:S(2)}, u32[]{:S(2)}) collective-permute-start(bf16[448,128]{1,0:T(8,128)(2,1)S(1)} %window_page.1), channel_id=1, source_target_pairs={{0,4},{4,8},{8,12},{12,0},{16,20},{20,24},{24,28},{28,16},{32,36},... | collective-permute-start | bytes 344072 | tf_op jit(solution)/shard_map/ppermute | solution.py:40
  9.6 3.6 %collective-permute-start.4 = (bf16[448,128]{1,0:T(8,128)(2,1)S(1)}, bf16[448,128]{1,0:T(8,128)(2,1)S(1)}, u32[]{:S(2)}, u32[]{:S(2)}) collective-permute-start(bf16[448,128]{1,0:T(8,128)(2,1)S(1)} %window_page.1), channel_id=1, source_target_pairs={{0,12},{4,0},{8,4},{12,8},{16,28},{20,16},{24,20},{28,24},{32,44},... | collective-permute-start | bytes 344072 | tf_op jit(solution)/shard_map/ppermute | solution.py:40
  11.1 6.2 %collective-permute-start.5 = (bf16[448,128]{1,0:T(8,128)(2,1)S(1)}, bf16[448,128]{1,0:T(8,128)(2,1)S(1)}, u32[]{:S(2)}, u32[]{:S(2)}) collective-permute-start(bf16[448,128]{1,0:T(8,128)(2,1)S(1)} %window_page.1), channel_id=1, source_target_pairs={{0,8},{4,12},{8,0},{12,4},{16,24},{20,28},{24,16},{28,20},{32,40},... | collective-permute-start | bytes 344072 | tf_op jit(solution)/shard_map/ppermute | solution.py:40
  18.2 27.2 %collective-permute-start.13 = (bf16[4,448,128]{2,1,0:T(8,128)(2,1)}, bf16[4,448,128]{2,1,0:T(8,128)(2,1)}, u32[]{:S(2)}, u32[]{:S(2)}) collective-permute-start(bf16[4,448,128]{2,1,0:T(8,128)(2,1)} %pad_maximum_fusion.refs_4_), channel_id=1, source_target_pairs={{0,64},{4,68},{8,72},{12,76},{16,80},{20,84},{24,88},{28,92},{32,9... | collective-permute-start | bytes 1376264 | tf_op jit(solution)/shard_map/ppermute | solution.py:32
  25.1 11.5 %collective-permute-start.6 = (f32[8,1792]{1,0:T(8,128)S(1)}, f32[8,1792]{1,0:T(8,128)S(1)}, u32[]{:S(2)}, u32[]{:S(2)}) collective-permute-start(f32[8,1792]{1,0:T(8,128)S(1)} %linear_layer.1), channel_id=1, source_target_pairs={{0,128},{1,129},{2,130},{3,131},{128,0},{129,1},{130,2},{131,3},{4... | collective-permute-start | bytes 172040 | tf_op jit(solution)/shard_map/ppermute | solution.py:50
  27.7 9.0 %collective-permute-start.7 = (f32[8,1792]{1,0:T(8,128)S(1)}, f32[8,1792]{1,0:T(8,128)S(1)}, u32[]{:S(2)}, u32[]{:S(2)}) collective-permute-start(f32[8,1792]{1,0:T(8,128)S(1)} %linear_layer.1), channel_id=1, source_target_pairs={{0,129},{1,130},{2,131},{3,128},{129,0},{130,1},{131,2},{128,3},{4... | collective-permute-start | bytes 172040 | tf_op jit(solution)/shard_map/ppermute | solution.py:50
  29.1 7.5 %collective-permute-start.8 = (f32[8,1792]{1,0:T(8,128)S(1)}, f32[8,1792]{1,0:T(8,128)S(1)}, u32[]{:S(2)}, u32[]{:S(2)}) collective-permute-start(f32[8,1792]{1,0:T(8,128)S(1)} %linear_layer.1), channel_id=1, source_target_pairs={{0,131},{1,128},{2,129},{3,130},{131,0},{128,1},{129,2},{130,3},{4... | collective-permute-start | bytes 172040 | tf_op jit(solution)/shard_map/ppermute | solution.py:50
  29.3 7.3 %collective-permute-start.9 = (f32[8,1792]{1,0:T(8,128)S(1)}, f32[8,1792]{1,0:T(8,128)S(1)}, u32[]{:S(2)}, u32[]{:S(2)}) collective-permute-start(f32[8,1792]{1,0:T(8,128)S(1)} %linear_layer.1), channel_id=1, source_target_pairs={{0,130},{1,131},{2,128},{3,129},{130,0},{131,1},{128,2},{129,3},{4... | collective-permute-start | bytes 172040 | tf_op jit(solution)/shard_map/ppermute | solution.py:50
  37.7 7.5 %collective-permute-start.10 = (bf16[8,512]{1,0:T(8,128)(2,1)S(1)}, bf16[8,512]{1,0:T(8,128)(2,1)S(1)}, u32[]{:S(2)}, u32[]{:S(2)}) collective-permute-start(bf16[8,512]{1,0:T(8,128)(2,1)S(1)} %get-tuple-element.108.refs_1_.refs_0_), channel_id=1, source_target_pairs={{0,16},{4,20},{8,24},{12,28},{16,32},{20,36},{24,40},{28,44},{32,4... | collective-permute-start | bytes 24584 | tf_op jit(solution)/shard_map/ppermute | solution.py:32
  38.5 6.8 %collective-permute-start.11 = (bf16[8,512]{1,0:T(8,128)(2,1)S(1)}, bf16[8,512]{1,0:T(8,128)(2,1)S(1)}, u32[]{:S(2)}, u32[]{:S(2)}) collective-permute-start(bf16[8,512]{1,0:T(8,128)(2,1)S(1)} %get-tuple-element.108.refs_1_.refs_0_), channel_id=1, source_target_pairs={{0,112},{4,116},{8,120},{12,124},{16,0},{20,4},{24,8},{28,12},{32,... | collective-permute-start | bytes 24584 | tf_op jit(solution)/shard_map/ppermute | solution.py:32
  40.4 4.9 %collective-permute-start.12 = (bf16[8,512]{1,0:T(8,128)(2,1)S(1)}, bf16[8,512]{1,0:T(8,128)(2,1)S(1)}, u32[]{:S(2)}, u32[]{:S(2)}) collective-permute-start(bf16[8,512]{1,0:T(8,128)(2,1)S(1)} %get-tuple-element.108.refs_1_.refs_0_), channel_id=1, source_target_pairs={{0,32},{4,36},{8,40},{12,44},{16,48},{20,52},{24,56},{28,60},{32,6... | collective-permute-start | bytes 24584 | tf_op jit(solution)/shard_map/ppermute | solution.py:32
  47.4 8.3 %collective-permute-start.14 = (f32[8,640]{1,0:T(8,128)S(1)}, f32[8,640]{1,0:T(8,128)S(1)}, u32[]{:S(2)}, u32[]{:S(2)}) collective-permute-start(f32[8,640]{1,0:T(8,128)S(1)} %get-tuple-element.121), channel_id=1, source_target_pairs={{0,112},{4,116},{8,120},{12,124},{16,0},{20,4},{24,8},{28,12},{32,... | collective-permute-start | bytes 61448 | tf_op jit(solution)/shard_map/ppermute | solution.py:32
  49.7 6.0 %collective-permute-start.15 = (f32[8,640]{1,0:T(8,128)S(1)}, f32[8,640]{1,0:T(8,128)S(1)}, u32[]{:S(2)}, u32[]{:S(2)}) collective-permute-start(f32[8,640]{1,0:T(8,128)S(1)} %get-tuple-element.122), channel_id=1, source_target_pairs={{0,16},{4,20},{8,24},{12,28},{16,32},{20,36},{24,40},{28,44},{32,4... | collective-permute-start | bytes 61448 | tf_op jit(solution)/shard_map/ppermute | solution.py:32
  49.7 6.0 %collective-permute-start.16 = (f32[8,640]{1,0:T(8,128)S(1)}, f32[8,640]{1,0:T(8,128)S(1)}, u32[]{:S(2)}, u32[]{:S(2)}) collective-permute-start(f32[8,640]{1,0:T(8,128)S(1)} %get-tuple-element.123), channel_id=1, source_target_pairs={{0,96},{4,100},{8,104},{12,108},{16,112},{20,116},{24,120},{28,124... | collective-permute-start | bytes 61448 | tf_op jit(solution)/shard_map/ppermute | solution.py:32
  53.8 1.9 %collective-permute-start.17 = (bf16[8,448]{1,0:T(8,128)(2,1)S(1)}, bf16[8,448]{1,0:T(8,128)(2,1)S(1)}, u32[]{:S(2)}, u32[]{:S(2)}) collective-permute-start(bf16[8,448]{1,0:T(8,128)(2,1)S(1)} %get-tuple-element.124), channel_id=1, source_target_pairs={{128,0},{0,128},{129,1},{1,129},{130,2},{2,130},{131,3},{3,131},{1... | collective-permute-start | bytes 21512 | tf_op jit(solution)/shard_map/ppermute | solution.py:657
  56.3 4.2 %collective-permute-start.20 = (f32[8,448]{1,0:T(8,128)S(1)}, f32[8,448]{1,0:T(8,128)S(1)}, u32[]{:S(2)}, u32[]{:S(2)}) collective-permute-start(f32[8,448]{1,0:T(8,128)S(1)} %get-tuple-element.136), channel_id=1, source_target_pairs={{0,2},{1,3},{2,0},{3,1},{4,6},{5,7},{6,4},{7,5},{8,10},{9,11},{10,... | collective-permute-start | bytes 43016 | tf_op jit(solution)/shard_map/ppermute | solution.py:28
  57.4 3.1 %collective-permute-start.19 = (f32[8,448]{1,0:T(8,128)S(1)}, f32[8,448]{1,0:T(8,128)S(1)}, u32[]{:S(2)}, u32[]{:S(2)}) collective-permute-start(f32[8,448]{1,0:T(8,128)S(1)} %get-tuple-element.135), channel_id=1, source_target_pairs={{0,3},{1,0},{2,1},{3,2},{4,7},{5,4},{6,5},{7,6},{8,11},{9,8},{10,9... | collective-permute-start | bytes 43016 | tf_op jit(solution)/shard_map/ppermute | solution.py:28
  59.1 3.8 %collective-permute-start.18 = (f32[8,448]{1,0:T(8,128)S(1)}, f32[8,448]{1,0:T(8,128)S(1)}, u32[]{:S(2)}, u32[]{:S(2)}) collective-permute-start(f32[8,448]{1,0:T(8,128)S(1)} %get-tuple-element.134), channel_id=1, source_target_pairs={{0,1},{1,2},{2,3},{3,0},{4,5},{5,6},{6,7},{7,4},{8,9},{9,10},{10,1... | collective-permute-start | bytes 43016 | tf_op jit(solution)/shard_map/ppermute | solution.py:28

commit v5 on v4

--- a/solution.py
+++ b/solution.py
@@ -23,13 +23,21 @@
 MASKED = -1e30
 
 
-def head_shift(value, steps):
+def shift_on(section, value, axis, moves):
+    count = lax.axis_size(axis)
+    pairs = [(section * count + i, section * count + j) for i, j in moves]
+    pairs += [((1 - section) * count + i,) * 2 for i in range(count)]
+    return lax.ppermute(value, ("section", axis), pairs)
+
+
+def head_shift(section, value, steps):
     count = lax.axis_size("head")
-    return lax.ppermute(value, "head", [(i, (i + steps) % count) for i in range(count)])
+    return shift_on(section, value, "head", [(i, (i + steps) % count) for i in range(count)])
 
 
 def z_shift(value, steps):
-    return lax.ppermute(
+    return shift_on(
+        1,
         value,
         "req",
         [(z * XN + i, (z + steps) % ZN * XN + i) for z in range(ZN) for i in range(XN)],
@@ -37,7 +45,8 @@
 
 
 def x_shift(value, steps):
-    return lax.ppermute(
+    return shift_on(
+        1,
         value,
         "req",
         [(z * XN + i, z * XN + (i + steps) % XN) for z in range(ZN) for i in range(XN)],
@@ -280,10 +289,8 @@
             query = jnp.where(in_head(lane, h), moved, query)
         moved = pltpu.roll(query_key, width - (h + 1) * HD, 1)[:, :LANES]
         key = jnp.where(in_head(lane, h), moved, key)
-    group = tags[:, 0:1].astype(jnp.float32)
-    start = jnp.minimum(tags[:, 1:2] - WINDOW, PAGE).astype(jnp.float32)
-    query = jnp.where(lane == share, group, query)
-    query = jnp.where(lane == share + 1, start, query)
+    query = jnp.where(lane == share, tags[:, 0:1], query)
+    query = jnp.where(lane == share + 1, tags[:, 1:2], query)
     asked[...] = query.astype(jnp.bfloat16)
     key_new[...] = key[:, :share].astype(jnp.bfloat16)
 
@@ -313,10 +320,32 @@
 
 
 def own_kernel(
-    ids, lengths, asked, key_new, value_new, pages, summed_out, highest_out, total_out
+    ids,
+    table,
+    lengths,
+    asked,
+    key_new,
+    value_new,
+    own_pages,
+    summed_out,
+    highest_out,
+    total_out,
+    pages,
+    sems,
 ):
     rows, share = key_new.shape
-    bounds = [(lengths[r], *window_pages(lengths, r)) for r in range(rows)]
+    count = own_pages.shape[0]
+    bounds = []
+    copies = []
+    for r in range(rows):
+        first, last = window_pages(lengths, r)
+        bounds.append((lengths[r], first, last))
+        for slot, logical in enumerate((first, last)):
+            page = jnp.clip(table[r, logical] - GROUPS - ids[1] * count, 0, count - 1)
+            copies.append(
+                pltpu.make_async_copy(own_pages.at[page], pages.at[r, slot], sems.at[r, slot])
+            )
+            copies[-1].start()
     head = lax.broadcasted_iota(jnp.int32, (8, share), 0)
     lane = lanes_of((8, share))
     mine = (lane >= head * HD) & (lane < (head + 1) * HD)
@@ -342,6 +371,8 @@
     scores = []
     for r in range(rows):
         low = wide[8 * r : 8 * r + 8].astype(jnp.bfloat16)
+        copies[2 * r].wait()
+        copies[2 * r + 1].wait()
         scores.append(
             jnp.concatenate(
                 [
@@ -375,16 +406,19 @@
             ref[r : r + 1, :] = jnp.sum(jnp.where(mine, value, 0.0), axis=0, keepdims=True)
 
 
-def own_attention(lengths, asked, key_new, value_new, near):
+def own_attention(table, lengths, asked, key_new, value_new, own_pages):
     rows, share = key_new.shape
     return kernel_call(
         own_kernel,
         1,
         "own_attention",
         [jax.ShapeDtypeStruct((rows, share), jnp.float32)] * 3,
-        [SMEM] + [VMEM] * 4,
-        [],
-        (lengths, asked, key_new, value_new, near["own_pages"]),
+        [SMEM] * 2 + [VMEM] * 3 + [HBM],
+        [
+            pltpu.VMEM((rows, 2) + own_pages.shape[1:], jnp.bfloat16),
+            pltpu.SemaphoreType.DMA((rows, 2)),
+        ],
+        (table, lengths, asked, key_new, value_new, own_pages),
     )
 
 
@@ -542,37 +576,33 @@
     return pl.CostEstimate(flops=0, bytes_accessed=2 * moved, transcendentals=0)
 
 
-def window_kernel(
-    ids, table, lengths, query_key_hbm, own_hbm, query_key_near, own_near, key_sem, sems
-):
-    rows = lengths.shape[0]
-    total = own_hbm.shape[0]
-    copies = [pltpu.make_async_copy(query_key_hbm, query_key_near, key_sem)]
-    for r in range(rows):
-        for slot, logical in enumerate(window_pages(lengths, r)):
-            page = jnp.clip(table[r, logical] - GROUPS - ids[1] * total, 0, total - 1)
-            copies.append(
-                pltpu.make_async_copy(own_hbm.at[page], own_near.at[r, slot], sems.at[r, slot])
-            )
-    for copy in copies:
-        copy.start()
-    for copy in copies:
-        copy.wait()
-
-
-def bring_windows(table, lengths, query_key_w, own_pages):
-    rows = lengths.shape[0]
-    windows = jax.ShapeDtypeStruct((rows, 2) + own_pages.shape[1:], own_pages.dtype)
+def query_kernel(ids, table, lengths, query_key_hbm, query_key_near, tags, sem):
+    copy = pltpu.make_async_copy(query_key_hbm, query_key_near, sem)
+    copy.start()
+    row = lax.broadcasted_iota(jnp.int32, tags.shape, 0)
+    first = lanes_of(tags.shape) == 0
+    marks = jnp.zeros(tags.shape, jnp.int32)
+    for r in range(tags.shape[0]):
+        start = jnp.minimum(lengths[r] - WINDOW, PAGE)
+        marks = jnp.where(row == r, jnp.where(first, table[r, 0], start), marks)
+    tags[...] = marks.astype(jnp.float32)
+    copy.wait()
+
+
+def bring_queries(table, lengths, query_key_w):
     return kernel_call(
-        window_kernel,
+        query_kernel,
         1,
-        "bring_windows",
-        [jax.ShapeDtypeStruct(query_key_w.shape, query_key_w.dtype), windows],
-        [SMEM] * 2 + [HBM] * 2,
-        [pltpu.SemaphoreType.DMA, pltpu.SemaphoreType.DMA((rows, 2))],
-        (table, lengths, query_key_w, own_pages),
+        "bring_queries",
+        [
+            jax.ShapeDtypeStruct(query_key_w.shape, query_key_w.dtype),
+            jax.ShapeDtypeStruct((lengths.shape[0], 128), jnp.float32),
+        ],
+        [SMEM] * 2 + [HBM],
+        [pltpu.SemaphoreType.DMA],
+        (table, lengths, query_key_w),
         4 << 20,
-        bytes_only([query_key_w, windows]),
+        bytes_only([query_key_w]),
     )
 
 
@@ -629,7 +659,7 @@
         }
     )
 
-    received = [head_shift(tokens, k) for k in (1, 3, 2)]
+    received = [head_shift(0, tokens, k) for k in (1, 3, 2)]
     page = window_page(pages_first)
     near, received = lax.optimization_barrier((near, received))
     page, received = lax.optimization_barrier((page, received))
@@ -639,17 +669,14 @@
     near_pages = jnp.stack([row_pages[0], page, row_pages[1], row_pages[2]])
     far_pages = z_shift(near_pages, ZN // 2)
     own_pages = own_pages.transpose(0, 1, 3, 2)
-    query_key_w, own_pages, page_table, ends, update = lax.optimization_barrier(
-        (query_key_w, own_pages, page_table, lengths, update)
-    )
-    near["query_key_w"], near["own_pages"] = bring_windows(
-        page_table, ends, query_key_w, own_pages
-    )
-    tags = jnp.concatenate([page_table[:, :1], ends[:, None]], axis=1)
+    query_key_w, table, ends, update = lax.optimization_barrier(
+        (query_key_w, page_table, lengths, update)
+    )
+    near["query_key_w"], tags = bring_queries(table, ends, query_key_w)
     swapped = [section_swap(update, k) for k in (0, 1, 3, 2)]
     one_share, packed, key_new, value_new = project(tags, swapped, near)
     asked = [packed] + [z_shift(packed, k) for k in (1, 7, 2)]
-    own = own_attention(lengths, packed, key_new, value_new, near)
+    own = own_attention(page_table, lengths, packed, key_new, value_new, own_pages)
     asked, own = lax.optimization_barrier((asked, own))
     answers = prompt_attention(asked, near_pages, far_pages)
     answers, one_share = lax.optimization_barrier((answers, one_share))
@@ -659,7 +686,7 @@
     slabs = combine(own, parts, near)
     section_index = lax.axis_index("section")
     total = one_share.astype(jnp.float32) + slabs[0]
-    for piece in [head_shift(slabs[k], k) for k in (1, 3, 2)]:
+    for piece in [head_shift(1, slabs[k], k) for k in (1, 3, 2)]:
         total = total + piece
     output = jnp.where(section_index == 0, one_back, total.astype(jnp.bfloat16))
     return output[None]

time: 63.7 us -> 80.8 us (1.27)
  starting transfers between devices: 35.4 us -> 56 us
  local copies, waits for them, and re-layouts: 1.57 us -> 0.02 us
  waiting for transfers between devices: 12.3 us -> 10.8 us
    ppermute x16, starting transfers between devices: 28.3 us -> 51.5 us  [shift_on(): return lax.ppermute(value, ('section', axis), pairs)]
    ppermute x16, waiting for transfers between devices: 11.5 us -> 7.56 us  [shift_on(): return lax.ppermute(value, ('section', axis), pairs)]
    ppermute x4, waiting for transfers between devices: 0.01 us -> 2.05 us  [section_swap(): lax.ppermute(value, ('section', 'head'), there + [(b, a) for a, b in there])]
    ppermute x4, starting transfers between devices: 6.01 us -> 4.38 us  [section_swap(): lax.ppermute(value, ('section', 'head'), there + [(b, a) for a, b in there])]
    ppermute x1, starting transfers between devices: 1.11 us -> 0.09 us  [body(): one_back = lax.ppermute(one_share, 'section', [(1, 0), (0, 1)])]
  transfers between devices with their start and end apart: 21 -> 21, of which waited for: 7 -> 5; matrix products, arithmetic and copies ran while one was open for 2% -> 0% of each run, Pallas kernels for 16% -> 14%
where the time goes in v5:
time: 80.8 us; the launch traced here: 80.1 us
  starting transfers between devices  56 us (69%)
  Pallas kernels  12.3 us (15%)
  waiting for transfers between devices  10.8 us (13%)
    ppermute x16, starting transfers between devices, shift_on(): return lax.ppermute(value, ('section', axis), pairs)  51.5 us
    pallas_call x8, Pallas kernels, kernel_call(): pl.pallas_call(run, out_shape=out_shape, in_specs=in_specs, out_specs=jax...  12.3 us
    ppermute x16, waiting for transfers between devices, shift_on(): return lax.ppermute(value, ('section', axis), pairs)  7.56 us
    ppermute x4, starting transfers between devices, section_swap(): lax.ppermute(value, ('section', 'head'), there + [(b, a) for a, b in there])  4.38 us
    ppermute x4, waiting for transfers between devices, section_swap(): lax.ppermute(value, ('section', 'head'), there + [(b, a) for a, b in there])  2.05 us
  transfers between devices with their start and end apart: 21, of which 5 were waited for; matrix products, arithmetic and copies ran while one was open for 0% of the time, Pallas kernels for 14%

profile of v5, /device:TPU:1, one launch (start us, length us, event | category | flops | bytes accessed | tf_op | source)
XLA Modules:
  0.0 80.1 jit_solution(867716541619968247)
XLA Ops:
  0.0 1.3 %collective-permute-start = (bf16[8,448]{1,0:T(8,128)(2,1)}, bf16[8,448]{1,0:T(8,128)(2,1)S(1)}, u32[]{:S(2)}, u32[]{:S(2)}) collective-permute-start(bf16[8,448]{1,0:T(8,128)(2,1)} %refs_0_.4), channel_id=1, source_target_pairs={{0,1},{1,2},{2,3},{3,0},{128,128},{129,129},{130,130},{131,131},{4... | collective-permute-start | bytes 21512 | tf_op jit(solution)/shard_map/ppermute | solution.py:30
  1.3 1.3 %collective-permute-start.1 = (bf16[8,448]{1,0:T(8,128)(2,1)}, bf16[8,448]{1,0:T(8,128)(2,1)S(1)}, u32[]{:S(2)}, u32[]{:S(2)}) collective-permute-start(bf16[8,448]{1,0:T(8,128)(2,1)} %refs_0_.4), channel_id=1, source_target_pairs={{0,3},{1,0},{2,1},{3,2},{128,128},{129,129},{130,130},{131,131},{4... | collective-permute-start | bytes 21512 | tf_op jit(solution)/shard_map/ppermute | solution.py:30
  2.7 1.3 %collective-permute-start.2 = (bf16[8,448]{1,0:T(8,128)(2,1)}, bf16[8,448]{1,0:T(8,128)(2,1)S(1)}, u32[]{:S(2)}, u32[]{:S(2)}) collective-permute-start(bf16[8,448]{1,0:T(8,128)(2,1)} %refs_0_.4), channel_id=1, source_target_pairs={{0,2},{1,3},{2,0},{3,1},{128,128},{129,129},{130,130},{131,131},{4... | collective-permute-start | bytes 21512 | tf_op jit(solution)/shard_map/ppermute | solution.py:30
  4.0 1.0 %window_page.1 = bf16[448,128]{1,0:T(8,128)(2,1)S(1)} custom-call(bf16[1,2,448,128]{3,2,1,0:T(8,128)(2,1)} %bitcast.20), custom_call_target="tpu_custom_call" | custom-call | bytes 16777216 | tf_op jit(solution)/shard_map/window_page/pallas_call | solution.py:114
  5.1 0.0 copy-start.1
  5.1 2.0 %bring_near.1 = (f32[1,1792]{1,0:T(1,128)S(1)}, bf16[1792,128]{1,0:T(8,128)(2,1)S(1)}, bf16[8736,112]{1,0:T(8,128)(2,1)S(1)}, f32[8,4,273]{2,1,0:T(4,128)S(1)}, ...) custom-call(f32[1,1792]{1,0:T(1,128)} %refs_0_.3, ...), custom_call_target="tpu_custom_call" | custom-call | bytes 11377408 | tf_op jit(solution)/shard_map/bring_near/pallas_call | solution.py:114
  7.1 0.0 collective-permute-done.refs_1_
  7.1 0.0 collective-permute-done.1.refs_2_
  7.2 0.0 copy-start
  7.2 0.0 copy-start.2
  7.2 3.9 %collective-permute-start.3 = (bf16[448,128]{1,0:T(8,128)(2,1)S(1)}, bf16[448,128]{1,0:T(8,128)(2,1)S(1)}, u32[]{:S(2)}, u32[]{:S(2)}) collective-permute-start(bf16[448,128]{1,0:T(8,128)(2,1)S(1)} %window_page.1), channel_id=1, source_target_pairs={{128,132},{132,136},{136,140},{140,128},{144,148},{148,152},{152,1... | collective-permute-start | bytes 344072 | tf_op jit(solution)/shard_map/ppermute | solution.py:30
  11.1 3.2 %collective-permute-start.4 = (bf16[448,128]{1,0:T(8,128)(2,1)S(1)}, bf16[448,128]{1,0:T(8,128)(2,1)S(1)}, u32[]{:S(2)}, u32[]{:S(2)}) collective-permute-start(bf16[448,128]{1,0:T(8,128)(2,1)S(1)} %window_page.1), channel_id=1, source_target_pairs={{128,140},{132,128},{136,132},{140,136},{144,156},{148,144},{152,1... | collective-permute-start | bytes 344072 | tf_op jit(solution)/shard_map/ppermute | solution.py:30
  14.3 3.6 %collective-permute-start.5 = (bf16[448,128]{1,0:T(8,128)(2,1)S(1)}, bf16[448,128]{1,0:T(8,128)(2,1)S(1)}, u32[]{:S(2)}, u32[]{:S(2)}) collective-permute-start(bf16[448,128]{1,0:T(8,128)(2,1)S(1)} %window_page.1), channel_id=1, source_target_pairs={{128,136},{132,140},{136,128},{140,132},{144,152},{148,156},{152,1... | collective-permute-start | bytes 344072 | tf_op jit(solution)/shard_map/ppermute | solution.py:30
  18.0 0.0 collective-permute-done.3
  18.0 3.3 %collective-permute-done.5 = bf16[448,128]{1,0:T(8,128)(2,1)S(1)} collective-permute-done((bf16[448,128]{1,0:T(8,128)(2,1)S(1)}, bf16[448,128]{1,0:T(8,128)(2,1)S(1)}, u32[]{:S(2)}, u32[]{:S(2)}) %collective-permute-start.5) | collective-permute-done | bytes 114720 | tf_op jit(solution)/shard_map/ppermute | solution.py:30
  21.4 0.1 pad_maximum_fusion.refs_4_
  21.4 9.0 %collective-permute-start.13 = (bf16[4,448,128]{2,1,0:T(8,128)(2,1)S(1)}, bf16[4,448,128]{2,1,0:T(8,128)(2,1)S(1)}, u32[]{:S(2)}, u32[]{:S(2)}) collective-permute-start(bf16[4,448,128]{2,1,0:T(8,128)(2,1)S(1)} %pad_maximum_fusion.refs_4_), channel_id=1, source_target_pairs={{128,192},{132,196},{136,200},{140,204},{144,208},{148,212},{152,2... | collective-permute-start | bytes 1376264 | tf_op jit(solution)/shard_map/ppermute | solution.py:30
  30.5 0.1 collective-permute-start.6
  30.6 3.1 %collective-permute-start.7 = (f32[8,1792]{1,0:T(8,128)S(1)}, f32[8,1792]{1,0:T(8,128)S(1)}, u32[]{:S(2)}, u32[]{:S(2)}) collective-permute-start(f32[8,1792]{1,0:T(8,128)S(1)} %linear_layer.1), channel_id=1, source_target_pairs={{0,129},{1,130},{2,131},{3,128},{129,0},{130,1},{131,2},{128,3},{4... | collective-permute-start | bytes 172040 | tf_op jit(solution)/shard_map/ppermute | solution.py:59
  33.7 1.2 %collective-permute-start.9 = (f32[8,1792]{1,0:T(8,128)S(1)}, f32[8,1792]{1,0:T(8,128)S(1)}, u32[]{:S(2)}, u32[]{:S(2)}) collective-permute-start(f32[8,1792]{1,0:T(8,128)S(1)} %linear_layer.1), channel_id=1, source_target_pairs={{0,130},{1,131},{2,128},{3,129},{130,0},{131,1},{128,2},{129,3},{4... | collective-permute-start | bytes 172040 | tf_op jit(solution)/shard_map/ppermute | solution.py:59
  34.8 2.6 %bring_queries.1 = (bf16[1792,896]{1,0:T(8,128)(2,1)S(1)}, f32[8,128]{1,0:T(8,128)S(1)}) custom-call(s32[8,256]{1,0:T(8,128)S(1)} %copy-done, s32[8]{0:T(128)S(1)} %copy-done.2, bf16[1792,896]{1,0:T(8,128)(2,1)} %refs_2_), custom_call_target="tpu_custom_call" | custom-call | bytes 6422528 | tf_op jit(solution)/shard_map/bring_queries/pallas_call | solution.py:114
  37.5 0.0 collective-permute-done.7.refs_2_
  37.5 2.0 %collective-permute-done.9.refs_4_ = f32[8,1792]{1,0:T(8,128)S(1)} collective-permute-done((f32[8,1792]{1,0:T(8,128)S(1)}, f32[8,1792]{1,0:T(8,128)S(1)}, u32[]{:S(2)}, u32[]{:S(2)}) %collective-permute-start.9) | collective-permute-done | bytes 57376 | tf_op jit(solution)/shard_map/ppermute | solution.py:59
  39.5 1.0 %project.1 = (bf16[8,448]{1,0:T(8,128)(2,1)S(1)}, bf16[8,512]{1,0:T(8,128)(2,1)S(1)}, bf16[8,448]{1,0:T(8,128)(2,1)S(1)}, bf16[8,448]{1,0:T(8,128)(2,1)S(1)}) custom-call(f32[8,128]{1,0:T(8,128)S(1)} %get-tuple-element.97.refs_0_, f32[8,1792]{1,0:T(8,128)S(1)} %collective-permute-done.6.refs_1_, f32[8,1792]{1,0:T(8,128)S(1)} %collective-permute-done.7.refs_2_, ...), custom_call_target="tpu_custom_call" | custom-call | tf_op jit(solution)/shard_map/project/pallas_call | solution.py:114
  40.6 2.7 %collective-permute-start.10 = (bf16[8,512]{1,0:T(8,128)(2,1)S(1)}, bf16[8,512]{1,0:T(8,128)(2,1)S(1)}, u32[]{:S(2)}, u32[]{:S(2)}) collective-permute-start(bf16[8,512]{1,0:T(8,128)(2,1)S(1)} %get-tuple-element.106.refs_2_.refs_0_), channel_id=1, source_target_pairs={{128,144},{132,148},{136,152},{140,156},{144,160},{148,164},{152,1... | collective-permute-start | bytes 24584 | tf_op jit(solution)/shard_map/ppermute | solution.py:30
  43.2 3.8 %collective-permute-start.11 = (bf16[8,512]{1,0:T(8,128)(2,1)S(1)}, bf16[8,512]{1,0:T(8,128)(2,1)S(1)}, u32[]{:S(2)}, u32[]{:S(2)}) collective-permute-start(bf16[8,512]{1,0:T(8,128)(2,1)S(1)} %get-tuple-element.106.refs_2_.refs_0_), channel_id=1, source_target_pairs={{128,240},{132,244},{136,248},{140,252},{144,128},{148,132},{152,1... | collective-permute-start | bytes 24584 | tf_op jit(solution)/shard_map/ppermute | solution.py:30
  47.1 1.9 %collective-permute-start.12 = (bf16[8,512]{1,0:T(8,128)(2,1)S(1)}, bf16[8,512]{1,0:T(8,128)(2,1)S(1)}, u32[]{:S(2)}, u32[]{:S(2)}) collective-permute-start(bf16[8,512]{1,0:T(8,128)(2,1)S(1)} %get-tuple-element.106.refs_2_.refs_0_), channel_id=1, source_target_pairs={{128,160},{132,164},{136,168},{140,172},{144,176},{148,180},{152,1... | collective-permute-start | bytes 24584 | tf_op jit(solution)/shard_map/ppermute | solution.py:30
  49.0 4.1 %own_attention.1 = (f32[8,448]{1,0:T(8,128)S(1)}, f32[8,448]{1,0:T(8,128)S(1)}, f32[8,448]{1,0:T(8,128)S(1)}) custom-call(s32[8,256]{1,0:T(8,128)S(1)} %copy-done, s32[8]{0:T(128)S(1)} %copy-done.2, bf16[8,512]{1,0:T(8,128)(2,1)S(1)} %get-tuple-element.106.refs_2_.refs_0_, bf16[8,448]{1,0:T(8,128)(2,1)S(1)} %get-tuple-element.101.refs_3_, ...), custom_call_target="tpu_custom_call" | custom-call | tf_op jit(solution)/shard_map/own_attention/pallas_call | solution.py:114
  53.2 0.0 collective-permute-done.11.refs_2_
  53.2 0.4 collective-permute-done.12.refs_3_
  53.6 0.0 collective-permute-done.13.refs_5_
  53.6 0.9 %prompt_attention.1 = (f32[8,640]{1,0:T(8,128)S(1)}, f32[8,640]{1,0:T(8,128)S(1)}, f32[8,640]{1,0:T(8,128)S(1)}, f32[8,640]{1,0:T(8,128)S(1)}) custom-call(bf16[8,512]{1,0:T(8,128)(2,1)S(1)} %get-tuple-element.106.refs_2_.refs_0_, bf16[8,512]{1,0:T(8,128)(2,1)S(1)} %collective-permute-done.10.refs_1_, bf16[8,512]{1,0:T(8,128)(2,1)S(1)} %collective-permute-done.11.refs_2_, ...), custom_call_target="tpu_custom_call" | custom-call | tf_op jit(solution)/shard_map/prompt_attention/pallas_call | solution.py:114
  54.5 3.7 %collective-permute-start.14 = (f32[8,640]{1,0:T(8,128)S(1)}, f32[8,640]{1,0:T(8,128)S(1)}, u32[]{:S(2)}, u32[]{:S(2)}) collective-permute-start(f32[8,640]{1,0:T(8,128)S(1)} %get-tuple-element.119), channel_id=1, source_target_pairs={{128,240},{132,244},{136,248},{140,252},{144,128},{148,132},{152,1... | collective-permute-start | bytes 61448 | tf_op jit(solution)/shard_map/ppermute | solution.py:30
  58.2 1.9 %collective-permute-start.15 = (f32[8,640]{1,0:T(8,128)S(1)}, f32[8,640]{1,0:T(8,128)S(1)}, u32[]{:S(2)}, u32[]{:S(2)}) collective-permute-start(f32[8,640]{1,0:T(8,128)S(1)} %get-tuple-element.120), channel_id=1, source_target_pairs={{128,144},{132,148},{136,152},{140,156},{144,160},{148,164},{152,1... | collective-permute-start | bytes 61448 | tf_op jit(solution)/shard_map/ppermute | solution.py:30
  60.1 4.8 %collective-permute-start.16 = (f32[8,640]{1,0:T(8,128)S(1)}, f32[8,640]{1,0:T(8,128)S(1)}, u32[]{:S(2)}, u32[]{:S(2)}) collective-permute-start(f32[8,640]{1,0:T(8,128)S(1)} %get-tuple-element.121), channel_id=1, source_target_pairs={{128,224},{132,228},{136,232},{140,236},{144,240},{148,244},{152,2... | collective-permute-start | bytes 61448 | tf_op jit(solution)/shard_map/ppermute | solution.py:30
  65.0 0.1 collective-permute-start.17
  65.1 1.2 %collective-permute-done.17 = bf16[8,448]{1,0:T(8,128)(2,1)S(1)} collective-permute-done((bf16[8,448]{1,0:T(8,128)(2,1)S(1)}, bf16[8,448]{1,0:T(8,128)(2,1)S(1)}, u32[]{:S(2)}, u32[]{:S(2)}) %collective-permute-start.17) | collective-permute-done | bytes 7200 | tf_op jit(solution)/shard_map/ppermute | solution.py:684
  66.2 0.0 collective-permute-done.14.refs_4_
  66.2 0.0 collective-permute-done.15.refs_5_
  66.3 0.0 collective-permute-done.16.refs_6_
  66.3 0.6 combine.1
  66.8 2.4 %collective-permute-start.20 = (f32[8,448]{1,0:T(8,128)S(1)}, f32[8,448]{1,0:T(8,128)S(1)}, u32[]{:S(2)}, u32[]{:S(2)}) collective-permute-start(f32[8,448]{1,0:T(8,128)S(1)} %get-tuple-element.134), channel_id=1, source_target_pairs={{128,130},{129,131},{130,128},{131,129},{0,0},{1,1},{2,2},{3,3},{1... | collective-permute-start | bytes 43016 | tf_op jit(solution)/shard_map/ppermute | solution.py:30
  69.3 4.5 %collective-permute-start.19 = (f32[8,448]{1,0:T(8,128)S(1)}, f32[8,448]{1,0:T(8,128)S(1)}, u32[]{:S(2)}, u32[]{:S(2)}) collective-permute-start(f32[8,448]{1,0:T(8,128)S(1)} %get-tuple-element.133), channel_id=1, source_target_pairs={{128,131},{129,128},{130,129},{131,130},{0,0},{1,1},{2,2},{3,3},{1... | collective-permute-start | bytes 43016 | tf_op jit(solution)/shard_map/ppermute | solution.py:30
  73.8 1.9 %collective-permute-start.18 = (f32[8,448]{1,0:T(8,128)S(1)}, f32[8,448]{1,0:T(8,128)S(1)}, u32[]{:S(2)}, u32[]{:S(2)}) collective-permute-start(f32[8,448]{1,0:T(8,128)S(1)} %get-tuple-element.132), channel_id=1, source_target_pairs={{128,129},{129,130},{130,131},{131,128},{0,0},{1,1},{2,2},{3,3},{1... | collective-permute-start | bytes 43016 | tf_op jit(solution)/shard_map/ppermute | solution.py:30
  75.7 0.0 collective-permute-done.20
  75.7 0.0 collective-permute-done.19
  75.7 3.7 %collective-permute-done.18 = f32[8,448]{1,0:T(8,128)S(1)} collective-permute-done((f32[8,448]{1,0:T(8,128)S(1)}, f32[8,448]{1,0:T(8,128)S(1)}, u32[]{:S(2)}, u32[]{:S(2)}) %collective-permute-start.18) | collective-permute-done | bytes 14368 | tf_op jit(solution)/shard_map/ppermute | solution.py:30
  79.4 0.6 fusion.1
  (10 shorter events, 0.0 us)
Async XLA Ops:
  0.0 7.1 %collective-permute-start = (bf16[8,448]{1,0:T(8,128)(2,1)}, bf16[8,448]{1,0:T(8,128)(2,1)S(1)}, u32[]{:S(2)}, u32[]{:S(2)}) collective-permute-start(bf16[8,448]{1,0:T(8,128)(2,1)} %refs_0_.4), channel_id=1, source_target_pairs={{0,1},{1,2},{2,3},{3,0},{128,128},{129,129},{130,130},{131,131},{4... | collective-permute-start | bytes 21512 | tf_op jit(solution)/shard_map/ppermute | solution.py:30
  1.3 5.8 %collective-permute-start.1 = (bf16[8,448]{1,0:T(8,128)(2,1)}, bf16[8,448]{1,0:T(8,128)(2,1)S(1)}, u32[]{:S(2)}, u32[]{:S(2)}) collective-permute-start(bf16[8,448]{1,0:T(8,128)(2,1)} %refs_0_.4), channel_id=1, source_target_pairs={{0,3},{1,0},{2,1},{3,2},{128,128},{129,129},{130,130},{131,131},{4... | collective-permute-start | bytes 21512 | tf_op jit(solution)/shard_map/ppermute | solution.py:30
  2.7 4.5 %collective-permute-start.2 = (bf16[8,448]{1,0:T(8,128)(2,1)}, bf16[8,448]{1,0:T(8,128)(2,1)S(1)}, u32[]{:S(2)}, u32[]{:S(2)}) collective-permute-start(bf16[8,448]{1,0:T(8,128)(2,1)} %refs_0_.4), channel_id=1, source_target_pairs={{0,2},{1,3},{2,0},{3,1},{128,128},{129,129},{130,130},{131,131},{4... | collective-permute-start | bytes 21512 | tf_op jit(solution)/shard_map/ppermute | solution.py:30
  5.1 12.9 %copy-start.1 = (bf16[8,448]{1,0:T(8,128)(2,1)S(1)}, bf16[8,448]{1,0:T(8,128)(2,1)}, u32[]{:S(2)}) copy-start(bf16[8,448]{1,0:T(8,128)(2,1)} %refs_0_.4) | copy-start | bytes 21508
  7.2 27.7 %copy-start = (s32[8,256]{1,0:T(8,128)S(1)}, s32[8,256]{1,0:T(8,128)}, u32[]{:S(2)}) copy-start(s32[8,256]{1,0:T(8,128)} %refs_0_.6) | copy-start | bytes 24580
  7.2 27.7 %copy-start.2 = (s32[8]{0:T(128)S(1)}, s32[8]{0:T(128)}, u32[]{:S(2)}) copy-start(s32[8]{0:T(128)} %refs_1_.4) | copy-start | bytes 100
  7.2 10.8 %collective-permute-start.3 = (bf16[448,128]{1,0:T(8,128)(2,1)S(1)}, bf16[448,128]{1,0:T(8,128)(2,1)S(1)}, u32[]{:S(2)}, u32[]{:S(2)}) collective-permute-start(bf16[448,128]{1,0:T(8,128)(2,1)S(1)} %window_page.1), channel_id=1, source_target_pairs={{128,132},{132,136},{136,140},{140,128},{144,148},{148,152},{152,1... | collective-permute-start | bytes 344072 | tf_op jit(solution)/shard_map/ppermute | solution.py:30
  11.1 6.9 %collective-permute-start.4 = (bf16[448,128]{1,0:T(8,128)(2,1)S(1)}, bf16[448,128]{1,0:T(8,128)(2,1)S(1)}, u32[]{:S(2)}, u32[]{:S(2)}) collective-permute-start(bf16[448,128]{1,0:T(8,128)(2,1)S(1)} %window_page.1), channel_id=1, source_target_pairs={{128,140},{132,128},{136,132},{140,136},{144,156},{148,144},{152,1... | collective-permute-start | bytes 344072 | tf_op jit(solution)/shard_map/ppermute | solution.py:30
  14.3 7.0 %collective-permute-start.5 = (bf16[448,128]{1,0:T(8,128)(2,1)S(1)}, bf16[448,128]{1,0:T(8,128)(2,1)S(1)}, u32[]{:S(2)}, u32[]{:S(2)}) collective-permute-start(bf16[448,128]{1,0:T(8,128)(2,1)S(1)} %window_page.1), channel_id=1, source_target_pairs={{128,136},{132,140},{136,128},{140,132},{144,152},{148,156},{152,1... | collective-permute-start | bytes 344072 | tf_op jit(solution)/shard_map/ppermute | solution.py:30
  21.4 32.2 %collective-permute-start.13 = (bf16[4,448,128]{2,1,0:T(8,128)(2,1)S(1)}, bf16[4,448,128]{2,1,0:T(8,128)(2,1)S(1)}, u32[]{:S(2)}, u32[]{:S(2)}) collective-permute-start(bf16[4,448,128]{2,1,0:T(8,128)(2,1)S(1)} %pad_maximum_fusion.refs_4_), channel_id=1, source_target_pairs={{128,192},{132,196},{136,200},{140,204},{144,208},{148,212},{152,2... | collective-permute-start | bytes 1376264 | tf_op jit(solution)/shard_map/ppermute | solution.py:30
  30.5 7.0 %collective-permute-start.6 = (f32[8,1792]{1,0:T(8,128)S(1)}, f32[8,1792]{1,0:T(8,128)S(1)}, u32[]{:S(2)}, u32[]{:S(2)}) collective-permute-start(f32[8,1792]{1,0:T(8,128)S(1)} %linear_layer.1), channel_id=1, source_target_pairs={{0,128},{1,129},{2,130},{3,131},{128,0},{129,1},{130,2},{131,3},{4... | collective-permute-start | bytes 172040 | tf_op jit(solution)/shard_map/ppermute | solution.py:59
  30.6 6.9 %collective-permute-start.7 = (f32[8,1792]{1,0:T(8,128)S(1)}, f32[8,1792]{1,0:T(8,128)S(1)}, u32[]{:S(2)}, u32[]{:S(2)}) collective-permute-start(f32[8,1792]{1,0:T(8,128)S(1)} %linear_layer.1), channel_id=1, source_target_pairs={{0,129},{1,130},{2,131},{3,128},{129,0},{130,1},{131,2},{128,3},{4... | collective-permute-start | bytes 172040 | tf_op jit(solution)/shard_map/ppermute | solution.py:59
  33.7 3.8 %collective-permute-start.8 = (f32[8,1792]{1,0:T(8,128)S(1)}, f32[8,1792]{1,0:T(8,128)S(1)}, u32[]{:S(2)}, u32[]{:S(2)}) collective-permute-start(f32[8,1792]{1,0:T(8,128)S(1)} %linear_layer.1), channel_id=1, source_target_pairs={{0,131},{1,128},{2,129},{3,130},{131,0},{128,1},{129,2},{130,3},{4... | collective-permute-start | bytes 172040 | tf_op jit(solution)/shard_map/ppermute | solution.py:59
  33.7 5.8 %collective-permute-start.9 = (f32[8,1792]{1,0:T(8,128)S(1)}, f32[8,1792]{1,0:T(8,128)S(1)}, u32[]{:S(2)}, u32[]{:S(2)}) collective-permute-start(f32[8,1792]{1,0:T(8,128)S(1)} %linear_layer.1), channel_id=1, source_target_pairs={{0,130},{1,131},{2,128},{3,129},{130,0},{131,1},{128,2},{129,3},{4... | collective-permute-start | bytes 172040 | tf_op jit(solution)/shard_map/ppermute | solution.py:59
  40.6 12.6 %collective-permute-start.10 = (bf16[8,512]{1,0:T(8,128)(2,1)S(1)}, bf16[8,512]{1,0:T(8,128)(2,1)S(1)}, u32[]{:S(2)}, u32[]{:S(2)}) collective-permute-start(bf16[8,512]{1,0:T(8,128)(2,1)S(1)} %get-tuple-element.106.refs_2_.refs_0_), channel_id=1, source_target_pairs={{128,144},{132,148},{136,152},{140,156},{144,160},{148,164},{152,1... | collective-permute-start | bytes 24584 | tf_op jit(solution)/shard_map/ppermute | solution.py:30
  43.2 9.9 %collective-permute-start.11 = (bf16[8,512]{1,0:T(8,128)(2,1)S(1)}, bf16[8,512]{1,0:T(8,128)(2,1)S(1)}, u32[]{:S(2)}, u32[]{:S(2)}) collective-permute-start(bf16[8,512]{1,0:T(8,128)(2,1)S(1)} %get-tuple-element.106.refs_2_.refs_0_), channel_id=1, source_target_pairs={{128,240},{132,244},{136,248},{140,252},{144,128},{148,132},{152,1... | collective-permute-start | bytes 24584 | tf_op jit(solution)/shard_map/ppermute | solution.py:30
  47.1 6.5 %collective-permute-start.12 = (bf16[8,512]{1,0:T(8,128)(2,1)S(1)}, bf16[8,512]{1,0:T(8,128)(2,1)S(1)}, u32[]{:S(2)}, u32[]{:S(2)}) collective-permute-start(bf16[8,512]{1,0:T(8,128)(2,1)S(1)} %get-tuple-element.106.refs_2_.refs_0_), channel_id=1, source_target_pairs={{128,160},{132,164},{136,168},{140,172},{144,176},{148,180},{152,1... | collective-permute-start | bytes 24584 | tf_op jit(solution)/shard_map/ppermute | solution.py:30
  54.5 11.7 %collective-permute-start.14 = (f32[8,640]{1,0:T(8,128)S(1)}, f32[8,640]{1,0:T(8,128)S(1)}, u32[]{:S(2)}, u32[]{:S(2)}) collective-permute-start(f32[8,640]{1,0:T(8,128)S(1)} %get-tuple-element.119), channel_id=1, source_target_pairs={{128,240},{132,244},{136,248},{140,252},{144,128},{148,132},{152,1... | collective-permute-start | bytes 61448 | tf_op jit(solution)/shard_map/ppermute | solution.py:30
  58.2 8.0 %collective-permute-start.15 = (f32[8,640]{1,0:T(8,128)S(1)}, f32[8,640]{1,0:T(8,128)S(1)}, u32[]{:S(2)}, u32[]{:S(2)}) collective-permute-start(f32[8,640]{1,0:T(8,128)S(1)} %get-tuple-element.120), channel_id=1, source_target_pairs={{128,144},{132,148},{136,152},{140,156},{144,160},{148,164},{152,1... | collective-permute-start | bytes 61448 | tf_op jit(solution)/shard_map/ppermute | solution.py:30
  60.1 6.1 %collective-permute-start.16 = (f32[8,640]{1,0:T(8,128)S(1)}, f32[8,640]{1,0:T(8,128)S(1)}, u32[]{:S(2)}, u32[]{:S(2)}) collective-permute-start(f32[8,640]{1,0:T(8,128)S(1)} %get-tuple-element.121), channel_id=1, source_target_pairs={{128,224},{132,228},{136,232},{140,236},{144,240},{148,244},{152,2... | collective-permute-start | bytes 61448 | tf_op jit(solution)/shard_map/ppermute | solution.py:30
  65.0 1.3 %collective-permute-start.17 = (bf16[8,448]{1,0:T(8,128)(2,1)S(1)}, bf16[8,448]{1,0:T(8,128)(2,1)S(1)}, u32[]{:S(2)}, u32[]{:S(2)}) collective-permute-start(bf16[8,448]{1,0:T(8,128)(2,1)S(1)} %get-tuple-element.122), channel_id=1, source_target_pairs={{128,0},{0,128},{129,1},{1,129},{130,2},{2,130},{131,3},{3,131},{1... | collective-permute-start | bytes 21512 | tf_op jit(solution)/shard_map/ppermute | solution.py:684
  66.8 8.9 %collective-permute-start.20 = (f32[8,448]{1,0:T(8,128)S(1)}, f32[8,448]{1,0:T(8,128)S(1)}, u32[]{:S(2)}, u32[]{:S(2)}) collective-permute-start(f32[8,448]{1,0:T(8,128)S(1)} %get-tuple-element.134), channel_id=1, source_target_pairs={{128,130},{129,131},{130,128},{131,129},{0,0},{1,1},{2,2},{3,3},{1... | collective-permute-start | bytes 43016 | tf_op jit(solution)/shard_map/ppermute | solution.py:30
  69.3 6.4 %collective-permute-start.19 = (f32[8,448]{1,0:T(8,128)S(1)}, f32[8,448]{1,0:T(8,128)S(1)}, u32[]{:S(2)}, u32[]{:S(2)}) collective-permute-start(f32[8,448]{1,0:T(8,128)S(1)} %get-tuple-element.133), channel_id=1, source_target_pairs={{128,131},{129,128},{130,129},{131,130},{0,0},{1,1},{2,2},{3,3},{1... | collective-permute-start | bytes 43016 | tf_op jit(solution)/shard_map/ppermute | solution.py:30
  73.8 5.7 %collective-permute-start.18 = (f32[8,448]{1,0:T(8,128)S(1)}, f32[8,448]{1,0:T(8,128)S(1)}, u32[]{:S(2)}, u32[]{:S(2)}) collective-permute-start(f32[8,448]{1,0:T(8,128)S(1)} %get-tuple-element.132), channel_id=1, source_target_pairs={{128,129},{129,130},{130,131},{131,128},{0,0},{1,1},{2,2},{3,3},{1... | collective-permute-start | bytes 43016 | tf_op jit(solution)/shard_map/ppermute | solution.py:30

commit v6 on v5

--- a/solution.py
+++ b/solution.py
@@ -23,33 +23,29 @@
 MASKED = -1e30
 
 
-def shift_on(section, value, axis, moves):
-    count = lax.axis_size(axis)
-    pairs = [(section * count + i, section * count + j) for i, j in moves]
-    pairs += [((1 - section) * count + i,) * 2 for i in range(count)]
-    return lax.ppermute(value, ("section", axis), pairs)
-
-
-def head_shift(section, value, steps):
+def head_shift(value, steps):
     count = lax.axis_size("head")
-    return shift_on(section, value, "head", [(i, (i + steps) % count) for i in range(count)])
+    return lax.ppermute(value, "head", [(i, (i + steps) % count) for i in range(count)])
 
 
 def z_shift(value, steps):
-    return shift_on(
-        1,
+    return lax.ppermute(
         value,
         "req",
         [(z * XN + i, (z + steps) % ZN * XN + i) for z in range(ZN) for i in range(XN)],
     )
 
 
-def x_shift(value, steps):
-    return shift_on(
-        1,
+def x_swap(value, flip):
+    return lax.ppermute(value, "req", [(i, i ^ flip) for i in range(XN * ZN)])
+
+
+def far_swap(value):
+    count = XN * ZN
+    return lax.ppermute(
         value,
-        "req",
-        [(z * XN + i, z * XN + (i + steps) % XN) for z in range(ZN) for i in range(XN)],
+        ("section", "req"),
+        [(count + i, count + (i + count // 2) % count) for i in range(count)],
     )
 
 
@@ -443,7 +439,7 @@
     z, x = ids[1] // XN, ids[1] % XN
     slot = token >> 7
     slot_group = jnp.where(slot < XN, z, (z + ZN // 2) & (ZN - 1)) * XN
-    slot_group = slot_group + ((slot + x + XN - 1) & (XN - 1))
+    slot_group = slot_group + (x ^ (slot & (XN - 1)))
     offset = token & (PAGE - 1)
     usable = (slot_group == group) & (offset < HALF) & (offset + HALF >= start)
     lane = lanes_of((count, share))
@@ -659,15 +655,14 @@
         }
     )
 
-    received = [head_shift(0, tokens, k) for k in (1, 3, 2)]
     page = window_page(pages_first)
+    two_pages = jnp.stack([page, x_swap(page, 1)])
+    received = [head_shift(tokens, k) for k in (1, 3, 2)]
+    near_pages = jnp.concatenate([two_pages, x_swap(two_pages, 2)])
     near, received = lax.optimization_barrier((near, received))
-    page, received = lax.optimization_barrier((page, received))
-    row_pages = [x_shift(page, k) for k in (1, 3, 2)]
+    near_pages, received = lax.optimization_barrier((near_pages, received))
+    far_pages = far_swap(near_pages)
     update = linear_layer([tokens] + received, near)
-    row_pages, update = lax.optimization_barrier((row_pages, update))
-    near_pages = jnp.stack([row_pages[0], page, row_pages[1], row_pages[2]])
-    far_pages = z_shift(near_pages, ZN // 2)
     own_pages = own_pages.transpose(0, 1, 3, 2)
     query_key_w, table, ends, update = lax.optimization_barrier(
         (query_key_w, page_table, lengths, update)
@@ -686,7 +681,7 @@
     slabs = combine(own, parts, near)
     section_index = lax.axis_index("section")
     total = one_share.astype(jnp.float32) + slabs[0]
-    for piece in [head_shift(1, slabs[k], k) for k in (1, 3, 2)]:
+    for piece in [head_shift(slabs[k], k) for k in (1, 3, 2)]:
         total = total + piece
     output = jnp.where(section_index == 0, one_back, total.astype(jnp.bfloat16))
     return output[None]

time: 80.8 us -> 57.1 us (0.71)
  starting transfers between devices: 56 us -> 33.4 us
    ppermute x16 -> x15, starting transfers between devices: 51.5 us -> 29.4 us  [the longest x1 8.82 us: far_swap(): lax.ppermute(value, ('section', 'req'), [(count + i, count + (i + count /...]
    ppermute x16 -> x15, waiting for transfers between devices: 7.56 us -> 7.43 us  [the longest x6 4.36 us: head_shift(): lax.ppermute(value, 'head', [(i, (i + steps) % count) for i in range(coun...]
  transfers between devices with their start and end apart: 21 -> 20, of which waited for: 5 -> 8; matrix products, arithmetic and copies ran while one was open for 0% -> 0% of each run, Pallas kernels for 14% -> 18%
where the time goes in v6:
time: 57.1 us; the launch traced here: 56.9 us
  starting transfers between devices  33.4 us (58%)
  Pallas kernels  12.6 us (22%)
  waiting for transfers between devices  10 us (18%)
  other arithmetic  0.68 us (1%)
    pallas_call x8, Pallas kernels, kernel_call(): pl.pallas_call(run, out_shape=out_shape, in_specs=in_specs, out_specs=jax...  12.6 us
    ppermute x1, starting transfers between devices, far_swap(): lax.ppermute(value, ('section', 'req'), [(count + i, count + (i + count /...  8.82 us
    ppermute x6, starting transfers between devices, head_shift(): lax.ppermute(value, 'head', [(i, (i + steps) % count) for i in range(coun...  7.41 us
    ppermute x6, starting transfers between devices, z_shift(): lax.ppermute(value, 'req', [(z * XN + i, (z + steps) % ZN * XN + i) for z...  7.04 us
    ppermute x2, starting transfers between devices, x_swap(): return lax.ppermute(value, 'req', [(i, i ^ flip) for i in range(XN * ZN)])  6.11 us
    ppermute x6, waiting for transfers between devices, head_shift(): lax.ppermute(value, 'head', [(i, (i + steps) % count) for i in range(coun...  4.36 us
    ppermute x4, starting transfers between devices, section_swap(): lax.ppermute(value, ('section', 'head'), there + [(b, a) for a, b in there])  4.01 us
    ppermute x2, waiting for transfers between devices, x_swap(): return lax.ppermute(value, 'req', [(i, i ^ flip) for i in range(XN * ZN)])  2.71 us
  transfers between devices with their start and end apart: 20, of which 8 were waited for; matrix products, arithmetic and copies ran while one was open for 0% of the time, Pallas kernels for 18%

profile of v6, /device:TPU:1, one launch (start us, length us, event | category | flops | bytes accessed | tf_op | source)
XLA Modules:
  0.0 56.9 jit_solution(13895775580839916710)
XLA Ops:
  0.0 1.0 %window_page.1 = bf16[448,128]{1,0:T(8,128)(2,1)S(1)} custom-call(bf16[1,2,448,128]{3,2,1,0:T(8,128)(2,1)} %bitcast.21), custom_call_target="tpu_custom_call" | custom-call | bytes 16777216 | tf_op jit(solution)/shard_map/window_page/pallas_call | solution.py:110
  1.1 2.1 %collective-permute-start = (bf16[448,128]{1,0:T(8,128)(2,1)S(1)}, bf16[448,128]{1,0:T(8,128)(2,1)S(1)}, u32[]{:S(2)}, u32[]{:S(2)}) collective-permute-start(bf16[448,128]{1,0:T(8,128)(2,1)S(1)} %window_page.1), channel_id=1, source_target_pairs={{0,4},{4,0},{8,12},{12,8},{16,20},{20,16},{24,28},{28,24},{32,36},... | collective-permute-start | bytes 344072 | tf_op jit(solution)/shard_map/ppermute | solution.py:40
  3.2 2.7 %collective-permute-done = bf16[448,128]{1,0:T(8,128)(2,1)S(1)} collective-permute-done((bf16[448,128]{1,0:T(8,128)(2,1)S(1)}, bf16[448,128]{1,0:T(8,128)(2,1)S(1)}, u32[]{:S(2)}, u32[]{:S(2)}) %collective-permute-start) | collective-permute-done | bytes 114720 | tf_op jit(solution)/shard_map/ppermute | solution.py:40
  5.9 4.0 %collective-permute-start.1 = (bf16[2,448,128]{2,1,0:T(8,128)(2,1)S(1)}, bf16[2,448,128]{2,1,0:T(8,128)(2,1)S(1)}, u32[]{:S(2)}, u32[]{:S(2)}) collective-permute-start(bf16[2,448,128]{2,1,0:T(8,128)(2,1)S(1)} %pad_maximum_fusion.1), channel_id=1, source_target_pairs={{0,8},{4,12},{8,0},{12,4},{16,24},{20,28},{24,16},{28,20},{32,40},... | collective-permute-start | bytes 688136 | tf_op jit(solution)/shard_map/ppermute | solution.py:40
  9.9 1.3 %collective-permute-start.2 = (bf16[8,448]{1,0:T(8,128)(2,1)}, bf16[8,448]{1,0:T(8,128)(2,1)S(1)}, u32[]{:S(2)}, u32[]{:S(2)}) collective-permute-start(bf16[8,448]{1,0:T(8,128)(2,1)} %refs_0_.4), channel_id=1, source_target_pairs={{0,1},{1,2},{2,3},{3,0},{4,5},{5,6},{6,7},{7,4},{8,9},{9,10},{10,1... | collective-permute-start | bytes 21512 | tf_op jit(solution)/shard_map/ppermute | solution.py:28
  11.2 1.4 %collective-permute-start.3 = (bf16[8,448]{1,0:T(8,128)(2,1)}, bf16[8,448]{1,0:T(8,128)(2,1)S(1)}, u32[]{:S(2)}, u32[]{:S(2)}) collective-permute-start(bf16[8,448]{1,0:T(8,128)(2,1)} %refs_0_.4), channel_id=1, source_target_pairs={{0,3},{1,0},{2,1},{3,2},{4,7},{5,4},{6,5},{7,6},{8,11},{9,8},{10,9... | collective-permute-start | bytes 21512 | tf_op jit(solution)/shard_map/ppermute | solution.py:28
  12.6 1.6 %collective-permute-start.4 = (bf16[8,448]{1,0:T(8,128)(2,1)}, bf16[8,448]{1,0:T(8,128)(2,1)S(1)}, u32[]{:S(2)}, u32[]{:S(2)}) collective-permute-start(bf16[8,448]{1,0:T(8,128)(2,1)} %refs_0_.4), channel_id=1, source_target_pairs={{0,2},{1,3},{2,0},{3,1},{4,6},{5,7},{6,4},{7,5},{8,10},{9,11},{10,... | collective-permute-start | bytes 21512 | tf_op jit(solution)/shard_map/ppermute | solution.py:28
  14.3 2.0 %bring_near.1 = (f32[1,1792]{1,0:T(1,128)S(1)}, bf16[1792,128]{1,0:T(8,128)(2,1)S(1)}, bf16[8736,112]{1,0:T(8,128)(2,1)S(1)}, f32[8,4,273]{2,1,0:T(4,128)S(1)}, ...) custom-call(f32[1,1792]{1,0:T(1,128)} %refs_0_.3, ...), custom_call_target="tpu_custom_call" | custom-call | bytes 11377408 | tf_op jit(solution)/shard_map/bring_near/pallas_call | solution.py:110
  16.3 0.0 collective-permute-done.2.refs_1_
  16.3 0.0 collective-permute-done.3.refs_2_
  16.3 0.5 collective-permute-done.4.refs_3_
  16.9 0.0 collective-permute-done.1
  16.9 0.0 copy-start
  16.9 0.0 copy-start.2
  16.9 8.8 %collective-permute-start.12 = (bf16[4,448,128]{2,1,0:T(8,128)(2,1)S(1)}, bf16[4,448,128]{2,1,0:T(8,128)(2,1)S(1)}, u32[]{:S(2)}, u32[]{:S(2)}) collective-permute-start(bf16[4,448,128]{2,1,0:T(8,128)(2,1)S(1)} %pad_maximum_fusion.refs_4_), channel_id=1, source_target_pairs={{128,192},{132,196},{136,200},{140,204},{144,208},{148,212},{152,2... | collective-permute-start | bytes 1376264 | tf_op jit(solution)/shard_map/ppermute | solution.py:45
  25.8 0.1 collective-permute-start.5
  25.9 2.1 %collective-permute-start.6 = (f32[8,1792]{1,0:T(8,128)S(1)}, f32[8,1792]{1,0:T(8,128)S(1)}, u32[]{:S(2)}, u32[]{:S(2)}) collective-permute-start(f32[8,1792]{1,0:T(8,128)S(1)} %linear_layer.1), channel_id=1, source_target_pairs={{0,129},{1,130},{2,131},{3,128},{129,0},{130,1},{131,2},{128,3},{4... | collective-permute-start | bytes 172040 | tf_op jit(solution)/shard_map/ppermute | solution.py:55
  28.0 0.0 collective-permute-start.7
  28.0 1.8 %collective-permute-start.8 = (f32[8,1792]{1,0:T(8,128)S(1)}, f32[8,1792]{1,0:T(8,128)S(1)}, u32[]{:S(2)}, u32[]{:S(2)}) collective-permute-start(f32[8,1792]{1,0:T(8,128)S(1)} %linear_layer.1), channel_id=1, source_target_pairs={{0,130},{1,131},{2,128},{3,129},{130,0},{131,1},{128,2},{129,3},{4... | collective-permute-start | bytes 172040 | tf_op jit(solution)/shard_map/ppermute | solution.py:55
  29.8 2.6 %bring_queries.1 = (bf16[1792,896]{1,0:T(8,128)(2,1)S(1)}, f32[8,128]{1,0:T(8,128)S(1)}) custom-call(s32[8,256]{1,0:T(8,128)S(1)} %copy-done, s32[8]{0:T(128)S(1)} %copy-done.2, bf16[1792,896]{1,0:T(8,128)(2,1)} %refs_2_), custom_call_target="tpu_custom_call" | custom-call | bytes 6422528 | tf_op jit(solution)/shard_map/bring_queries/pallas_call | solution.py:110
  32.4 0.0 collective-permute-done.5.refs_1_
  32.4 0.0 collective-permute-done.6.refs_2_
  32.4 0.0 collective-permute-done.7.refs_3_
  32.5 1.4 %collective-permute-done.8.refs_4_ = f32[8,1792]{1,0:T(8,128)S(1)} collective-permute-done((f32[8,1792]{1,0:T(8,128)S(1)}, f32[8,1792]{1,0:T(8,128)S(1)}, u32[]{:S(2)}, u32[]{:S(2)}) %collective-permute-start.8) | collective-permute-done | bytes 57376 | tf_op jit(solution)/shard_map/ppermute | solution.py:55
  33.9 1.0 %project.1 = (bf16[8,448]{1,0:T(8,128)(2,1)S(1)}, bf16[8,512]{1,0:T(8,128)(2,1)S(1)}, bf16[8,448]{1,0:T(8,128)(2,1)S(1)}, bf16[8,448]{1,0:T(8,128)(2,1)S(1)}) custom-call(f32[8,128]{1,0:T(8,128)S(1)} %get-tuple-element.91.refs_0_, f32[8,1792]{1,0:T(8,128)S(1)} %collective-permute-done.5.refs_1_, f32[8,1792]{1,0:T(8,128)S(1)} %collective-permute-done.6.refs_2_, ...), custom_call_target="tpu_custom_call" | custom-call | tf_op jit(solution)/shard_map/project/pallas_call | solution.py:110
  34.9 1.9 %collective-permute-start.10 = (bf16[8,512]{1,0:T(8,128)(2,1)S(1)}, bf16[8,512]{1,0:T(8,128)(2,1)S(1)}, u32[]{:S(2)}, u32[]{:S(2)}) collective-permute-start(bf16[8,512]{1,0:T(8,128)(2,1)S(1)} %get-tuple-element.100.refs_2_.refs_0_), channel_id=1, source_target_pairs={{0,112},{4,116},{8,120},{12,124},{16,0},{20,4},{24,8},{28,12},{32,... | collective-permute-start | bytes 24584 | tf_op jit(solution)/shard_map/ppermute | solution.py:32
  36.8 0.1 collective-permute-start.11
  36.9 0.7 %collective-permute-start.9 = (bf16[8,512]{1,0:T(8,128)(2,1)S(1)}, bf16[8,512]{1,0:T(8,128)(2,1)S(1)}, u32[]{:S(2)}, u32[]{:S(2)}) collective-permute-start(bf16[8,512]{1,0:T(8,128)(2,1)S(1)} %get-tuple-element.100.refs_2_.refs_0_), channel_id=1, source_target_pairs={{0,16},{4,20},{8,24},{12,28},{16,32},{20,36},{24,40},{28,44},{32,4... | collective-permute-start | bytes 24584 | tf_op jit(solution)/shard_map/ppermute | solution.py:32
  37.6 4.4 %own_attention.1 = (f32[8,448]{1,0:T(8,128)S(1)}, f32[8,448]{1,0:T(8,128)S(1)}, f32[8,448]{1,0:T(8,128)S(1)}) custom-call(s32[8,256]{1,0:T(8,128)S(1)} %copy-done, s32[8]{0:T(128)S(1)} %copy-done.2, bf16[8,512]{1,0:T(8,128)(2,1)S(1)} %get-tuple-element.100.refs_2_.refs_0_, bf16[8,448]{1,0:T(8,128)(2,1)S(1)} %get-tuple-element.95.refs_3_, ...), custom_call_target="tpu_custom_call" | custom-call | tf_op jit(solution)/shard_map/own_attention/pallas_call | solution.py:110
  42.0 0.0 collective-permute-done.10.refs_2_
  42.0 0.0 collective-permute-done.11.refs_3_
  42.1 0.0 collective-permute-done.9.refs_1_
  42.1 0.0 collective-permute-done.12.refs_5_
  42.1 0.9 %prompt_attention.1 = (f32[8,640]{1,0:T(8,128)S(1)}, f32[8,640]{1,0:T(8,128)S(1)}, f32[8,640]{1,0:T(8,128)S(1)}, f32[8,640]{1,0:T(8,128)S(1)}) custom-call(bf16[8,512]{1,0:T(8,128)(2,1)S(1)} %get-tuple-element.100.refs_2_.refs_0_, bf16[8,512]{1,0:T(8,128)(2,1)S(1)} %collective-permute-done.9.refs_1_, bf16[8,512]{1,0:T(8,128)(2,1)S(1)} %collective-permute-done.10.refs_2_, ...), custom_call_target="tpu_custom_call" | custom-call | tf_op jit(solution)/shard_map/prompt_attention/pallas_call | solution.py:110
  43.0 2.0 %collective-permute-start.13 = (f32[8,640]{1,0:T(8,128)S(1)}, f32[8,640]{1,0:T(8,128)S(1)}, u32[]{:S(2)}, u32[]{:S(2)}) collective-permute-start(f32[8,640]{1,0:T(8,128)S(1)} %get-tuple-element.111), channel_id=1, source_target_pairs={{0,112},{4,116},{8,120},{12,124},{16,0},{20,4},{24,8},{28,12},{32,... | collective-permute-start | bytes 61448 | tf_op jit(solution)/shard_map/ppermute | solution.py:32
  45.0 0.1 collective-permute-start.14
  45.2 2.2 %collective-permute-start.15 = (f32[8,640]{1,0:T(8,128)S(1)}, f32[8,640]{1,0:T(8,128)S(1)}, u32[]{:S(2)}, u32[]{:S(2)}) collective-permute-start(f32[8,640]{1,0:T(8,128)S(1)} %get-tuple-element.113), channel_id=1, source_target_pairs={{0,96},{4,100},{8,104},{12,108},{16,112},{20,116},{24,120},{28,124... | collective-permute-start | bytes 61448 | tf_op jit(solution)/shard_map/ppermute | solution.py:32
  47.3 0.0 collective-permute-start.16
  47.3 1.2 %collective-permute-done.16 = bf16[8,448]{1,0:T(8,128)(2,1)S(1)} collective-permute-done((bf16[8,448]{1,0:T(8,128)(2,1)S(1)}, bf16[8,448]{1,0:T(8,128)(2,1)S(1)}, u32[]{:S(2)}, u32[]{:S(2)}) %collective-permute-start.16) | collective-permute-done | bytes 7200 | tf_op jit(solution)/shard_map/ppermute | solution.py:679
  48.5 0.3 collective-permute-done.14.refs_5_
  48.9 0.6 combine.1
  49.4 1.1 %collective-permute-start.17 = (f32[8,448]{1,0:T(8,128)S(1)}, f32[8,448]{1,0:T(8,128)S(1)}, u32[]{:S(2)}, u32[]{:S(2)}) collective-permute-start(f32[8,448]{1,0:T(8,128)S(1)} %get-tuple-element.124), channel_id=1, source_target_pairs={{0,1},{1,2},{2,3},{3,0},{4,5},{5,6},{6,7},{7,4},{8,9},{9,10},{10,1... | collective-permute-start | bytes 43016 | tf_op jit(solution)/shard_map/ppermute | solution.py:28
  50.6 1.6 %collective-permute-start.18 = (f32[8,448]{1,0:T(8,128)S(1)}, f32[8,448]{1,0:T(8,128)S(1)}, u32[]{:S(2)}, u32[]{:S(2)}) collective-permute-start(f32[8,448]{1,0:T(8,128)S(1)} %get-tuple-element.125), channel_id=1, source_target_pairs={{0,3},{1,0},{2,1},{3,2},{4,7},{5,4},{6,5},{7,6},{8,11},{9,8},{10,9... | collective-permute-start | bytes 43016 | tf_op jit(solution)/shard_map/ppermute | solution.py:28
  52.2 0.3 collective-permute-start.19
  52.5 0.8 %collective-permute-done.17 = f32[8,448]{1,0:T(8,128)S(1)} collective-permute-done((f32[8,448]{1,0:T(8,128)S(1)}, f32[8,448]{1,0:T(8,128)S(1)}, u32[]{:S(2)}, u32[]{:S(2)}) %collective-permute-start.17) | collective-permute-done | bytes 14368 | tf_op jit(solution)/shard_map/ppermute | solution.py:28
  53.3 0.2 collective-permute-done.18
  53.5 2.8 %collective-permute-done.19 = f32[8,448]{1,0:T(8,128)S(1)} collective-permute-done((f32[8,448]{1,0:T(8,128)S(1)}, f32[8,448]{1,0:T(8,128)S(1)}, u32[]{:S(2)}, u32[]{:S(2)}) %collective-permute-start.19) | collective-permute-done | bytes 14368 | tf_op jit(solution)/shard_map/ppermute | solution.py:28
  56.3 0.6 %fusion.1 = bf16[1,8,448]{2,1,0:T(8,128)(2,1)} fusion(bf16[8,448]{1,0:T(8,128)(2,1)S(1)} %collective-permute-done.16, f32[8,448]{1,0:T(8,128)S(1)} %collective-permute-done.19, f32[8,448]{1,0:T(8,128)S(1)} %collective-permute-done.18, f32[8,448]{1,0:T(8,128)S(1)} %collective-permute-done.17, f32[8,448]{1,0:T(8,128)S(1)} %get-tuple-element.123, ...), kind=kLoop, calls=%fused_computation.4 | loop fusion | flops 25088 | bytes 78849 | tf_op jit(solution)/shard_map/broadcast_in_dim | solution.py:687
  (9 shorter events, 0.1 us)
Async XLA Ops:
  1.1 4.8 %collective-permute-start = (bf16[448,128]{1,0:T(8,128)(2,1)S(1)}, bf16[448,128]{1,0:T(8,128)(2,1)S(1)}, u32[]{:S(2)}, u32[]{:S(2)}) collective-permute-start(bf16[448,128]{1,0:T(8,128)(2,1)S(1)} %window_page.1), channel_id=1, source_target_pairs={{0,4},{4,0},{8,12},{12,8},{16,20},{20,16},{24,28},{28,24},{32,36},... | collective-permute-start | bytes 344072 | tf_op jit(solution)/shard_map/ppermute | solution.py:40
  5.9 10.9 %collective-permute-start.1 = (bf16[2,448,128]{2,1,0:T(8,128)(2,1)S(1)}, bf16[2,448,128]{2,1,0:T(8,128)(2,1)S(1)}, u32[]{:S(2)}, u32[]{:S(2)}) collective-permute-start(bf16[2,448,128]{2,1,0:T(8,128)(2,1)S(1)} %pad_maximum_fusion.1), channel_id=1, source_target_pairs={{0,8},{4,12},{8,0},{12,4},{16,24},{20,28},{24,16},{28,20},{32,40},... | collective-permute-start | bytes 688136 | tf_op jit(solution)/shard_map/ppermute | solution.py:40
  9.9 6.4 %collective-permute-start.2 = (bf16[8,448]{1,0:T(8,128)(2,1)}, bf16[8,448]{1,0:T(8,128)(2,1)S(1)}, u32[]{:S(2)}, u32[]{:S(2)}) collective-permute-start(bf16[8,448]{1,0:T(8,128)(2,1)} %refs_0_.4), channel_id=1, source_target_pairs={{0,1},{1,2},{2,3},{3,0},{4,5},{5,6},{6,7},{7,4},{8,9},{9,10},{10,1... | collective-permute-start | bytes 21512 | tf_op jit(solution)/shard_map/ppermute | solution.py:28
  11.2 5.1 %collective-permute-start.3 = (bf16[8,448]{1,0:T(8,128)(2,1)}, bf16[8,448]{1,0:T(8,128)(2,1)S(1)}, u32[]{:S(2)}, u32[]{:S(2)}) collective-permute-start(bf16[8,448]{1,0:T(8,128)(2,1)} %refs_0_.4), channel_id=1, source_target_pairs={{0,3},{1,0},{2,1},{3,2},{4,7},{5,4},{6,5},{7,6},{8,11},{9,8},{10,9... | collective-permute-start | bytes 21512 | tf_op jit(solution)/shard_map/ppermute | solution.py:28
  12.6 4.2 %collective-permute-start.4 = (bf16[8,448]{1,0:T(8,128)(2,1)}, bf16[8,448]{1,0:T(8,128)(2,1)S(1)}, u32[]{:S(2)}, u32[]{:S(2)}) collective-permute-start(bf16[8,448]{1,0:T(8,128)(2,1)} %refs_0_.4), channel_id=1, source_target_pairs={{0,2},{1,3},{2,0},{3,1},{4,6},{5,7},{6,4},{7,5},{8,10},{9,11},{10,... | collective-permute-start | bytes 21512 | tf_op jit(solution)/shard_map/ppermute | solution.py:28
  14.3 11.5 %copy-start.1 = (bf16[8,448]{1,0:T(8,128)(2,1)S(1)}, bf16[8,448]{1,0:T(8,128)(2,1)}, u32[]{:S(2)}) copy-start(bf16[8,448]{1,0:T(8,128)(2,1)} %refs_0_.4) | copy-start | bytes 21508
  16.9 12.9 %copy-start = (s32[8,256]{1,0:T(8,128)S(1)}, s32[8,256]{1,0:T(8,128)}, u32[]{:S(2)}) copy-start(s32[8,256]{1,0:T(8,128)} %refs_0_.6) | copy-start | bytes 24580
  16.9 12.9 %copy-start.2 = (s32[8]{0:T(128)S(1)}, s32[8]{0:T(128)}, u32[]{:S(2)}) copy-start(s32[8]{0:T(128)} %refs_1_.4) | copy-start | bytes 100
  16.9 25.1 %collective-permute-start.12 = (bf16[4,448,128]{2,1,0:T(8,128)(2,1)S(1)}, bf16[4,448,128]{2,1,0:T(8,128)(2,1)S(1)}, u32[]{:S(2)}, u32[]{:S(2)}) collective-permute-start(bf16[4,448,128]{2,1,0:T(8,128)(2,1)S(1)} %pad_maximum_fusion.refs_4_), channel_id=1, source_target_pairs={{128,192},{132,196},{136,200},{140,204},{144,208},{148,212},{152,2... | collective-permute-start | bytes 1376264 | tf_op jit(solution)/shard_map/ppermute | solution.py:45
  25.8 6.6 %collective-permute-start.5 = (f32[8,1792]{1,0:T(8,128)S(1)}, f32[8,1792]{1,0:T(8,128)S(1)}, u32[]{:S(2)}, u32[]{:S(2)}) collective-permute-start(f32[8,1792]{1,0:T(8,128)S(1)} %linear_layer.1), channel_id=1, source_target_pairs={{0,128},{1,129},{2,130},{3,131},{128,0},{129,1},{130,2},{131,3},{4... | collective-permute-start | bytes 172040 | tf_op jit(solution)/shard_map/ppermute | solution.py:55
  25.9 6.5 %collective-permute-start.6 = (f32[8,1792]{1,0:T(8,128)S(1)}, f32[8,1792]{1,0:T(8,128)S(1)}, u32[]{:S(2)}, u32[]{:S(2)}) collective-permute-start(f32[8,1792]{1,0:T(8,128)S(1)} %linear_layer.1), channel_id=1, source_target_pairs={{0,129},{1,130},{2,131},{3,128},{129,0},{130,1},{131,2},{128,3},{4... | collective-permute-start | bytes 172040 | tf_op jit(solution)/shard_map/ppermute | solution.py:55
  28.0 4.4 %collective-permute-start.7 = (f32[8,1792]{1,0:T(8,128)S(1)}, f32[8,1792]{1,0:T(8,128)S(1)}, u32[]{:S(2)}, u32[]{:S(2)}) collective-permute-start(f32[8,1792]{1,0:T(8,128)S(1)} %linear_layer.1), channel_id=1, source_target_pairs={{0,131},{1,128},{2,129},{3,130},{131,0},{128,1},{129,2},{130,3},{4... | collective-permute-start | bytes 172040 | tf_op jit(solution)/shard_map/ppermute | solution.py:55
  28.0 5.8 %collective-permute-start.8 = (f32[8,1792]{1,0:T(8,128)S(1)}, f32[8,1792]{1,0:T(8,128)S(1)}, u32[]{:S(2)}, u32[]{:S(2)}) collective-permute-start(f32[8,1792]{1,0:T(8,128)S(1)} %linear_layer.1), channel_id=1, source_target_pairs={{0,130},{1,131},{2,128},{3,129},{130,0},{131,1},{128,2},{129,3},{4... | collective-permute-start | bytes 172040 | tf_op jit(solution)/shard_map/ppermute | solution.py:55
  34.9 7.1 %collective-permute-start.10 = (bf16[8,512]{1,0:T(8,128)(2,1)S(1)}, bf16[8,512]{1,0:T(8,128)(2,1)S(1)}, u32[]{:S(2)}, u32[]{:S(2)}) collective-permute-start(bf16[8,512]{1,0:T(8,128)(2,1)S(1)} %get-tuple-element.100.refs_2_.refs_0_), channel_id=1, source_target_pairs={{0,112},{4,116},{8,120},{12,124},{16,0},{20,4},{24,8},{28,12},{32,... | collective-permute-start | bytes 24584 | tf_op jit(solution)/shard_map/ppermute | solution.py:32
  36.8 5.2 %collective-permute-start.11 = (bf16[8,512]{1,0:T(8,128)(2,1)S(1)}, bf16[8,512]{1,0:T(8,128)(2,1)S(1)}, u32[]{:S(2)}, u32[]{:S(2)}) collective-permute-start(bf16[8,512]{1,0:T(8,128)(2,1)S(1)} %get-tuple-element.100.refs_2_.refs_0_), channel_id=1, source_target_pairs={{0,32},{4,36},{8,40},{12,44},{16,48},{20,52},{24,56},{28,60},{32,6... | collective-permute-start | bytes 24584 | tf_op jit(solution)/shard_map/ppermute | solution.py:32
  36.9 5.2 %collective-permute-start.9 = (bf16[8,512]{1,0:T(8,128)(2,1)S(1)}, bf16[8,512]{1,0:T(8,128)(2,1)S(1)}, u32[]{:S(2)}, u32[]{:S(2)}) collective-permute-start(bf16[8,512]{1,0:T(8,128)(2,1)S(1)} %get-tuple-element.100.refs_2_.refs_0_), channel_id=1, source_target_pairs={{0,16},{4,20},{8,24},{12,28},{16,32},{20,36},{24,40},{28,44},{32,4... | collective-permute-start | bytes 24584 | tf_op jit(solution)/shard_map/ppermute | solution.py:32
  43.0 5.5 %collective-permute-start.13 = (f32[8,640]{1,0:T(8,128)S(1)}, f32[8,640]{1,0:T(8,128)S(1)}, u32[]{:S(2)}, u32[]{:S(2)}) collective-permute-start(f32[8,640]{1,0:T(8,128)S(1)} %get-tuple-element.111), channel_id=1, source_target_pairs={{0,112},{4,116},{8,120},{12,124},{16,0},{20,4},{24,8},{28,12},{32,... | collective-permute-start | bytes 61448 | tf_op jit(solution)/shard_map/ppermute | solution.py:32
  45.0 3.8 %collective-permute-start.14 = (f32[8,640]{1,0:T(8,128)S(1)}, f32[8,640]{1,0:T(8,128)S(1)}, u32[]{:S(2)}, u32[]{:S(2)}) collective-permute-start(f32[8,640]{1,0:T(8,128)S(1)} %get-tuple-element.112), channel_id=1, source_target_pairs={{0,16},{4,20},{8,24},{12,28},{16,32},{20,36},{24,40},{28,44},{32,4... | collective-permute-start | bytes 61448 | tf_op jit(solution)/shard_map/ppermute | solution.py:32
  45.2 3.7 %collective-permute-start.15 = (f32[8,640]{1,0:T(8,128)S(1)}, f32[8,640]{1,0:T(8,128)S(1)}, u32[]{:S(2)}, u32[]{:S(2)}) collective-permute-start(f32[8,640]{1,0:T(8,128)S(1)} %get-tuple-element.113), channel_id=1, source_target_pairs={{0,96},{4,100},{8,104},{12,108},{16,112},{20,116},{24,120},{28,124... | collective-permute-start | bytes 61448 | tf_op jit(solution)/shard_map/ppermute | solution.py:32
  47.3 1.2 %collective-permute-start.16 = (bf16[8,448]{1,0:T(8,128)(2,1)S(1)}, bf16[8,448]{1,0:T(8,128)(2,1)S(1)}, u32[]{:S(2)}, u32[]{:S(2)}) collective-permute-start(bf16[8,448]{1,0:T(8,128)(2,1)S(1)} %get-tuple-element.114), channel_id=1, source_target_pairs={{128,0},{0,128},{129,1},{1,129},{130,2},{2,130},{131,3},{3,131},{1... | collective-permute-start | bytes 21512 | tf_op jit(solution)/shard_map/ppermute | solution.py:679
  49.4 3.9 %collective-permute-start.17 = (f32[8,448]{1,0:T(8,128)S(1)}, f32[8,448]{1,0:T(8,128)S(1)}, u32[]{:S(2)}, u32[]{:S(2)}) collective-permute-start(f32[8,448]{1,0:T(8,128)S(1)} %get-tuple-element.124), channel_id=1, source_target_pairs={{0,1},{1,2},{2,3},{3,0},{4,5},{5,6},{6,7},{7,4},{8,9},{9,10},{10,1... | collective-permute-start | bytes 43016 | tf_op jit(solution)/shard_map/ppermute | solution.py:28
  50.6 2.9 %collective-permute-start.18 = (f32[8,448]{1,0:T(8,128)S(1)}, f32[8,448]{1,0:T(8,128)S(1)}, u32[]{:S(2)}, u32[]{:S(2)}) collective-permute-start(f32[8,448]{1,0:T(8,128)S(1)} %get-tuple-element.125), channel_id=1, source_target_pairs={{0,3},{1,0},{2,1},{3,2},{4,7},{5,4},{6,5},{7,6},{8,11},{9,8},{10,9... | collective-permute-start | bytes 43016 | tf_op jit(solution)/shard_map/ppermute | solution.py:28
  52.2 4.1 %collective-permute-start.19 = (f32[8,448]{1,0:T(8,128)S(1)}, f32[8,448]{1,0:T(8,128)S(1)}, u32[]{:S(2)}, u32[]{:S(2)}) collective-permute-start(f32[8,448]{1,0:T(8,128)S(1)} %get-tuple-element.126), channel_id=1, source_target_pairs={{0,2},{1,3},{2,0},{3,1},{4,6},{5,7},{6,4},{7,5},{8,10},{9,11},{10,... | collective-permute-start | bytes 43016 | tf_op jit(solution)/shard_map/ppermute | solution.py:28

commit v7 on v4

--- a/solution.py
+++ b/solution.py
@@ -36,11 +36,16 @@
     )
 
 
-def x_shift(value, steps):
+def x_swap(value, flip):
+    return lax.ppermute(value, "req", [(i, i ^ flip) for i in range(XN * ZN)])
+
+
+def far_swap(value):
+    count = XN * ZN
     return lax.ppermute(
         value,
-        "req",
-        [(z * XN + i, z * XN + (i + steps) % XN) for z in range(ZN) for i in range(XN)],
+        ("section", "req"),
+        [(count + i, count + (i + count // 2) % count) for i in range(count)],
     )
 
 
@@ -81,7 +86,7 @@
     in_specs,
     scratch_shapes,
     args,
-    vmem=10 << 20,
+    vmem=6 << 20,
     cost=None,
     elsewhere=None,
 ):
@@ -280,10 +285,8 @@
             query = jnp.where(in_head(lane, h), moved, query)
         moved = pltpu.roll(query_key, width - (h + 1) * HD, 1)[:, :LANES]
         key = jnp.where(in_head(lane, h), moved, key)
-    group = tags[:, 0:1].astype(jnp.float32)
-    start = jnp.minimum(tags[:, 1:2] - WINDOW, PAGE).astype(jnp.float32)
-    query = jnp.where(lane == share, group, query)
-    query = jnp.where(lane == share + 1, start, query)
+    query = jnp.where(lane == share, tags[:, 0:1], query)
+    query = jnp.where(lane == share + 1, tags[:, 1:2], query)
     asked[...] = query.astype(jnp.bfloat16)
     key_new[...] = key[:, :share].astype(jnp.bfloat16)
 
@@ -409,7 +412,7 @@
     z, x = ids[1] // XN, ids[1] % XN
     slot = token >> 7
     slot_group = jnp.where(slot < XN, z, (z + ZN // 2) & (ZN - 1)) * XN
-    slot_group = slot_group + ((slot + x + XN - 1) & (XN - 1))
+    slot_group = slot_group + (x ^ (slot & (XN - 1)))
     offset = token & (PAGE - 1)
     usable = (slot_group == group) & (offset < HALF) & (offset + HALF >= start)
     lane = lanes_of((count, share))
@@ -543,9 +546,9 @@
 
 
 def window_kernel(
-    ids, table, lengths, query_key_hbm, own_hbm, query_key_near, own_near, key_sem, sems
+    ids, table, lengths, query_key_hbm, own_hbm, query_key_near, own_near, tags, key_sem, sems
 ):
-    rows = lengths.shape[0]
+    rows = tags.shape[0]
     total = own_hbm.shape[0]
     copies = [pltpu.make_async_copy(query_key_hbm, query_key_near, key_sem)]
     for r in range(rows):
@@ -556,6 +559,13 @@
             )
     for copy in copies:
         copy.start()
+    row = lax.broadcasted_iota(jnp.int32, tags.shape, 0)
+    first = lanes_of(tags.shape) == 0
+    marks = jnp.zeros(tags.shape, jnp.int32)
+    for r in range(rows):
+        start = jnp.minimum(lengths[r] - WINDOW, PAGE)
+        marks = jnp.where(row == r, jnp.where(first, table[r, 0], start), marks)
+    tags[...] = marks.astype(jnp.float32)
     for copy in copies:
         copy.wait()
 
@@ -567,11 +577,15 @@
         window_kernel,
         1,
         "bring_windows",
-        [jax.ShapeDtypeStruct(query_key_w.shape, query_key_w.dtype), windows],
+        [
+            jax.ShapeDtypeStruct(query_key_w.shape, query_key_w.dtype),
+            windows,
+            jax.ShapeDtypeStruct((rows, 128), jnp.float32),
+        ],
         [SMEM] * 2 + [HBM] * 2,
         [pltpu.SemaphoreType.DMA, pltpu.SemaphoreType.DMA((rows, 2))],
         (table, lengths, query_key_w, own_pages),
-        4 << 20,
+        1 << 20,
         bytes_only([query_key_w, windows]),
     )
 
@@ -616,36 +630,34 @@
     lengths,
 ):
     pages_first = prompt_pages.transpose(0, 1, 3, 2)
-    near = bring_near(
-        {
-            "gain": norm_gain,
-            "feature_w": feature_w,
-            "state": lin_state.transpose(0, 2, 1, 3).reshape(-1, HD),
-            "lin_norm": lin_norm,
-            "conv_w": conv_w,
-            "conv_state": conv_state,
-            "value_w": value_w.transpose(0, 2, 1)[0],
-            "out_w": out_w[0],
-        }
-    )
-
+    stored = {
+        "gain": norm_gain,
+        "feature_w": feature_w,
+        "state": lin_state.transpose(0, 2, 1, 3).reshape(-1, HD),
+        "lin_norm": lin_norm,
+        "conv_w": conv_w,
+        "conv_state": conv_state,
+        "value_w": value_w.transpose(0, 2, 1)[0],
+        "out_w": out_w[0],
+    }
+
+    page = window_page(pages_first)
+    other = x_swap(page, 1)
     received = [head_shift(tokens, k) for k in (1, 3, 2)]
-    page = window_page(pages_first)
-    near, received = lax.optimization_barrier((near, received))
-    page, received = lax.optimization_barrier((page, received))
-    row_pages = [x_shift(page, k) for k in (1, 3, 2)]
+    other, received = lax.optimization_barrier((other, received))
+    stored, two_pages = lax.optimization_barrier((stored, jnp.stack([page, other])))
+    near = bring_near(stored)
     update = linear_layer([tokens] + received, near)
-    row_pages, update = lax.optimization_barrier((row_pages, update))
-    near_pages = jnp.stack([row_pages[0], page, row_pages[1], row_pages[2]])
-    far_pages = z_shift(near_pages, ZN // 2)
+    next_pages, update = lax.optimization_barrier((x_swap(two_pages, 2), update))
+    near_pages = jnp.concatenate([two_pages, next_pages])
+    far_pages = far_swap(near_pages)
     own_pages = own_pages.transpose(0, 1, 3, 2)
-    query_key_w, own_pages, page_table, ends, update = lax.optimization_barrier(
+    query_key_w, own_pages, table, ends, update = lax.optimization_barrier(
         (query_key_w, own_pages, page_table, lengths, update)
     )
-    near["query_key_w"], near["own_pages"] = bring_windows(
-        page_table, ends, query_key_w, own_pages
-    )
-    tags = jnp.concatenate([page_table[:, :1], ends[:, None]], axis=1)
+    near["query_key_w"], near["own_pages"], tags = bring_windows(
+        table, ends, query_key_w, own_pages
+    )
     swapped = [section_swap(update, k) for k in (0, 1, 3, 2)]
     one_share, packed, key_new, value_new = project(tags, swapped, near)
     asked = [packed] + [z_shift(packed, k) for k in (1, 7, 2)]

time: 63.7 us -> 55.9 us (0.88)
  starting transfers between devices: 35.4 us -> 31.7 us
  local copies, waits for them, and re-layouts: 1.57 us -> 0.07 us
  Pallas kernels: 12.6 us -> 11.2 us
  other arithmetic: 1.45 us -> 0.63 us
  waiting for transfers between devices: 12.3 us -> 11.6 us
    ppermute x7 -> x6, starting transfers between devices: 16 us -> 5.62 us  [z_shift(): lax.ppermute(value, 'req', [(z * XN + i, (z + steps) % ZN * XN + i) for z...]
    ppermute x3, starting transfers between devices: 4.29 us -> 13.8 us  [the longest x1 9.14 us: far_swap(): lax.ppermute(value, ('section', 'req'), [(count + i, count + (i + count /...]
    ppermute x3, waiting for transfers between devices: 4.68 us -> 2.17 us  [the longest x2 2.17 us: x_swap(): return lax.ppermute(value, 'req', [(i, i ^ flip) for i in range(XN * ZN)])]
    ppermute x4, starting transfers between devices: 6.01 us -> 4.01 us  [section_swap(): lax.ppermute(value, ('section', 'head'), there + [(b, a) for a, b in there])]
    ppermute x6, waiting for transfers between devices: 3.8 us -> 5.65 us  [head_shift(): lax.ppermute(value, 'head', [(i, (i + steps) % count) for i in range(coun...]
    pallas_call x8, Pallas kernels: 12.6 us -> 11.2 us  [kernel_call(): pl.pallas_call(run, out_shape=out_shape, in_specs=in_specs, out_specs=jax...]
    ppermute x1, starting transfers between devices: 1.11 us -> 0.1 us  [body(): one_back = lax.ppermute(one_share, 'section', [(1, 0), (0, 1)])]
    another operation x1, other arithmetic: 0.83 us -> 0.02 us  [body(): jnp.stack([page, other])]
  transfers between devices with their start and end apart: 21 -> 20, of which waited for: 7 -> 9; matrix products, arithmetic and copies ran while one was open for 2% -> 0% of each run, Pallas kernels for 16% -> 16%
where the time goes in v7:
time: 55.9 us; the launch traced here: 55.4 us
  starting transfers between devices  31.7 us (57%)
  waiting for transfers between devices  11.6 us (21%)
  Pallas kernels  11.2 us (20%)
  other arithmetic  0.63 us (1%)
    pallas_call x8, Pallas kernels, kernel_call(): pl.pallas_call(run, out_shape=out_shape, in_specs=in_specs, out_specs=jax...  11.2 us
    ppermute x1, starting transfers between devices, far_swap(): lax.ppermute(value, ('section', 'req'), [(count + i, count + (i + count /...  9.14 us
    ppermute x6, starting transfers between devices, head_shift(): lax.ppermute(value, 'head', [(i, (i + steps) % count) for i in range(coun...  8.15 us
    ppermute x6, waiting for transfers between devices, head_shift(): lax.ppermute(value, 'head', [(i, (i + steps) % count) for i in range(coun...  5.65 us
    ppermute x6, starting transfers between devices, z_shift(): lax.ppermute(value, 'req', [(z * XN + i, (z + steps) % ZN * XN + i) for z...  5.62 us
    ppermute x2, starting transfers between devices, x_swap(): return lax.ppermute(value, 'req', [(i, i ^ flip) for i in range(XN * ZN)])  4.66 us
    ppermute x4, starting transfers between devices, section_swap(): lax.ppermute(value, ('section', 'head'), there + [(b, a) for a, b in there])  4.01 us
    ppermute x6, waiting for transfers between devices, z_shift(): lax.ppermute(value, 'req', [(z * XN + i, (z + steps) % ZN * XN + i) for z...  2.71 us
  transfers between devices with their start and end apart: 20, of which 9 were waited for; matrix products, arithmetic and copies ran while one was open for 0% of the time, Pallas kernels for 16%

profile of v7, /device:TPU:1, one launch (start us, length us, event | category | flops | bytes accessed | tf_op | source)
XLA Modules:
  0.0 55.4 jit_solution(6470560849788201444)
XLA Ops:
  0.0 1.0 %window_page.1 = bf16[448,128]{1,0:T(8,128)(2,1)S(1)} custom-call(bf16[1,2,448,128]{3,2,1,0:T(8,128)(2,1)} %bitcast.18), custom_call_target="tpu_custom_call" | custom-call | bytes 16777216 | tf_op jit(solution)/shard_map/window_page/pallas_call | solution.py:110
  1.1 2.1 %collective-permute-start = (bf16[448,128]{1,0:T(8,128)(2,1)S(1)}, bf16[448,128]{1,0:T(8,128)(2,1)S(1)}, u32[]{:S(2)}, u32[]{:S(2)}) collective-permute-start(bf16[448,128]{1,0:T(8,128)(2,1)S(1)} %window_page.1), channel_id=1, source_target_pairs={{0,4},{4,0},{8,12},{12,8},{16,20},{20,16},{24,28},{28,24},{32,36},... | collective-permute-start | bytes 344072 | tf_op jit(solution)/shard_map/ppermute | solution.py:40
  3.2 1.3 %collective-permute-start.1 = (bf16[8,448]{1,0:T(8,128)(2,1)}, bf16[8,448]{1,0:T(8,128)(2,1)S(1)}, u32[]{:S(2)}, u32[]{:S(2)}) collective-permute-start(bf16[8,448]{1,0:T(8,128)(2,1)} %refs_0_.3), channel_id=1, source_target_pairs={{0,1},{1,2},{2,3},{3,0},{4,5},{5,6},{6,7},{7,4},{8,9},{9,10},{10,1... | collective-permute-start | bytes 21512 | tf_op jit(solution)/shard_map/ppermute | solution.py:28
  4.5 1.4 %collective-permute-start.2 = (bf16[8,448]{1,0:T(8,128)(2,1)}, bf16[8,448]{1,0:T(8,128)(2,1)S(1)}, u32[]{:S(2)}, u32[]{:S(2)}) collective-permute-start(bf16[8,448]{1,0:T(8,128)(2,1)} %refs_0_.3), channel_id=1, source_target_pairs={{0,3},{1,0},{2,1},{3,2},{4,7},{5,4},{6,5},{7,6},{8,11},{9,8},{10,9... | collective-permute-start | bytes 21512 | tf_op jit(solution)/shard_map/ppermute | solution.py:28
  5.9 1.6 %collective-permute-start.3 = (bf16[8,448]{1,0:T(8,128)(2,1)}, bf16[8,448]{1,0:T(8,128)(2,1)S(1)}, u32[]{:S(2)}, u32[]{:S(2)}) collective-permute-start(bf16[8,448]{1,0:T(8,128)(2,1)} %refs_0_.3), channel_id=1, source_target_pairs={{0,2},{1,3},{2,0},{3,1},{4,6},{5,7},{6,4},{7,5},{8,10},{9,11},{10,... | collective-permute-start | bytes 21512 | tf_op jit(solution)/shard_map/ppermute | solution.py:28
  7.6 0.0 collective-permute-done.1.refs_1_
  7.6 0.0 collective-permute-done.2.refs_2_
  7.6 2.6 %collective-permute-done.3.refs_3_ = bf16[8,448]{1,0:T(8,128)(2,1)S(1)} collective-permute-done((bf16[8,448]{1,0:T(8,128)(2,1)}, bf16[8,448]{1,0:T(8,128)(2,1)S(1)}, u32[]{:S(2)}, u32[]{:S(2)}) %collective-permute-start.3) | collective-permute-done | bytes 7200 | tf_op jit(solution)/shard_map/ppermute | solution.py:28
  10.1 0.0 collective-permute-done
  10.2 0.0 copy-start
  10.2 2.5 %collective-permute-start.4 = (bf16[2,448,128]{2,1,0:T(8,128)(2,1)S(1)}, bf16[2,448,128]{2,1,0:T(8,128)(2,1)S(1)}, u32[]{:S(2)}, u32[]{:S(2)}) collective-permute-start(bf16[2,448,128]{2,1,0:T(8,128)(2,1)S(1)} %pad_maximum_fusion), channel_id=1, source_target_pairs={{0,8},{4,12},{8,0},{12,4},{16,24},{20,28},{24,16},{28,20},{32,40},... | collective-permute-start | bytes 688136 | tf_op jit(solution)/shard_map/ppermute | solution.py:40
  12.7 2.0 %bring_near.1 = (bf16[8,2,448]{2,1,0:T(2,128)(2,1)S(1)}, f32[3,448]{1,0:T(4,128)S(1)}, bf16[1792,128]{1,0:T(8,128)(2,1)S(1)}, f32[1,1792]{1,0:T(1,128)S(1)}, f32...) custom-call(bf16[8,2,448]{2,1,0:T(2,128)(2,1)} %refs_0_.2, ...), custom_call_target="tpu_custom_call" | custom-call | bytes 11377408 | tf_op jit(solution)/shard_map/bring_near/pallas_call | solution.py:110
  14.7 0.0 copy-start.1
  14.7 0.0 copy-start.2
  14.8 2.2 %collective-permute-done.4 = bf16[2,448,128]{2,1,0:T(8,128)(2,1)S(1)} collective-permute-done((bf16[2,448,128]{2,1,0:T(8,128)(2,1)S(1)}, bf16[2,448,128]{2,1,0:T(8,128)(2,1)S(1)}, u32[]{:S(2)}, u32[]{:S(2)}) %collective-permute-start.4) | collective-permute-done | bytes 229408 | tf_op jit(solution)/shard_map/ppermute | solution.py:40
  17.0 9.1 %collective-permute-start.12 = (bf16[4,448,128]{2,1,0:T(8,128)(2,1)S(1)}, bf16[4,448,128]{2,1,0:T(8,128)(2,1)S(1)}, u32[]{:S(2)}, u32[]{:S(2)}) collective-permute-start(bf16[4,448,128]{2,1,0:T(8,128)(2,1)S(1)} %constant_dynamic-update-slice_fusion.refs_4_), channel_id=1, source_target_pairs={{128,192},{132,196},{136,200},{140,204},{144,208},{148,212},{152,2... | collective-permute-start | bytes 1376264 | tf_op jit(solution)/shard_map/ppermute | solution.py:45
  26.1 0.1 collective-permute-start.5
  26.2 1.8 %collective-permute-start.6 = (f32[8,1792]{1,0:T(8,128)S(1)}, f32[8,1792]{1,0:T(8,128)S(1)}, u32[]{:S(2)}, u32[]{:S(2)}) collective-permute-start(f32[8,1792]{1,0:T(8,128)S(1)} %linear_layer.1), channel_id=1, source_target_pairs={{0,129},{1,130},{2,131},{3,128},{129,0},{130,1},{131,2},{128,3},{4... | collective-permute-start | bytes 172040 | tf_op jit(solution)/shard_map/ppermute | solution.py:55
  28.0 2.1 %collective-permute-start.8 = (f32[8,1792]{1,0:T(8,128)S(1)}, f32[8,1792]{1,0:T(8,128)S(1)}, u32[]{:S(2)}, u32[]{:S(2)}) collective-permute-start(f32[8,1792]{1,0:T(8,128)S(1)} %linear_layer.1), channel_id=1, source_target_pairs={{0,130},{1,131},{2,128},{3,129},{130,0},{131,1},{128,2},{129,3},{4... | collective-permute-start | bytes 172040 | tf_op jit(solution)/shard_map/ppermute | solution.py:55
  30.2 3.9 %bring_windows.1 = (bf16[1792,896]{1,0:T(8,128)(2,1)S(1)}, bf16[8,2,2,448,128]{4,3,2,1,0:T(8,128)(2,1)S(1)}, f32[8,128]{1,0:T(8,128)S(1)}) custom-call(s32[8,256]{1,0:T(8,128)S(1)} %copy-done.1, s32[8]{0:T(128)S(1)} %copy-done.2, bf16[1792,896]{1,0:T(8,128)(2,1)} %refs_2_.1, bf16[16,2,448,128]{3,2,1,0:T(8,128)(2,1)} %bitcast.14), custom_call_target="tpu_custom_call" | custom-call | bytes 13762560 | tf_op jit(solution)/shard_map/bring_windows/pallas_call | solution.py:110
  34.1 0.0 collective-permute-done.5.refs_1_
  34.1 0.0 collective-permute-done.7.refs_3_
  34.1 0.0 collective-permute-done.8.refs_4_
  34.2 1.1 %project.1 = (bf16[8,448]{1,0:T(8,128)(2,1)S(1)}, bf16[8,512]{1,0:T(8,128)(2,1)S(1)}, bf16[8,448]{1,0:T(8,128)(2,1)S(1)}, bf16[8,448]{1,0:T(8,128)(2,1)S(1)}) custom-call(f32[8,128]{1,0:T(8,128)S(1)} %get-tuple-element.94.refs_0_, f32[8,1792]{1,0:T(8,128)S(1)} %collective-permute-done.5.refs_1_, f32[8,1792]{1,0:T(8,128)S(1)} %collective-permute-done.6.refs_2_, ...), custom_call_target="tpu_custom_call" | custom-call | tf_op jit(solution)/shard_map/project/pallas_call | solution.py:110
  35.2 0.1 collective-permute-start.10
  35.3 1.9 %collective-permute-start.11 = (bf16[8,512]{1,0:T(8,128)(2,1)S(1)}, bf16[8,512]{1,0:T(8,128)(2,1)S(1)}, u32[]{:S(2)}, u32[]{:S(2)}) collective-permute-start(bf16[8,512]{1,0:T(8,128)(2,1)S(1)} %get-tuple-element.104.refs_1_.refs_0_), channel_id=1, source_target_pairs={{0,32},{4,36},{8,40},{12,44},{16,48},{20,52},{24,56},{28,60},{32,6... | collective-permute-start | bytes 24584 | tf_op jit(solution)/shard_map/ppermute | solution.py:32
  37.2 0.7 %collective-permute-start.9 = (bf16[8,512]{1,0:T(8,128)(2,1)S(1)}, bf16[8,512]{1,0:T(8,128)(2,1)S(1)}, u32[]{:S(2)}, u32[]{:S(2)}) collective-permute-start(bf16[8,512]{1,0:T(8,128)(2,1)S(1)} %get-tuple-element.104.refs_1_.refs_0_), channel_id=1, source_target_pairs={{0,16},{4,20},{8,24},{12,28},{16,32},{20,36},{24,40},{28,44},{32,4... | collective-permute-start | bytes 24584 | tf_op jit(solution)/shard_map/ppermute | solution.py:32
  37.9 1.7 %own_attention.1 = (f32[8,448]{1,0:T(8,128)S(1)}, f32[8,448]{1,0:T(8,128)S(1)}, f32[8,448]{1,0:T(8,128)S(1)}) custom-call(s32[8]{0:T(128)S(1)} %copy-done.2, bf16[8,512]{1,0:T(8,128)(2,1)S(1)} %get-tuple-element.104.refs_1_.refs_0_, bf16[8,448]{1,0:T(8,128)(2,1)S(1)} %get-tuple-element.98.refs_2_, bf16[8,448]{1,0:T(8,128)(2,1)S(1)} %get-tuple-element.99.refs_3_, ...), custom_call_target="tpu_custom_call" | custom-call | tf_op jit(solution)/shard_map/own_attention/pallas_call | solution.py:110
  39.6 0.0 collective-permute-done.10.refs_2_
  39.6 0.4 collective-permute-done.11.refs_3_
  40.0 0.9 %collective-permute-done.9.refs_1_ = bf16[8,512]{1,0:T(8,128)(2,1)S(1)} collective-permute-done((bf16[8,512]{1,0:T(8,128)(2,1)S(1)}, bf16[8,512]{1,0:T(8,128)(2,1)S(1)}, u32[]{:S(2)}, u32[]{:S(2)}) %collective-permute-start.9) | collective-permute-done | bytes 8224 | tf_op jit(solution)/shard_map/ppermute | solution.py:32
  40.9 0.9 %prompt_attention.1 = (f32[8,640]{1,0:T(8,128)S(1)}, f32[8,640]{1,0:T(8,128)S(1)}, f32[8,640]{1,0:T(8,128)S(1)}, f32[8,640]{1,0:T(8,128)S(1)}) custom-call(bf16[8,512]{1,0:T(8,128)(2,1)S(1)} %get-tuple-element.104.refs_1_.refs_0_, bf16[8,512]{1,0:T(8,128)(2,1)S(1)} %collective-permute-done.9.refs_1_, bf16[8,512]{1,0:T(8,128)(2,1)S(1)} %collective-permute-done.10.refs_2_, ...), custom_call_target="tpu_custom_call" | custom-call | tf_op jit(solution)/shard_map/prompt_attention/pallas_call | solution.py:110
  41.8 1.2 %collective-permute-start.13 = (f32[8,640]{1,0:T(8,128)S(1)}, f32[8,640]{1,0:T(8,128)S(1)}, u32[]{:S(2)}, u32[]{:S(2)}) collective-permute-start(f32[8,640]{1,0:T(8,128)S(1)} %get-tuple-element.115), channel_id=1, source_target_pairs={{0,112},{4,116},{8,120},{12,124},{16,0},{20,4},{24,8},{28,12},{32,... | collective-permute-start | bytes 61448 | tf_op jit(solution)/shard_map/ppermute | solution.py:32
  43.1 0.5 collective-permute-start.14
  43.6 1.2 %collective-permute-start.15 = (f32[8,640]{1,0:T(8,128)S(1)}, f32[8,640]{1,0:T(8,128)S(1)}, u32[]{:S(2)}, u32[]{:S(2)}) collective-permute-start(f32[8,640]{1,0:T(8,128)S(1)} %get-tuple-element.117), channel_id=1, source_target_pairs={{0,96},{4,100},{8,104},{12,108},{16,112},{20,116},{24,120},{28,124... | collective-permute-start | bytes 61448 | tf_op jit(solution)/shard_map/ppermute | solution.py:32
  44.8 0.1 collective-permute-start.16
  44.9 1.1 %collective-permute-done.16 = bf16[8,448]{1,0:T(8,128)(2,1)S(1)} collective-permute-done((bf16[8,448]{1,0:T(8,128)(2,1)S(1)}, bf16[8,448]{1,0:T(8,128)(2,1)S(1)}, u32[]{:S(2)}, u32[]{:S(2)}) %collective-permute-start.16) | collective-permute-done | bytes 7200 | tf_op jit(solution)/shard_map/ppermute | solution.py:669
  46.0 0.0 collective-permute-done.13.refs_4_
  46.0 1.3 %collective-permute-done.14.refs_5_ = f32[8,640]{1,0:T(8,128)S(1)} collective-permute-done((f32[8,640]{1,0:T(8,128)S(1)}, f32[8,640]{1,0:T(8,128)S(1)}, u32[]{:S(2)}, u32[]{:S(2)}) %collective-permute-start.14) | collective-permute-done | bytes 20512 | tf_op jit(solution)/shard_map/ppermute | solution.py:32
  47.2 0.2 collective-permute-done.15.refs_6_
  47.4 0.6 %combine.1 = (f32[8,448]{1,0:T(8,128)S(1)}, f32[8,448]{1,0:T(8,128)S(1)}, f32[8,448]{1,0:T(8,128)S(1)}, f32[8,448]{1,0:T(8,128)S(1)}) custom-call(f32[8,448]{1,0:T(8,128)S(1)} %get-tuple-element.120.refs_0_, f32[8,448]{1,0:T(8,128)S(1)} %get-tuple-element.121.refs_1_, f32[8,448]{1,0:T(8,128)S(1)} %get-tuple-element.122.refs_2_, ...), custom_call_target="tpu_custom_call" | custom-call | tf_op jit(solution)/shard_map/combine/pallas_call | solution.py:110
  48.0 0.2 collective-permute-start.17
  48.2 2.6 %collective-permute-start.18 = (f32[8,448]{1,0:T(8,128)S(1)}, f32[8,448]{1,0:T(8,128)S(1)}, u32[]{:S(2)}, u32[]{:S(2)}) collective-permute-start(f32[8,448]{1,0:T(8,128)S(1)} %get-tuple-element.129), channel_id=1, source_target_pairs={{0,3},{1,0},{2,1},{3,2},{4,7},{5,4},{6,5},{7,6},{8,11},{9,8},{10,9... | collective-permute-start | bytes 43016 | tf_op jit(solution)/shard_map/ppermute | solution.py:28
  50.7 1.0 %collective-permute-start.19 = (f32[8,448]{1,0:T(8,128)S(1)}, f32[8,448]{1,0:T(8,128)S(1)}, u32[]{:S(2)}, u32[]{:S(2)}) collective-permute-start(f32[8,448]{1,0:T(8,128)S(1)} %get-tuple-element.130), channel_id=1, source_target_pairs={{0,2},{1,3},{2,0},{3,1},{4,6},{5,7},{6,4},{7,5},{8,10},{9,11},{10,... | collective-permute-start | bytes 43016 | tf_op jit(solution)/shard_map/ppermute | solution.py:28
  51.7 0.1 collective-permute-done.17
  51.8 0.0 collective-permute-done.18
  51.8 3.0 %collective-permute-done.19 = f32[8,448]{1,0:T(8,128)S(1)} collective-permute-done((f32[8,448]{1,0:T(8,128)S(1)}, f32[8,448]{1,0:T(8,128)S(1)}, u32[]{:S(2)}, u32[]{:S(2)}) %collective-permute-start.19) | collective-permute-done | bytes 14368 | tf_op jit(solution)/shard_map/ppermute | solution.py:28
  54.8 0.6 %fusion.1 = bf16[1,8,448]{2,1,0:T(8,128)(2,1)} fusion(bf16[8,448]{1,0:T(8,128)(2,1)S(1)} %collective-permute-done.16, f32[8,448]{1,0:T(8,128)S(1)} %collective-permute-done.19, f32[8,448]{1,0:T(8,128)S(1)} %collective-permute-done.18, f32[8,448]{1,0:T(8,128)S(1)} %collective-permute-done.17, f32[8,448]{1,0:T(8,128)S(1)} %get-tuple-element.127, ...), kind=kLoop, calls=%fused_computation.3 | loop fusion | flops 25088 | bytes 78849 | tf_op jit(solution)/shard_map/broadcast_in_dim | solution.py:677
  (10 shorter events, 0.1 us)
Async XLA Ops:
  1.1 9.1 %collective-permute-start = (bf16[448,128]{1,0:T(8,128)(2,1)S(1)}, bf16[448,128]{1,0:T(8,128)(2,1)S(1)}, u32[]{:S(2)}, u32[]{:S(2)}) collective-permute-start(bf16[448,128]{1,0:T(8,128)(2,1)S(1)} %window_page.1), channel_id=1, source_target_pairs={{0,4},{4,0},{8,12},{12,8},{16,20},{20,16},{24,28},{28,24},{32,36},... | collective-permute-start | bytes 344072 | tf_op jit(solution)/shard_map/ppermute | solution.py:40
  3.2 4.4 %collective-permute-start.1 = (bf16[8,448]{1,0:T(8,128)(2,1)}, bf16[8,448]{1,0:T(8,128)(2,1)S(1)}, u32[]{:S(2)}, u32[]{:S(2)}) collective-permute-start(bf16[8,448]{1,0:T(8,128)(2,1)} %refs_0_.3), channel_id=1, source_target_pairs={{0,1},{1,2},{2,3},{3,0},{4,5},{5,6},{6,7},{7,4},{8,9},{9,10},{10,1... | collective-permute-start | bytes 21512 | tf_op jit(solution)/shard_map/ppermute | solution.py:28
  4.5 3.1 %collective-permute-start.2 = (bf16[8,448]{1,0:T(8,128)(2,1)}, bf16[8,448]{1,0:T(8,128)(2,1)S(1)}, u32[]{:S(2)}, u32[]{:S(2)}) collective-permute-start(bf16[8,448]{1,0:T(8,128)(2,1)} %refs_0_.3), channel_id=1, source_target_pairs={{0,3},{1,0},{2,1},{3,2},{4,7},{5,4},{6,5},{7,6},{8,11},{9,8},{10,9... | collective-permute-start | bytes 21512 | tf_op jit(solution)/shard_map/ppermute | solution.py:28
  5.9 4.2 %collective-permute-start.3 = (bf16[8,448]{1,0:T(8,128)(2,1)}, bf16[8,448]{1,0:T(8,128)(2,1)S(1)}, u32[]{:S(2)}, u32[]{:S(2)}) collective-permute-start(bf16[8,448]{1,0:T(8,128)(2,1)} %refs_0_.3), channel_id=1, source_target_pairs={{0,2},{1,3},{2,0},{3,1},{4,6},{5,7},{6,4},{7,5},{8,10},{9,11},{10,... | collective-permute-start | bytes 21512 | tf_op jit(solution)/shard_map/ppermute | solution.py:28
  10.2 4.5 %copy-start = (bf16[8,448]{1,0:T(8,128)(2,1)S(1)}, bf16[8,448]{1,0:T(8,128)(2,1)}, u32[]{:S(2)}) copy-start(bf16[8,448]{1,0:T(8,128)(2,1)} %refs_0_.3) | copy-start | bytes 21508
  10.2 6.8 %collective-permute-start.4 = (bf16[2,448,128]{2,1,0:T(8,128)(2,1)S(1)}, bf16[2,448,128]{2,1,0:T(8,128)(2,1)S(1)}, u32[]{:S(2)}, u32[]{:S(2)}) collective-permute-start(bf16[2,448,128]{2,1,0:T(8,128)(2,1)S(1)} %pad_maximum_fusion), channel_id=1, source_target_pairs={{0,8},{4,12},{8,0},{12,4},{16,24},{20,28},{24,16},{28,20},{32,40},... | collective-permute-start | bytes 688136 | tf_op jit(solution)/shard_map/ppermute | solution.py:40
  14.7 15.4 %copy-start.1 = (s32[8,256]{1,0:T(8,128)S(1)}, s32[8,256]{1,0:T(8,128)}, u32[]{:S(2)}) copy-start(s32[8,256]{1,0:T(8,128)} %refs_0_.4) | copy-start | bytes 24580
  14.7 15.4 %copy-start.2 = (s32[8]{0:T(128)S(1)}, s32[8]{0:T(128)}, u32[]{:S(2)}) copy-start(s32[8]{0:T(128)} %refs_0_.5) | copy-start | bytes 100
  17.0 23.9 %collective-permute-start.12 = (bf16[4,448,128]{2,1,0:T(8,128)(2,1)S(1)}, bf16[4,448,128]{2,1,0:T(8,128)(2,1)S(1)}, u32[]{:S(2)}, u32[]{:S(2)}) collective-permute-start(bf16[4,448,128]{2,1,0:T(8,128)(2,1)S(1)} %constant_dynamic-update-slice_fusion.refs_4_), channel_id=1, source_target_pairs={{128,192},{132,196},{136,200},{140,204},{144,208},{148,212},{152,2... | collective-permute-start | bytes 1376264 | tf_op jit(solution)/shard_map/ppermute | solution.py:45
  26.1 8.0 %collective-permute-start.5 = (f32[8,1792]{1,0:T(8,128)S(1)}, f32[8,1792]{1,0:T(8,128)S(1)}, u32[]{:S(2)}, u32[]{:S(2)}) collective-permute-start(f32[8,1792]{1,0:T(8,128)S(1)} %linear_layer.1), channel_id=1, source_target_pairs={{0,128},{1,129},{2,130},{3,131},{128,0},{129,1},{130,2},{131,3},{4... | collective-permute-start | bytes 172040 | tf_op jit(solution)/shard_map/ppermute | solution.py:55
  26.2 7.9 %collective-permute-start.6 = (f32[8,1792]{1,0:T(8,128)S(1)}, f32[8,1792]{1,0:T(8,128)S(1)}, u32[]{:S(2)}, u32[]{:S(2)}) collective-permute-start(f32[8,1792]{1,0:T(8,128)S(1)} %linear_layer.1), channel_id=1, source_target_pairs={{0,129},{1,130},{2,131},{3,128},{129,0},{130,1},{131,2},{128,3},{4... | collective-permute-start | bytes 172040 | tf_op jit(solution)/shard_map/ppermute | solution.py:55
  28.0 6.1 %collective-permute-start.7 = (f32[8,1792]{1,0:T(8,128)S(1)}, f32[8,1792]{1,0:T(8,128)S(1)}, u32[]{:S(2)}, u32[]{:S(2)}) collective-permute-start(f32[8,1792]{1,0:T(8,128)S(1)} %linear_layer.1), channel_id=1, source_target_pairs={{0,131},{1,128},{2,129},{3,130},{131,0},{128,1},{129,2},{130,3},{4... | collective-permute-start | bytes 172040 | tf_op jit(solution)/shard_map/ppermute | solution.py:55
  28.0 6.1 %collective-permute-start.8 = (f32[8,1792]{1,0:T(8,128)S(1)}, f32[8,1792]{1,0:T(8,128)S(1)}, u32[]{:S(2)}, u32[]{:S(2)}) collective-permute-start(f32[8,1792]{1,0:T(8,128)S(1)} %linear_layer.1), channel_id=1, source_target_pairs={{0,130},{1,131},{2,128},{3,129},{130,0},{131,1},{128,2},{129,3},{4... | collective-permute-start | bytes 172040 | tf_op jit(solution)/shard_map/ppermute | solution.py:55
  35.2 4.4 %collective-permute-start.10 = (bf16[8,512]{1,0:T(8,128)(2,1)S(1)}, bf16[8,512]{1,0:T(8,128)(2,1)S(1)}, u32[]{:S(2)}, u32[]{:S(2)}) collective-permute-start(bf16[8,512]{1,0:T(8,128)(2,1)S(1)} %get-tuple-element.104.refs_1_.refs_0_), channel_id=1, source_target_pairs={{0,112},{4,116},{8,120},{12,124},{16,0},{20,4},{24,8},{28,12},{32,... | collective-permute-start | bytes 24584 | tf_op jit(solution)/shard_map/ppermute | solution.py:32
  35.3 4.7 %collective-permute-start.11 = (bf16[8,512]{1,0:T(8,128)(2,1)S(1)}, bf16[8,512]{1,0:T(8,128)(2,1)S(1)}, u32[]{:S(2)}, u32[]{:S(2)}) collective-permute-start(bf16[8,512]{1,0:T(8,128)(2,1)S(1)} %get-tuple-element.104.refs_1_.refs_0_), channel_id=1, source_target_pairs={{0,32},{4,36},{8,40},{12,44},{16,48},{20,52},{24,56},{28,60},{32,6... | collective-permute-start | bytes 24584 | tf_op jit(solution)/shard_map/ppermute | solution.py:32
  37.2 3.7 %collective-permute-start.9 = (bf16[8,512]{1,0:T(8,128)(2,1)S(1)}, bf16[8,512]{1,0:T(8,128)(2,1)S(1)}, u32[]{:S(2)}, u32[]{:S(2)}) collective-permute-start(bf16[8,512]{1,0:T(8,128)(2,1)S(1)} %get-tuple-element.104.refs_1_.refs_0_), channel_id=1, source_target_pairs={{0,16},{4,20},{8,24},{12,28},{16,32},{20,36},{24,40},{28,44},{32,4... | collective-permute-start | bytes 24584 | tf_op jit(solution)/shard_map/ppermute | solution.py:32
  41.8 4.1 %collective-permute-start.13 = (f32[8,640]{1,0:T(8,128)S(1)}, f32[8,640]{1,0:T(8,128)S(1)}, u32[]{:S(2)}, u32[]{:S(2)}) collective-permute-start(f32[8,640]{1,0:T(8,128)S(1)} %get-tuple-element.115), channel_id=1, source_target_pairs={{0,112},{4,116},{8,120},{12,124},{16,0},{20,4},{24,8},{28,12},{32,... | collective-permute-start | bytes 61448 | tf_op jit(solution)/shard_map/ppermute | solution.py:32
  43.1 4.1 %collective-permute-start.14 = (f32[8,640]{1,0:T(8,128)S(1)}, f32[8,640]{1,0:T(8,128)S(1)}, u32[]{:S(2)}, u32[]{:S(2)}) collective-permute-start(f32[8,640]{1,0:T(8,128)S(1)} %get-tuple-element.116), channel_id=1, source_target_pairs={{0,16},{4,20},{8,24},{12,28},{16,32},{20,36},{24,40},{28,44},{32,4... | collective-permute-start | bytes 61448 | tf_op jit(solution)/shard_map/ppermute | solution.py:32
  43.6 3.8 %collective-permute-start.15 = (f32[8,640]{1,0:T(8,128)S(1)}, f32[8,640]{1,0:T(8,128)S(1)}, u32[]{:S(2)}, u32[]{:S(2)}) collective-permute-start(f32[8,640]{1,0:T(8,128)S(1)} %get-tuple-element.117), channel_id=1, source_target_pairs={{0,96},{4,100},{8,104},{12,108},{16,112},{20,116},{24,120},{28,124... | collective-permute-start | bytes 61448 | tf_op jit(solution)/shard_map/ppermute | solution.py:32
  44.8 1.2 %collective-permute-start.16 = (bf16[8,448]{1,0:T(8,128)(2,1)S(1)}, bf16[8,448]{1,0:T(8,128)(2,1)S(1)}, u32[]{:S(2)}, u32[]{:S(2)}) collective-permute-start(bf16[8,448]{1,0:T(8,128)(2,1)S(1)} %get-tuple-element.118), channel_id=1, source_target_pairs={{128,0},{0,128},{129,1},{1,129},{130,2},{2,130},{131,3},{3,131},{1... | collective-permute-start | bytes 21512 | tf_op jit(solution)/shard_map/ppermute | solution.py:669
  48.0 3.9 %collective-permute-start.17 = (f32[8,448]{1,0:T(8,128)S(1)}, f32[8,448]{1,0:T(8,128)S(1)}, u32[]{:S(2)}, u32[]{:S(2)}) collective-permute-start(f32[8,448]{1,0:T(8,128)S(1)} %get-tuple-element.128), channel_id=1, source_target_pairs={{0,1},{1,2},{2,3},{3,0},{4,5},{5,6},{6,7},{7,4},{8,9},{9,10},{10,1... | collective-permute-start | bytes 43016 | tf_op jit(solution)/shard_map/ppermute | solution.py:28
  48.2 3.7 %collective-permute-start.18 = (f32[8,448]{1,0:T(8,128)S(1)}, f32[8,448]{1,0:T(8,128)S(1)}, u32[]{:S(2)}, u32[]{:S(2)}) collective-permute-start(f32[8,448]{1,0:T(8,128)S(1)} %get-tuple-element.129), channel_id=1, source_target_pairs={{0,3},{1,0},{2,1},{3,2},{4,7},{5,4},{6,5},{7,6},{8,11},{9,8},{10,9... | collective-permute-start | bytes 43016 | tf_op jit(solution)/shard_map/ppermute | solution.py:28
  50.7 4.1 %collective-permute-start.19 = (f32[8,448]{1,0:T(8,128)S(1)}, f32[8,448]{1,0:T(8,128)S(1)}, u32[]{:S(2)}, u32[]{:S(2)}) collective-permute-start(f32[8,448]{1,0:T(8,128)S(1)} %get-tuple-element.130), channel_id=1, source_target_pairs={{0,2},{1,3},{2,0},{3,1},{4,6},{5,7},{6,4},{7,5},{8,10},{9,11},{10,... | collective-permute-start | bytes 43016 | tf_op jit(solution)/shard_map/ppermute | solution.py:28

commit v8 on v7

--- a/solution.py
+++ b/solution.py
@@ -38,15 +38,6 @@
 
 def x_swap(value, flip):
     return lax.ppermute(value, "req", [(i, i ^ flip) for i in range(XN * ZN)])
-
-
-def far_swap(value):
-    count = XN * ZN
-    return lax.ppermute(
-        value,
-        ("section", "req"),
-        [(count + i, count + (i + count // 2) % count) for i in range(count)],
-    )
 
 
 def section_swap(value, steps):
@@ -93,7 +84,7 @@
     def run(*refs):
         ids = place()
 
-        @pl.when(ids[0] == section)
+        @pl.when(section is None or ids[0] == section)
         def _():
             kernel(ids, *refs)
 
@@ -603,7 +594,7 @@
     shape = prompt_pages.shape[1:]
     return kernel_call(
         page_kernel,
-        1,
+        None,
         "window_page",
         jax.ShapeDtypeStruct(shape[1:], jnp.bfloat16),
         [HBM],
@@ -641,16 +632,20 @@
         "out_w": out_w[0],
     }
 
+    section_index = lax.axis_index("section")
     page = window_page(pages_first)
-    other = x_swap(page, 1)
+    far_page = z_shift(page, ZN // 2)
     received = [head_shift(tokens, k) for k in (1, 3, 2)]
-    other, received = lax.optimization_barrier((other, received))
-    stored, two_pages = lax.optimization_barrier((stored, jnp.stack([page, other])))
+    far_page, received = lax.optimization_barrier((far_page, received))
+    page = jnp.where(section_index == 0, far_page, page)
+    stored, page = lax.optimization_barrier((stored, page))
     near = bring_near(stored)
+    other, near = lax.optimization_barrier((x_swap(page, 1), near))
+    two_pages = jnp.stack([page, other])
     update = linear_layer([tokens] + received, near)
     next_pages, update = lax.optimization_barrier((x_swap(two_pages, 2), update))
     near_pages = jnp.concatenate([two_pages, next_pages])
-    far_pages = far_swap(near_pages)
+    far_pages = lax.ppermute(near_pages, "section", [(0, 1), (1, 0)])
     own_pages = own_pages.transpose(0, 1, 3, 2)
     query_key_w, own_pages, table, ends, update = lax.optimization_barrier(
         (query_key_w, own_pages, page_table, lengths, update)
@@ -669,7 +664,6 @@
     one_back = lax.ppermute(one_share, "section", [(1, 0), (0, 1)])
     parts, one_back = lax.optimization_barrier((parts, one_back))
     slabs = combine(own, parts, near)
-    section_index = lax.axis_index("section")
     total = one_share.astype(jnp.float32) + slabs[0]
     for piece in [head_shift(slabs[k], k) for k in (1, 3, 2)]:
         total = total + piece

time: 55.9 us -> 64.4 us (1.15)
  the two profiles are of different devices: /device:TPU:1 before, /device:TPU:6 now
where the time goes in v8:
time: 64.4 us; the launch traced here: 64.3 us
  starting transfers between devices  28.3 us (44%)
  waiting for transfers between devices  27.4 us (43%)
  Pallas kernels  7.8 us (12%)
  other arithmetic  0.69 us (1%)
    ppermute x7, starting transfers between devices, z_shift(): lax.ppermute(value, 'req', [(z * XN + i, (z + steps) % ZN * XN + i) for z...  13.2 us
    ppermute x6, starting transfers between devices, head_shift(): lax.ppermute(value, 'head', [(i, (i + steps) % count) for i in range(coun...  9.02 us
    ppermute x6, waiting for transfers between devices, head_shift(): lax.ppermute(value, 'head', [(i, (i + steps) % count) for i in range(coun...  8.33 us
    ppermute x7, waiting for transfers between devices, z_shift(): lax.ppermute(value, 'req', [(z * XN + i, (z + steps) % ZN * XN + i) for z...  7.91 us
    pallas_call x8, Pallas kernels, kernel_call(): pl.pallas_call(run, out_shape=out_shape, in_specs=in_specs, out_specs=jax...  7.8 us
    ppermute x2, waiting for transfers between devices, x_swap(): return lax.ppermute(value, 'req', [(i, i ^ flip) for i in range(XN * ZN)])  7.3 us
    ppermute x4, starting transfers between devices, section_swap(): lax.ppermute(value, ('section', 'head'), there + [(b, a) for a, b in there])  4.62 us
    ppermute x4, waiting for transfers between devices, section_swap(): lax.ppermute(value, ('section', 'head'), there + [(b, a) for a, b in there])  2.86 us
  transfers between devices with their start and end apart: 21, of which 13 were waited for; matrix products, arithmetic and copies ran while one was open for 0% of the time, Pallas kernels for 10%

profile of v8, /device:TPU:6, one launch (start us, length us, event | category | flops | bytes accessed | tf_op | source)
XLA Modules:
  0.0 64.3 jit_solution(12586748180662687100)
XLA Ops:
  0.0 1.0 %window_page.1 = bf16[448,128]{1,0:T(8,128)(2,1)S(1)} custom-call(bf16[1,2,448,128]{3,2,1,0:T(8,128)(2,1)} %bitcast.21), custom_call_target="tpu_custom_call" | custom-call | bytes 16777216 | tf_op jit(solution)/shard_map/window_page/pallas_call | solution.py:101
  1.1 7.3 %collective-permute-start = (bf16[448,128]{1,0:T(8,128)(2,1)S(1)}, bf16[448,128]{1,0:T(8,128)(2,1)S(1)}, u32[]{:S(2)}, u32[]{:S(2)}) collective-permute-start(bf16[448,128]{1,0:T(8,128)(2,1)S(1)} %window_page.1), channel_id=1, source_target_pairs={{0,64},{4,68},{8,72},{12,76},{16,80},{20,84},{24,88},{28,92},{32,9... | collective-permute-start | bytes 344072 | tf_op jit(solution)/shard_map/ppermute | solution.py:32
  8.3 1.6 %collective-permute-start.1 = (bf16[8,448]{1,0:T(8,128)(2,1)}, bf16[8,448]{1,0:T(8,128)(2,1)S(1)}, u32[]{:S(2)}, u32[]{:S(2)}) collective-permute-start(bf16[8,448]{1,0:T(8,128)(2,1)} %refs_0_.3), channel_id=1, source_target_pairs={{0,1},{1,2},{2,3},{3,0},{4,5},{5,6},{6,7},{7,4},{8,9},{9,10},{10,1... | collective-permute-start | bytes 21512 | tf_op jit(solution)/shard_map/ppermute | solution.py:28
  9.9 1.7 %collective-permute-start.2 = (bf16[8,448]{1,0:T(8,128)(2,1)}, bf16[8,448]{1,0:T(8,128)(2,1)S(1)}, u32[]{:S(2)}, u32[]{:S(2)}) collective-permute-start(bf16[8,448]{1,0:T(8,128)(2,1)} %refs_0_.3), channel_id=1, source_target_pairs={{0,3},{1,0},{2,1},{3,2},{4,7},{5,4},{6,5},{7,6},{8,11},{9,8},{10,9... | collective-permute-start | bytes 21512 | tf_op jit(solution)/shard_map/ppermute | solution.py:28
  11.6 2.0 %collective-permute-start.3 = (bf16[8,448]{1,0:T(8,128)(2,1)}, bf16[8,448]{1,0:T(8,128)(2,1)S(1)}, u32[]{:S(2)}, u32[]{:S(2)}) collective-permute-start(bf16[8,448]{1,0:T(8,128)(2,1)} %refs_0_.3), channel_id=1, source_target_pairs={{0,2},{1,3},{2,0},{3,1},{4,6},{5,7},{6,4},{7,5},{8,10},{9,11},{10,... | collective-permute-start | bytes 21512 | tf_op jit(solution)/shard_map/ppermute | solution.py:28
  13.6 0.0 collective-permute-done.1.refs_1_
  13.6 0.2 collective-permute-done.2.refs_2_
  13.8 3.2 %collective-permute-done.3.refs_3_ = bf16[8,448]{1,0:T(8,128)(2,1)S(1)} collective-permute-done((bf16[8,448]{1,0:T(8,128)(2,1)}, bf16[8,448]{1,0:T(8,128)(2,1)S(1)}, u32[]{:S(2)}, u32[]{:S(2)}) %collective-permute-start.3) | collective-permute-done | bytes 7200 | tf_op jit(solution)/shard_map/ppermute | solution.py:28
  16.9 0.0 collective-permute-done
  17.0 0.0 copy-start
  17.0 0.9 %collective-permute-start.4 = (bf16[448,128]{1,0:T(8,128)(2,1)S(1)}, bf16[448,128]{1,0:T(8,128)(2,1)S(1)}, u32[]{:S(2)}, u32[]{:S(2)}) collective-permute-start(bf16[448,128]{1,0:T(8,128)(2,1)S(1)} %broadcast_select_fusion), channel_id=1, source_target_pairs={{0,4},{4,0},{8,12},{12,8},{16,20},{20,16},{24,28},{28,24},{32,36},... | collective-permute-start | bytes 344072 | tf_op jit(solution)/shard_map/ppermute | solution.py:40
  17.9 2.9 %bring_near.1 = (bf16[8,2,448]{2,1,0:T(2,128)(2,1)S(1)}, f32[3,448]{1,0:T(4,128)S(1)}, bf16[1792,128]{1,0:T(8,128)(2,1)S(1)}, f32[1,1792]{1,0:T(1,128)S(1)}, f32...) custom-call(bf16[8,2,448]{2,1,0:T(2,128)(2,1)} %refs_0_.2, ...), custom_call_target="tpu_custom_call" | custom-call | bytes 11377408 | tf_op jit(solution)/shard_map/bring_near/pallas_call | solution.py:101
  20.8 2.3 %collective-permute-done.4 = bf16[448,128]{1,0:T(8,128)(2,1)S(1)} collective-permute-done((bf16[448,128]{1,0:T(8,128)(2,1)S(1)}, bf16[448,128]{1,0:T(8,128)(2,1)S(1)}, u32[]{:S(2)}, u32[]{:S(2)}) %collective-permute-start.4) | collective-permute-done | bytes 114720 | tf_op jit(solution)/shard_map/ppermute | solution.py:40
  23.1 0.0 copy-start.1
  23.1 0.0 copy-start.2
  23.1 0.3 collective-permute-start.5
  23.4 2.3 %linear_layer.1 = f32[8,1792]{1,0:T(8,128)S(1)} custom-call(bf16[8,448]{1,0:T(8,128)(2,1)S(1)} %copy-done, bf16[8,448]{1,0:T(8,128)(2,1)S(1)} %collective-permute-done.1.refs_1_, bf16[8,448]{1,0:T(8,128)(2,1)S(1)} %collective-permute-done.2.refs_2_, bf16[8,448]{1,0:T(8,128)(2,1)S(1)} %collective-permute-done.3.refs_3_, ...), custom_call_target="tpu_custom_call" | custom-call | tf_op jit(solution)/shard_map/linear_layer/pallas_call | solution.py:101
  25.7 5.0 %collective-permute-done.5 = bf16[2,448,128]{2,1,0:T(8,128)(2,1)S(1)} collective-permute-done((bf16[2,448,128]{2,1,0:T(8,128)(2,1)S(1)}, bf16[2,448,128]{2,1,0:T(8,128)(2,1)S(1)}, u32[]{:S(2)}, u32[]{:S(2)}) %collective-permute-start.5) | collective-permute-done | bytes 229408 | tf_op jit(solution)/shard_map/ppermute | solution.py:40
  30.8 0.1 collective-permute-start.13
  30.9 0.5 collective-permute-start.6
  31.4 0.1 collective-permute-start.7
  31.5 2.2 %collective-permute-start.8 = (f32[8,1792]{1,0:T(8,128)S(1)}, f32[8,1792]{1,0:T(8,128)S(1)}, u32[]{:S(2)}, u32[]{:S(2)}) collective-permute-start(f32[8,1792]{1,0:T(8,128)S(1)} %linear_layer.1), channel_id=1, source_target_pairs={{0,131},{1,128},{2,129},{3,130},{131,0},{128,1},{129,2},{130,3},{4... | collective-permute-start | bytes 172040 | tf_op jit(solution)/shard_map/ppermute | solution.py:46
  33.7 1.8 %collective-permute-start.9 = (f32[8,1792]{1,0:T(8,128)S(1)}, f32[8,1792]{1,0:T(8,128)S(1)}, u32[]{:S(2)}, u32[]{:S(2)}) collective-permute-start(f32[8,1792]{1,0:T(8,128)S(1)} %linear_layer.1), channel_id=1, source_target_pairs={{0,130},{1,131},{2,128},{3,129},{130,0},{131,1},{128,2},{129,3},{4... | collective-permute-start | bytes 172040 | tf_op jit(solution)/shard_map/ppermute | solution.py:46
  35.5 0.8 %bring_windows.1 = (bf16[1792,896]{1,0:T(8,128)(2,1)S(1)}, bf16[8,2,2,448,128]{4,3,2,1,0:T(8,128)(2,1)S(1)}, f32[8,128]{1,0:T(8,128)S(1)}) custom-call(s32[8,256]{1,0:T(8,128)S(1)} %copy-done.1, s32[8]{0:T(128)S(1)} %copy-done.2, bf16[1792,896]{1,0:T(8,128)(2,1)} %refs_2_.1, bf16[16,2,448,128]{3,2,1,0:T(8,128)(2,1)} %bitcast.13), custom_call_target="tpu_custom_call" | custom-call | bytes 13762560 | tf_op jit(solution)/shard_map/bring_windows/pallas_call | solution.py:101
  36.3 0.0 collective-permute-done.6.refs_1_
  36.3 0.0 collective-permute-done.7.refs_2_
  36.4 0.3 collective-permute-done.8.refs_3_
  36.7 2.5 %collective-permute-done.9.refs_4_ = f32[8,1792]{1,0:T(8,128)S(1)} collective-permute-done((f32[8,1792]{1,0:T(8,128)S(1)}, f32[8,1792]{1,0:T(8,128)S(1)}, u32[]{:S(2)}, u32[]{:S(2)}) %collective-permute-start.9) | collective-permute-done | bytes 57376 | tf_op jit(solution)/shard_map/ppermute | solution.py:46
  39.2 0.8 %collective-permute-start.10 = (bf16[8,512]{1,0:T(8,128)(2,1)S(1)}, bf16[8,512]{1,0:T(8,128)(2,1)S(1)}, u32[]{:S(2)}, u32[]{:S(2)}) collective-permute-start(bf16[8,512]{1,0:T(8,128)(2,1)S(1)} %get-tuple-element.122.refs_1_.refs_0_), channel_id=1, source_target_pairs={{0,16},{4,20},{8,24},{12,28},{16,32},{20,36},{24,40},{28,44},{32,4... | collective-permute-start | bytes 24584 | tf_op jit(solution)/shard_map/ppermute | solution.py:32
  40.0 2.5 %collective-permute-start.11 = (bf16[8,512]{1,0:T(8,128)(2,1)S(1)}, bf16[8,512]{1,0:T(8,128)(2,1)S(1)}, u32[]{:S(2)}, u32[]{:S(2)}) collective-permute-start(bf16[8,512]{1,0:T(8,128)(2,1)S(1)} %get-tuple-element.122.refs_1_.refs_0_), channel_id=1, source_target_pairs={{0,112},{4,116},{8,120},{12,124},{16,0},{20,4},{24,8},{28,12},{32,... | collective-permute-start | bytes 24584 | tf_op jit(solution)/shard_map/ppermute | solution.py:32
  42.4 0.0 collective-permute-start.12
  42.5 0.7 %own_attention.1 = (f32[8,448]{1,0:T(8,128)S(1)}, f32[8,448]{1,0:T(8,128)S(1)}, f32[8,448]{1,0:T(8,128)S(1)}) custom-call(s32[8]{0:T(128)S(1)} %copy-done.2, bf16[8,512]{1,0:T(8,128)(2,1)S(1)} %get-tuple-element.122.refs_1_.refs_0_, bf16[8,448]{1,0:T(8,128)(2,1)S(1)} %get-tuple-element.116.refs_2_, bf16[8,448]{1,0:T(8,128)(2,1)S(1)} %get-tuple-element.117.refs_3_, ...), custom_call_target="tpu_custom_call" | custom-call | tf_op jit(solution)/shard_map/own_attention/pallas_call | solution.py:101
  43.2 0.9 %collective-permute-done.10.refs_1_ = bf16[8,512]{1,0:T(8,128)(2,1)S(1)} collective-permute-done((bf16[8,512]{1,0:T(8,128)(2,1)S(1)}, bf16[8,512]{1,0:T(8,128)(2,1)S(1)}, u32[]{:S(2)}, u32[]{:S(2)}) %collective-permute-start.10) | collective-permute-done | bytes 8224 | tf_op jit(solution)/shard_map/ppermute | solution.py:32
  44.1 4.1 %collective-permute-done.12.refs_3_ = bf16[8,512]{1,0:T(8,128)(2,1)S(1)} collective-permute-done((bf16[8,512]{1,0:T(8,128)(2,1)S(1)}, bf16[8,512]{1,0:T(8,128)(2,1)S(1)}, u32[]{:S(2)}, u32[]{:S(2)}) %collective-permute-start.12) | collective-permute-done | bytes 8224 | tf_op jit(solution)/shard_map/ppermute | solution.py:32
  48.2 0.0 collective-permute-done.13.refs_5_
  48.2 2.0 %collective-permute-start.15 = (f32[8,640]{1,0:T(8,128)S(1)}, f32[8,640]{1,0:T(8,128)S(1)}, u32[]{:S(2)}, u32[]{:S(2)}) collective-permute-start(f32[8,640]{1,0:T(8,128)S(1)} %get-tuple-element.134), channel_id=1, source_target_pairs={{0,16},{4,20},{8,24},{12,28},{16,32},{20,36},{24,40},{28,44},{32,4... | collective-permute-start | bytes 61448 | tf_op jit(solution)/shard_map/ppermute | solution.py:32
  50.2 0.7 %collective-permute-start.16 = (f32[8,640]{1,0:T(8,128)S(1)}, f32[8,640]{1,0:T(8,128)S(1)}, u32[]{:S(2)}, u32[]{:S(2)}) collective-permute-start(f32[8,640]{1,0:T(8,128)S(1)} %get-tuple-element.135), channel_id=1, source_target_pairs={{0,96},{4,100},{8,104},{12,108},{16,112},{20,116},{24,120},{28,124... | collective-permute-start | bytes 61448 | tf_op jit(solution)/shard_map/ppermute | solution.py:32
  50.9 0.2 collective-permute-start.17
  51.1 1.0 %collective-permute-done.17 = bf16[8,448]{1,0:T(8,128)(2,1)S(1)} collective-permute-done((bf16[8,448]{1,0:T(8,128)(2,1)S(1)}, bf16[8,448]{1,0:T(8,128)(2,1)S(1)}, u32[]{:S(2)}, u32[]{:S(2)}) %collective-permute-start.17) | collective-permute-done | bytes 7200 | tf_op jit(solution)/shard_map/ppermute | solution.py:664
  52.1 0.0 collective-permute-done.14.refs_4_
  52.1 1.2 %collective-permute-done.15.refs_5_ = f32[8,640]{1,0:T(8,128)S(1)} collective-permute-done((f32[8,640]{1,0:T(8,128)S(1)}, f32[8,640]{1,0:T(8,128)S(1)}, u32[]{:S(2)}, u32[]{:S(2)}) %collective-permute-start.15) | collective-permute-done | bytes 20512 | tf_op jit(solution)/shard_map/ppermute | solution.py:32
  53.3 1.7 %collective-permute-done.16.refs_6_ = f32[8,640]{1,0:T(8,128)S(1)} collective-permute-done((f32[8,640]{1,0:T(8,128)S(1)}, f32[8,640]{1,0:T(8,128)S(1)}, u32[]{:S(2)}, u32[]{:S(2)}) %collective-permute-start.16) | collective-permute-done | bytes 20512 | tf_op jit(solution)/shard_map/ppermute | solution.py:32
  55.0 1.2 %collective-permute-start.20 = (f32[8,448]{1,0:T(8,128)S(1)}, f32[8,448]{1,0:T(8,128)S(1)}, u32[]{:S(2)}, u32[]{:S(2)}) collective-permute-start(f32[8,448]{1,0:T(8,128)S(1)} %get-tuple-element.148), channel_id=1, source_target_pairs={{0,2},{1,3},{2,0},{3,1},{4,6},{5,7},{6,4},{7,5},{8,10},{9,11},{10,... | collective-permute-start | bytes 43016 | tf_op jit(solution)/shard_map/ppermute | solution.py:28
  56.2 2.5 %collective-permute-start.19 = (f32[8,448]{1,0:T(8,128)S(1)}, f32[8,448]{1,0:T(8,128)S(1)}, u32[]{:S(2)}, u32[]{:S(2)}) collective-permute-start(f32[8,448]{1,0:T(8,128)S(1)} %get-tuple-element.147), channel_id=1, source_target_pairs={{0,3},{1,0},{2,1},{3,2},{4,7},{5,4},{6,5},{7,6},{8,11},{9,8},{10,9... | collective-permute-start | bytes 43016 | tf_op jit(solution)/shard_map/ppermute | solution.py:28
  58.8 0.0 collective-permute-start.18
  58.8 1.6 %collective-permute-done.20 = f32[8,448]{1,0:T(8,128)S(1)} collective-permute-done((f32[8,448]{1,0:T(8,128)S(1)}, f32[8,448]{1,0:T(8,128)S(1)}, u32[]{:S(2)}, u32[]{:S(2)}) %collective-permute-start.20) | collective-permute-done | bytes 14368 | tf_op jit(solution)/shard_map/ppermute | solution.py:28
  60.4 3.3 %collective-permute-done.18 = f32[8,448]{1,0:T(8,128)S(1)} collective-permute-done((f32[8,448]{1,0:T(8,128)S(1)}, f32[8,448]{1,0:T(8,128)S(1)}, u32[]{:S(2)}, u32[]{:S(2)}) %collective-permute-start.18) | collective-permute-done | bytes 14368 | tf_op jit(solution)/shard_map/ppermute | solution.py:28
  63.7 0.6 fusion.1
  (12 shorter events, 0.1 us)
Async XLA Ops:
  1.1 15.9 %collective-permute-start = (bf16[448,128]{1,0:T(8,128)(2,1)S(1)}, bf16[448,128]{1,0:T(8,128)(2,1)S(1)}, u32[]{:S(2)}, u32[]{:S(2)}) collective-permute-start(bf16[448,128]{1,0:T(8,128)(2,1)S(1)} %window_page.1), channel_id=1, source_target_pairs={{0,64},{4,68},{8,72},{12,76},{16,80},{20,84},{24,88},{28,92},{32,9... | collective-permute-start | bytes 344072 | tf_op jit(solution)/shard_map/ppermute | solution.py:32
  8.3 5.2 %collective-permute-start.1 = (bf16[8,448]{1,0:T(8,128)(2,1)}, bf16[8,448]{1,0:T(8,128)(2,1)S(1)}, u32[]{:S(2)}, u32[]{:S(2)}) collective-permute-start(bf16[8,448]{1,0:T(8,128)(2,1)} %refs_0_.3), channel_id=1, source_target_pairs={{0,1},{1,2},{2,3},{3,0},{4,5},{5,6},{6,7},{7,4},{8,9},{9,10},{10,1... | collective-permute-start | bytes 21512 | tf_op jit(solution)/shard_map/ppermute | solution.py:28
  9.9 3.9 %collective-permute-start.2 = (bf16[8,448]{1,0:T(8,128)(2,1)}, bf16[8,448]{1,0:T(8,128)(2,1)S(1)}, u32[]{:S(2)}, u32[]{:S(2)}) collective-permute-start(bf16[8,448]{1,0:T(8,128)(2,1)} %refs_0_.3), channel_id=1, source_target_pairs={{0,3},{1,0},{2,1},{3,2},{4,7},{5,4},{6,5},{7,6},{8,11},{9,8},{10,9... | collective-permute-start | bytes 21512 | tf_op jit(solution)/shard_map/ppermute | solution.py:28
  11.6 5.4 %collective-permute-start.3 = (bf16[8,448]{1,0:T(8,128)(2,1)}, bf16[8,448]{1,0:T(8,128)(2,1)S(1)}, u32[]{:S(2)}, u32[]{:S(2)}) collective-permute-start(bf16[8,448]{1,0:T(8,128)(2,1)} %refs_0_.3), channel_id=1, source_target_pairs={{0,2},{1,3},{2,0},{3,1},{4,6},{5,7},{6,4},{7,5},{8,10},{9,11},{10,... | collective-permute-start | bytes 21512 | tf_op jit(solution)/shard_map/ppermute | solution.py:28
  17.0 6.4 %copy-start = (bf16[8,448]{1,0:T(8,128)(2,1)S(1)}, bf16[8,448]{1,0:T(8,128)(2,1)}, u32[]{:S(2)}) copy-start(bf16[8,448]{1,0:T(8,128)(2,1)} %refs_0_.3) | copy-start | bytes 21508
  17.0 6.1 %collective-permute-start.4 = (bf16[448,128]{1,0:T(8,128)(2,1)S(1)}, bf16[448,128]{1,0:T(8,128)(2,1)S(1)}, u32[]{:S(2)}, u32[]{:S(2)}) collective-permute-start(bf16[448,128]{1,0:T(8,128)(2,1)S(1)} %broadcast_select_fusion), channel_id=1, source_target_pairs={{0,4},{4,0},{8,12},{12,8},{16,20},{20,16},{24,28},{28,24},{32,36},... | collective-permute-start | bytes 344072 | tf_op jit(solution)/shard_map/ppermute | solution.py:40
  23.1 12.4 %copy-start.1 = (s32[8,256]{1,0:T(8,128)S(1)}, s32[8,256]{1,0:T(8,128)}, u32[]{:S(2)}) copy-start(s32[8,256]{1,0:T(8,128)} %refs_0_.4) | copy-start | bytes 24580
  23.1 12.4 %copy-start.2 = (s32[8]{0:T(128)S(1)}, s32[8]{0:T(128)}, u32[]{:S(2)}) copy-start(s32[8]{0:T(128)} %refs_0_.5) | copy-start | bytes 100
  23.1 7.6 %collective-permute-start.5 = (bf16[2,448,128]{2,1,0:T(8,128)(2,1)S(1)}, bf16[2,448,128]{2,1,0:T(8,128)(2,1)S(1)}, u32[]{:S(2)}, u32[]{:S(2)}) collective-permute-start(bf16[2,448,128]{2,1,0:T(8,128)(2,1)S(1)} %pad_maximum_fusion.1), channel_id=1, source_target_pairs={{0,8},{4,12},{8,0},{12,4},{16,24},{20,28},{24,16},{28,20},{32,40},... | collective-permute-start | bytes 688136 | tf_op jit(solution)/shard_map/ppermute | solution.py:40
  30.8 17.4 %collective-permute-start.13 = (bf16[4,448,128]{2,1,0:T(8,128)(2,1)S(1)}, bf16[4,448,128]{2,1,0:T(8,128)(2,1)S(1)}, u32[]{:S(2)}, u32[]{:S(2)}) collective-permute-start(bf16[4,448,128]{2,1,0:T(8,128)(2,1)S(1)} %pad_maximum_fusion.refs_4_), channel_id=1, source_target_pairs={{0,128},{128,0},{1,129},{129,1},{2,130},{130,2},{3,131},{131,3},{4... | collective-permute-start | bytes 1376264 | tf_op jit(solution)/shard_map/ppermute | solution.py:648
  30.9 5.5 %collective-permute-start.6 = (f32[8,1792]{1,0:T(8,128)S(1)}, f32[8,1792]{1,0:T(8,128)S(1)}, u32[]{:S(2)}, u32[]{:S(2)}) collective-permute-start(f32[8,1792]{1,0:T(8,128)S(1)} %linear_layer.1), channel_id=1, source_target_pairs={{0,128},{1,129},{2,130},{3,131},{128,0},{129,1},{130,2},{131,3},{4... | collective-permute-start | bytes 172040 | tf_op jit(solution)/shard_map/ppermute | solution.py:46
  31.4 5.0 %collective-permute-start.7 = (f32[8,1792]{1,0:T(8,128)S(1)}, f32[8,1792]{1,0:T(8,128)S(1)}, u32[]{:S(2)}, u32[]{:S(2)}) collective-permute-start(f32[8,1792]{1,0:T(8,128)S(1)} %linear_layer.1), channel_id=1, source_target_pairs={{0,129},{1,130},{2,131},{3,128},{129,0},{130,1},{131,2},{128,3},{4... | collective-permute-start | bytes 172040 | tf_op jit(solution)/shard_map/ppermute | solution.py:46
  31.5 5.2 %collective-permute-start.8 = (f32[8,1792]{1,0:T(8,128)S(1)}, f32[8,1792]{1,0:T(8,128)S(1)}, u32[]{:S(2)}, u32[]{:S(2)}) collective-permute-start(f32[8,1792]{1,0:T(8,128)S(1)} %linear_layer.1), channel_id=1, source_target_pairs={{0,131},{1,128},{2,129},{3,130},{131,0},{128,1},{129,2},{130,3},{4... | collective-permute-start | bytes 172040 | tf_op jit(solution)/shard_map/ppermute | solution.py:46
  33.7 5.6 %collective-permute-start.9 = (f32[8,1792]{1,0:T(8,128)S(1)}, f32[8,1792]{1,0:T(8,128)S(1)}, u32[]{:S(2)}, u32[]{:S(2)}) collective-permute-start(f32[8,1792]{1,0:T(8,128)S(1)} %linear_layer.1), channel_id=1, source_target_pairs={{0,130},{1,131},{2,128},{3,129},{130,0},{131,1},{128,2},{129,3},{4... | collective-permute-start | bytes 172040 | tf_op jit(solution)/shard_map/ppermute | solution.py:46
  39.2 4.9 %collective-permute-start.10 = (bf16[8,512]{1,0:T(8,128)(2,1)S(1)}, bf16[8,512]{1,0:T(8,128)(2,1)S(1)}, u32[]{:S(2)}, u32[]{:S(2)}) collective-permute-start(bf16[8,512]{1,0:T(8,128)(2,1)S(1)} %get-tuple-element.122.refs_1_.refs_0_), channel_id=1, source_target_pairs={{0,16},{4,20},{8,24},{12,28},{16,32},{20,36},{24,40},{28,44},{32,4... | collective-permute-start | bytes 24584 | tf_op jit(solution)/shard_map/ppermute | solution.py:32
  40.0 4.1 %collective-permute-start.11 = (bf16[8,512]{1,0:T(8,128)(2,1)S(1)}, bf16[8,512]{1,0:T(8,128)(2,1)S(1)}, u32[]{:S(2)}, u32[]{:S(2)}) collective-permute-start(bf16[8,512]{1,0:T(8,128)(2,1)S(1)} %get-tuple-element.122.refs_1_.refs_0_), channel_id=1, source_target_pairs={{0,112},{4,116},{8,120},{12,124},{16,0},{20,4},{24,8},{28,12},{32,... | collective-permute-start | bytes 24584 | tf_op jit(solution)/shard_map/ppermute | solution.py:32
  42.4 5.8 %collective-permute-start.12 = (bf16[8,512]{1,0:T(8,128)(2,1)S(1)}, bf16[8,512]{1,0:T(8,128)(2,1)S(1)}, u32[]{:S(2)}, u32[]{:S(2)}) collective-permute-start(bf16[8,512]{1,0:T(8,128)(2,1)S(1)} %get-tuple-element.122.refs_1_.refs_0_), channel_id=1, source_target_pairs={{0,32},{4,36},{8,40},{12,44},{16,48},{20,52},{24,56},{28,60},{32,6... | collective-permute-start | bytes 24584 | tf_op jit(solution)/shard_map/ppermute | solution.py:32
  48.2 3.9 %collective-permute-start.14 = (f32[8,640]{1,0:T(8,128)S(1)}, f32[8,640]{1,0:T(8,128)S(1)}, u32[]{:S(2)}, u32[]{:S(2)}) collective-permute-start(f32[8,640]{1,0:T(8,128)S(1)} %get-tuple-element.133), channel_id=1, source_target_pairs={{0,112},{4,116},{8,120},{12,124},{16,0},{20,4},{24,8},{28,12},{32,... | collective-permute-start | bytes 61448 | tf_op jit(solution)/shard_map/ppermute | solution.py:32
  48.2 5.1 %collective-permute-start.15 = (f32[8,640]{1,0:T(8,128)S(1)}, f32[8,640]{1,0:T(8,128)S(1)}, u32[]{:S(2)}, u32[]{:S(2)}) collective-permute-start(f32[8,640]{1,0:T(8,128)S(1)} %get-tuple-element.134), channel_id=1, source_target_pairs={{0,16},{4,20},{8,24},{12,28},{16,32},{20,36},{24,40},{28,44},{32,4... | collective-permute-start | bytes 61448 | tf_op jit(solution)/shard_map/ppermute | solution.py:32
  50.2 4.7 %collective-permute-start.16 = (f32[8,640]{1,0:T(8,128)S(1)}, f32[8,640]{1,0:T(8,128)S(1)}, u32[]{:S(2)}, u32[]{:S(2)}) collective-permute-start(f32[8,640]{1,0:T(8,128)S(1)} %get-tuple-element.135), channel_id=1, source_target_pairs={{0,96},{4,100},{8,104},{12,108},{16,112},{20,116},{24,120},{28,124... | collective-permute-start | bytes 61448 | tf_op jit(solution)/shard_map/ppermute | solution.py:32
  50.9 1.2 %collective-permute-start.17 = (bf16[8,448]{1,0:T(8,128)(2,1)S(1)}, bf16[8,448]{1,0:T(8,128)(2,1)S(1)}, u32[]{:S(2)}, u32[]{:S(2)}) collective-permute-start(bf16[8,448]{1,0:T(8,128)(2,1)S(1)} %get-tuple-element.136), channel_id=1, source_target_pairs={{128,0},{0,128},{129,1},{1,129},{130,2},{2,130},{131,3},{3,131},{1... | collective-permute-start | bytes 21512 | tf_op jit(solution)/shard_map/ppermute | solution.py:664
  55.0 5.4 %collective-permute-start.20 = (f32[8,448]{1,0:T(8,128)S(1)}, f32[8,448]{1,0:T(8,128)S(1)}, u32[]{:S(2)}, u32[]{:S(2)}) collective-permute-start(f32[8,448]{1,0:T(8,128)S(1)} %get-tuple-element.148), channel_id=1, source_target_pairs={{0,2},{1,3},{2,0},{3,1},{4,6},{5,7},{6,4},{7,5},{8,10},{9,11},{10,... | collective-permute-start | bytes 43016 | tf_op jit(solution)/shard_map/ppermute | solution.py:28
  56.2 4.2 %collective-permute-start.19 = (f32[8,448]{1,0:T(8,128)S(1)}, f32[8,448]{1,0:T(8,128)S(1)}, u32[]{:S(2)}, u32[]{:S(2)}) collective-permute-start(f32[8,448]{1,0:T(8,128)S(1)} %get-tuple-element.147), channel_id=1, source_target_pairs={{0,3},{1,0},{2,1},{3,2},{4,7},{5,4},{6,5},{7,6},{8,11},{9,8},{10,9... | collective-permute-start | bytes 43016 | tf_op jit(solution)/shard_map/ppermute | solution.py:28
  58.8 4.9 %collective-permute-start.18 = (f32[8,448]{1,0:T(8,128)S(1)}, f32[8,448]{1,0:T(8,128)S(1)}, u32[]{:S(2)}, u32[]{:S(2)}) collective-permute-start(f32[8,448]{1,0:T(8,128)S(1)} %get-tuple-element.146), channel_id=1, source_target_pairs={{0,1},{1,2},{2,3},{3,0},{4,5},{5,6},{6,7},{7,4},{8,9},{9,10},{10,1... | collective-permute-start | bytes 43016 | tf_op jit(solution)/shard_map/ppermute | solution.py:28

commit v9 on v7

--- a/solution.py
+++ b/solution.py
@@ -36,8 +36,12 @@
     )
 
 
-def x_swap(value, flip):
-    return lax.ppermute(value, "req", [(i, i ^ flip) for i in range(XN * ZN)])
+def x_shift(value, steps):
+    return lax.ppermute(
+        value,
+        "req",
+        [(z * XN + i, z * XN + (i + steps) % XN) for z in range(ZN) for i in range(XN)],
+    )
 
 
 def far_swap(value):
@@ -412,7 +416,7 @@
     z, x = ids[1] // XN, ids[1] % XN
     slot = token >> 7
     slot_group = jnp.where(slot < XN, z, (z + ZN // 2) & (ZN - 1)) * XN
-    slot_group = slot_group + (x ^ (slot & (XN - 1)))
+    slot_group = slot_group + ((slot + x + XN - 1) & (XN - 1))
     offset = token & (PAGE - 1)
     usable = (slot_group == group) & (offset < HALF) & (offset + HALF >= start)
     lane = lanes_of((count, share))
@@ -642,15 +646,14 @@
     }
 
     page = window_page(pages_first)
-    other = x_swap(page, 1)
-    received = [head_shift(tokens, k) for k in (1, 3, 2)]
-    other, received = lax.optimization_barrier((other, received))
-    stored, two_pages = lax.optimization_barrier((stored, jnp.stack([page, other])))
-    near = bring_near(stored)
+    row_pages = [x_shift(page, k) for k in (1, 3, 2)]
+    row_pages[0], last_tokens = lax.optimization_barrier((row_pages[0], tokens))
+    received = [head_shift(tokens, 1), head_shift(tokens, 3), head_shift(last_tokens, 2)]
+    near, received = lax.optimization_barrier((bring_near(stored), received))
+    near_pages = jnp.stack([row_pages[0], page, row_pages[1], row_pages[2]])
+    near_pages, received = lax.optimization_barrier((near_pages, received))
+    far_pages = far_swap(near_pages)
     update = linear_layer([tokens] + received, near)
-    next_pages, update = lax.optimization_barrier((x_swap(two_pages, 2), update))
-    near_pages = jnp.concatenate([two_pages, next_pages])
-    far_pages = far_swap(near_pages)
     own_pages = own_pages.transpose(0, 1, 3, 2)
     query_key_w, own_pages, table, ends, update = lax.optimization_barrier(
         (query_key_w, own_pages, page_table, lengths, update)

time: 55.9 us -> 55.2 us (0.987)
  waiting for transfers between devices: 11.6 us -> 10 us
    ppermute x2 -> x3, waiting for transfers between devices: 2.17 us -> 0.01 us  [x_shift(): lax.ppermute(value, 'req', [(z * XN + i, z * XN + (i + steps) % XN) for z...]
    ppermute x6, waiting for transfers between devices: 2.71 us -> 3.86 us  [z_shift(): lax.ppermute(value, 'req', [(z * XN + i, (z + steps) % ZN * XN + i) for z...]
    ppermute x2 -> x3, starting transfers between devices: 4.66 us -> 5.12 us  [x_shift(): lax.ppermute(value, 'req', [(z * XN + i, z * XN + (i + steps) % XN) for z...]
  transfers between devices with their start and end apart: 20 -> 21, of which waited for: 9 -> 7; matrix products, arithmetic and copies ran while one was open for 0% -> 0% of each run, Pallas kernels for 16% -> 16%
where the time goes in v9:
time: 55.2 us; the launch traced here: 54.5 us
  starting transfers between devices  32.1 us (58%)
  Pallas kernels  11.4 us (21%)
  waiting for transfers between devices  10 us (18%)
  other arithmetic  0.67 us (1%)
    pallas_call x8, Pallas kernels, kernel_call(): pl.pallas_call(run, out_shape=out_shape, in_specs=in_specs, out_specs=jax...  11.4 us
    ppermute x1, starting transfers between devices, far_swap(): lax.ppermute(value, ('section', 'req'), [(count + i, count + (i + count /...  8.94 us
    ppermute x6, starting transfers between devices, head_shift(): lax.ppermute(value, 'head', [(i, (i + steps) % count) for i in range(coun...  8.26 us
    ppermute x6, waiting for transfers between devices, head_shift(): lax.ppermute(value, 'head', [(i, (i + steps) % count) for i in range(coun...  5.33 us
    ppermute x6, starting transfers between devices, z_shift(): lax.ppermute(value, 'req', [(z * XN + i, (z + steps) % ZN * XN + i) for z...  5.24 us
    ppermute x3, starting transfers between devices, x_shift(): lax.ppermute(value, 'req', [(z * XN + i, z * XN + (i + steps) % XN) for z...  5.12 us
    ppermute x4, starting transfers between devices, section_swap(): lax.ppermute(value, ('section', 'head'), there + [(b, a) for a, b in there])  4.01 us
    ppermute x6, waiting for transfers between devices, z_shift(): lax.ppermute(value, 'req', [(z * XN + i, (z + steps) % ZN * XN + i) for z...  3.86 us
  transfers between devices with their start and end apart: 21, of which 7 were waited for; matrix products, arithmetic and copies ran while one was open for 0% of the time, Pallas kernels for 16%

profile of v9, /device:TPU:1, one launch (start us, length us, event | category | flops | bytes accessed | tf_op | source)
XLA Modules:
  0.0 54.5 jit_solution(5999545602022774230)
XLA Ops:
  0.0 1.0 %window_page.1 = bf16[448,128]{1,0:T(8,128)(2,1)S(1)} custom-call(bf16[1,2,448,128]{3,2,1,0:T(8,128)(2,1)} %bitcast.20), custom_call_target="tpu_custom_call" | custom-call | bytes 16777216 | tf_op jit(solution)/shard_map/window_page/pallas_call | solution.py:114
  1.1 2.1 %collective-permute-start = (bf16[448,128]{1,0:T(8,128)(2,1)S(1)}, bf16[448,128]{1,0:T(8,128)(2,1)S(1)}, u32[]{:S(2)}, u32[]{:S(2)}) collective-permute-start(bf16[448,128]{1,0:T(8,128)(2,1)S(1)} %window_page.1), channel_id=1, source_target_pairs={{0,4},{4,8},{8,12},{12,0},{16,20},{20,24},{24,28},{28,16},{32,36},... | collective-permute-start | bytes 344072 | tf_op jit(solution)/shard_map/ppermute | solution.py:40
  3.2 1.4 %collective-permute-start.1 = (bf16[448,128]{1,0:T(8,128)(2,1)S(1)}, bf16[448,128]{1,0:T(8,128)(2,1)S(1)}, u32[]{:S(2)}, u32[]{:S(2)}) collective-permute-start(bf16[448,128]{1,0:T(8,128)(2,1)S(1)} %window_page.1), channel_id=1, source_target_pairs={{0,12},{4,0},{8,4},{12,8},{16,28},{20,16},{24,20},{28,24},{32,44},... | collective-permute-start | bytes 344072 | tf_op jit(solution)/shard_map/ppermute | solution.py:40
  4.5 1.6 %collective-permute-start.2 = (bf16[448,128]{1,0:T(8,128)(2,1)S(1)}, bf16[448,128]{1,0:T(8,128)(2,1)S(1)}, u32[]{:S(2)}, u32[]{:S(2)}) collective-permute-start(bf16[448,128]{1,0:T(8,128)(2,1)S(1)} %window_page.1), channel_id=1, source_target_pairs={{0,8},{4,12},{8,0},{12,4},{16,24},{20,28},{24,16},{28,20},{32,40},... | collective-permute-start | bytes 344072 | tf_op jit(solution)/shard_map/ppermute | solution.py:40
  6.2 1.3 %collective-permute-start.3 = (bf16[8,448]{1,0:T(8,128)(2,1)}, bf16[8,448]{1,0:T(8,128)(2,1)S(1)}, u32[]{:S(2)}, u32[]{:S(2)}) collective-permute-start(bf16[8,448]{1,0:T(8,128)(2,1)} %refs_0_.4), channel_id=1, source_target_pairs={{0,1},{1,2},{2,3},{3,0},{4,5},{5,6},{6,7},{7,4},{8,9},{9,10},{10,1... | collective-permute-start | bytes 21512 | tf_op jit(solution)/shard_map/ppermute | solution.py:28
  7.5 1.4 %collective-permute-start.4 = (bf16[8,448]{1,0:T(8,128)(2,1)}, bf16[8,448]{1,0:T(8,128)(2,1)S(1)}, u32[]{:S(2)}, u32[]{:S(2)}) collective-permute-start(bf16[8,448]{1,0:T(8,128)(2,1)} %refs_0_.4), channel_id=1, source_target_pairs={{0,3},{1,0},{2,1},{3,2},{4,7},{5,4},{6,5},{7,6},{8,11},{9,8},{10,9... | collective-permute-start | bytes 21512 | tf_op jit(solution)/shard_map/ppermute | solution.py:28
  8.9 2.0 %bring_near.1 = (f32[1,1792]{1,0:T(1,128)S(1)}, bf16[1792,128]{1,0:T(8,128)(2,1)S(1)}, bf16[8736,112]{1,0:T(8,128)(2,1)S(1)}, f32[8,4,273]{2,1,0:T(4,128)S(1)}, ...) custom-call(f32[1,1792]{1,0:T(1,128)} %refs_0_.3, ...), custom_call_target="tpu_custom_call" | custom-call | bytes 11377408 | tf_op jit(solution)/shard_map/bring_near/pallas_call | solution.py:114
  10.9 0.0 collective-permute-done
  10.9 1.7 %collective-permute-start.5 = (bf16[8,448]{1,0:T(8,128)(2,1)S(1)}, bf16[8,448]{1,0:T(8,128)(2,1)S(1)}, u32[]{:S(2)}, u32[]{:S(2)}) collective-permute-start(bf16[8,448]{1,0:T(8,128)(2,1)S(1)} %copy-done), channel_id=1, source_target_pairs={{0,2},{1,3},{2,0},{3,1},{4,6},{5,7},{6,4},{7,5},{8,10},{9,11},{10,... | collective-permute-start | bytes 21512 | tf_op jit(solution)/shard_map/ppermute | solution.py:28
  12.7 0.0 collective-permute-done.1
  12.7 0.0 collective-permute-done.2
  12.7 0.1 pad_maximum_fusion.refs_4_
  12.7 0.0 collective-permute-done.3.refs_1_
  12.8 0.0 collective-permute-done.4.refs_2_
  12.8 2.3 %collective-permute-done.5.refs_3_ = bf16[8,448]{1,0:T(8,128)(2,1)S(1)} collective-permute-done((bf16[8,448]{1,0:T(8,128)(2,1)S(1)}, bf16[8,448]{1,0:T(8,128)(2,1)S(1)}, u32[]{:S(2)}, u32[]{:S(2)}) %collective-permute-start.5) | collective-permute-done | bytes 7200 | tf_op jit(solution)/shard_map/ppermute | solution.py:28
  15.0 8.9 %collective-permute-start.13 = (bf16[4,448,128]{2,1,0:T(8,128)(2,1)S(1)}, bf16[4,448,128]{2,1,0:T(8,128)(2,1)S(1)}, u32[]{:S(2)}, u32[]{:S(2)}) collective-permute-start(bf16[4,448,128]{2,1,0:T(8,128)(2,1)S(1)} %pad_maximum_fusion.refs_4_), channel_id=1, source_target_pairs={{128,192},{132,196},{136,200},{140,204},{144,208},{148,212},{152,2... | collective-permute-start | bytes 1376264 | tf_op jit(solution)/shard_map/ppermute | solution.py:49
  24.0 0.1 collective-permute-start.6
  24.1 1.8 %collective-permute-start.7 = (f32[8,1792]{1,0:T(8,128)S(1)}, f32[8,1792]{1,0:T(8,128)S(1)}, u32[]{:S(2)}, u32[]{:S(2)}) collective-permute-start(f32[8,1792]{1,0:T(8,128)S(1)} %linear_layer.1), channel_id=1, source_target_pairs={{0,129},{1,130},{2,131},{3,128},{129,0},{130,1},{131,2},{128,3},{4... | collective-permute-start | bytes 172040 | tf_op jit(solution)/shard_map/ppermute | solution.py:59
  26.0 0.0 collective-permute-start.8
  26.0 2.1 %collective-permute-start.9 = (f32[8,1792]{1,0:T(8,128)S(1)}, f32[8,1792]{1,0:T(8,128)S(1)}, u32[]{:S(2)}, u32[]{:S(2)}) collective-permute-start(f32[8,1792]{1,0:T(8,128)S(1)} %linear_layer.1), channel_id=1, source_target_pairs={{0,130},{1,131},{2,128},{3,129},{130,0},{131,1},{128,2},{129,3},{4... | collective-permute-start | bytes 172040 | tf_op jit(solution)/shard_map/ppermute | solution.py:59
  28.0 3.9 %bring_windows.1 = (bf16[1792,896]{1,0:T(8,128)(2,1)S(1)}, bf16[8,2,2,448,128]{4,3,2,1,0:T(8,128)(2,1)S(1)}, f32[8,128]{1,0:T(8,128)S(1)}) custom-call(s32[8,256]{1,0:T(8,128)S(1)} %copy-done.1, s32[8]{0:T(128)S(1)} %copy-done.2, bf16[1792,896]{1,0:T(8,128)(2,1)} %refs_2_, bf16[16,2,448,128]{3,2,1,0:T(8,128)(2,1)} %bitcast.16), custom_call_target="tpu_custom_call" | custom-call | bytes 13762560 | tf_op jit(solution)/shard_map/bring_windows/pallas_call | solution.py:114
  32.0 0.0 collective-permute-done.6.refs_1_
  32.0 0.0 collective-permute-done.7.refs_2_
  32.0 0.0 collective-permute-done.8.refs_3_
  32.0 0.0 collective-permute-done.9.refs_4_
  32.0 1.1 %project.1 = (bf16[8,448]{1,0:T(8,128)(2,1)S(1)}, bf16[8,512]{1,0:T(8,128)(2,1)S(1)}, bf16[8,448]{1,0:T(8,128)(2,1)S(1)}, bf16[8,448]{1,0:T(8,128)(2,1)S(1)}) custom-call(f32[8,128]{1,0:T(8,128)S(1)} %get-tuple-element.98.refs_0_, f32[8,1792]{1,0:T(8,128)S(1)} %collective-permute-done.6.refs_1_, f32[8,1792]{1,0:T(8,128)S(1)} %collective-permute-done.7.refs_2_, ...), custom_call_target="tpu_custom_call" | custom-call | tf_op jit(solution)/shard_map/project/pallas_call | solution.py:114
  33.1 0.8 %collective-permute-start.10 = (bf16[8,512]{1,0:T(8,128)(2,1)S(1)}, bf16[8,512]{1,0:T(8,128)(2,1)S(1)}, u32[]{:S(2)}, u32[]{:S(2)}) collective-permute-start(bf16[8,512]{1,0:T(8,128)(2,1)S(1)} %get-tuple-element.108.refs_1_.refs_0_), channel_id=1, source_target_pairs={{0,16},{4,20},{8,24},{12,28},{16,32},{20,36},{24,40},{28,44},{32,4... | collective-permute-start | bytes 24584 | tf_op jit(solution)/shard_map/ppermute | solution.py:32
  33.9 1.9 %collective-permute-start.11 = (bf16[8,512]{1,0:T(8,128)(2,1)S(1)}, bf16[8,512]{1,0:T(8,128)(2,1)S(1)}, u32[]{:S(2)}, u32[]{:S(2)}) collective-permute-start(bf16[8,512]{1,0:T(8,128)(2,1)S(1)} %get-tuple-element.108.refs_1_.refs_0_), channel_id=1, source_target_pairs={{0,112},{4,116},{8,120},{12,124},{16,0},{20,4},{24,8},{28,12},{32,... | collective-permute-start | bytes 24584 | tf_op jit(solution)/shard_map/ppermute | solution.py:32
  35.8 0.0 collective-permute-start.12
  35.8 1.9 %own_attention.1 = (f32[8,448]{1,0:T(8,128)S(1)}, f32[8,448]{1,0:T(8,128)S(1)}, f32[8,448]{1,0:T(8,128)S(1)}) custom-call(s32[8]{0:T(128)S(1)} %copy-done.2, bf16[8,512]{1,0:T(8,128)(2,1)S(1)} %get-tuple-element.108.refs_1_.refs_0_, bf16[8,448]{1,0:T(8,128)(2,1)S(1)} %get-tuple-element.102.refs_2_, bf16[8,448]{1,0:T(8,128)(2,1)S(1)} %get-tuple-element.103.refs_3_, ...), custom_call_target="tpu_custom_call" | custom-call | tf_op jit(solution)/shard_map/own_attention/pallas_call | solution.py:114
  37.7 0.0 collective-permute-done.10.refs_1_
  37.8 2.7 %collective-permute-done.12.refs_3_ = bf16[8,512]{1,0:T(8,128)(2,1)S(1)} collective-permute-done((bf16[8,512]{1,0:T(8,128)(2,1)S(1)}, bf16[8,512]{1,0:T(8,128)(2,1)S(1)}, u32[]{:S(2)}, u32[]{:S(2)}) %collective-permute-start.12) | collective-permute-done | bytes 8224 | tf_op jit(solution)/shard_map/ppermute | solution.py:32
  40.4 0.9 %prompt_attention.1 = (f32[8,640]{1,0:T(8,128)S(1)}, f32[8,640]{1,0:T(8,128)S(1)}, f32[8,640]{1,0:T(8,128)S(1)}, f32[8,640]{1,0:T(8,128)S(1)}) custom-call(bf16[8,512]{1,0:T(8,128)(2,1)S(1)} %get-tuple-element.108.refs_1_.refs_0_, bf16[8,512]{1,0:T(8,128)(2,1)S(1)} %collective-permute-done.10.refs_1_, bf16[8,512]{1,0:T(8,128)(2,1)S(1)} %collective-permute-done.11.refs_2_, ...), custom_call_target="tpu_custom_call" | custom-call | tf_op jit(solution)/shard_map/prompt_attention/pallas_call | solution.py:114
  41.4 0.1 collective-permute-start.14
  41.5 1.4 %collective-permute-start.15 = (f32[8,640]{1,0:T(8,128)S(1)}, f32[8,640]{1,0:T(8,128)S(1)}, u32[]{:S(2)}, u32[]{:S(2)}) collective-permute-start(f32[8,640]{1,0:T(8,128)S(1)} %get-tuple-element.120), channel_id=1, source_target_pairs={{0,16},{4,20},{8,24},{12,28},{16,32},{20,36},{24,40},{28,44},{32,4... | collective-permute-start | bytes 61448 | tf_op jit(solution)/shard_map/ppermute | solution.py:32
  42.9 1.0 %collective-permute-start.16 = (f32[8,640]{1,0:T(8,128)S(1)}, f32[8,640]{1,0:T(8,128)S(1)}, u32[]{:S(2)}, u32[]{:S(2)}) collective-permute-start(f32[8,640]{1,0:T(8,128)S(1)} %get-tuple-element.121), channel_id=1, source_target_pairs={{0,96},{4,100},{8,104},{12,108},{16,112},{20,116},{24,120},{28,124... | collective-permute-start | bytes 61448 | tf_op jit(solution)/shard_map/ppermute | solution.py:32
  43.9 0.6 %collective-permute-start.17 = (bf16[8,448]{1,0:T(8,128)(2,1)S(1)}, bf16[8,448]{1,0:T(8,128)(2,1)S(1)}, u32[]{:S(2)}, u32[]{:S(2)}) collective-permute-start(bf16[8,448]{1,0:T(8,128)(2,1)S(1)} %get-tuple-element.122), channel_id=1, source_target_pairs={{128,0},{0,128},{129,1},{1,129},{130,2},{2,130},{131,3},{3,131},{1... | collective-permute-start | bytes 21512 | tf_op jit(solution)/shard_map/ppermute | solution.py:672
  44.4 0.8 %collective-permute-done.17 = bf16[8,448]{1,0:T(8,128)(2,1)S(1)} collective-permute-done((bf16[8,448]{1,0:T(8,128)(2,1)S(1)}, bf16[8,448]{1,0:T(8,128)(2,1)S(1)}, u32[]{:S(2)}, u32[]{:S(2)}) %collective-permute-start.17) | collective-permute-done | bytes 7200 | tf_op jit(solution)/shard_map/ppermute | solution.py:672
  45.3 0.1 collective-permute-done.15.refs_5_
  45.4 1.1 %collective-permute-done.16.refs_6_ = f32[8,640]{1,0:T(8,128)S(1)} collective-permute-done((f32[8,640]{1,0:T(8,128)S(1)}, f32[8,640]{1,0:T(8,128)S(1)}, u32[]{:S(2)}, u32[]{:S(2)}) %collective-permute-start.16) | collective-permute-done | bytes 20512 | tf_op jit(solution)/shard_map/ppermute | solution.py:32
  46.5 0.6 %combine.1 = (f32[8,448]{1,0:T(8,128)S(1)}, f32[8,448]{1,0:T(8,128)S(1)}, f32[8,448]{1,0:T(8,128)S(1)}, f32[8,448]{1,0:T(8,128)S(1)}) custom-call(f32[8,448]{1,0:T(8,128)S(1)} %get-tuple-element.124.refs_0_, f32[8,448]{1,0:T(8,128)S(1)} %get-tuple-element.125.refs_1_, f32[8,448]{1,0:T(8,128)S(1)} %get-tuple-element.126.refs_2_, ...), custom_call_target="tpu_custom_call" | custom-call | tf_op jit(solution)/shard_map/combine/pallas_call | solution.py:114
  47.0 1.0 %collective-permute-start.18 = (f32[8,448]{1,0:T(8,128)S(1)}, f32[8,448]{1,0:T(8,128)S(1)}, u32[]{:S(2)}, u32[]{:S(2)}) collective-permute-start(f32[8,448]{1,0:T(8,128)S(1)} %get-tuple-element.132), channel_id=1, source_target_pairs={{0,1},{1,2},{2,3},{3,0},{4,5},{5,6},{6,7},{7,4},{8,9},{9,10},{10,1... | collective-permute-start | bytes 43016 | tf_op jit(solution)/shard_map/ppermute | solution.py:28
  48.0 1.7 %collective-permute-start.19 = (f32[8,448]{1,0:T(8,128)S(1)}, f32[8,448]{1,0:T(8,128)S(1)}, u32[]{:S(2)}, u32[]{:S(2)}) collective-permute-start(f32[8,448]{1,0:T(8,128)S(1)} %get-tuple-element.133), channel_id=1, source_target_pairs={{0,3},{1,0},{2,1},{3,2},{4,7},{5,4},{6,5},{7,6},{8,11},{9,8},{10,9... | collective-permute-start | bytes 43016 | tf_op jit(solution)/shard_map/ppermute | solution.py:28
  49.8 1.0 %collective-permute-start.20 = (f32[8,448]{1,0:T(8,128)S(1)}, f32[8,448]{1,0:T(8,128)S(1)}, u32[]{:S(2)}, u32[]{:S(2)}) collective-permute-start(f32[8,448]{1,0:T(8,128)S(1)} %get-tuple-element.134), channel_id=1, source_target_pairs={{0,2},{1,3},{2,0},{3,1},{4,6},{5,7},{6,4},{7,5},{8,10},{9,11},{10,... | collective-permute-start | bytes 43016 | tf_op jit(solution)/shard_map/ppermute | solution.py:28
  50.8 0.1 collective-permute-done.18
  50.9 0.0 collective-permute-done.19
  50.9 3.0 %collective-permute-done.20 = f32[8,448]{1,0:T(8,128)S(1)} collective-permute-done((f32[8,448]{1,0:T(8,128)S(1)}, f32[8,448]{1,0:T(8,128)S(1)}, u32[]{:S(2)}, u32[]{:S(2)}) %collective-permute-start.20) | collective-permute-done | bytes 14368 | tf_op jit(solution)/shard_map/ppermute | solution.py:28
  53.9 0.6 %fusion.1 = bf16[1,8,448]{2,1,0:T(8,128)(2,1)} fusion(bf16[8,448]{1,0:T(8,128)(2,1)S(1)} %collective-permute-done.17, f32[8,448]{1,0:T(8,128)S(1)} %collective-permute-done.20, f32[8,448]{1,0:T(8,128)S(1)} %collective-permute-done.19, f32[8,448]{1,0:T(8,128)S(1)} %collective-permute-done.18, f32[8,448]{1,0:T(8,128)S(1)} %get-tuple-element.131, ...), kind=kLoop, calls=%fused_computation.3 | loop fusion | flops 25088 | bytes 78849 | tf_op jit(solution)/shard_map/broadcast_in_dim | solution.py:680
  (10 shorter events, 0.0 us)
Async XLA Ops:
  1.1 9.9 %collective-permute-start = (bf16[448,128]{1,0:T(8,128)(2,1)S(1)}, bf16[448,128]{1,0:T(8,128)(2,1)S(1)}, u32[]{:S(2)}, u32[]{:S(2)}) collective-permute-start(bf16[448,128]{1,0:T(8,128)(2,1)S(1)} %window_page.1), channel_id=1, source_target_pairs={{0,4},{4,8},{8,12},{12,0},{16,20},{20,24},{24,28},{28,16},{32,36},... | collective-permute-start | bytes 344072 | tf_op jit(solution)/shard_map/ppermute | solution.py:40
  3.2 9.5 %collective-permute-start.1 = (bf16[448,128]{1,0:T(8,128)(2,1)S(1)}, bf16[448,128]{1,0:T(8,128)(2,1)S(1)}, u32[]{:S(2)}, u32[]{:S(2)}) collective-permute-start(bf16[448,128]{1,0:T(8,128)(2,1)S(1)} %window_page.1), channel_id=1, source_target_pairs={{0,12},{4,0},{8,4},{12,8},{16,28},{20,16},{24,20},{28,24},{32,44},... | collective-permute-start | bytes 344072 | tf_op jit(solution)/shard_map/ppermute | solution.py:40
  4.5 8.1 %collective-permute-start.2 = (bf16[448,128]{1,0:T(8,128)(2,1)S(1)}, bf16[448,128]{1,0:T(8,128)(2,1)S(1)}, u32[]{:S(2)}, u32[]{:S(2)}) collective-permute-start(bf16[448,128]{1,0:T(8,128)(2,1)S(1)} %window_page.1), channel_id=1, source_target_pairs={{0,8},{4,12},{8,0},{12,4},{16,24},{20,28},{24,16},{28,20},{32,40},... | collective-permute-start | bytes 344072 | tf_op jit(solution)/shard_map/ppermute | solution.py:40
  6.2 6.6 %collective-permute-start.3 = (bf16[8,448]{1,0:T(8,128)(2,1)}, bf16[8,448]{1,0:T(8,128)(2,1)S(1)}, u32[]{:S(2)}, u32[]{:S(2)}) collective-permute-start(bf16[8,448]{1,0:T(8,128)(2,1)} %refs_0_.4), channel_id=1, source_target_pairs={{0,1},{1,2},{2,3},{3,0},{4,5},{5,6},{6,7},{7,4},{8,9},{9,10},{10,1... | collective-permute-start | bytes 21512 | tf_op jit(solution)/shard_map/ppermute | solution.py:28
  7.5 5.3 %collective-permute-start.4 = (bf16[8,448]{1,0:T(8,128)(2,1)}, bf16[8,448]{1,0:T(8,128)(2,1)S(1)}, u32[]{:S(2)}, u32[]{:S(2)}) collective-permute-start(bf16[8,448]{1,0:T(8,128)(2,1)} %refs_0_.4), channel_id=1, source_target_pairs={{0,3},{1,0},{2,1},{3,2},{4,7},{5,4},{6,5},{7,6},{8,11},{9,8},{10,9... | collective-permute-start | bytes 21512 | tf_op jit(solution)/shard_map/ppermute | solution.py:28
  8.9 2.0 %copy-start = (bf16[8,448]{1,0:T(8,128)(2,1)S(1)}, bf16[8,448]{1,0:T(8,128)(2,1)}, u32[]{:S(2)}) copy-start(bf16[8,448]{1,0:T(8,128)(2,1)} %refs_0_.4) | copy-start | bytes 21508
  10.9 4.1 %collective-permute-start.5 = (bf16[8,448]{1,0:T(8,128)(2,1)S(1)}, bf16[8,448]{1,0:T(8,128)(2,1)S(1)}, u32[]{:S(2)}, u32[]{:S(2)}) collective-permute-start(bf16[8,448]{1,0:T(8,128)(2,1)S(1)} %copy-done), channel_id=1, source_target_pairs={{0,2},{1,3},{2,0},{3,1},{4,6},{5,7},{6,4},{7,5},{8,10},{9,11},{10,... | collective-permute-start | bytes 21512 | tf_op jit(solution)/shard_map/ppermute | solution.py:28
  15.0 13.0 %copy-start.1 = (s32[8,256]{1,0:T(8,128)S(1)}, s32[8,256]{1,0:T(8,128)}, u32[]{:S(2)}) copy-start(s32[8,256]{1,0:T(8,128)} %refs_0_.5) | copy-start | bytes 24580
  15.0 13.0 %copy-start.2 = (s32[8]{0:T(128)S(1)}, s32[8]{0:T(128)}, u32[]{:S(2)}) copy-start(s32[8]{0:T(128)} %refs_0_.6) | copy-start | bytes 100
  15.0 25.4 %collective-permute-start.13 = (bf16[4,448,128]{2,1,0:T(8,128)(2,1)S(1)}, bf16[4,448,128]{2,1,0:T(8,128)(2,1)S(1)}, u32[]{:S(2)}, u32[]{:S(2)}) collective-permute-start(bf16[4,448,128]{2,1,0:T(8,128)(2,1)S(1)} %pad_maximum_fusion.refs_4_), channel_id=1, source_target_pairs={{128,192},{132,196},{136,200},{140,204},{144,208},{148,212},{152,2... | collective-permute-start | bytes 1376264 | tf_op jit(solution)/shard_map/ppermute | solution.py:49
  24.0 8.0 %collective-permute-start.6 = (f32[8,1792]{1,0:T(8,128)S(1)}, f32[8,1792]{1,0:T(8,128)S(1)}, u32[]{:S(2)}, u32[]{:S(2)}) collective-permute-start(f32[8,1792]{1,0:T(8,128)S(1)} %linear_layer.1), channel_id=1, source_target_pairs={{0,128},{1,129},{2,130},{3,131},{128,0},{129,1},{130,2},{131,3},{4... | collective-permute-start | bytes 172040 | tf_op jit(solution)/shard_map/ppermute | solution.py:59
  24.1 7.9 %collective-permute-start.7 = (f32[8,1792]{1,0:T(8,128)S(1)}, f32[8,1792]{1,0:T(8,128)S(1)}, u32[]{:S(2)}, u32[]{:S(2)}) collective-permute-start(f32[8,1792]{1,0:T(8,128)S(1)} %linear_layer.1), channel_id=1, source_target_pairs={{0,129},{1,130},{2,131},{3,128},{129,0},{130,1},{131,2},{128,3},{4... | collective-permute-start | bytes 172040 | tf_op jit(solution)/shard_map/ppermute | solution.py:59
  26.0 6.0 %collective-permute-start.8 = (f32[8,1792]{1,0:T(8,128)S(1)}, f32[8,1792]{1,0:T(8,128)S(1)}, u32[]{:S(2)}, u32[]{:S(2)}) collective-permute-start(f32[8,1792]{1,0:T(8,128)S(1)} %linear_layer.1), channel_id=1, source_target_pairs={{0,131},{1,128},{2,129},{3,130},{131,0},{128,1},{129,2},{130,3},{4... | collective-permute-start | bytes 172040 | tf_op jit(solution)/shard_map/ppermute | solution.py:59
  26.0 6.1 %collective-permute-start.9 = (f32[8,1792]{1,0:T(8,128)S(1)}, f32[8,1792]{1,0:T(8,128)S(1)}, u32[]{:S(2)}, u32[]{:S(2)}) collective-permute-start(f32[8,1792]{1,0:T(8,128)S(1)} %linear_layer.1), channel_id=1, source_target_pairs={{0,130},{1,131},{2,128},{3,129},{130,0},{131,1},{128,2},{129,3},{4... | collective-permute-start | bytes 172040 | tf_op jit(solution)/shard_map/ppermute | solution.py:59
  33.1 4.7 %collective-permute-start.10 = (bf16[8,512]{1,0:T(8,128)(2,1)S(1)}, bf16[8,512]{1,0:T(8,128)(2,1)S(1)}, u32[]{:S(2)}, u32[]{:S(2)}) collective-permute-start(bf16[8,512]{1,0:T(8,128)(2,1)S(1)} %get-tuple-element.108.refs_1_.refs_0_), channel_id=1, source_target_pairs={{0,16},{4,20},{8,24},{12,28},{16,32},{20,36},{24,40},{28,44},{32,4... | collective-permute-start | bytes 24584 | tf_op jit(solution)/shard_map/ppermute | solution.py:32
  33.9 3.9 %collective-permute-start.11 = (bf16[8,512]{1,0:T(8,128)(2,1)S(1)}, bf16[8,512]{1,0:T(8,128)(2,1)S(1)}, u32[]{:S(2)}, u32[]{:S(2)}) collective-permute-start(bf16[8,512]{1,0:T(8,128)(2,1)S(1)} %get-tuple-element.108.refs_1_.refs_0_), channel_id=1, source_target_pairs={{0,112},{4,116},{8,120},{12,124},{16,0},{20,4},{24,8},{28,12},{32,... | collective-permute-start | bytes 24584 | tf_op jit(solution)/shard_map/ppermute | solution.py:32
  35.8 4.6 %collective-permute-start.12 = (bf16[8,512]{1,0:T(8,128)(2,1)S(1)}, bf16[8,512]{1,0:T(8,128)(2,1)S(1)}, u32[]{:S(2)}, u32[]{:S(2)}) collective-permute-start(bf16[8,512]{1,0:T(8,128)(2,1)S(1)} %get-tuple-element.108.refs_1_.refs_0_), channel_id=1, source_target_pairs={{0,32},{4,36},{8,40},{12,44},{16,48},{20,52},{24,56},{28,60},{32,6... | collective-permute-start | bytes 24584 | tf_op jit(solution)/shard_map/ppermute | solution.py:32
  41.4 3.9 %collective-permute-start.14 = (f32[8,640]{1,0:T(8,128)S(1)}, f32[8,640]{1,0:T(8,128)S(1)}, u32[]{:S(2)}, u32[]{:S(2)}) collective-permute-start(f32[8,640]{1,0:T(8,128)S(1)} %get-tuple-element.119), channel_id=1, source_target_pairs={{0,112},{4,116},{8,120},{12,124},{16,0},{20,4},{24,8},{28,12},{32,... | collective-permute-start | bytes 61448 | tf_op jit(solution)/shard_map/ppermute | solution.py:32
  41.5 3.9 %collective-permute-start.15 = (f32[8,640]{1,0:T(8,128)S(1)}, f32[8,640]{1,0:T(8,128)S(1)}, u32[]{:S(2)}, u32[]{:S(2)}) collective-permute-start(f32[8,640]{1,0:T(8,128)S(1)} %get-tuple-element.120), channel_id=1, source_target_pairs={{0,16},{4,20},{8,24},{12,28},{16,32},{20,36},{24,40},{28,44},{32,4... | collective-permute-start | bytes 61448 | tf_op jit(solution)/shard_map/ppermute | solution.py:32
  42.9 3.5 %collective-permute-start.16 = (f32[8,640]{1,0:T(8,128)S(1)}, f32[8,640]{1,0:T(8,128)S(1)}, u32[]{:S(2)}, u32[]{:S(2)}) collective-permute-start(f32[8,640]{1,0:T(8,128)S(1)} %get-tuple-element.121), channel_id=1, source_target_pairs={{0,96},{4,100},{8,104},{12,108},{16,112},{20,116},{24,120},{28,124... | collective-permute-start | bytes 61448 | tf_op jit(solution)/shard_map/ppermute | solution.py:32
  43.9 1.4 %collective-permute-start.17 = (bf16[8,448]{1,0:T(8,128)(2,1)S(1)}, bf16[8,448]{1,0:T(8,128)(2,1)S(1)}, u32[]{:S(2)}, u32[]{:S(2)}) collective-permute-start(bf16[8,448]{1,0:T(8,128)(2,1)S(1)} %get-tuple-element.122), channel_id=1, source_target_pairs={{128,0},{0,128},{129,1},{1,129},{130,2},{2,130},{131,3},{3,131},{1... | collective-permute-start | bytes 21512 | tf_op jit(solution)/shard_map/ppermute | solution.py:672
  47.0 3.9 %collective-permute-start.18 = (f32[8,448]{1,0:T(8,128)S(1)}, f32[8,448]{1,0:T(8,128)S(1)}, u32[]{:S(2)}, u32[]{:S(2)}) collective-permute-start(f32[8,448]{1,0:T(8,128)S(1)} %get-tuple-element.132), channel_id=1, source_target_pairs={{0,1},{1,2},{2,3},{3,0},{4,5},{5,6},{6,7},{7,4},{8,9},{9,10},{10,1... | collective-permute-start | bytes 43016 | tf_op jit(solution)/shard_map/ppermute | solution.py:28
  48.0 2.9 %collective-permute-start.19 = (f32[8,448]{1,0:T(8,128)S(1)}, f32[8,448]{1,0:T(8,128)S(1)}, u32[]{:S(2)}, u32[]{:S(2)}) collective-permute-start(f32[8,448]{1,0:T(8,128)S(1)} %get-tuple-element.133), channel_id=1, source_target_pairs={{0,3},{1,0},{2,1},{3,2},{4,7},{5,4},{6,5},{7,6},{8,11},{9,8},{10,9... | collective-permute-start | bytes 43016 | tf_op jit(solution)/shard_map/ppermute | solution.py:28
  49.8 4.1 %collective-permute-start.20 = (f32[8,448]{1,0:T(8,128)S(1)}, f32[8,448]{1,0:T(8,128)S(1)}, u32[]{:S(2)}, u32[]{:S(2)}) collective-permute-start(f32[8,448]{1,0:T(8,128)S(1)} %get-tuple-element.134), channel_id=1, source_target_pairs={{0,2},{1,3},{2,0},{3,1},{4,6},{5,7},{6,4},{7,5},{8,10},{9,11},{10,... | collective-permute-start | bytes 43016 | tf_op jit(solution)/shard_map/ppermute | solution.py:28

commit v10 on v9

--- a/solution.py
+++ b/solution.py
@@ -236,7 +236,7 @@
         total = total + jnp.dot(
             attended, out_w[h * HD : (h + 1) * HD, :], preferred_element_type=jnp.float32
         )
-    update[...] = total
+    update[...] = total.astype(jnp.bfloat16)
 
 
 def linear_layer(pieces, near):
@@ -244,7 +244,7 @@
         linear_kernel,
         0,
         "linear_layer",
-        jax.ShapeDtypeStruct((pieces[0].shape[0], near["out_w"].shape[1]), jnp.float32),
+        jax.ShapeDtypeStruct((pieces[0].shape[0], near["out_w"].shape[1]), jnp.bfloat16),
         [VMEM] * 12,
         [],
         (*pieces, *(near[name] for name in LINEAR_NEAR)),
@@ -268,7 +268,7 @@
 ):
     rows, share = one.shape
     heads = share // HD
-    layer_one = (p0[...] + p1[...] + p2[...] + p3[...]).astype(jnp.bfloat16)
+    layer_one = sum(ref[...].astype(jnp.float32) for ref in (p0, p1, p2, p3)).astype(jnp.bfloat16)
     rounded = layer_one.astype(jnp.float32)
     mine = rounded[:, :share]
     for h in range(1, heads):
@@ -479,7 +479,7 @@
     prompt_factor = jnp.exp(prompt_highest - peak)
     whole = total[...] * own_factor + prompt_total * prompt_factor
     attended = (summed[...] * own_factor + prompt_summed * prompt_factor) / whole
-    second = jnp.dot(attended.astype(jnp.bfloat16), out_w[...], preferred_element_type=jnp.float32)
+    second = jnp.dot(attended.astype(jnp.bfloat16), out_w[0], preferred_element_type=jnp.float32)
     for steps, ref in enumerate((s0, s1, s2, s3)):
         slab = second[:, :share]
         for h in range(1, heads):
@@ -489,7 +489,7 @@
         ref[...] = slab
 
 
-def combine(own, parts, near):
+def combine(own, parts, out_w):
     return kernel_call(
         combine_kernel,
         1,
@@ -497,7 +497,7 @@
         [jax.ShapeDtypeStruct(own[0].shape, jnp.float32)] * 4,
         [VMEM] * 8,
         [],
-        (*own, *parts, near["out_w"]),
+        (*own, *parts, out_w),
     )
 
 
@@ -511,13 +511,14 @@
     "value_w",
     "out_w",
 )
-SHARED_NEAR = ("gain", "value_w", "out_w")
+WINDOW_NEAR = ("gain", "value_w", "query_key_w")
 
 
 def bring_near(arrays):
     names = list(arrays)
     count = len(names)
-    both = [at for at, name in enumerate(names) if name in SHARED_NEAR]
+    first = [at for at, name in enumerate(names) if name in LINEAR_NEAR]
+    second = [at for at, name in enumerate(names) if name in WINDOW_NEAR]
 
     def copy_some(chosen, refs):
         sems = refs[-1]
@@ -530,7 +531,7 @@
             copy.wait()
 
     near = kernel_call(
-        lambda ids, *refs: copy_some(range(count), refs),
+        lambda ids, *refs: copy_some(first, refs),
         0,
         "bring_near",
         [jax.ShapeDtypeStruct(array.shape, array.dtype) for array in arrays.values()],
@@ -539,7 +540,7 @@
         tuple(arrays.values()),
         4 << 20,
         bytes_only(arrays.values()),
-        lambda ids, *refs: copy_some(both, refs),
+        lambda ids, *refs: copy_some(second, refs),
     )
     return dict(zip(names, near))
 
@@ -550,11 +551,11 @@
 
 
 def window_kernel(
-    ids, table, lengths, query_key_hbm, own_hbm, query_key_near, own_near, tags, key_sem, sems
+    ids, table, lengths, own_hbm, own_near, tags, sems
 ):
     rows = tags.shape[0]
     total = own_hbm.shape[0]
-    copies = [pltpu.make_async_copy(query_key_hbm, query_key_near, key_sem)]
+    copies = []
     for r in range(rows):
         for slot, logical in enumerate(window_pages(lengths, r)):
             page = jnp.clip(table[r, logical] - GROUPS - ids[1] * total, 0, total - 1)
@@ -574,7 +575,7 @@
         copy.wait()
 
 
-def bring_windows(table, lengths, query_key_w, own_pages):
+def bring_windows(table, lengths, own_pages):
     rows = lengths.shape[0]
     windows = jax.ShapeDtypeStruct((rows, 2) + own_pages.shape[1:], own_pages.dtype)
     return kernel_call(
@@ -582,15 +583,14 @@
         1,
         "bring_windows",
         [
-            jax.ShapeDtypeStruct(query_key_w.shape, query_key_w.dtype),
             windows,
             jax.ShapeDtypeStruct((rows, 128), jnp.float32),
         ],
-        [SMEM] * 2 + [HBM] * 2,
-        [pltpu.SemaphoreType.DMA, pltpu.SemaphoreType.DMA((rows, 2))],
-        (table, lengths, query_key_w, own_pages),
+        [SMEM] * 2 + [HBM],
+        [pltpu.SemaphoreType.DMA((rows, 2))],
+        (table, lengths, own_pages),
         1 << 20,
-        bytes_only([query_key_w, windows]),
+        bytes_only([windows]),
     )
 
 
@@ -643,11 +643,12 @@
         "conv_state": conv_state,
         "value_w": value_w.transpose(0, 2, 1)[0],
         "out_w": out_w[0],
+        "query_key_w": query_key_w,
     }
 
     page = window_page(pages_first)
     row_pages = [x_shift(page, k) for k in (1, 3, 2)]
-    row_pages[0], last_tokens = lax.optimization_barrier((row_pages[0], tokens))
+    row_pages[0], last_tokens, stored = lax.optimization_barrier((row_pages[0], tokens, stored))
     received = [head_shift(tokens, 1), head_shift(tokens, 3), head_shift(last_tokens, 2)]
     near, received = lax.optimization_barrier((bring_near(stored), received))
     near_pages = jnp.stack([row_pages[0], page, row_pages[1], row_pages[2]])
@@ -655,12 +656,10 @@
     far_pages = far_swap(near_pages)
     update = linear_layer([tokens] + received, near)
     own_pages = own_pages.transpose(0, 1, 3, 2)
-    query_key_w, own_pages, table, ends, update = lax.optimization_barrier(
-        (query_key_w, own_pages, page_table, lengths, update)
-    )
-    near["query_key_w"], near["own_pages"], tags = bring_windows(
-        table, ends, query_key_w, own_pages
-    )
+    own_pages, table, ends, update = lax.optimization_barrier(
+        (own_pages, page_table, lengths, update)
+    )
+    near["own_pages"], tags = bring_windows(table, ends, own_pages)
     swapped = [section_swap(update, k) for k in (0, 1, 3, 2)]
     one_share, packed, key_new, value_new = project(tags, swapped, near)
     asked = [packed] + [z_shift(packed, k) for k in (1, 7, 2)]
@@ -671,7 +670,7 @@
     parts = [answers[0]] + [z_shift(answers[at], -k) for at, k in ((1, 1), (2, 7), (3, 2))]
     one_back = lax.ppermute(one_share, "section", [(1, 0), (0, 1)])
     parts, one_back = lax.optimization_barrier((parts, one_back))
-    slabs = combine(own, parts, near)
+    slabs = combine(own, parts, out_w)
     section_index = lax.axis_index("section")
     total = one_share.astype(jnp.float32) + slabs[0]
     for piece in [head_shift(slabs[k], k) for k in (1, 3, 2)]:

time: 55.2 us -> 55.5 us (level)
  the two profiles are of different devices: /device:TPU:1 before, /device:TPU:4 now
where the time goes in v10:
time: 55.5 us; the launch traced here: 55.3 us
  starting transfers between devices  29.3 us (53%)
  waiting for transfers between devices  18.4 us (33%)
  Pallas kernels  6.8 us (12%)
  other arithmetic  0.67 us (1%)
    ppermute x4, starting transfers between devices, section_swap(): lax.ppermute(value, ('section', 'head'), there + [(b, a) for a, b in there])  9.2 us
    ppermute x6, starting transfers between devices, head_shift(): lax.ppermute(value, 'head', [(i, (i + steps) % count) for i in range(coun...  8.05 us
    ppermute x6, waiting for transfers between devices, z_shift(): lax.ppermute(value, 'req', [(z * XN + i, (z + steps) % ZN * XN + i) for z...  7.94 us
    pallas_call x8, Pallas kernels, kernel_call(): pl.pallas_call(run, out_shape=out_shape, in_specs=in_specs, out_specs=jax...  6.8 us
    ppermute x6, starting transfers between devices, z_shift(): lax.ppermute(value, 'req', [(z * XN + i, (z + steps) % ZN * XN + i) for z...  5.54 us
    ppermute x6, waiting for transfers between devices, head_shift(): lax.ppermute(value, 'head', [(i, (i + steps) % count) for i in range(coun...  5.22 us
    ppermute x3, starting transfers between devices, x_shift(): lax.ppermute(value, 'req', [(z * XN + i, z * XN + (i + steps) % XN) for z...  4.95 us
    ppermute x4, waiting for transfers between devices, section_swap(): lax.ppermute(value, ('section', 'head'), there + [(b, a) for a, b in there])  3.34 us
  transfers between devices with their start and end apart: 21, of which 12 were waited for; matrix products, arithmetic and copies ran while one was open for 0% of the time, Pallas kernels for 12%

profile of v10, /device:TPU:4, one launch (start us, length us, event | category | flops | bytes accessed | tf_op | source)
XLA Modules:
  0.0 55.3 jit_solution(13277419852756989323)
XLA Ops:
  0.0 1.3 %collective-permute-start = (bf16[448,128]{1,0:T(8,128)(2,1)S(1)}, bf16[448,128]{1,0:T(8,128)(2,1)S(1)}, u32[]{:S(2)}, u32[]{:S(2)}) collective-permute-start(bf16[448,128]{1,0:T(8,128)(2,1)S(1)} %window_page.1), channel_id=1, source_target_pairs={{0,4},{4,8},{8,12},{12,0},{16,20},{20,24},{24,28},{28,16},{32,36},... | collective-permute-start | bytes 344072 | tf_op jit(solution)/shard_map/ppermute | solution.py:40
  1.3 1.1 %collective-permute-start.2 = (bf16[448,128]{1,0:T(8,128)(2,1)S(1)}, bf16[448,128]{1,0:T(8,128)(2,1)S(1)}, u32[]{:S(2)}, u32[]{:S(2)}) collective-permute-start(bf16[448,128]{1,0:T(8,128)(2,1)S(1)} %window_page.1), channel_id=1, source_target_pairs={{0,8},{4,12},{8,0},{12,4},{16,24},{20,28},{24,16},{28,20},{32,40},... | collective-permute-start | bytes 344072 | tf_op jit(solution)/shard_map/ppermute | solution.py:40
  2.4 2.5 %collective-permute-start.1 = (bf16[448,128]{1,0:T(8,128)(2,1)S(1)}, bf16[448,128]{1,0:T(8,128)(2,1)S(1)}, u32[]{:S(2)}, u32[]{:S(2)}) collective-permute-start(bf16[448,128]{1,0:T(8,128)(2,1)S(1)} %window_page.1), channel_id=1, source_target_pairs={{0,12},{4,0},{8,4},{12,8},{16,28},{20,16},{24,20},{28,24},{32,44},... | collective-permute-start | bytes 344072 | tf_op jit(solution)/shard_map/ppermute | solution.py:40
  5.0 0.0 collective-permute-start.3
  5.0 3.2 %collective-permute-start.4 = (bf16[8,448]{1,0:T(8,128)(2,1)}, bf16[8,448]{1,0:T(8,128)(2,1)S(1)}, u32[]{:S(2)}, u32[]{:S(2)}) collective-permute-start(bf16[8,448]{1,0:T(8,128)(2,1)} %refs_0_.3), channel_id=1, source_target_pairs={{0,3},{1,0},{2,1},{3,2},{4,7},{5,4},{6,5},{7,6},{8,11},{9,8},{10,9... | collective-permute-start | bytes 21512 | tf_op jit(solution)/shard_map/ppermute | solution.py:28
  8.2 0.0 collective-permute-done
  8.2 1.0 %collective-permute-start.5 = (bf16[8,448]{1,0:T(8,128)(2,1)}, bf16[8,448]{1,0:T(8,128)(2,1)S(1)}, u32[]{:S(2)}, u32[]{:S(2)}) collective-permute-start(bf16[8,448]{1,0:T(8,128)(2,1)} %refs_0_.3), channel_id=1, source_target_pairs={{0,2},{1,3},{2,0},{3,1},{4,6},{5,7},{6,4},{7,5},{8,10},{9,11},{10,... | collective-permute-start | bytes 21512 | tf_op jit(solution)/shard_map/ppermute | solution.py:28
  9.2 0.0 collective-permute-done.2
  9.2 1.1 %collective-permute-done.1 = bf16[448,128]{1,0:T(8,128)(2,1)S(1)} collective-permute-done((bf16[448,128]{1,0:T(8,128)(2,1)S(1)}, bf16[448,128]{1,0:T(8,128)(2,1)S(1)}, u32[]{:S(2)}, u32[]{:S(2)}) %collective-permute-start.1) | collective-permute-done | bytes 114720 | tf_op jit(solution)/shard_map/ppermute | solution.py:40
  10.3 0.1 pad_maximum_fusion.refs_4_
  10.4 0.0 copy-start.1
  10.4 2.9 %bring_near.1 = (bf16[8,2,448]{2,1,0:T(2,128)(2,1)S(1)}, f32[3,448]{1,0:T(4,128)S(1)}, bf16[1792,128]{1,0:T(8,128)(2,1)S(1)}, f32[1,1792]{1,0:T(1,128)S(1)}, f32...) custom-call(bf16[8,2,448]{2,1,0:T(2,128)(2,1)} %refs_0_.2, ...), custom_call_target="tpu_custom_call" | custom-call | bytes 17799936 | tf_op jit(solution)/shard_map/bring_near/pallas_call | solution.py:114
  13.3 0.0 collective-permute-done.3.refs_1_
  13.3 0.0 collective-permute-done.4.refs_2_
  13.3 0.3 collective-permute-done.5.refs_3_
  13.6 0.8 %collective-permute-start.13 = (bf16[4,448,128]{2,1,0:T(8,128)(2,1)S(1)}, bf16[4,448,128]{2,1,0:T(8,128)(2,1)S(1)}, u32[]{:S(2)}, u32[]{:S(2)}) collective-permute-start(bf16[4,448,128]{2,1,0:T(8,128)(2,1)S(1)} %pad_maximum_fusion.refs_4_), channel_id=1, source_target_pairs={{128,192},{132,196},{136,200},{140,204},{144,208},{148,212},{152,2... | collective-permute-start | bytes 1376264 | tf_op jit(solution)/shard_map/ppermute | solution.py:49
  14.4 2.3 %linear_layer.1 = bf16[8,1792]{1,0:T(8,128)(2,1)S(1)} custom-call(bf16[8,448]{1,0:T(8,128)(2,1)S(1)} %copy-done.1, bf16[8,448]{1,0:T(8,128)(2,1)S(1)} %collective-permute-done.3.refs_1_, bf16[8,448]{1,0:T(8,128)(2,1)S(1)} %collective-permute-done.4.refs_2_, bf16[8,448]{1,0:T(8,128)(2,1)S(1)} %collective-permute-done.5.refs_3_, ...), custom_call_target="tpu_custom_call" | custom-call | tf_op jit(solution)/shard_map/linear_layer/pallas_call | solution.py:114
  16.7 5.0 %collective-permute-start.6 = (bf16[8,1792]{1,0:T(8,128)(2,1)S(1)}, bf16[8,1792]{1,0:T(8,128)(2,1)S(1)}, u32[]{:S(2)}, u32[]{:S(2)}) collective-permute-start(bf16[8,1792]{1,0:T(8,128)(2,1)S(1)} %linear_layer.1), channel_id=1, source_target_pairs={{0,128},{1,129},{2,130},{3,131},{128,0},{129,1},{130,2},{131,3},{4... | collective-permute-start | bytes 86024 | tf_op jit(solution)/shard_map/ppermute | solution.py:59
  21.7 1.3 %collective-permute-start.7 = (bf16[8,1792]{1,0:T(8,128)(2,1)S(1)}, bf16[8,1792]{1,0:T(8,128)(2,1)S(1)}, u32[]{:S(2)}, u32[]{:S(2)}) collective-permute-start(bf16[8,1792]{1,0:T(8,128)(2,1)S(1)} %linear_layer.1), channel_id=1, source_target_pairs={{0,129},{1,130},{2,131},{3,128},{129,0},{130,1},{131,2},{128,3},{4... | collective-permute-start | bytes 86024 | tf_op jit(solution)/shard_map/ppermute | solution.py:59
  23.0 2.2 %collective-permute-start.8 = (bf16[8,1792]{1,0:T(8,128)(2,1)S(1)}, bf16[8,1792]{1,0:T(8,128)(2,1)S(1)}, u32[]{:S(2)}, u32[]{:S(2)}) collective-permute-start(bf16[8,1792]{1,0:T(8,128)(2,1)S(1)} %linear_layer.1), channel_id=1, source_target_pairs={{0,131},{1,128},{2,129},{3,130},{131,0},{128,1},{129,2},{130,3},{4... | collective-permute-start | bytes 86024 | tf_op jit(solution)/shard_map/ppermute | solution.py:59
  25.2 0.7 %collective-permute-start.9 = (bf16[8,1792]{1,0:T(8,128)(2,1)S(1)}, bf16[8,1792]{1,0:T(8,128)(2,1)S(1)}, u32[]{:S(2)}, u32[]{:S(2)}) collective-permute-start(bf16[8,1792]{1,0:T(8,128)(2,1)S(1)} %linear_layer.1), channel_id=1, source_target_pairs={{0,130},{1,131},{2,128},{3,129},{130,0},{131,1},{128,2},{129,3},{4... | collective-permute-start | bytes 86024 | tf_op jit(solution)/shard_map/ppermute | solution.py:59
  26.0 0.8 %bring_windows.1 = (bf16[8,2,2,448,128]{4,3,2,1,0:T(8,128)(2,1)S(1)}, f32[8,128]{1,0:T(8,128)S(1)}) custom-call(s32[8,256]{1,0:T(8,128)S(1)} %copy-done.2, s32[8]{0:T(128)S(1)} %copy-done.3, bf16[16,2,448,128]{3,2,1,0:T(8,128)(2,1)} %bitcast.17), custom_call_target="tpu_custom_call" | custom-call | bytes 7340032 | tf_op jit(solution)/shard_map/bring_windows/pallas_call | solution.py:114
  26.8 0.0 collective-permute-done.6.refs_1_
  26.8 0.0 collective-permute-done.7.refs_2_
  26.8 0.7 %collective-permute-done.8.refs_3_ = bf16[8,1792]{1,0:T(8,128)(2,1)S(1)} collective-permute-done((bf16[8,1792]{1,0:T(8,128)(2,1)S(1)}, bf16[8,1792]{1,0:T(8,128)(2,1)S(1)}, u32[]{:S(2)}, u32[]{:S(2)}) %collective-permute-start.8) | collective-permute-done | bytes 28704 | tf_op jit(solution)/shard_map/ppermute | solution.py:59
  27.5 2.6 %collective-permute-done.9.refs_4_ = bf16[8,1792]{1,0:T(8,128)(2,1)S(1)} collective-permute-done((bf16[8,1792]{1,0:T(8,128)(2,1)S(1)}, bf16[8,1792]{1,0:T(8,128)(2,1)S(1)}, u32[]{:S(2)}, u32[]{:S(2)}) %collective-permute-start.9) | collective-permute-done | bytes 28704 | tf_op jit(solution)/shard_map/ppermute | solution.py:59
  30.2 1.0 %collective-permute-start.10 = (bf16[8,512]{1,0:T(8,128)(2,1)S(1)}, bf16[8,512]{1,0:T(8,128)(2,1)S(1)}, u32[]{:S(2)}, u32[]{:S(2)}) collective-permute-start(bf16[8,512]{1,0:T(8,128)(2,1)S(1)} %get-tuple-element.126.refs_1_.refs_0_), channel_id=1, source_target_pairs={{0,16},{4,20},{8,24},{12,28},{16,32},{20,36},{24,40},{28,44},{32,4... | collective-permute-start | bytes 24584 | tf_op jit(solution)/shard_map/ppermute | solution.py:32
  31.2 2.2 %collective-permute-start.11 = (bf16[8,512]{1,0:T(8,128)(2,1)S(1)}, bf16[8,512]{1,0:T(8,128)(2,1)S(1)}, u32[]{:S(2)}, u32[]{:S(2)}) collective-permute-start(bf16[8,512]{1,0:T(8,128)(2,1)S(1)} %get-tuple-element.126.refs_1_.refs_0_), channel_id=1, source_target_pairs={{0,112},{4,116},{8,120},{12,124},{16,0},{20,4},{24,8},{28,12},{32,... | collective-permute-start | bytes 24584 | tf_op jit(solution)/shard_map/ppermute | solution.py:32
  33.4 0.3 collective-permute-start.12
  33.7 0.7 %own_attention.1 = (f32[8,448]{1,0:T(8,128)S(1)}, f32[8,448]{1,0:T(8,128)S(1)}, f32[8,448]{1,0:T(8,128)S(1)}) custom-call(s32[8]{0:T(128)S(1)} %copy-done.3, bf16[8,512]{1,0:T(8,128)(2,1)S(1)} %get-tuple-element.126.refs_1_.refs_0_, bf16[8,448]{1,0:T(8,128)(2,1)S(1)} %get-tuple-element.120.refs_2_, bf16[8,448]{1,0:T(8,128)(2,1)S(1)} %get-tuple-element.121.refs_3_, ...), custom_call_target="tpu_custom_call" | custom-call | tf_op jit(solution)/shard_map/own_attention/pallas_call | solution.py:114
  34.4 0.6 %collective-permute-done.10.refs_1_ = bf16[8,512]{1,0:T(8,128)(2,1)S(1)} collective-permute-done((bf16[8,512]{1,0:T(8,128)(2,1)S(1)}, bf16[8,512]{1,0:T(8,128)(2,1)S(1)}, u32[]{:S(2)}, u32[]{:S(2)}) %collective-permute-start.10) | collective-permute-done | bytes 8224 | tf_op jit(solution)/shard_map/ppermute | solution.py:32
  35.0 0.0 collective-permute-done.11.refs_2_
  35.0 4.1 %collective-permute-done.12.refs_3_ = bf16[8,512]{1,0:T(8,128)(2,1)S(1)} collective-permute-done((bf16[8,512]{1,0:T(8,128)(2,1)S(1)}, bf16[8,512]{1,0:T(8,128)(2,1)S(1)}, u32[]{:S(2)}, u32[]{:S(2)}) %collective-permute-start.12) | collective-permute-done | bytes 8224 | tf_op jit(solution)/shard_map/ppermute | solution.py:32
  39.2 0.0 collective-permute-done.13.refs_5_
  39.2 0.0 collective-permute-start.14
  39.2 2.0 %collective-permute-start.15 = (f32[8,640]{1,0:T(8,128)S(1)}, f32[8,640]{1,0:T(8,128)S(1)}, u32[]{:S(2)}, u32[]{:S(2)}) collective-permute-start(f32[8,640]{1,0:T(8,128)S(1)} %get-tuple-element.138), channel_id=1, source_target_pairs={{0,16},{4,20},{8,24},{12,28},{16,32},{20,36},{24,40},{28,44},{32,4... | collective-permute-start | bytes 61448 | tf_op jit(solution)/shard_map/ppermute | solution.py:32
  41.2 0.0 collective-permute-start.16
  41.2 0.7 %collective-permute-start.17 = (bf16[8,448]{1,0:T(8,128)(2,1)S(1)}, bf16[8,448]{1,0:T(8,128)(2,1)S(1)}, u32[]{:S(2)}, u32[]{:S(2)}) collective-permute-start(bf16[8,448]{1,0:T(8,128)(2,1)S(1)} %get-tuple-element.140), channel_id=1, source_target_pairs={{128,0},{0,128},{129,1},{1,129},{130,2},{2,130},{131,3},{3,131},{1... | collective-permute-start | bytes 21512 | tf_op jit(solution)/shard_map/ppermute | solution.py:671
  41.9 0.8 %collective-permute-done.17 = bf16[8,448]{1,0:T(8,128)(2,1)S(1)} collective-permute-done((bf16[8,448]{1,0:T(8,128)(2,1)S(1)}, bf16[8,448]{1,0:T(8,128)(2,1)S(1)}, u32[]{:S(2)}, u32[]{:S(2)}) %collective-permute-start.17) | collective-permute-done | bytes 7200 | tf_op jit(solution)/shard_map/ppermute | solution.py:671
  42.7 0.2 collective-permute-done.14.refs_4_
  43.0 1.3 %collective-permute-done.15.refs_5_ = f32[8,640]{1,0:T(8,128)S(1)} collective-permute-done((f32[8,640]{1,0:T(8,128)S(1)}, f32[8,640]{1,0:T(8,128)S(1)}, u32[]{:S(2)}, u32[]{:S(2)}) %collective-permute-start.15) | collective-permute-done | bytes 20512 | tf_op jit(solution)/shard_map/ppermute | solution.py:32
  44.2 1.7 %collective-permute-done.16.refs_6_ = f32[8,640]{1,0:T(8,128)S(1)} collective-permute-done((f32[8,640]{1,0:T(8,128)S(1)}, f32[8,640]{1,0:T(8,128)S(1)}, u32[]{:S(2)}, u32[]{:S(2)}) %collective-permute-start.16) | collective-permute-done | bytes 20512 | tf_op jit(solution)/shard_map/ppermute | solution.py:32
  45.9 0.7 %collective-permute-start.20 = (f32[8,448]{1,0:T(8,128)S(1)}, f32[8,448]{1,0:T(8,128)S(1)}, u32[]{:S(2)}, u32[]{:S(2)}) collective-permute-start(f32[8,448]{1,0:T(8,128)S(1)} %get-tuple-element.152), channel_id=1, source_target_pairs={{0,2},{1,3},{2,0},{3,1},{4,6},{5,7},{6,4},{7,5},{8,10},{9,11},{10,... | collective-permute-start | bytes 43016 | tf_op jit(solution)/shard_map/ppermute | solution.py:28
  46.7 3.1 %collective-permute-start.19 = (f32[8,448]{1,0:T(8,128)S(1)}, f32[8,448]{1,0:T(8,128)S(1)}, u32[]{:S(2)}, u32[]{:S(2)}) collective-permute-start(f32[8,448]{1,0:T(8,128)S(1)} %get-tuple-element.151), channel_id=1, source_target_pairs={{0,3},{1,0},{2,1},{3,2},{4,7},{5,4},{6,5},{7,6},{8,11},{9,8},{10,9... | collective-permute-start | bytes 43016 | tf_op jit(solution)/shard_map/ppermute | solution.py:28
  49.7 0.0 collective-permute-start.18
  49.7 1.4 %collective-permute-done.20 = f32[8,448]{1,0:T(8,128)S(1)} collective-permute-done((f32[8,448]{1,0:T(8,128)S(1)}, f32[8,448]{1,0:T(8,128)S(1)}, u32[]{:S(2)}, u32[]{:S(2)}) %collective-permute-start.20) | collective-permute-done | bytes 14368 | tf_op jit(solution)/shard_map/ppermute | solution.py:28
  51.2 3.5 %collective-permute-done.18 = f32[8,448]{1,0:T(8,128)S(1)} collective-permute-done((f32[8,448]{1,0:T(8,128)S(1)}, f32[8,448]{1,0:T(8,128)S(1)}, u32[]{:S(2)}, u32[]{:S(2)}) %collective-permute-start.18) | collective-permute-done | bytes 14368 | tf_op jit(solution)/shard_map/ppermute | solution.py:28
  54.7 0.6 %fusion.1 = bf16[1,8,448]{2,1,0:T(8,128)(2,1)} fusion(bf16[8,448]{1,0:T(8,128)(2,1)S(1)} %collective-permute-done.17, f32[8,448]{1,0:T(8,128)S(1)} %collective-permute-done.20, f32[8,448]{1,0:T(8,128)S(1)} %collective-permute-done.19, f32[8,448]{1,0:T(8,128)S(1)} %collective-permute-done.18, f32[8,448]{1,0:T(8,128)S(1)} %get-tuple-element.149, ...), kind=kLoop, calls=%fused_computation.3 | loop fusion | flops 25088 | bytes 78849 | tf_op jit(solution)/shard_map/broadcast_in_dim | solution.py:679
  (12 shorter events, 0.0 us)
Async XLA Ops:
  0.0 8.2 %collective-permute-start = (bf16[448,128]{1,0:T(8,128)(2,1)S(1)}, bf16[448,128]{1,0:T(8,128)(2,1)S(1)}, u32[]{:S(2)}, u32[]{:S(2)}) collective-permute-start(bf16[448,128]{1,0:T(8,128)(2,1)S(1)} %window_page.1), channel_id=1, source_target_pairs={{0,4},{4,8},{8,12},{12,0},{16,20},{20,24},{24,28},{28,16},{32,36},... | collective-permute-start | bytes 344072 | tf_op jit(solution)/shard_map/ppermute | solution.py:40
  1.3 7.9 %collective-permute-start.2 = (bf16[448,128]{1,0:T(8,128)(2,1)S(1)}, bf16[448,128]{1,0:T(8,128)(2,1)S(1)}, u32[]{:S(2)}, u32[]{:S(2)}) collective-permute-start(bf16[448,128]{1,0:T(8,128)(2,1)S(1)} %window_page.1), channel_id=1, source_target_pairs={{0,8},{4,12},{8,0},{12,4},{16,24},{20,28},{24,16},{28,20},{32,40},... | collective-permute-start | bytes 344072 | tf_op jit(solution)/shard_map/ppermute | solution.py:40
  2.4 7.9 %collective-permute-start.1 = (bf16[448,128]{1,0:T(8,128)(2,1)S(1)}, bf16[448,128]{1,0:T(8,128)(2,1)S(1)}, u32[]{:S(2)}, u32[]{:S(2)}) collective-permute-start(bf16[448,128]{1,0:T(8,128)(2,1)S(1)} %window_page.1), channel_id=1, source_target_pairs={{0,12},{4,0},{8,4},{12,8},{16,28},{20,16},{24,20},{28,24},{32,44},... | collective-permute-start | bytes 344072 | tf_op jit(solution)/shard_map/ppermute | solution.py:40
  5.0 8.3 %collective-permute-start.3 = (bf16[8,448]{1,0:T(8,128)(2,1)}, bf16[8,448]{1,0:T(8,128)(2,1)S(1)}, u32[]{:S(2)}, u32[]{:S(2)}) collective-permute-start(bf16[8,448]{1,0:T(8,128)(2,1)} %refs_0_.3), channel_id=1, source_target_pairs={{0,1},{1,2},{2,3},{3,0},{4,5},{5,6},{6,7},{7,4},{8,9},{9,10},{10,1... | collective-permute-start | bytes 21512 | tf_op jit(solution)/shard_map/ppermute | solution.py:28
  5.0 8.3 %collective-permute-start.4 = (bf16[8,448]{1,0:T(8,128)(2,1)}, bf16[8,448]{1,0:T(8,128)(2,1)S(1)}, u32[]{:S(2)}, u32[]{:S(2)}) collective-permute-start(bf16[8,448]{1,0:T(8,128)(2,1)} %refs_0_.3), channel_id=1, source_target_pairs={{0,3},{1,0},{2,1},{3,2},{4,7},{5,4},{6,5},{7,6},{8,11},{9,8},{10,9... | collective-permute-start | bytes 21512 | tf_op jit(solution)/shard_map/ppermute | solution.py:28
  8.2 5.4 %collective-permute-start.5 = (bf16[8,448]{1,0:T(8,128)(2,1)}, bf16[8,448]{1,0:T(8,128)(2,1)S(1)}, u32[]{:S(2)}, u32[]{:S(2)}) collective-permute-start(bf16[8,448]{1,0:T(8,128)(2,1)} %refs_0_.3), channel_id=1, source_target_pairs={{0,2},{1,3},{2,0},{3,1},{4,6},{5,7},{6,4},{7,5},{8,10},{9,11},{10,... | collective-permute-start | bytes 21512 | tf_op jit(solution)/shard_map/ppermute | solution.py:28
  10.4 4.0 %copy-start.1 = (bf16[8,448]{1,0:T(8,128)(2,1)S(1)}, bf16[8,448]{1,0:T(8,128)(2,1)}, u32[]{:S(2)}) copy-start(bf16[8,448]{1,0:T(8,128)(2,1)} %refs_0_.3) | copy-start | bytes 21508
  13.6 12.4 %copy-start.2 = (s32[8,256]{1,0:T(8,128)S(1)}, s32[8,256]{1,0:T(8,128)}, u32[]{:S(2)}) copy-start(s32[8,256]{1,0:T(8,128)} %refs_0_.4) | copy-start | bytes 24580
  13.6 12.4 %copy-start.3 = (s32[8]{0:T(128)S(1)}, s32[8]{0:T(128)}, u32[]{:S(2)}) copy-start(s32[8]{0:T(128)} %refs_0_.5) | copy-start | bytes 100
  13.6 25.6 %collective-permute-start.13 = (bf16[4,448,128]{2,1,0:T(8,128)(2,1)S(1)}, bf16[4,448,128]{2,1,0:T(8,128)(2,1)S(1)}, u32[]{:S(2)}, u32[]{:S(2)}) collective-permute-start(bf16[4,448,128]{2,1,0:T(8,128)(2,1)S(1)} %pad_maximum_fusion.refs_4_), channel_id=1, source_target_pairs={{128,192},{132,196},{136,200},{140,204},{144,208},{148,212},{152,2... | collective-permute-start | bytes 1376264 | tf_op jit(solution)/shard_map/ppermute | solution.py:49
  16.7 10.0 %collective-permute-start.6 = (bf16[8,1792]{1,0:T(8,128)(2,1)S(1)}, bf16[8,1792]{1,0:T(8,128)(2,1)S(1)}, u32[]{:S(2)}, u32[]{:S(2)}) collective-permute-start(bf16[8,1792]{1,0:T(8,128)(2,1)S(1)} %linear_layer.1), channel_id=1, source_target_pairs={{0,128},{1,129},{2,130},{3,131},{128,0},{129,1},{130,2},{131,3},{4... | collective-permute-start | bytes 86024 | tf_op jit(solution)/shard_map/ppermute | solution.py:59
  21.7 5.1 %collective-permute-start.7 = (bf16[8,1792]{1,0:T(8,128)(2,1)S(1)}, bf16[8,1792]{1,0:T(8,128)(2,1)S(1)}, u32[]{:S(2)}, u32[]{:S(2)}) collective-permute-start(bf16[8,1792]{1,0:T(8,128)(2,1)S(1)} %linear_layer.1), channel_id=1, source_target_pairs={{0,129},{1,130},{2,131},{3,128},{129,0},{130,1},{131,2},{128,3},{4... | collective-permute-start | bytes 86024 | tf_op jit(solution)/shard_map/ppermute | solution.py:59
  23.0 4.5 %collective-permute-start.8 = (bf16[8,1792]{1,0:T(8,128)(2,1)S(1)}, bf16[8,1792]{1,0:T(8,128)(2,1)S(1)}, u32[]{:S(2)}, u32[]{:S(2)}) collective-permute-start(bf16[8,1792]{1,0:T(8,128)(2,1)S(1)} %linear_layer.1), channel_id=1, source_target_pairs={{0,131},{1,128},{2,129},{3,130},{131,0},{128,1},{129,2},{130,3},{4... | collective-permute-start | bytes 86024 | tf_op jit(solution)/shard_map/ppermute | solution.py:59
  25.2 4.9 %collective-permute-start.9 = (bf16[8,1792]{1,0:T(8,128)(2,1)S(1)}, bf16[8,1792]{1,0:T(8,128)(2,1)S(1)}, u32[]{:S(2)}, u32[]{:S(2)}) collective-permute-start(bf16[8,1792]{1,0:T(8,128)(2,1)S(1)} %linear_layer.1), channel_id=1, source_target_pairs={{0,130},{1,131},{2,128},{3,129},{130,0},{131,1},{128,2},{129,3},{4... | collective-permute-start | bytes 86024 | tf_op jit(solution)/shard_map/ppermute | solution.py:59
  30.2 4.9 %collective-permute-start.10 = (bf16[8,512]{1,0:T(8,128)(2,1)S(1)}, bf16[8,512]{1,0:T(8,128)(2,1)S(1)}, u32[]{:S(2)}, u32[]{:S(2)}) collective-permute-start(bf16[8,512]{1,0:T(8,128)(2,1)S(1)} %get-tuple-element.126.refs_1_.refs_0_), channel_id=1, source_target_pairs={{0,16},{4,20},{8,24},{12,28},{16,32},{20,36},{24,40},{28,44},{32,4... | collective-permute-start | bytes 24584 | tf_op jit(solution)/shard_map/ppermute | solution.py:32
  31.2 3.9 %collective-permute-start.11 = (bf16[8,512]{1,0:T(8,128)(2,1)S(1)}, bf16[8,512]{1,0:T(8,128)(2,1)S(1)}, u32[]{:S(2)}, u32[]{:S(2)}) collective-permute-start(bf16[8,512]{1,0:T(8,128)(2,1)S(1)} %get-tuple-element.126.refs_1_.refs_0_), channel_id=1, source_target_pairs={{0,112},{4,116},{8,120},{12,124},{16,0},{20,4},{24,8},{28,12},{32,... | collective-permute-start | bytes 24584 | tf_op jit(solution)/shard_map/ppermute | solution.py:32
  33.4 5.8 %collective-permute-start.12 = (bf16[8,512]{1,0:T(8,128)(2,1)S(1)}, bf16[8,512]{1,0:T(8,128)(2,1)S(1)}, u32[]{:S(2)}, u32[]{:S(2)}) collective-permute-start(bf16[8,512]{1,0:T(8,128)(2,1)S(1)} %get-tuple-element.126.refs_1_.refs_0_), channel_id=1, source_target_pairs={{0,32},{4,36},{8,40},{12,44},{16,48},{20,52},{24,56},{28,60},{32,6... | collective-permute-start | bytes 24584 | tf_op jit(solution)/shard_map/ppermute | solution.py:32
  33.7 12.3 %copy-start = (bf16[1,448,1792]{2,1,0:T(8,128)(2,1)S(1)}, bf16[1,448,1792]{2,1,0:T(8,128)(2,1)}, u32[]{:S(2)}) copy-start(bf16[1,448,1792]{2,1,0:T(8,128)(2,1)} %refs_7_.1) | copy-start | bytes 4816900
  39.2 3.8 %collective-permute-start.14 = (f32[8,640]{1,0:T(8,128)S(1)}, f32[8,640]{1,0:T(8,128)S(1)}, u32[]{:S(2)}, u32[]{:S(2)}) collective-permute-start(f32[8,640]{1,0:T(8,128)S(1)} %get-tuple-element.137), channel_id=1, source_target_pairs={{0,112},{4,116},{8,120},{12,124},{16,0},{20,4},{24,8},{28,12},{32,... | collective-permute-start | bytes 61448 | tf_op jit(solution)/shard_map/ppermute | solution.py:32
  39.2 5.1 %collective-permute-start.15 = (f32[8,640]{1,0:T(8,128)S(1)}, f32[8,640]{1,0:T(8,128)S(1)}, u32[]{:S(2)}, u32[]{:S(2)}) collective-permute-start(f32[8,640]{1,0:T(8,128)S(1)} %get-tuple-element.138), channel_id=1, source_target_pairs={{0,16},{4,20},{8,24},{12,28},{16,32},{20,36},{24,40},{28,44},{32,4... | collective-permute-start | bytes 61448 | tf_op jit(solution)/shard_map/ppermute | solution.py:32
  41.2 4.7 %collective-permute-start.16 = (f32[8,640]{1,0:T(8,128)S(1)}, f32[8,640]{1,0:T(8,128)S(1)}, u32[]{:S(2)}, u32[]{:S(2)}) collective-permute-start(f32[8,640]{1,0:T(8,128)S(1)} %get-tuple-element.139), channel_id=1, source_target_pairs={{0,96},{4,100},{8,104},{12,108},{16,112},{20,116},{24,120},{28,124... | collective-permute-start | bytes 61448 | tf_op jit(solution)/shard_map/ppermute | solution.py:32
  41.2 1.5 %collective-permute-start.17 = (bf16[8,448]{1,0:T(8,128)(2,1)S(1)}, bf16[8,448]{1,0:T(8,128)(2,1)S(1)}, u32[]{:S(2)}, u32[]{:S(2)}) collective-permute-start(bf16[8,448]{1,0:T(8,128)(2,1)S(1)} %get-tuple-element.140), channel_id=1, source_target_pairs={{128,0},{0,128},{129,1},{1,129},{130,2},{2,130},{131,3},{3,131},{1... | collective-permute-start | bytes 21512 | tf_op jit(solution)/shard_map/ppermute | solution.py:671
  45.9 5.2 %collective-permute-start.20 = (f32[8,448]{1,0:T(8,128)S(1)}, f32[8,448]{1,0:T(8,128)S(1)}, u32[]{:S(2)}, u32[]{:S(2)}) collective-permute-start(f32[8,448]{1,0:T(8,128)S(1)} %get-tuple-element.152), channel_id=1, source_target_pairs={{0,2},{1,3},{2,0},{3,1},{4,6},{5,7},{6,4},{7,5},{8,10},{9,11},{10,... | collective-permute-start | bytes 43016 | tf_op jit(solution)/shard_map/ppermute | solution.py:28
  46.7 4.5 %collective-permute-start.19 = (f32[8,448]{1,0:T(8,128)S(1)}, f32[8,448]{1,0:T(8,128)S(1)}, u32[]{:S(2)}, u32[]{:S(2)}) collective-permute-start(f32[8,448]{1,0:T(8,128)S(1)} %get-tuple-element.151), channel_id=1, source_target_pairs={{0,3},{1,0},{2,1},{3,2},{4,7},{5,4},{6,5},{7,6},{8,11},{9,8},{10,9... | collective-permute-start | bytes 43016 | tf_op jit(solution)/shard_map/ppermute | solution.py:28
  49.7 4.9 %collective-permute-start.18 = (f32[8,448]{1,0:T(8,128)S(1)}, f32[8,448]{1,0:T(8,128)S(1)}, u32[]{:S(2)}, u32[]{:S(2)}) collective-permute-start(f32[8,448]{1,0:T(8,128)S(1)} %get-tuple-element.150), channel_id=1, source_target_pairs={{0,1},{1,2},{2,3},{3,0},{4,5},{5,6},{6,7},{7,4},{8,9},{9,10},{10,1... | collective-permute-start | bytes 43016 | tf_op jit(solution)/shard_map/ppermute | solution.py:28

commit v11 on v10

--- a/solution.py
+++ b/solution.py
@@ -649,8 +649,8 @@
     page = window_page(pages_first)
     row_pages = [x_shift(page, k) for k in (1, 3, 2)]
     row_pages[0], last_tokens, stored = lax.optimization_barrier((row_pages[0], tokens, stored))
-    received = [head_shift(tokens, 1), head_shift(tokens, 3), head_shift(last_tokens, 2)]
-    near, received = lax.optimization_barrier((bring_near(stored), received))
+    received = [head_shift(last_tokens, 1), head_shift(tokens, 3), head_shift(tokens, 2)]
+    near, received, row_pages = lax.optimization_barrier((bring_near(stored), received, row_pages))
     near_pages = jnp.stack([row_pages[0], page, row_pages[1], row_pages[2]])
     near_pages, received = lax.optimization_barrier((near_pages, received))
     far_pages = far_swap(near_pages)
@@ -660,20 +660,20 @@
         (own_pages, page_table, lengths, update)
     )
     near["own_pages"], tags = bring_windows(table, ends, own_pages)
-    swapped = [section_swap(update, k) for k in (0, 1, 3, 2)]
+    swapped = [section_swap(update, k) for k in (2, 1, 3, 0)]
     one_share, packed, key_new, value_new = project(tags, swapped, near)
-    asked = [packed] + [z_shift(packed, k) for k in (1, 7, 2)]
+    asked = [packed] + [z_shift(packed, k) for k in (2, 1, 7)]
     own = own_attention(lengths, packed, key_new, value_new, near)
     asked, own = lax.optimization_barrier((asked, own))
     answers = prompt_attention(asked, near_pages, far_pages)
     answers, one_share = lax.optimization_barrier((answers, one_share))
-    parts = [answers[0]] + [z_shift(answers[at], -k) for at, k in ((1, 1), (2, 7), (3, 2))]
+    parts = [answers[0]] + [z_shift(answers[at], -k) for at, k in ((1, 2), (2, 1), (3, 7))]
     one_back = lax.ppermute(one_share, "section", [(1, 0), (0, 1)])
     parts, one_back = lax.optimization_barrier((parts, one_back))
     slabs = combine(own, parts, out_w)
     section_index = lax.axis_index("section")
     total = one_share.astype(jnp.float32) + slabs[0]
-    for piece in [head_shift(slabs[k], k) for k in (1, 3, 2)]:
+    for piece in [head_shift(slabs[k], k) for k in (2, 1, 3)]:
         total = total + piece
     output = jnp.where(section_index == 0, one_back, total.astype(jnp.bfloat16))
     return output[None]

time: 55.5 us -> 50.3 us (0.906)
  the two profiles are of different devices: /device:TPU:4 before, /device:TPU:1 now
where the time goes in v11:
time: 50.3 us; the launch traced here: 50.1 us
  starting transfers between devices  33.8 us (67%)
  Pallas kernels  11 us (22%)
  waiting for transfers between devices  4.49 us (9%)
  other arithmetic  0.67 us (1%)
    pallas_call x8, Pallas kernels, kernel_call(): pl.pallas_call(run, out_shape=out_shape, in_specs=in_specs, out_specs=jax...  11 us
    ppermute x1, starting transfers between devices, far_swap(): lax.ppermute(value, ('section', 'req'), [(count + i, count + (i + count /...  8.82 us
    ppermute x6, starting transfers between devices, head_shift(): lax.ppermute(value, 'head', [(i, (i + steps) % count) for i in range(coun...  8.19 us
    ppermute x6, starting transfers between devices, z_shift(): lax.ppermute(value, 'req', [(z * XN + i, (z + steps) % ZN * XN + i) for z...  7.34 us
    ppermute x3, starting transfers between devices, x_shift(): lax.ppermute(value, 'req', [(z * XN + i, z * XN + (i + steps) % XN) for z...  5.12 us
    ppermute x4, starting transfers between devices, section_swap(): lax.ppermute(value, ('section', 'head'), there + [(b, a) for a, b in there])  4.01 us
    ppermute x6, waiting for transfers between devices, head_shift(): lax.ppermute(value, 'head', [(i, (i + steps) % count) for i in range(coun...  1.88 us
    ppermute x6, waiting for transfers between devices, z_shift(): lax.ppermute(value, 'req', [(z * XN + i, (z + steps) % ZN * XN + i) for z...  1.71 us
  transfers between devices with their start and end apart: 21, of which 6 were waited for; matrix products, arithmetic and copies ran while one was open for 0% of the time, Pallas kernels for 17%

profile of v11, /device:TPU:1, one launch (start us, length us, event | category | flops | bytes accessed | tf_op | source)
XLA Modules:
  0.0 50.1 jit_solution(13802099042675203643)
XLA Ops:
  0.0 1.0 %window_page.1 = bf16[448,128]{1,0:T(8,128)(2,1)S(1)} custom-call(bf16[1,2,448,128]{3,2,1,0:T(8,128)(2,1)} %bitcast.20), custom_call_target="tpu_custom_call" | custom-call | bytes 16777216 | tf_op jit(solution)/shard_map/window_page/pallas_call | solution.py:114
  1.1 2.1 %collective-permute-start = (bf16[448,128]{1,0:T(8,128)(2,1)S(1)}, bf16[448,128]{1,0:T(8,128)(2,1)S(1)}, u32[]{:S(2)}, u32[]{:S(2)}) collective-permute-start(bf16[448,128]{1,0:T(8,128)(2,1)S(1)} %window_page.1), channel_id=1, source_target_pairs={{0,4},{4,8},{8,12},{12,0},{16,20},{20,24},{24,28},{28,16},{32,36},... | collective-permute-start | bytes 344072 | tf_op jit(solution)/shard_map/ppermute | solution.py:40
  3.2 1.4 %collective-permute-start.4 = (bf16[448,128]{1,0:T(8,128)(2,1)S(1)}, bf16[448,128]{1,0:T(8,128)(2,1)S(1)}, u32[]{:S(2)}, u32[]{:S(2)}) collective-permute-start(bf16[448,128]{1,0:T(8,128)(2,1)S(1)} %window_page.1), channel_id=1, source_target_pairs={{0,12},{4,0},{8,4},{12,8},{16,28},{20,16},{24,20},{28,24},{32,44},... | collective-permute-start | bytes 344072 | tf_op jit(solution)/shard_map/ppermute | solution.py:40
  4.5 1.6 %collective-permute-start.5 = (bf16[448,128]{1,0:T(8,128)(2,1)S(1)}, bf16[448,128]{1,0:T(8,128)(2,1)S(1)}, u32[]{:S(2)}, u32[]{:S(2)}) collective-permute-start(bf16[448,128]{1,0:T(8,128)(2,1)S(1)} %window_page.1), channel_id=1, source_target_pairs={{0,8},{4,12},{8,0},{12,4},{16,24},{20,28},{24,16},{28,20},{32,40},... | collective-permute-start | bytes 344072 | tf_op jit(solution)/shard_map/ppermute | solution.py:40
  6.2 2.7 %collective-permute-start.2 = (bf16[8,448]{1,0:T(8,128)(2,1)}, bf16[8,448]{1,0:T(8,128)(2,1)S(1)}, u32[]{:S(2)}, u32[]{:S(2)}) collective-permute-start(bf16[8,448]{1,0:T(8,128)(2,1)} %refs_0_.3), channel_id=1, source_target_pairs={{0,3},{1,0},{2,1},{3,2},{4,7},{5,4},{6,5},{7,6},{8,11},{9,8},{10,9... | collective-permute-start | bytes 21512 | tf_op jit(solution)/shard_map/ppermute | solution.py:28
  8.9 0.3 collective-permute-start.3
  9.3 0.0 collective-permute-done
  9.3 0.7 %collective-permute-start.1 = (bf16[8,448]{1,0:T(8,128)(2,1)}, bf16[8,448]{1,0:T(8,128)(2,1)S(1)}, u32[]{:S(2)}, u32[]{:S(2)}) collective-permute-start(bf16[8,448]{1,0:T(8,128)(2,1)} %refs_0_.3), channel_id=1, source_target_pairs={{0,1},{1,2},{2,3},{3,0},{4,5},{5,6},{6,7},{7,4},{8,9},{9,10},{10,1... | collective-permute-start | bytes 21512 | tf_op jit(solution)/shard_map/ppermute | solution.py:28
  10.0 2.5 %bring_near.1 = (bf16[8,2,448]{2,1,0:T(2,128)(2,1)S(1)}, f32[3,448]{1,0:T(4,128)S(1)}, bf16[1792,128]{1,0:T(8,128)(2,1)S(1)}, f32[1,1792]{1,0:T(1,128)S(1)}, f32...) custom-call(bf16[8,2,448]{2,1,0:T(2,128)(2,1)} %refs_0_.2, ...), custom_call_target="tpu_custom_call" | custom-call | bytes 17799936 | tf_op jit(solution)/shard_map/bring_near/pallas_call | solution.py:114
  12.4 0.0 collective-permute-done.2.refs_2_
  12.5 0.7 %collective-permute-done.3.refs_3_ = bf16[8,448]{1,0:T(8,128)(2,1)S(1)} collective-permute-done((bf16[8,448]{1,0:T(8,128)(2,1)}, bf16[8,448]{1,0:T(8,128)(2,1)S(1)}, u32[]{:S(2)}, u32[]{:S(2)}) %collective-permute-start.3) | collective-permute-done | bytes 7200 | tf_op jit(solution)/shard_map/ppermute | solution.py:28
  13.1 0.0 collective-permute-done.4
  13.1 0.0 collective-permute-done.5
  13.1 0.1 collective-permute-done.1.refs_1_
  13.2 0.1 pad_maximum_fusion.refs_4_
  13.3 0.0 copy-start.2
  13.3 0.0 copy-start.3
  13.3 8.8 %collective-permute-start.13 = (bf16[4,448,128]{2,1,0:T(8,128)(2,1)S(1)}, bf16[4,448,128]{2,1,0:T(8,128)(2,1)S(1)}, u32[]{:S(2)}, u32[]{:S(2)}) collective-permute-start(bf16[4,448,128]{2,1,0:T(8,128)(2,1)S(1)} %pad_maximum_fusion.refs_4_), channel_id=1, source_target_pairs={{128,192},{132,196},{136,200},{140,204},{144,208},{148,212},{152,2... | collective-permute-start | bytes 1376264 | tf_op jit(solution)/shard_map/ppermute | solution.py:49
  22.2 0.1 collective-permute-start.6
  22.3 3.6 %collective-permute-start.7 = (bf16[8,1792]{1,0:T(8,128)(2,1)S(1)}, bf16[8,1792]{1,0:T(8,128)(2,1)S(1)}, u32[]{:S(2)}, u32[]{:S(2)}) collective-permute-start(bf16[8,1792]{1,0:T(8,128)(2,1)S(1)} %linear_layer.1), channel_id=1, source_target_pairs={{0,129},{1,130},{2,131},{3,128},{129,0},{130,1},{131,2},{128,3},{4... | collective-permute-start | bytes 86024 | tf_op jit(solution)/shard_map/ppermute | solution.py:59
  25.8 0.3 collective-permute-start.9
  26.2 3.0 %bring_windows.1 = (bf16[8,2,2,448,128]{4,3,2,1,0:T(8,128)(2,1)S(1)}, f32[8,128]{1,0:T(8,128)S(1)}) custom-call(s32[8,256]{1,0:T(8,128)S(1)} %copy-done.2, s32[8]{0:T(128)S(1)} %copy-done.3, bf16[16,2,448,128]{3,2,1,0:T(8,128)(2,1)} %bitcast.17), custom_call_target="tpu_custom_call" | custom-call | bytes 7340032 | tf_op jit(solution)/shard_map/bring_windows/pallas_call | solution.py:114
  29.2 0.0 collective-permute-done.6.refs_1_
  29.2 0.0 collective-permute-done.8.refs_3_
  29.2 0.0 collective-permute-done.9.refs_4_
  29.2 1.1 %project.1 = (bf16[8,448]{1,0:T(8,128)(2,1)S(1)}, bf16[8,512]{1,0:T(8,128)(2,1)S(1)}, bf16[8,448]{1,0:T(8,128)(2,1)S(1)}, bf16[8,448]{1,0:T(8,128)(2,1)S(1)}) custom-call(f32[8,128]{1,0:T(8,128)S(1)} %get-tuple-element.122.refs_0_, bf16[8,1792]{1,0:T(8,128)(2,1)S(1)} %collective-permute-done.6.refs_1_, bf16[8,1792]{1,0:T(8,128)(2,1)S(1)} %collective-permute-done.7.refs_2_, ...), custom_call_target="tpu_custom_call" | custom-call | tf_op jit(solution)/shard_map/project/pallas_call | solution.py:114
  30.3 1.3 %collective-permute-start.10 = (bf16[8,512]{1,0:T(8,128)(2,1)S(1)}, bf16[8,512]{1,0:T(8,128)(2,1)S(1)}, u32[]{:S(2)}, u32[]{:S(2)}) collective-permute-start(bf16[8,512]{1,0:T(8,128)(2,1)S(1)} %get-tuple-element.132.refs_1_.refs_0_), channel_id=1, source_target_pairs={{0,32},{4,36},{8,40},{12,44},{16,48},{20,52},{24,56},{28,60},{32,6... | collective-permute-start | bytes 24584 | tf_op jit(solution)/shard_map/ppermute | solution.py:32
  31.5 0.7 %collective-permute-start.11 = (bf16[8,512]{1,0:T(8,128)(2,1)S(1)}, bf16[8,512]{1,0:T(8,128)(2,1)S(1)}, u32[]{:S(2)}, u32[]{:S(2)}) collective-permute-start(bf16[8,512]{1,0:T(8,128)(2,1)S(1)} %get-tuple-element.132.refs_1_.refs_0_), channel_id=1, source_target_pairs={{0,16},{4,20},{8,24},{12,28},{16,32},{20,36},{24,40},{28,44},{32,4... | collective-permute-start | bytes 24584 | tf_op jit(solution)/shard_map/ppermute | solution.py:32
  32.2 2.0 %collective-permute-start.12 = (bf16[8,512]{1,0:T(8,128)(2,1)S(1)}, bf16[8,512]{1,0:T(8,128)(2,1)S(1)}, u32[]{:S(2)}, u32[]{:S(2)}) collective-permute-start(bf16[8,512]{1,0:T(8,128)(2,1)S(1)} %get-tuple-element.132.refs_1_.refs_0_), channel_id=1, source_target_pairs={{0,112},{4,116},{8,120},{12,124},{16,0},{20,4},{24,8},{28,12},{32,... | collective-permute-start | bytes 24584 | tf_op jit(solution)/shard_map/ppermute | solution.py:32
  34.2 1.9 %own_attention.1 = (f32[8,448]{1,0:T(8,128)S(1)}, f32[8,448]{1,0:T(8,128)S(1)}, f32[8,448]{1,0:T(8,128)S(1)}) custom-call(s32[8]{0:T(128)S(1)} %copy-done.3, bf16[8,512]{1,0:T(8,128)(2,1)S(1)} %get-tuple-element.132.refs_1_.refs_0_, bf16[8,448]{1,0:T(8,128)(2,1)S(1)} %get-tuple-element.126.refs_2_, bf16[8,448]{1,0:T(8,128)(2,1)S(1)} %get-tuple-element.127.refs_3_, ...), custom_call_target="tpu_custom_call" | custom-call | tf_op jit(solution)/shard_map/own_attention/pallas_call | solution.py:114
  36.1 0.0 collective-permute-done.11.refs_2_
  36.1 0.0 collective-permute-done.12.refs_3_
  36.2 0.9 %prompt_attention.1 = (f32[8,640]{1,0:T(8,128)S(1)}, f32[8,640]{1,0:T(8,128)S(1)}, f32[8,640]{1,0:T(8,128)S(1)}, f32[8,640]{1,0:T(8,128)S(1)}) custom-call(bf16[8,512]{1,0:T(8,128)(2,1)S(1)} %get-tuple-element.132.refs_1_.refs_0_, bf16[8,512]{1,0:T(8,128)(2,1)S(1)} %collective-permute-done.10.refs_1_, bf16[8,512]{1,0:T(8,128)(2,1)S(1)} %collective-permute-done.11.refs_2_, ...), custom_call_target="tpu_custom_call" | custom-call | tf_op jit(solution)/shard_map/prompt_attention/pallas_call | solution.py:114
  37.1 1.9 %collective-permute-start.14 = (f32[8,640]{1,0:T(8,128)S(1)}, f32[8,640]{1,0:T(8,128)S(1)}, u32[]{:S(2)}, u32[]{:S(2)}) collective-permute-start(f32[8,640]{1,0:T(8,128)S(1)} %get-tuple-element.143), channel_id=1, source_target_pairs={{0,96},{4,100},{8,104},{12,108},{16,112},{20,116},{24,120},{28,124... | collective-permute-start | bytes 61448 | tf_op jit(solution)/shard_map/ppermute | solution.py:32
  39.0 0.5 collective-permute-start.15
  39.5 1.0 %collective-permute-start.16 = (f32[8,640]{1,0:T(8,128)S(1)}, f32[8,640]{1,0:T(8,128)S(1)}, u32[]{:S(2)}, u32[]{:S(2)}) collective-permute-start(f32[8,640]{1,0:T(8,128)S(1)} %get-tuple-element.145), channel_id=1, source_target_pairs={{0,16},{4,20},{8,24},{12,28},{16,32},{20,36},{24,40},{28,44},{32,4... | collective-permute-start | bytes 61448 | tf_op jit(solution)/shard_map/ppermute | solution.py:32
  40.5 0.3 collective-permute-start.17
  40.8 0.9 %collective-permute-done.17 = bf16[8,448]{1,0:T(8,128)(2,1)S(1)} collective-permute-done((bf16[8,448]{1,0:T(8,128)(2,1)S(1)}, bf16[8,448]{1,0:T(8,128)(2,1)S(1)}, u32[]{:S(2)}, u32[]{:S(2)}) %collective-permute-start.17) | collective-permute-done | bytes 7200 | tf_op jit(solution)/shard_map/ppermute | solution.py:671
  41.7 0.0 collective-permute-done.14.refs_4_
  41.7 0.3 collective-permute-done.15.refs_5_
  42.0 1.4 %collective-permute-done.16.refs_6_ = f32[8,640]{1,0:T(8,128)S(1)} collective-permute-done((f32[8,640]{1,0:T(8,128)S(1)}, f32[8,640]{1,0:T(8,128)S(1)}, u32[]{:S(2)}, u32[]{:S(2)}) %collective-permute-start.16) | collective-permute-done | bytes 20512 | tf_op jit(solution)/shard_map/ppermute | solution.py:32
  43.4 0.6 %combine.1 = (f32[8,448]{1,0:T(8,128)S(1)}, f32[8,448]{1,0:T(8,128)S(1)}, f32[8,448]{1,0:T(8,128)S(1)}, f32[8,448]{1,0:T(8,128)S(1)}) custom-call(f32[8,448]{1,0:T(8,128)S(1)} %get-tuple-element.148.refs_0_, f32[8,448]{1,0:T(8,128)S(1)} %get-tuple-element.149.refs_1_, f32[8,448]{1,0:T(8,128)S(1)} %get-tuple-element.150.refs_2_, ...), custom_call_target="tpu_custom_call" | custom-call | tf_op jit(solution)/shard_map/combine/pallas_call | solution.py:114
  44.0 1.7 %collective-permute-start.18 = (f32[8,448]{1,0:T(8,128)S(1)}, f32[8,448]{1,0:T(8,128)S(1)}, u32[]{:S(2)}, u32[]{:S(2)}) collective-permute-start(f32[8,448]{1,0:T(8,128)S(1)} %get-tuple-element.156), channel_id=1, source_target_pairs={{0,2},{1,3},{2,0},{3,1},{4,6},{5,7},{6,4},{7,5},{8,10},{9,11},{10,... | collective-permute-start | bytes 43016 | tf_op jit(solution)/shard_map/ppermute | solution.py:28
  45.7 0.2 collective-permute-start.19
  45.9 2.4 %collective-permute-start.20 = (f32[8,448]{1,0:T(8,128)S(1)}, f32[8,448]{1,0:T(8,128)S(1)}, u32[]{:S(2)}, u32[]{:S(2)}) collective-permute-start(f32[8,448]{1,0:T(8,128)S(1)} %get-tuple-element.158), channel_id=1, source_target_pairs={{0,3},{1,0},{2,1},{3,2},{4,7},{5,4},{6,5},{7,6},{8,11},{9,8},{10,9... | collective-permute-start | bytes 43016 | tf_op jit(solution)/shard_map/ppermute | solution.py:28
  48.4 0.0 collective-permute-done.18
  48.4 1.1 %collective-permute-done.19 = f32[8,448]{1,0:T(8,128)S(1)} collective-permute-done((f32[8,448]{1,0:T(8,128)S(1)}, f32[8,448]{1,0:T(8,128)S(1)}, u32[]{:S(2)}, u32[]{:S(2)}) %collective-permute-start.19) | collective-permute-done | bytes 14368 | tf_op jit(solution)/shard_map/ppermute | solution.py:28
  49.5 0.6 %fusion.1 = bf16[1,8,448]{2,1,0:T(8,128)(2,1)} fusion(bf16[8,448]{1,0:T(8,128)(2,1)S(1)} %collective-permute-done.17, f32[8,448]{1,0:T(8,128)S(1)} %collective-permute-done.20, f32[8,448]{1,0:T(8,128)S(1)} %collective-permute-done.19, f32[8,448]{1,0:T(8,128)S(1)} %collective-permute-done.18, f32[8,448]{1,0:T(8,128)S(1)} %get-tuple-element.155, ...), kind=kLoop, calls=%fused_computation.3 | loop fusion | flops 25088 | bytes 78849 | tf_op jit(solution)/shard_map/broadcast_in_dim | solution.py:679
  (12 shorter events, 0.0 us)
Async XLA Ops:
  1.1 8.2 %collective-permute-start = (bf16[448,128]{1,0:T(8,128)(2,1)S(1)}, bf16[448,128]{1,0:T(8,128)(2,1)S(1)}, u32[]{:S(2)}, u32[]{:S(2)}) collective-permute-start(bf16[448,128]{1,0:T(8,128)(2,1)S(1)} %window_page.1), channel_id=1, source_target_pairs={{0,4},{4,8},{8,12},{12,0},{16,20},{20,24},{24,28},{28,16},{32,36},... | collective-permute-start | bytes 344072 | tf_op jit(solution)/shard_map/ppermute | solution.py:40
  3.2 10.0 %collective-permute-start.4 = (bf16[448,128]{1,0:T(8,128)(2,1)S(1)}, bf16[448,128]{1,0:T(8,128)(2,1)S(1)}, u32[]{:S(2)}, u32[]{:S(2)}) collective-permute-start(bf16[448,128]{1,0:T(8,128)(2,1)S(1)} %window_page.1), channel_id=1, source_target_pairs={{0,12},{4,0},{8,4},{12,8},{16,28},{20,16},{24,20},{28,24},{32,44},... | collective-permute-start | bytes 344072 | tf_op jit(solution)/shard_map/ppermute | solution.py:40
  4.5 8.6 %collective-permute-start.5 = (bf16[448,128]{1,0:T(8,128)(2,1)S(1)}, bf16[448,128]{1,0:T(8,128)(2,1)S(1)}, u32[]{:S(2)}, u32[]{:S(2)}) collective-permute-start(bf16[448,128]{1,0:T(8,128)(2,1)S(1)} %window_page.1), channel_id=1, source_target_pairs={{0,8},{4,12},{8,0},{12,4},{16,24},{20,28},{24,16},{28,20},{32,40},... | collective-permute-start | bytes 344072 | tf_op jit(solution)/shard_map/ppermute | solution.py:40
  6.2 6.3 %collective-permute-start.2 = (bf16[8,448]{1,0:T(8,128)(2,1)}, bf16[8,448]{1,0:T(8,128)(2,1)S(1)}, u32[]{:S(2)}, u32[]{:S(2)}) collective-permute-start(bf16[8,448]{1,0:T(8,128)(2,1)} %refs_0_.3), channel_id=1, source_target_pairs={{0,3},{1,0},{2,1},{3,2},{4,7},{5,4},{6,5},{7,6},{8,11},{9,8},{10,9... | collective-permute-start | bytes 21512 | tf_op jit(solution)/shard_map/ppermute | solution.py:28
  8.9 4.2 %collective-permute-start.3 = (bf16[8,448]{1,0:T(8,128)(2,1)}, bf16[8,448]{1,0:T(8,128)(2,1)S(1)}, u32[]{:S(2)}, u32[]{:S(2)}) collective-permute-start(bf16[8,448]{1,0:T(8,128)(2,1)} %refs_0_.3), channel_id=1, source_target_pairs={{0,2},{1,3},{2,0},{3,1},{4,6},{5,7},{6,4},{7,5},{8,10},{9,11},{10,... | collective-permute-start | bytes 21512 | tf_op jit(solution)/shard_map/ppermute | solution.py:28
  9.3 12.9 %copy-start.1 = (bf16[8,448]{1,0:T(8,128)(2,1)S(1)}, bf16[8,448]{1,0:T(8,128)(2,1)}, u32[]{:S(2)}) copy-start(bf16[8,448]{1,0:T(8,128)(2,1)} %refs_0_.3) | copy-start | bytes 21508
  9.3 3.9 %collective-permute-start.1 = (bf16[8,448]{1,0:T(8,128)(2,1)}, bf16[8,448]{1,0:T(8,128)(2,1)S(1)}, u32[]{:S(2)}, u32[]{:S(2)}) collective-permute-start(bf16[8,448]{1,0:T(8,128)(2,1)} %refs_0_.3), channel_id=1, source_target_pairs={{0,1},{1,2},{2,3},{3,0},{4,5},{5,6},{6,7},{7,4},{8,9},{9,10},{10,1... | collective-permute-start | bytes 21512 | tf_op jit(solution)/shard_map/ppermute | solution.py:28
  13.3 12.9 %copy-start.2 = (s32[8,256]{1,0:T(8,128)S(1)}, s32[8,256]{1,0:T(8,128)}, u32[]{:S(2)}) copy-start(s32[8,256]{1,0:T(8,128)} %refs_0_.4) | copy-start | bytes 24580
  13.3 12.9 %copy-start.3 = (s32[8]{0:T(128)S(1)}, s32[8]{0:T(128)}, u32[]{:S(2)}) copy-start(s32[8]{0:T(128)} %refs_0_.5) | copy-start | bytes 100
  13.3 22.8 %collective-permute-start.13 = (bf16[4,448,128]{2,1,0:T(8,128)(2,1)S(1)}, bf16[4,448,128]{2,1,0:T(8,128)(2,1)S(1)}, u32[]{:S(2)}, u32[]{:S(2)}) collective-permute-start(bf16[4,448,128]{2,1,0:T(8,128)(2,1)S(1)} %pad_maximum_fusion.refs_4_), channel_id=1, source_target_pairs={{128,192},{132,196},{136,200},{140,204},{144,208},{148,212},{152,2... | collective-permute-start | bytes 1376264 | tf_op jit(solution)/shard_map/ppermute | solution.py:49
  22.2 7.0 %collective-permute-start.6 = (bf16[8,1792]{1,0:T(8,128)(2,1)S(1)}, bf16[8,1792]{1,0:T(8,128)(2,1)S(1)}, u32[]{:S(2)}, u32[]{:S(2)}) collective-permute-start(bf16[8,1792]{1,0:T(8,128)(2,1)S(1)} %linear_layer.1), channel_id=1, source_target_pairs={{0,130},{1,131},{2,128},{3,129},{130,0},{131,1},{128,2},{129,3},{4... | collective-permute-start | bytes 86024 | tf_op jit(solution)/shard_map/ppermute | solution.py:59
  22.3 6.9 %collective-permute-start.7 = (bf16[8,1792]{1,0:T(8,128)(2,1)S(1)}, bf16[8,1792]{1,0:T(8,128)(2,1)S(1)}, u32[]{:S(2)}, u32[]{:S(2)}) collective-permute-start(bf16[8,1792]{1,0:T(8,128)(2,1)S(1)} %linear_layer.1), channel_id=1, source_target_pairs={{0,129},{1,130},{2,131},{3,128},{129,0},{130,1},{131,2},{128,3},{4... | collective-permute-start | bytes 86024 | tf_op jit(solution)/shard_map/ppermute | solution.py:59
  25.8 3.4 %collective-permute-start.8 = (bf16[8,1792]{1,0:T(8,128)(2,1)S(1)}, bf16[8,1792]{1,0:T(8,128)(2,1)S(1)}, u32[]{:S(2)}, u32[]{:S(2)}) collective-permute-start(bf16[8,1792]{1,0:T(8,128)(2,1)S(1)} %linear_layer.1), channel_id=1, source_target_pairs={{0,131},{1,128},{2,129},{3,130},{131,0},{128,1},{129,2},{130,3},{4... | collective-permute-start | bytes 86024 | tf_op jit(solution)/shard_map/ppermute | solution.py:59
  25.8 3.4 %collective-permute-start.9 = (bf16[8,1792]{1,0:T(8,128)(2,1)S(1)}, bf16[8,1792]{1,0:T(8,128)(2,1)S(1)}, u32[]{:S(2)}, u32[]{:S(2)}) collective-permute-start(bf16[8,1792]{1,0:T(8,128)(2,1)S(1)} %linear_layer.1), channel_id=1, source_target_pairs={{0,128},{1,129},{2,130},{3,131},{128,0},{129,1},{130,2},{131,3},{4... | collective-permute-start | bytes 86024 | tf_op jit(solution)/shard_map/ppermute | solution.py:59
  30.3 5.8 %collective-permute-start.10 = (bf16[8,512]{1,0:T(8,128)(2,1)S(1)}, bf16[8,512]{1,0:T(8,128)(2,1)S(1)}, u32[]{:S(2)}, u32[]{:S(2)}) collective-permute-start(bf16[8,512]{1,0:T(8,128)(2,1)S(1)} %get-tuple-element.132.refs_1_.refs_0_), channel_id=1, source_target_pairs={{0,32},{4,36},{8,40},{12,44},{16,48},{20,52},{24,56},{28,60},{32,6... | collective-permute-start | bytes 24584 | tf_op jit(solution)/shard_map/ppermute | solution.py:32
  31.5 4.6 %collective-permute-start.11 = (bf16[8,512]{1,0:T(8,128)(2,1)S(1)}, bf16[8,512]{1,0:T(8,128)(2,1)S(1)}, u32[]{:S(2)}, u32[]{:S(2)}) collective-permute-start(bf16[8,512]{1,0:T(8,128)(2,1)S(1)} %get-tuple-element.132.refs_1_.refs_0_), channel_id=1, source_target_pairs={{0,16},{4,20},{8,24},{12,28},{16,32},{20,36},{24,40},{28,44},{32,4... | collective-permute-start | bytes 24584 | tf_op jit(solution)/shard_map/ppermute | solution.py:32
  32.2 3.9 %collective-permute-start.12 = (bf16[8,512]{1,0:T(8,128)(2,1)S(1)}, bf16[8,512]{1,0:T(8,128)(2,1)S(1)}, u32[]{:S(2)}, u32[]{:S(2)}) collective-permute-start(bf16[8,512]{1,0:T(8,128)(2,1)S(1)} %get-tuple-element.132.refs_1_.refs_0_), channel_id=1, source_target_pairs={{0,112},{4,116},{8,120},{12,124},{16,0},{20,4},{24,8},{28,12},{32,... | collective-permute-start | bytes 24584 | tf_op jit(solution)/shard_map/ppermute | solution.py:32
  34.2 9.2 %copy-start = (bf16[1,448,1792]{2,1,0:T(8,128)(2,1)S(1)}, bf16[1,448,1792]{2,1,0:T(8,128)(2,1)}, u32[]{:S(2)}) copy-start(bf16[1,448,1792]{2,1,0:T(8,128)(2,1)} %refs_7_.1) | copy-start | bytes 4816900
  37.1 4.6 %collective-permute-start.14 = (f32[8,640]{1,0:T(8,128)S(1)}, f32[8,640]{1,0:T(8,128)S(1)}, u32[]{:S(2)}, u32[]{:S(2)}) collective-permute-start(f32[8,640]{1,0:T(8,128)S(1)} %get-tuple-element.143), channel_id=1, source_target_pairs={{0,96},{4,100},{8,104},{12,108},{16,112},{20,116},{24,120},{28,124... | collective-permute-start | bytes 61448 | tf_op jit(solution)/shard_map/ppermute | solution.py:32
  39.0 3.0 %collective-permute-start.15 = (f32[8,640]{1,0:T(8,128)S(1)}, f32[8,640]{1,0:T(8,128)S(1)}, u32[]{:S(2)}, u32[]{:S(2)}) collective-permute-start(f32[8,640]{1,0:T(8,128)S(1)} %get-tuple-element.144), channel_id=1, source_target_pairs={{0,112},{4,116},{8,120},{12,124},{16,0},{20,4},{24,8},{28,12},{32,... | collective-permute-start | bytes 61448 | tf_op jit(solution)/shard_map/ppermute | solution.py:32
  39.5 3.8 %collective-permute-start.16 = (f32[8,640]{1,0:T(8,128)S(1)}, f32[8,640]{1,0:T(8,128)S(1)}, u32[]{:S(2)}, u32[]{:S(2)}) collective-permute-start(f32[8,640]{1,0:T(8,128)S(1)} %get-tuple-element.145), channel_id=1, source_target_pairs={{0,16},{4,20},{8,24},{12,28},{16,32},{20,36},{24,40},{28,44},{32,4... | collective-permute-start | bytes 61448 | tf_op jit(solution)/shard_map/ppermute | solution.py:32
  40.5 1.2 %collective-permute-start.17 = (bf16[8,448]{1,0:T(8,128)(2,1)S(1)}, bf16[8,448]{1,0:T(8,128)(2,1)S(1)}, u32[]{:S(2)}, u32[]{:S(2)}) collective-permute-start(bf16[8,448]{1,0:T(8,128)(2,1)S(1)} %get-tuple-element.146), channel_id=1, source_target_pairs={{128,0},{0,128},{129,1},{1,129},{130,2},{2,130},{131,3},{3,131},{1... | collective-permute-start | bytes 21512 | tf_op jit(solution)/shard_map/ppermute | solution.py:671
  44.0 4.4 %collective-permute-start.18 = (f32[8,448]{1,0:T(8,128)S(1)}, f32[8,448]{1,0:T(8,128)S(1)}, u32[]{:S(2)}, u32[]{:S(2)}) collective-permute-start(f32[8,448]{1,0:T(8,128)S(1)} %get-tuple-element.156), channel_id=1, source_target_pairs={{0,2},{1,3},{2,0},{3,1},{4,6},{5,7},{6,4},{7,5},{8,10},{9,11},{10,... | collective-permute-start | bytes 43016 | tf_op jit(solution)/shard_map/ppermute | solution.py:28
  45.7 3.8 %collective-permute-start.19 = (f32[8,448]{1,0:T(8,128)S(1)}, f32[8,448]{1,0:T(8,128)S(1)}, u32[]{:S(2)}, u32[]{:S(2)}) collective-permute-start(f32[8,448]{1,0:T(8,128)S(1)} %get-tuple-element.157), channel_id=1, source_target_pairs={{0,1},{1,2},{2,3},{3,0},{4,5},{5,6},{6,7},{7,4},{8,9},{9,10},{10,1... | collective-permute-start | bytes 43016 | tf_op jit(solution)/shard_map/ppermute | solution.py:28
  45.9 3.6 %collective-permute-start.20 = (f32[8,448]{1,0:T(8,128)S(1)}, f32[8,448]{1,0:T(8,128)S(1)}, u32[]{:S(2)}, u32[]{:S(2)}) collective-permute-start(f32[8,448]{1,0:T(8,128)S(1)} %get-tuple-element.158), channel_id=1, source_target_pairs={{0,3},{1,0},{2,1},{3,2},{4,7},{5,4},{6,5},{7,6},{8,11},{9,8},{10,9... | collective-permute-start | bytes 43016 | tf_op jit(solution)/shard_map/ppermute | solution.py:28

commit v12 on v11

--- a/solution.py
+++ b/solution.py
@@ -156,12 +156,16 @@
     conv_w,
     conv_state,
     value_w,
+    out_hbm,
+    update,
     out_w,
-    update,
+    sem,
 ):
     rows, share = t0.shape
     heads = share // HD
     span = TAYLOR * heads
+    copy = pltpu.make_async_copy(out_hbm.at[0], out_w, sem)
+    copy.start()
     by_state = expansion(128, SPREAD, heads)
     by_norm = expansion(128, TAYLOR_LANES, 1)
     expand = jnp.concatenate([by_state, by_norm], axis=1)
@@ -224,6 +228,7 @@
     older = conv_state[...].astype(jnp.float32)
     mixed = conv_w[0:1] * older[:, 0] + conv_w[1:2] * older[:, 1] + conv_w[2:3] * fresh
     total = tokens * 0.25
+    copy.wait()
     for h in range(heads):
         here = slice(h * rows, (h + 1) * rows)
         denominator = (
@@ -239,15 +244,15 @@
     update[...] = total.astype(jnp.bfloat16)
 
 
-def linear_layer(pieces, near):
+def linear_layer(pieces, near, out_w):
     return kernel_call(
         linear_kernel,
         0,
         "linear_layer",
-        jax.ShapeDtypeStruct((pieces[0].shape[0], near["out_w"].shape[1]), jnp.bfloat16),
-        [VMEM] * 12,
-        [],
-        (*pieces, *(near[name] for name in LINEAR_NEAR)),
+        jax.ShapeDtypeStruct((pieces[0].shape[0], out_w.shape[2]), jnp.bfloat16),
+        [VMEM] * 11 + [HBM],
+        [pltpu.VMEM(out_w.shape[1:], jnp.bfloat16), pltpu.SemaphoreType.DMA],
+        (*pieces, *(near[name] for name in LINEAR_NEAR), out_w),
     )
 
 
@@ -259,14 +264,18 @@
     p2,
     p3,
     gain,
-    v_w,
     qk_w,
+    v_hbm,
     one,
     asked,
     key_new,
     value_new,
+    v_w,
+    sem,
 ):
     rows, share = one.shape
+    copy = pltpu.make_async_copy(v_hbm.at[0], v_w, sem)
+    copy.start()
     heads = share // HD
     layer_one = sum(ref[...].astype(jnp.float32) for ref in (p0, p1, p2, p3)).astype(jnp.bfloat16)
     rounded = layer_one.astype(jnp.float32)
@@ -275,9 +284,6 @@
         mine = jnp.where(ids[2] == h, rounded[:, h * share : (h + 1) * share], mine)
     one[...] = mine.astype(jnp.bfloat16)
     normed = normed_rows(rounded, gain[...])
-    value_new[...] = lax.dot_general(
-        normed, v_w[...], FLAT, preferred_element_type=jnp.float32
-    ).astype(jnp.bfloat16)
     query_key = jnp.dot(normed, qk_w[...], preferred_element_type=jnp.float32)
     width = query_key.shape[1]
     lane = lanes_of((rows, LANES))
@@ -293,11 +299,15 @@
     query = jnp.where(lane == share + 1, tags[:, 1:2], query)
     asked[...] = query.astype(jnp.bfloat16)
     key_new[...] = key[:, :share].astype(jnp.bfloat16)
-
-
-def project(tags, pieces, near):
+    copy.wait()
+    value_new[...] = lax.dot_general(
+        normed, v_w[...], FLAT, preferred_element_type=jnp.float32
+    ).astype(jnp.bfloat16)
+
+
+def project(tags, pieces, near, value_w):
     rows = pieces[0].shape[0]
-    share = near["value_w"].shape[0]
+    share = value_w.shape[1]
     return kernel_call(
         project_kernel,
         1,
@@ -308,9 +318,9 @@
             jax.ShapeDtypeStruct((rows, share), jnp.bfloat16),
             jax.ShapeDtypeStruct((rows, share), jnp.bfloat16),
         ],
-        [VMEM] * 8,
-        [],
-        (tags, *pieces, near["gain"], near["value_w"], near["query_key_w"]),
+        [VMEM] * 7 + [HBM],
+        [pltpu.VMEM(value_w.shape[1:], jnp.bfloat16), pltpu.SemaphoreType.DMA],
+        (tags, *pieces, near["gain"], near["query_key_w"], value_w),
     )
 
 
@@ -320,10 +330,9 @@
 
 
 def own_kernel(
-    ids, lengths, asked, key_new, value_new, pages, summed_out, highest_out, total_out
+    ids, tags, asked, key_new, value_new, pages, summed_out, highest_out, total_out
 ):
     rows, share = key_new.shape
-    bounds = [(lengths[r], *window_pages(lengths, r)) for r in range(rows)]
     head = lax.broadcasted_iota(jnp.int32, (8, share), 0)
     lane = lanes_of((8, share))
     mine = (lane >= head * HD) & (lane < (head + 1) * HD)
@@ -337,14 +346,15 @@
     )
     new_score = jnp.sum(wide * keys, axis=-1, keepdims=True) * scale
     token = lanes_of((8 * rows, 2 * PAGE))
-    request = lax.broadcasted_iota(jnp.int32, (8 * rows, 2 * PAGE), 0) >> 3
-    length = jnp.zeros(token.shape, jnp.int32)
-    base = jnp.zeros(token.shape, jnp.int32)
-    for r in range(rows):
-        length = jnp.where(request == r, bounds[r][0], length)
-        second = jnp.where(bounds[r][1] != bounds[r][2], bounds[r][2] - 1, -MAXP) * PAGE
-        base = jnp.where(request == r, jnp.where(token < PAGE, bounds[r][1] * PAGE, second), base)
-    position = base + token
+
+    def by_request(at):
+        return jnp.concatenate(
+            [jnp.broadcast_to(tags[r : r + 1, at : at + 1], (8, 2 * PAGE)) for r in range(rows)],
+            axis=0,
+        )
+
+    length = by_request(2)
+    position = token.astype(jnp.float32) + jnp.where(token < PAGE, by_request(3), by_request(4))
     usable = (position >= length - WINDOW) & (position <= length - 2)
     scores = []
     for r in range(rows):
@@ -382,16 +392,16 @@
             ref[r : r + 1, :] = jnp.sum(jnp.where(mine, value, 0.0), axis=0, keepdims=True)
 
 
-def own_attention(lengths, asked, key_new, value_new, near):
+def own_attention(tags, asked, key_new, value_new, near):
     rows, share = key_new.shape
     return kernel_call(
         own_kernel,
         1,
         "own_attention",
         [jax.ShapeDtypeStruct((rows, share), jnp.float32)] * 3,
-        [SMEM] + [VMEM] * 4,
+        [VMEM] * 5,
         [],
-        (lengths, asked, key_new, value_new, near["own_pages"]),
+        (tags, asked, key_new, value_new, near["own_pages"]),
     )
 
 
@@ -459,7 +469,7 @@
     )
 
 
-def combine_kernel(ids, summed, highest, total, r0, r1, r2, r3, out_w, s0, s1, s2, s3):
+def combine_kernel(ids, summed, highest, total, r0, r1, r2, r3, update, out_w, s0, s1, s2, s3):
     rows, share = summed.shape
     heads = share // HD
     refs = (r0, r1, r2, r3)
@@ -480,24 +490,34 @@
     whole = total[...] * own_factor + prompt_total * prompt_factor
     attended = (summed[...] * own_factor + prompt_summed * prompt_factor) / whole
     second = jnp.dot(attended.astype(jnp.bfloat16), out_w[0], preferred_element_type=jnp.float32)
-    for steps, ref in enumerate((s0, s1, s2, s3)):
-        slab = second[:, :share]
+    write_slabs(ids, second, (s0, s1, s2, s3))
+
+
+def write_slabs(ids, rows_whole, refs):
+    heads = len(refs)
+    share = refs[0].shape[1]
+    for steps, ref in enumerate(refs):
+        slab = rows_whole[:, :share]
         for h in range(1, heads):
-            slab = jnp.where(
-                ((ids[2] + steps) & (heads - 1)) == h, second[:, h * share : (h + 1) * share], slab
-            )
+            there = rows_whole[:, h * share : (h + 1) * share]
+            slab = jnp.where(((ids[2] + steps) & (heads - 1)) == h, there, slab)
         ref[...] = slab
 
 
-def combine(own, parts, out_w):
+def own_slabs(ids, *refs):
+    write_slabs(ids, refs[7][...].astype(jnp.float32), refs[9:])
+
+
+def combine(own, parts, update, out_w):
     return kernel_call(
         combine_kernel,
         1,
         "combine",
         [jax.ShapeDtypeStruct(own[0].shape, jnp.float32)] * 4,
-        [VMEM] * 8,
+        [VMEM] * 9,
         [],
-        (*own, *parts, out_w),
+        (*own, *parts, update, out_w),
+        elsewhere=own_slabs,
     )
 
 
@@ -509,9 +529,8 @@
     "conv_w",
     "conv_state",
     "value_w",
-    "out_w",
 )
-WINDOW_NEAR = ("gain", "value_w", "query_key_w")
+WINDOW_NEAR = ("gain", "query_key_w")
 
 
 def bring_near(arrays):
@@ -565,11 +584,15 @@
     for copy in copies:
         copy.start()
     row = lax.broadcasted_iota(jnp.int32, tags.shape, 0)
-    first = lanes_of(tags.shape) == 0
+    lane = lanes_of(tags.shape)
     marks = jnp.zeros(tags.shape, jnp.int32)
     for r in range(rows):
-        start = jnp.minimum(lengths[r] - WINDOW, PAGE)
-        marks = jnp.where(row == r, jnp.where(first, table[r, 0], start), marks)
+        length = lengths[r]
+        first, last = window_pages(lengths, r)
+        second = jnp.where(first != last, last - 1, -MAXP) * PAGE
+        start = jnp.minimum(length - WINDOW, PAGE)
+        for at, mark in enumerate((table[r, 0], start, length, first * PAGE, second)):
+            marks = jnp.where((row == r) & (lane == at), mark, marks)
     tags[...] = marks.astype(jnp.float32)
     for copy in copies:
         copy.wait()
@@ -634,6 +657,7 @@
     lengths,
 ):
     pages_first = prompt_pages.transpose(0, 1, 3, 2)
+    value_w = value_w.transpose(0, 2, 1)
     stored = {
         "gain": norm_gain,
         "feature_w": feature_w,
@@ -641,8 +665,7 @@
         "lin_norm": lin_norm,
         "conv_w": conv_w,
         "conv_state": conv_state,
-        "value_w": value_w.transpose(0, 2, 1)[0],
-        "out_w": out_w[0],
+        "value_w": value_w[0],
         "query_key_w": query_key_w,
     }
 
@@ -654,29 +677,25 @@
     near_pages = jnp.stack([row_pages[0], page, row_pages[1], row_pages[2]])
     near_pages, received = lax.optimization_barrier((near_pages, received))
     far_pages = far_swap(near_pages)
-    update = linear_layer([tokens] + received, near)
+    update = linear_layer([tokens] + received, near, out_w)
     own_pages = own_pages.transpose(0, 1, 3, 2)
     own_pages, table, ends, update = lax.optimization_barrier(
         (own_pages, page_table, lengths, update)
     )
     near["own_pages"], tags = bring_windows(table, ends, own_pages)
     swapped = [section_swap(update, k) for k in (2, 1, 3, 0)]
-    one_share, packed, key_new, value_new = project(tags, swapped, near)
+    one_share, packed, key_new, value_new = project(tags, swapped, near, value_w)
     asked = [packed] + [z_shift(packed, k) for k in (2, 1, 7)]
-    own = own_attention(lengths, packed, key_new, value_new, near)
+    own = own_attention(tags, packed, key_new, value_new, near)
     asked, own = lax.optimization_barrier((asked, own))
     answers = prompt_attention(asked, near_pages, far_pages)
-    answers, one_share = lax.optimization_barrier((answers, one_share))
     parts = [answers[0]] + [z_shift(answers[at], -k) for at, k in ((1, 2), (2, 1), (3, 7))]
-    one_back = lax.ppermute(one_share, "section", [(1, 0), (0, 1)])
-    parts, one_back = lax.optimization_barrier((parts, one_back))
-    slabs = combine(own, parts, out_w)
-    section_index = lax.axis_index("section")
-    total = one_share.astype(jnp.float32) + slabs[0]
+    slabs = combine(own, parts, update, out_w)
+    here = lax.axis_index("section") == 1
+    total = jnp.where(here, one_share.astype(jnp.float32), 0.0) + slabs[0]
     for piece in [head_shift(slabs[k], k) for k in (2, 1, 3)]:
         total = total + piece
-    output = jnp.where(section_index == 0, one_back, total.astype(jnp.bfloat16))
-    return output[None]
+    return total.astype(jnp.bfloat16)[None]
 
 
 def solution(mesh):

time: 50.3 us -> 50.9 us (1.012)
  waiting for transfers between devices: 4.49 us -> 5.39 us
    ppermute x6, waiting for transfers between devices: 1.71 us -> 3.01 us  [z_shift(): lax.ppermute(value, 'req', [(z * XN + i, (z + steps) % ZN * XN + i) for z...]
    ppermute x1 -> x0, waiting for transfers between devices: 0.88 us -> none  [body(): one_back = lax.ppermute(one_share, 'section', [(1, 0), (0, 1)])]
  transfers between devices with their start and end apart: 21 -> 20, of which waited for: 6 -> 6; matrix products, arithmetic and copies ran while one was open for 0% -> 0% of each run, Pallas kernels for 17% -> 16%
where the time goes in v12:
time: 50.9 us; the launch traced here: 50.7 us
  starting transfers between devices  33.7 us (66%)
  Pallas kernels  10.8 us (21%)
  waiting for transfers between devices  5.39 us (11%)
  other arithmetic  0.67 us (1%)
    pallas_call x8, Pallas kernels, kernel_call(): pl.pallas_call(run, out_shape=out_shape, in_specs=in_specs, out_specs=jax...  10.8 us
    ppermute x1, starting transfers between devices, far_swap(): lax.ppermute(value, ('section', 'req'), [(count + i, count + (i + count /...  8.82 us
    ppermute x6, starting transfers between devices, head_shift(): lax.ppermute(value, 'head', [(i, (i + steps) % count) for i in range(coun...  8.07 us
    ppermute x6, starting transfers between devices, z_shift(): lax.ppermute(value, 'req', [(z * XN + i, (z + steps) % ZN * XN + i) for z...  7.66 us
    ppermute x3, starting transfers between devices, x_shift(): lax.ppermute(value, 'req', [(z * XN + i, z * XN + (i + steps) % XN) for z...  5.12 us
    ppermute x4, starting transfers between devices, section_swap(): lax.ppermute(value, ('section', 'head'), there + [(b, a) for a, b in there])  4.01 us
    ppermute x6, waiting for transfers between devices, z_shift(): lax.ppermute(value, 'req', [(z * XN + i, (z + steps) % ZN * XN + i) for z...  3.01 us
    ppermute x6, waiting for transfers between devices, head_shift(): lax.ppermute(value, 'head', [(i, (i + steps) % count) for i in range(coun...  2.36 us
  transfers between devices with their start and end apart: 20, of which 6 were waited for; matrix products, arithmetic and copies ran while one was open for 0% of the time, Pallas kernels for 16%

profile of v12, /device:TPU:1, one launch (start us, length us, event | category | flops | bytes accessed | tf_op | source)
XLA Modules:
  0.0 50.7 jit_solution(13184106233798056978)
XLA Ops:
  0.0 1.0 %window_page.1 = bf16[448,128]{1,0:T(8,128)(2,1)S(1)} custom-call(bf16[1,2,448,128]{3,2,1,0:T(8,128)(2,1)} %bitcast.19), custom_call_target="tpu_custom_call" | custom-call | bytes 16777216 | tf_op jit(solution)/shard_map/window_page/pallas_call | solution.py:114
  1.1 2.1 %collective-permute-start = (bf16[448,128]{1,0:T(8,128)(2,1)S(1)}, bf16[448,128]{1,0:T(8,128)(2,1)S(1)}, u32[]{:S(2)}, u32[]{:S(2)}) collective-permute-start(bf16[448,128]{1,0:T(8,128)(2,1)S(1)} %window_page.1), channel_id=1, source_target_pairs={{0,4},{4,8},{8,12},{12,0},{16,20},{20,24},{24,28},{28,16},{32,36},... | collective-permute-start | bytes 344072 | tf_op jit(solution)/shard_map/ppermute | solution.py:40
  3.2 1.4 %collective-permute-start.4 = (bf16[448,128]{1,0:T(8,128)(2,1)S(1)}, bf16[448,128]{1,0:T(8,128)(2,1)S(1)}, u32[]{:S(2)}, u32[]{:S(2)}) collective-permute-start(bf16[448,128]{1,0:T(8,128)(2,1)S(1)} %window_page.1), channel_id=1, source_target_pairs={{0,12},{4,0},{8,4},{12,8},{16,28},{20,16},{24,20},{28,24},{32,44},... | collective-permute-start | bytes 344072 | tf_op jit(solution)/shard_map/ppermute | solution.py:40
  4.5 1.6 %collective-permute-start.5 = (bf16[448,128]{1,0:T(8,128)(2,1)S(1)}, bf16[448,128]{1,0:T(8,128)(2,1)S(1)}, u32[]{:S(2)}, u32[]{:S(2)}) collective-permute-start(bf16[448,128]{1,0:T(8,128)(2,1)S(1)} %window_page.1), channel_id=1, source_target_pairs={{0,8},{4,12},{8,0},{12,4},{16,24},{20,28},{24,16},{28,20},{32,40},... | collective-permute-start | bytes 344072 | tf_op jit(solution)/shard_map/ppermute | solution.py:40
  6.2 2.7 %collective-permute-start.2 = (bf16[8,448]{1,0:T(8,128)(2,1)}, bf16[8,448]{1,0:T(8,128)(2,1)S(1)}, u32[]{:S(2)}, u32[]{:S(2)}) collective-permute-start(bf16[8,448]{1,0:T(8,128)(2,1)} %refs_0_.2), channel_id=1, source_target_pairs={{0,3},{1,0},{2,1},{3,2},{4,7},{5,4},{6,5},{7,6},{8,11},{9,8},{10,9... | collective-permute-start | bytes 21512 | tf_op jit(solution)/shard_map/ppermute | solution.py:28
  8.9 0.3 collective-permute-start.3
  9.3 0.0 collective-permute-done
  9.3 0.7 %collective-permute-start.1 = (bf16[8,448]{1,0:T(8,128)(2,1)}, bf16[8,448]{1,0:T(8,128)(2,1)S(1)}, u32[]{:S(2)}, u32[]{:S(2)}) collective-permute-start(bf16[8,448]{1,0:T(8,128)(2,1)} %refs_0_.2), channel_id=1, source_target_pairs={{0,1},{1,2},{2,3},{3,0},{4,5},{5,6},{6,7},{7,4},{8,9},{9,10},{10,1... | collective-permute-start | bytes 21512 | tf_op jit(solution)/shard_map/ppermute | solution.py:28
  10.0 2.0 %bring_near.1 = (bf16[8,2,448]{2,1,0:T(2,128)(2,1)S(1)}, f32[3,448]{1,0:T(4,128)S(1)}, bf16[1792,128]{1,0:T(8,128)(2,1)S(1)}, f32[1,1792]{1,0:T(1,128)S(1)}, f32...) custom-call(bf16[8,2,448]{2,1,0:T(2,128)(2,1)} %refs_0_.1, ...), custom_call_target="tpu_custom_call" | custom-call | bytes 14588672 | tf_op jit(solution)/shard_map/bring_near/pallas_call | solution.py:114
  12.0 0.0 collective-permute-done.2.refs_2_
  12.0 1.2 %collective-permute-done.3.refs_3_ = bf16[8,448]{1,0:T(8,128)(2,1)S(1)} collective-permute-done((bf16[8,448]{1,0:T(8,128)(2,1)}, bf16[8,448]{1,0:T(8,128)(2,1)S(1)}, u32[]{:S(2)}, u32[]{:S(2)}) %collective-permute-start.3) | collective-permute-done | bytes 7200 | tf_op jit(solution)/shard_map/ppermute | solution.py:28
  13.1 0.0 collective-permute-done.4
  13.1 0.0 collective-permute-done.5
  13.1 0.1 collective-permute-done.1.refs_1_
  13.2 0.1 pad_maximum_fusion.refs_4_
  13.3 0.0 copy-start.2
  13.3 0.0 copy-start.3
  13.3 8.8 %collective-permute-start.13 = (bf16[4,448,128]{2,1,0:T(8,128)(2,1)S(1)}, bf16[4,448,128]{2,1,0:T(8,128)(2,1)S(1)}, u32[]{:S(2)}, u32[]{:S(2)}) collective-permute-start(bf16[4,448,128]{2,1,0:T(8,128)(2,1)S(1)} %pad_maximum_fusion.refs_4_), channel_id=1, source_target_pairs={{128,192},{132,196},{136,200},{140,204},{144,208},{148,212},{152,2... | collective-permute-start | bytes 1376264 | tf_op jit(solution)/shard_map/ppermute | solution.py:49
  22.2 0.1 collective-permute-start.6
  22.3 3.1 %collective-permute-start.7 = (bf16[8,1792]{1,0:T(8,128)(2,1)S(1)}, bf16[8,1792]{1,0:T(8,128)(2,1)S(1)}, u32[]{:S(2)}, u32[]{:S(2)}) collective-permute-start(bf16[8,1792]{1,0:T(8,128)(2,1)S(1)} %linear_layer.1.refs_7_), channel_id=1, source_target_pairs={{0,129},{1,130},{2,131},{3,128},{129,0},{130,1},{131,2},{128,3},{4... | collective-permute-start | bytes 86024 | tf_op jit(solution)/shard_map/ppermute | solution.py:59
  25.3 0.0 collective-permute-start.8
  25.3 0.8 %collective-permute-start.9 = (bf16[8,1792]{1,0:T(8,128)(2,1)S(1)}, bf16[8,1792]{1,0:T(8,128)(2,1)S(1)}, u32[]{:S(2)}, u32[]{:S(2)}) collective-permute-start(bf16[8,1792]{1,0:T(8,128)(2,1)S(1)} %linear_layer.1.refs_7_), channel_id=1, source_target_pairs={{0,128},{1,129},{2,130},{3,131},{128,0},{129,1},{130,2},{131,3},{4... | collective-permute-start | bytes 86024 | tf_op jit(solution)/shard_map/ppermute | solution.py:59
  26.2 3.0 %bring_windows.1 = (bf16[8,2,2,448,128]{4,3,2,1,0:T(8,128)(2,1)S(1)}, f32[8,128]{1,0:T(8,128)S(1)}) custom-call(s32[8,256]{1,0:T(8,128)S(1)} %copy-done.2, s32[8]{0:T(128)S(1)} %copy-done.3, bf16[16,2,448,128]{3,2,1,0:T(8,128)(2,1)} %bitcast.17), custom_call_target="tpu_custom_call" | custom-call | bytes 7340032 | tf_op jit(solution)/shard_map/bring_windows/pallas_call | solution.py:114
  29.2 0.0 collective-permute-done.6.refs_1_
  29.2 0.0 collective-permute-done.8.refs_3_
  29.2 0.0 collective-permute-done.9.refs_4_
  29.2 2.0 %project.1 = (bf16[8,448]{1,0:T(8,128)(2,1)S(1)}, bf16[8,512]{1,0:T(8,128)(2,1)S(1)}, bf16[8,448]{1,0:T(8,128)(2,1)S(1)}, bf16[8,448]{1,0:T(8,128)(2,1)S(1)}) custom-call(f32[8,128]{1,0:T(8,128)S(1)} %get-tuple-element.106.refs_0_, bf16[8,1792]{1,0:T(8,128)(2,1)S(1)} %collective-permute-done.6.refs_1_, bf16[8,1792]{1,0:T(8,128)(2,1)S(1)} %collective-permute-done.7.refs_2_, ...), custom_call_target="tpu_custom_call" | custom-call | tf_op jit(solution)/shard_map/project/pallas_call | solution.py:114
  31.3 1.3 %collective-permute-start.10 = (bf16[8,512]{1,0:T(8,128)(2,1)S(1)}, bf16[8,512]{1,0:T(8,128)(2,1)S(1)}, u32[]{:S(2)}, u32[]{:S(2)}) collective-permute-start(bf16[8,512]{1,0:T(8,128)(2,1)S(1)} %get-tuple-element.120.refs_1_.refs_0_), channel_id=1, source_target_pairs={{0,32},{4,36},{8,40},{12,44},{16,48},{20,52},{24,56},{28,60},{32,6... | collective-permute-start | bytes 24584 | tf_op jit(solution)/shard_map/ppermute | solution.py:32
  32.5 0.7 %collective-permute-start.11 = (bf16[8,512]{1,0:T(8,128)(2,1)S(1)}, bf16[8,512]{1,0:T(8,128)(2,1)S(1)}, u32[]{:S(2)}, u32[]{:S(2)}) collective-permute-start(bf16[8,512]{1,0:T(8,128)(2,1)S(1)} %get-tuple-element.120.refs_1_.refs_0_), channel_id=1, source_target_pairs={{0,16},{4,20},{8,24},{12,28},{16,32},{20,36},{24,40},{28,44},{32,4... | collective-permute-start | bytes 24584 | tf_op jit(solution)/shard_map/ppermute | solution.py:32
  33.3 1.9 %collective-permute-start.12 = (bf16[8,512]{1,0:T(8,128)(2,1)S(1)}, bf16[8,512]{1,0:T(8,128)(2,1)S(1)}, u32[]{:S(2)}, u32[]{:S(2)}) collective-permute-start(bf16[8,512]{1,0:T(8,128)(2,1)S(1)} %get-tuple-element.120.refs_1_.refs_0_), channel_id=1, source_target_pairs={{0,112},{4,116},{8,120},{12,124},{16,0},{20,4},{24,8},{28,12},{32,... | collective-permute-start | bytes 24584 | tf_op jit(solution)/shard_map/ppermute | solution.py:32
  35.2 1.2 %own_attention.1 = (f32[8,448]{1,0:T(8,128)S(1)}, f32[8,448]{1,0:T(8,128)S(1)}, f32[8,448]{1,0:T(8,128)S(1)}) custom-call(f32[8,128]{1,0:T(8,128)S(1)} %get-tuple-element.106.refs_0_, bf16[8,512]{1,0:T(8,128)(2,1)S(1)} %get-tuple-element.120.refs_1_.refs_0_, bf16[8,448]{1,0:T(8,128)(2,1)S(1)} %get-tuple-element.111.refs_2_, ...), custom_call_target="tpu_custom_call" | custom-call | tf_op jit(solution)/shard_map/own_attention/pallas_call | solution.py:114
  36.4 0.0 collective-permute-done.11.refs_2_
  36.4 0.0 collective-permute-done.12.refs_3_
  36.5 0.9 %prompt_attention.1 = (f32[8,640]{1,0:T(8,128)S(1)}, f32[8,640]{1,0:T(8,128)S(1)}, f32[8,640]{1,0:T(8,128)S(1)}, f32[8,640]{1,0:T(8,128)S(1)}) custom-call(bf16[8,512]{1,0:T(8,128)(2,1)S(1)} %get-tuple-element.120.refs_1_.refs_0_, bf16[8,512]{1,0:T(8,128)(2,1)S(1)} %collective-permute-done.10.refs_1_, bf16[8,512]{1,0:T(8,128)(2,1)S(1)} %collective-permute-done.11.refs_2_, ...), custom_call_target="tpu_custom_call" | custom-call | tf_op jit(solution)/shard_map/prompt_attention/pallas_call | solution.py:114
  37.4 1.8 %collective-permute-start.14 = (f32[8,640]{1,0:T(8,128)S(1)}, f32[8,640]{1,0:T(8,128)S(1)}, u32[]{:S(2)}, u32[]{:S(2)}) collective-permute-start(f32[8,640]{1,0:T(8,128)S(1)} %get-tuple-element.126), channel_id=1, source_target_pairs={{0,96},{4,100},{8,104},{12,108},{16,112},{20,116},{24,120},{28,124... | collective-permute-start | bytes 61448 | tf_op jit(solution)/shard_map/ppermute | solution.py:32
  39.2 0.8 %collective-permute-start.15 = (f32[8,640]{1,0:T(8,128)S(1)}, f32[8,640]{1,0:T(8,128)S(1)}, u32[]{:S(2)}, u32[]{:S(2)}) collective-permute-start(f32[8,640]{1,0:T(8,128)S(1)} %get-tuple-element.127), channel_id=1, source_target_pairs={{0,112},{4,116},{8,120},{12,124},{16,0},{20,4},{24,8},{28,12},{32,... | collective-permute-start | bytes 61448 | tf_op jit(solution)/shard_map/ppermute | solution.py:32
  40.0 1.1 %collective-permute-start.16 = (f32[8,640]{1,0:T(8,128)S(1)}, f32[8,640]{1,0:T(8,128)S(1)}, u32[]{:S(2)}, u32[]{:S(2)}) collective-permute-start(f32[8,640]{1,0:T(8,128)S(1)} %get-tuple-element.128), channel_id=1, source_target_pairs={{0,16},{4,20},{8,24},{12,28},{16,32},{20,36},{24,40},{28,44},{32,4... | collective-permute-start | bytes 61448 | tf_op jit(solution)/shard_map/ppermute | solution.py:32
  41.1 0.1 collective-permute-done.14.refs_4_
  41.2 1.3 %collective-permute-done.15.refs_5_ = f32[8,640]{1,0:T(8,128)S(1)} collective-permute-done((f32[8,640]{1,0:T(8,128)S(1)}, f32[8,640]{1,0:T(8,128)S(1)}, u32[]{:S(2)}, u32[]{:S(2)}) %collective-permute-start.15) | collective-permute-done | bytes 20512 | tf_op jit(solution)/shard_map/ppermute | solution.py:32
  42.5 1.6 %collective-permute-done.16.refs_6_ = f32[8,640]{1,0:T(8,128)S(1)} collective-permute-done((f32[8,640]{1,0:T(8,128)S(1)}, f32[8,640]{1,0:T(8,128)S(1)}, u32[]{:S(2)}, u32[]{:S(2)}) %collective-permute-start.16) | collective-permute-done | bytes 20512 | tf_op jit(solution)/shard_map/ppermute | solution.py:32
  44.1 0.6 %combine.1 = (f32[8,448]{1,0:T(8,128)S(1)}, f32[8,448]{1,0:T(8,128)S(1)}, f32[8,448]{1,0:T(8,128)S(1)}, f32[8,448]{1,0:T(8,128)S(1)}) custom-call(f32[8,448]{1,0:T(8,128)S(1)} %get-tuple-element.117.refs_0_, f32[8,448]{1,0:T(8,128)S(1)} %get-tuple-element.118.refs_1_, f32[8,448]{1,0:T(8,128)S(1)} %get-tuple-element.119.refs_2_, ...), custom_call_target="tpu_custom_call" | custom-call | tf_op jit(solution)/shard_map/combine/pallas_call | solution.py:114
  44.7 1.6 %collective-permute-start.17 = (f32[8,448]{1,0:T(8,128)S(1)}, f32[8,448]{1,0:T(8,128)S(1)}, u32[]{:S(2)}, u32[]{:S(2)}) collective-permute-start(f32[8,448]{1,0:T(8,128)S(1)} %get-tuple-element.130), channel_id=1, source_target_pairs={{0,2},{1,3},{2,0},{3,1},{4,6},{5,7},{6,4},{7,5},{8,10},{9,11},{10,... | collective-permute-start | bytes 43016 | tf_op jit(solution)/shard_map/ppermute | solution.py:28
  46.3 0.1 collective-permute-start.18
  46.4 2.6 %collective-permute-start.19 = (f32[8,448]{1,0:T(8,128)S(1)}, f32[8,448]{1,0:T(8,128)S(1)}, u32[]{:S(2)}, u32[]{:S(2)}) collective-permute-start(f32[8,448]{1,0:T(8,128)S(1)} %get-tuple-element.132), channel_id=1, source_target_pairs={{0,3},{1,0},{2,1},{3,2},{4,7},{5,4},{6,5},{7,6},{8,11},{9,8},{10,9... | collective-permute-start | bytes 43016 | tf_op jit(solution)/shard_map/ppermute | solution.py:28
  49.0 0.0 collective-permute-done.17
  49.0 1.1 %collective-permute-done.18 = f32[8,448]{1,0:T(8,128)S(1)} collective-permute-done((f32[8,448]{1,0:T(8,128)S(1)}, f32[8,448]{1,0:T(8,128)S(1)}, u32[]{:S(2)}, u32[]{:S(2)}) %collective-permute-start.18) | collective-permute-done | bytes 14368 | tf_op jit(solution)/shard_map/ppermute | solution.py:28
  50.1 0.0 collective-permute-done.19
  50.1 0.6 %fusion = bf16[1,8,448]{2,1,0:T(8,128)(2,1)} fusion(f32[8,448]{1,0:T(8,128)S(1)} %collective-permute-done.19, f32[8,448]{1,0:T(8,128)S(1)} %collective-permute-done.18, f32[8,448]{1,0:T(8,128)S(1)} %collective-permute-done.17, f32[8,448]{1,0:T(8,128)S(1)} %get-tuple-element.129, bf16[8,448]{1,0:T(8,128)(2,1)S(1)} %get-tuple-element.109, pred[]{:T(512)S(6)} %eq.3), kind=kLoop, calls=%fused_computation.2 | loop fusion | flops 25088 | bytes 71681 | tf_op jit(solution)/shard_map/broadcast_in_dim | solution.py:698
  (10 shorter events, 0.0 us)
Async XLA Ops:
  1.1 8.2 %collective-permute-start = (bf16[448,128]{1,0:T(8,128)(2,1)S(1)}, bf16[448,128]{1,0:T(8,128)(2,1)S(1)}, u32[]{:S(2)}, u32[]{:S(2)}) collective-permute-start(bf16[448,128]{1,0:T(8,128)(2,1)S(1)} %window_page.1), channel_id=1, source_target_pairs={{0,4},{4,8},{8,12},{12,0},{16,20},{20,24},{24,28},{28,16},{32,36},... | collective-permute-start | bytes 344072 | tf_op jit(solution)/shard_map/ppermute | solution.py:40
  3.2 10.0 %collective-permute-start.4 = (bf16[448,128]{1,0:T(8,128)(2,1)S(1)}, bf16[448,128]{1,0:T(8,128)(2,1)S(1)}, u32[]{:S(2)}, u32[]{:S(2)}) collective-permute-start(bf16[448,128]{1,0:T(8,128)(2,1)S(1)} %window_page.1), channel_id=1, source_target_pairs={{0,12},{4,0},{8,4},{12,8},{16,28},{20,16},{24,20},{28,24},{32,44},... | collective-permute-start | bytes 344072 | tf_op jit(solution)/shard_map/ppermute | solution.py:40
  4.5 8.6 %collective-permute-start.5 = (bf16[448,128]{1,0:T(8,128)(2,1)S(1)}, bf16[448,128]{1,0:T(8,128)(2,1)S(1)}, u32[]{:S(2)}, u32[]{:S(2)}) collective-permute-start(bf16[448,128]{1,0:T(8,128)(2,1)S(1)} %window_page.1), channel_id=1, source_target_pairs={{0,8},{4,12},{8,0},{12,4},{16,24},{20,28},{24,16},{28,20},{32,40},... | collective-permute-start | bytes 344072 | tf_op jit(solution)/shard_map/ppermute | solution.py:40
  6.2 5.8 %collective-permute-start.2 = (bf16[8,448]{1,0:T(8,128)(2,1)}, bf16[8,448]{1,0:T(8,128)(2,1)S(1)}, u32[]{:S(2)}, u32[]{:S(2)}) collective-permute-start(bf16[8,448]{1,0:T(8,128)(2,1)} %refs_0_.2), channel_id=1, source_target_pairs={{0,3},{1,0},{2,1},{3,2},{4,7},{5,4},{6,5},{7,6},{8,11},{9,8},{10,9... | collective-permute-start | bytes 21512 | tf_op jit(solution)/shard_map/ppermute | solution.py:28
  8.9 4.2 %collective-permute-start.3 = (bf16[8,448]{1,0:T(8,128)(2,1)}, bf16[8,448]{1,0:T(8,128)(2,1)S(1)}, u32[]{:S(2)}, u32[]{:S(2)}) collective-permute-start(bf16[8,448]{1,0:T(8,128)(2,1)} %refs_0_.2), channel_id=1, source_target_pairs={{0,2},{1,3},{2,0},{3,1},{4,6},{5,7},{6,4},{7,5},{8,10},{9,11},{10,... | collective-permute-start | bytes 21512 | tf_op jit(solution)/shard_map/ppermute | solution.py:28
  9.3 12.9 %copy-start.1 = (bf16[8,448]{1,0:T(8,128)(2,1)S(1)}, bf16[8,448]{1,0:T(8,128)(2,1)}, u32[]{:S(2)}) copy-start(bf16[8,448]{1,0:T(8,128)(2,1)} %refs_0_.2) | copy-start | bytes 21508
  9.3 3.9 %collective-permute-start.1 = (bf16[8,448]{1,0:T(8,128)(2,1)}, bf16[8,448]{1,0:T(8,128)(2,1)S(1)}, u32[]{:S(2)}, u32[]{:S(2)}) collective-permute-start(bf16[8,448]{1,0:T(8,128)(2,1)} %refs_0_.2), channel_id=1, source_target_pairs={{0,1},{1,2},{2,3},{3,0},{4,5},{5,6},{6,7},{7,4},{8,9},{9,10},{10,1... | collective-permute-start | bytes 21512 | tf_op jit(solution)/shard_map/ppermute | solution.py:28
  13.3 12.9 %copy-start.2 = (s32[8,256]{1,0:T(8,128)S(1)}, s32[8,256]{1,0:T(8,128)}, u32[]{:S(2)}) copy-start(s32[8,256]{1,0:T(8,128)} %refs_0_.3) | copy-start | bytes 24580
  13.3 12.9 %copy-start.3 = (s32[8]{0:T(128)S(1)}, s32[8]{0:T(128)}, u32[]{:S(2)}) copy-start(s32[8]{0:T(128)} %refs_1_.1) | copy-start | bytes 100
  13.3 23.2 %collective-permute-start.13 = (bf16[4,448,128]{2,1,0:T(8,128)(2,1)S(1)}, bf16[4,448,128]{2,1,0:T(8,128)(2,1)S(1)}, u32[]{:S(2)}, u32[]{:S(2)}) collective-permute-start(bf16[4,448,128]{2,1,0:T(8,128)(2,1)S(1)} %pad_maximum_fusion.refs_4_), channel_id=1, source_target_pairs={{128,192},{132,196},{136,200},{140,204},{144,208},{148,212},{152,2... | collective-permute-start | bytes 1376264 | tf_op jit(solution)/shard_map/ppermute | solution.py:49
  22.2 7.0 %collective-permute-start.6 = (bf16[8,1792]{1,0:T(8,128)(2,1)S(1)}, bf16[8,1792]{1,0:T(8,128)(2,1)S(1)}, u32[]{:S(2)}, u32[]{:S(2)}) collective-permute-start(bf16[8,1792]{1,0:T(8,128)(2,1)S(1)} %linear_layer.1.refs_7_), channel_id=1, source_target_pairs={{0,130},{1,131},{2,128},{3,129},{130,0},{131,1},{128,2},{129,3},{4... | collective-permute-start | bytes 86024 | tf_op jit(solution)/shard_map/ppermute | solution.py:59
  22.3 6.9 %collective-permute-start.7 = (bf16[8,1792]{1,0:T(8,128)(2,1)S(1)}, bf16[8,1792]{1,0:T(8,128)(2,1)S(1)}, u32[]{:S(2)}, u32[]{:S(2)}) collective-permute-start(bf16[8,1792]{1,0:T(8,128)(2,1)S(1)} %linear_layer.1.refs_7_), channel_id=1, source_target_pairs={{0,129},{1,130},{2,131},{3,128},{129,0},{130,1},{131,2},{128,3},{4... | collective-permute-start | bytes 86024 | tf_op jit(solution)/shard_map/ppermute | solution.py:59
  25.3 3.9 %collective-permute-start.8 = (bf16[8,1792]{1,0:T(8,128)(2,1)S(1)}, bf16[8,1792]{1,0:T(8,128)(2,1)S(1)}, u32[]{:S(2)}, u32[]{:S(2)}) collective-permute-start(bf16[8,1792]{1,0:T(8,128)(2,1)S(1)} %linear_layer.1.refs_7_), channel_id=1, source_target_pairs={{0,131},{1,128},{2,129},{3,130},{131,0},{128,1},{129,2},{130,3},{4... | collective-permute-start | bytes 86024 | tf_op jit(solution)/shard_map/ppermute | solution.py:59
  25.3 3.9 %collective-permute-start.9 = (bf16[8,1792]{1,0:T(8,128)(2,1)S(1)}, bf16[8,1792]{1,0:T(8,128)(2,1)S(1)}, u32[]{:S(2)}, u32[]{:S(2)}) collective-permute-start(bf16[8,1792]{1,0:T(8,128)(2,1)S(1)} %linear_layer.1.refs_7_), channel_id=1, source_target_pairs={{0,128},{1,129},{2,130},{3,131},{128,0},{129,1},{130,2},{131,3},{4... | collective-permute-start | bytes 86024 | tf_op jit(solution)/shard_map/ppermute | solution.py:59
  31.3 5.2 %collective-permute-start.10 = (bf16[8,512]{1,0:T(8,128)(2,1)S(1)}, bf16[8,512]{1,0:T(8,128)(2,1)S(1)}, u32[]{:S(2)}, u32[]{:S(2)}) collective-permute-start(bf16[8,512]{1,0:T(8,128)(2,1)S(1)} %get-tuple-element.120.refs_1_.refs_0_), channel_id=1, source_target_pairs={{0,32},{4,36},{8,40},{12,44},{16,48},{20,52},{24,56},{28,60},{32,6... | collective-permute-start | bytes 24584 | tf_op jit(solution)/shard_map/ppermute | solution.py:32
  32.5 3.9 %collective-permute-start.11 = (bf16[8,512]{1,0:T(8,128)(2,1)S(1)}, bf16[8,512]{1,0:T(8,128)(2,1)S(1)}, u32[]{:S(2)}, u32[]{:S(2)}) collective-permute-start(bf16[8,512]{1,0:T(8,128)(2,1)S(1)} %get-tuple-element.120.refs_1_.refs_0_), channel_id=1, source_target_pairs={{0,16},{4,20},{8,24},{12,28},{16,32},{20,36},{24,40},{28,44},{32,4... | collective-permute-start | bytes 24584 | tf_op jit(solution)/shard_map/ppermute | solution.py:32
  33.3 3.2 %collective-permute-start.12 = (bf16[8,512]{1,0:T(8,128)(2,1)S(1)}, bf16[8,512]{1,0:T(8,128)(2,1)S(1)}, u32[]{:S(2)}, u32[]{:S(2)}) collective-permute-start(bf16[8,512]{1,0:T(8,128)(2,1)S(1)} %get-tuple-element.120.refs_1_.refs_0_), channel_id=1, source_target_pairs={{0,112},{4,116},{8,120},{12,124},{16,0},{20,4},{24,8},{28,12},{32,... | collective-permute-start | bytes 24584 | tf_op jit(solution)/shard_map/ppermute | solution.py:32
  35.2 8.9 %copy-start = (bf16[1,448,1792]{2,1,0:T(8,128)(2,1)S(1)}, bf16[1,448,1792]{2,1,0:T(8,128)(2,1)}, u32[]{:S(2)}) copy-start(bf16[1,448,1792]{2,1,0:T(8,128)(2,1)} %refs_8_.1) | copy-start | bytes 4816900
  37.4 3.8 %collective-permute-start.14 = (f32[8,640]{1,0:T(8,128)S(1)}, f32[8,640]{1,0:T(8,128)S(1)}, u32[]{:S(2)}, u32[]{:S(2)}) collective-permute-start(f32[8,640]{1,0:T(8,128)S(1)} %get-tuple-element.126), channel_id=1, source_target_pairs={{0,96},{4,100},{8,104},{12,108},{16,112},{20,116},{24,120},{28,124... | collective-permute-start | bytes 61448 | tf_op jit(solution)/shard_map/ppermute | solution.py:32
  39.2 3.3 %collective-permute-start.15 = (f32[8,640]{1,0:T(8,128)S(1)}, f32[8,640]{1,0:T(8,128)S(1)}, u32[]{:S(2)}, u32[]{:S(2)}) collective-permute-start(f32[8,640]{1,0:T(8,128)S(1)} %get-tuple-element.127), channel_id=1, source_target_pairs={{0,112},{4,116},{8,120},{12,124},{16,0},{20,4},{24,8},{28,12},{32,... | collective-permute-start | bytes 61448 | tf_op jit(solution)/shard_map/ppermute | solution.py:32
  40.0 4.1 %collective-permute-start.16 = (f32[8,640]{1,0:T(8,128)S(1)}, f32[8,640]{1,0:T(8,128)S(1)}, u32[]{:S(2)}, u32[]{:S(2)}) collective-permute-start(f32[8,640]{1,0:T(8,128)S(1)} %get-tuple-element.128), channel_id=1, source_target_pairs={{0,16},{4,20},{8,24},{12,28},{16,32},{20,36},{24,40},{28,44},{32,4... | collective-permute-start | bytes 61448 | tf_op jit(solution)/shard_map/ppermute | solution.py:32
  44.7 4.3 %collective-permute-start.17 = (f32[8,448]{1,0:T(8,128)S(1)}, f32[8,448]{1,0:T(8,128)S(1)}, u32[]{:S(2)}, u32[]{:S(2)}) collective-permute-start(f32[8,448]{1,0:T(8,128)S(1)} %get-tuple-element.130), channel_id=1, source_target_pairs={{0,2},{1,3},{2,0},{3,1},{4,6},{5,7},{6,4},{7,5},{8,10},{9,11},{10,... | collective-permute-start | bytes 43016 | tf_op jit(solution)/shard_map/ppermute | solution.py:28
  46.3 3.8 %collective-permute-start.18 = (f32[8,448]{1,0:T(8,128)S(1)}, f32[8,448]{1,0:T(8,128)S(1)}, u32[]{:S(2)}, u32[]{:S(2)}) collective-permute-start(f32[8,448]{1,0:T(8,128)S(1)} %get-tuple-element.131), channel_id=1, source_target_pairs={{0,1},{1,2},{2,3},{3,0},{4,5},{5,6},{6,7},{7,4},{8,9},{9,10},{10,1... | collective-permute-start | bytes 43016 | tf_op jit(solution)/shard_map/ppermute | solution.py:28
  46.4 3.7 %collective-permute-start.19 = (f32[8,448]{1,0:T(8,128)S(1)}, f32[8,448]{1,0:T(8,128)S(1)}, u32[]{:S(2)}, u32[]{:S(2)}) collective-permute-start(f32[8,448]{1,0:T(8,128)S(1)} %get-tuple-element.132), channel_id=1, source_target_pairs={{0,3},{1,0},{2,1},{3,2},{4,7},{5,4},{6,5},{7,6},{8,11},{9,8},{10,9... | collective-permute-start | bytes 43016 | tf_op jit(solution)/shard_map/ppermute | solution.py:28

commit v13 on v12

--- a/solution.py
+++ b/solution.py
@@ -265,17 +265,13 @@
     p3,
     gain,
     qk_w,
-    v_hbm,
+    v_w,
     one,
     asked,
     key_new,
     value_new,
-    v_w,
-    sem,
 ):
     rows, share = one.shape
-    copy = pltpu.make_async_copy(v_hbm.at[0], v_w, sem)
-    copy.start()
     heads = share // HD
     layer_one = sum(ref[...].astype(jnp.float32) for ref in (p0, p1, p2, p3)).astype(jnp.bfloat16)
     rounded = layer_one.astype(jnp.float32)
@@ -299,15 +295,14 @@
     query = jnp.where(lane == share + 1, tags[:, 1:2], query)
     asked[...] = query.astype(jnp.bfloat16)
     key_new[...] = key[:, :share].astype(jnp.bfloat16)
-    copy.wait()
     value_new[...] = lax.dot_general(
         normed, v_w[...], FLAT, preferred_element_type=jnp.float32
     ).astype(jnp.bfloat16)
 
 
-def project(tags, pieces, near, value_w):
+def project(tags, pieces, near):
     rows = pieces[0].shape[0]
-    share = value_w.shape[1]
+    share = near["value_w"].shape[0]
     return kernel_call(
         project_kernel,
         1,
@@ -318,9 +313,9 @@
             jax.ShapeDtypeStruct((rows, share), jnp.bfloat16),
             jax.ShapeDtypeStruct((rows, share), jnp.bfloat16),
         ],
-        [VMEM] * 7 + [HBM],
-        [pltpu.VMEM(value_w.shape[1:], jnp.bfloat16), pltpu.SemaphoreType.DMA],
-        (tags, *pieces, near["gain"], near["query_key_w"], value_w),
+        [VMEM] * 8,
+        [],
+        (tags, *pieces, near["gain"], near["query_key_w"], near["value_w"]),
     )
 
 
@@ -330,9 +325,33 @@
 
 
 def own_kernel(
-    ids, tags, asked, key_new, value_new, pages, summed_out, highest_out, total_out
+    ids,
+    table,
+    lengths,
+    tags,
+    asked,
+    key_new,
+    value_new,
+    key_pages,
+    own_hbm,
+    summed_out,
+    highest_out,
+    total_out,
+    value_pages,
+    sems,
 ):
     rows, share = key_new.shape
+    total_pages = own_hbm.shape[0]
+    copies = []
+    for r in range(rows):
+        for slot, logical in enumerate(window_pages(lengths, r)):
+            page = jnp.clip(table[r, logical] - GROUPS - ids[1] * total_pages, 0, total_pages - 1)
+            copies.append(
+                pltpu.make_async_copy(
+                    own_hbm.at[page, 1], value_pages.at[r, slot], sems.at[r, slot]
+                )
+            )
+            copies[-1].start()
     head = lax.broadcasted_iota(jnp.int32, (8, share), 0)
     lane = lanes_of((8, share))
     mine = (lane >= head * HD) & (lane < (head + 1) * HD)
@@ -362,7 +381,7 @@
         scores.append(
             jnp.concatenate(
                 [
-                    jnp.dot(low, pages[r, slot, 0], preferred_element_type=jnp.float32)
+                    jnp.dot(low, key_pages[r, slot], preferred_element_type=jnp.float32)
                     for slot in range(2)
                 ],
                 axis=1,
@@ -378,9 +397,10 @@
         low = exps[here].astype(jnp.bfloat16)
         found = exp_new[here] * new_value[r : r + 1]
         for slot in range(2):
+            copies[2 * r + slot].wait()
             found = found + lax.dot_general(
                 low[:, slot * PAGE : (slot + 1) * PAGE],
-                pages[r, slot, 1],
+                value_pages[r, slot],
                 FLAT,
                 preferred_element_type=jnp.float32,
             )
@@ -392,16 +412,19 @@
             ref[r : r + 1, :] = jnp.sum(jnp.where(mine, value, 0.0), axis=0, keepdims=True)
 
 
-def own_attention(tags, asked, key_new, value_new, near):
+def own_attention(table, lengths, tags, asked, key_new, value_new, near, own_pages):
     rows, share = key_new.shape
     return kernel_call(
         own_kernel,
         1,
         "own_attention",
         [jax.ShapeDtypeStruct((rows, share), jnp.float32)] * 3,
-        [VMEM] * 5,
-        [],
-        (tags, asked, key_new, value_new, near["own_pages"]),
+        [SMEM] * 2 + [VMEM] * 5 + [HBM],
+        [
+            pltpu.VMEM((rows, 2) + own_pages.shape[2:], jnp.bfloat16),
+            pltpu.SemaphoreType.DMA((rows, 2)),
+        ],
+        (table, lengths, tags, asked, key_new, value_new, near["own_keys"], own_pages),
     )
 
 
@@ -530,7 +553,7 @@
     "conv_state",
     "value_w",
 )
-WINDOW_NEAR = ("gain", "query_key_w")
+WINDOW_NEAR = ("gain", "value_w", "query_key_w")
 
 
 def bring_near(arrays):
@@ -579,7 +602,7 @@
         for slot, logical in enumerate(window_pages(lengths, r)):
             page = jnp.clip(table[r, logical] - GROUPS - ids[1] * total, 0, total - 1)
             copies.append(
-                pltpu.make_async_copy(own_hbm.at[page], own_near.at[r, slot], sems.at[r, slot])
+                pltpu.make_async_copy(own_hbm.at[page, 0], own_near.at[r, slot], sems.at[r, slot])
             )
     for copy in copies:
         copy.start()
@@ -600,7 +623,7 @@
 
 def bring_windows(table, lengths, own_pages):
     rows = lengths.shape[0]
-    windows = jax.ShapeDtypeStruct((rows, 2) + own_pages.shape[1:], own_pages.dtype)
+    windows = jax.ShapeDtypeStruct((rows, 2) + own_pages.shape[2:], own_pages.dtype)
     return kernel_call(
         window_kernel,
         1,
@@ -682,11 +705,11 @@
     own_pages, table, ends, update = lax.optimization_barrier(
         (own_pages, page_table, lengths, update)
     )
-    near["own_pages"], tags = bring_windows(table, ends, own_pages)
+    near["own_keys"], tags = bring_windows(table, ends, own_pages)
     swapped = [section_swap(update, k) for k in (2, 1, 3, 0)]
-    one_share, packed, key_new, value_new = project(tags, swapped, near, value_w)
+    one_share, packed, key_new, value_new = project(tags, swapped, near)
     asked = [packed] + [z_shift(packed, k) for k in (2, 1, 7)]
-    own = own_attention(tags, packed, key_new, value_new, near)
+    own = own_attention(table, ends, tags, packed, key_new, value_new, near, own_pages)
     asked, own = lax.optimization_barrier((asked, own))
     answers = prompt_attention(asked, near_pages, far_pages)
     parts = [answers[0]] + [z_shift(answers[at], -k) for at, k in ((1, 2), (2, 1), (3, 7))]

time: 50.9 us -> 52.2 us (1.026)
  Pallas kernels: 10.8 us -> 13.2 us
  starting transfers between devices: 33.7 us -> 33 us
  waiting for transfers between devices: 5.39 us -> 4.83 us
    pallas_call x8, Pallas kernels: 10.8 us -> 13.2 us  [kernel_call(): pl.pallas_call(run, out_shape=out_shape, in_specs=in_specs, out_specs=jax...]
    ppermute x6, starting transfers between devices: 7.66 us -> 6.58 us  [z_shift(): lax.ppermute(value, 'req', [(z * XN + i, (z + steps) % ZN * XN + i) for z...]
    ppermute x6, waiting for transfers between devices: 3.01 us -> 2.41 us  [z_shift(): lax.ppermute(value, 'req', [(z * XN + i, (z + steps) % ZN * XN + i) for z...]
  transfers between devices with their start and end apart: 20 -> 20, of which waited for: 6 -> 7; matrix products, arithmetic and copies ran while one was open for 0% -> 0% of each run, Pallas kernels for 16% -> 21%
where the time goes in v13:
time: 52.2 us; the launch traced here: 51.9 us
  starting transfers between devices  33 us (63%)
  Pallas kernels  13.2 us (25%)
  waiting for transfers between devices  4.83 us (9%)
  other arithmetic  0.67 us (1%)
    pallas_call x8, Pallas kernels, kernel_call(): pl.pallas_call(run, out_shape=out_shape, in_specs=in_specs, out_specs=jax...  13.2 us
    ppermute x1, starting transfers between devices, far_swap(): lax.ppermute(value, ('section', 'req'), [(count + i, count + (i + count /...  8.82 us
    ppermute x6, starting transfers between devices, head_shift(): lax.ppermute(value, 'head', [(i, (i + steps) % count) for i in range(coun...  8.49 us
    ppermute x6, starting transfers between devices, z_shift(): lax.ppermute(value, 'req', [(z * XN + i, (z + steps) % ZN * XN + i) for z...  6.58 us
    ppermute x3, starting transfers between devices, x_shift(): lax.ppermute(value, 'req', [(z * XN + i, z * XN + (i + steps) % XN) for z...  5.12 us
    ppermute x4, starting transfers between devices, section_swap(): lax.ppermute(value, ('section', 'head'), there + [(b, a) for a, b in there])  4.01 us
    ppermute x6, waiting for transfers between devices, z_shift(): lax.ppermute(value, 'req', [(z * XN + i, (z + steps) % ZN * XN + i) for z...  2.41 us
    ppermute x6, waiting for transfers between devices, head_shift(): lax.ppermute(value, 'head', [(i, (i + steps) % count) for i in range(coun...  1.89 us
  transfers between devices with their start and end apart: 20, of which 7 were waited for; matrix products, arithmetic and copies ran while one was open for 0% of the time, Pallas kernels for 21%

profile of v13, /device:TPU:1, one launch (start us, length us, event | category | flops | bytes accessed | tf_op | source)
XLA Modules:
  0.0 51.9 jit_solution(15928735818655694741)
XLA Ops:
  0.0 1.0 %window_page.1 = bf16[448,128]{1,0:T(8,128)(2,1)S(1)} custom-call(bf16[1,2,448,128]{3,2,1,0:T(8,128)(2,1)} %bitcast.19), custom_call_target="tpu_custom_call" | custom-call | bytes 16777216 | tf_op jit(solution)/shard_map/window_page/pallas_call | solution.py:114
  1.1 2.1 %collective-permute-start = (bf16[448,128]{1,0:T(8,128)(2,1)S(1)}, bf16[448,128]{1,0:T(8,128)(2,1)S(1)}, u32[]{:S(2)}, u32[]{:S(2)}) collective-permute-start(bf16[448,128]{1,0:T(8,128)(2,1)S(1)} %window_page.1), channel_id=1, source_target_pairs={{0,4},{4,8},{8,12},{12,0},{16,20},{20,24},{24,28},{28,16},{32,36},... | collective-permute-start | bytes 344072 | tf_op jit(solution)/shard_map/ppermute | solution.py:40
  3.2 1.4 %collective-permute-start.4 = (bf16[448,128]{1,0:T(8,128)(2,1)S(1)}, bf16[448,128]{1,0:T(8,128)(2,1)S(1)}, u32[]{:S(2)}, u32[]{:S(2)}) collective-permute-start(bf16[448,128]{1,0:T(8,128)(2,1)S(1)} %window_page.1), channel_id=1, source_target_pairs={{0,12},{4,0},{8,4},{12,8},{16,28},{20,16},{24,20},{28,24},{32,44},... | collective-permute-start | bytes 344072 | tf_op jit(solution)/shard_map/ppermute | solution.py:40
  4.5 1.6 %collective-permute-start.5 = (bf16[448,128]{1,0:T(8,128)(2,1)S(1)}, bf16[448,128]{1,0:T(8,128)(2,1)S(1)}, u32[]{:S(2)}, u32[]{:S(2)}) collective-permute-start(bf16[448,128]{1,0:T(8,128)(2,1)S(1)} %window_page.1), channel_id=1, source_target_pairs={{0,8},{4,12},{8,0},{12,4},{16,24},{20,28},{24,16},{28,20},{32,40},... | collective-permute-start | bytes 344072 | tf_op jit(solution)/shard_map/ppermute | solution.py:40
  6.2 2.7 %collective-permute-start.2 = (bf16[8,448]{1,0:T(8,128)(2,1)}, bf16[8,448]{1,0:T(8,128)(2,1)S(1)}, u32[]{:S(2)}, u32[]{:S(2)}) collective-permute-start(bf16[8,448]{1,0:T(8,128)(2,1)} %refs_0_.2), channel_id=1, source_target_pairs={{0,3},{1,0},{2,1},{3,2},{4,7},{5,4},{6,5},{7,6},{8,11},{9,8},{10,9... | collective-permute-start | bytes 21512 | tf_op jit(solution)/shard_map/ppermute | solution.py:28
  8.9 0.3 collective-permute-start.3
  9.3 0.0 collective-permute-done
  9.3 0.7 %collective-permute-start.1 = (bf16[8,448]{1,0:T(8,128)(2,1)}, bf16[8,448]{1,0:T(8,128)(2,1)S(1)}, u32[]{:S(2)}, u32[]{:S(2)}) collective-permute-start(bf16[8,448]{1,0:T(8,128)(2,1)} %refs_0_.2), channel_id=1, source_target_pairs={{0,1},{1,2},{2,3},{3,0},{4,5},{5,6},{6,7},{7,4},{8,9},{9,10},{10,1... | collective-permute-start | bytes 21512 | tf_op jit(solution)/shard_map/ppermute | solution.py:28
  10.0 2.5 %bring_near.1 = (bf16[8,2,448]{2,1,0:T(2,128)(2,1)S(1)}, f32[3,448]{1,0:T(4,128)S(1)}, bf16[1792,128]{1,0:T(8,128)(2,1)S(1)}, f32[1,1792]{1,0:T(1,128)S(1)}, f32...) custom-call(bf16[8,2,448]{2,1,0:T(2,128)(2,1)} %refs_0_.1, ...), custom_call_target="tpu_custom_call" | custom-call | bytes 14588672 | tf_op jit(solution)/shard_map/bring_near/pallas_call | solution.py:114
  12.4 0.0 collective-permute-done.2.refs_2_
  12.4 0.7 %collective-permute-done.3.refs_3_ = bf16[8,448]{1,0:T(8,128)(2,1)S(1)} collective-permute-done((bf16[8,448]{1,0:T(8,128)(2,1)}, bf16[8,448]{1,0:T(8,128)(2,1)S(1)}, u32[]{:S(2)}, u32[]{:S(2)}) %collective-permute-start.3) | collective-permute-done | bytes 7200 | tf_op jit(solution)/shard_map/ppermute | solution.py:28
  13.1 0.0 collective-permute-done.4
  13.1 0.0 collective-permute-done.5
  13.1 0.1 collective-permute-done.1.refs_1_
  13.2 0.1 pad_maximum_fusion.refs_4_
  13.3 0.0 copy-start.1
  13.3 0.0 copy-start.3
  13.3 8.8 %collective-permute-start.13 = (bf16[4,448,128]{2,1,0:T(8,128)(2,1)S(1)}, bf16[4,448,128]{2,1,0:T(8,128)(2,1)S(1)}, u32[]{:S(2)}, u32[]{:S(2)}) collective-permute-start(bf16[4,448,128]{2,1,0:T(8,128)(2,1)S(1)} %pad_maximum_fusion.refs_4_), channel_id=1, source_target_pairs={{128,192},{132,196},{136,200},{140,204},{144,208},{148,212},{152,2... | collective-permute-start | bytes 1376264 | tf_op jit(solution)/shard_map/ppermute | solution.py:49
  22.2 0.1 collective-permute-start.6
  22.3 3.6 %collective-permute-start.7 = (bf16[8,1792]{1,0:T(8,128)(2,1)S(1)}, bf16[8,1792]{1,0:T(8,128)(2,1)S(1)}, u32[]{:S(2)}, u32[]{:S(2)}) collective-permute-start(bf16[8,1792]{1,0:T(8,128)(2,1)S(1)} %linear_layer.1.refs_7_), channel_id=1, source_target_pairs={{0,129},{1,130},{2,131},{3,128},{129,0},{130,1},{131,2},{128,3},{4... | collective-permute-start | bytes 86024 | tf_op jit(solution)/shard_map/ppermute | solution.py:59
  25.8 0.0 collective-permute-start.8
  25.8 0.3 collective-permute-start.9
  26.2 2.4 %bring_windows.1 = (bf16[8,2,448,128]{3,2,1,0:T(8,128)(2,1)S(1)}, f32[8,128]{1,0:T(8,128)S(1)}) custom-call(s32[8,256]{1,0:T(8,128)S(1)} %copy-done.1, s32[8]{0:T(128)S(1)} %copy-done.3, bf16[16,2,448,128]{3,2,1,0:T(8,128)(2,1)} %bitcast.15), custom_call_target="tpu_custom_call" | custom-call | bytes 3670016 | tf_op jit(solution)/shard_map/bring_windows/pallas_call | solution.py:114
  28.6 0.0 collective-permute-done.6.refs_1_
  28.6 0.0 collective-permute-done.7.refs_2_
  28.6 0.5 collective-permute-done.8.refs_3_
  29.1 0.0 collective-permute-done.9.refs_4_
  29.1 1.0 %project.1 = (bf16[8,448]{1,0:T(8,128)(2,1)S(1)}, bf16[8,512]{1,0:T(8,128)(2,1)S(1)}, bf16[8,448]{1,0:T(8,128)(2,1)S(1)}, bf16[8,448]{1,0:T(8,128)(2,1)S(1)}) custom-call(f32[8,128]{1,0:T(8,128)S(1)} %get-tuple-element.106.refs_0_.refs_2_, bf16[8,1792]{1,0:T(8,128)(2,1)S(1)} %collective-permute-done.6.refs_1_, ...), custom_call_target="tpu_custom_call" | custom-call | tf_op jit(solution)/shard_map/project/pallas_call | solution.py:114
  30.1 1.2 %collective-permute-start.10 = (bf16[8,512]{1,0:T(8,128)(2,1)S(1)}, bf16[8,512]{1,0:T(8,128)(2,1)S(1)}, u32[]{:S(2)}, u32[]{:S(2)}) collective-permute-start(bf16[8,512]{1,0:T(8,128)(2,1)S(1)} %get-tuple-element.120.refs_3_.refs_0_), channel_id=1, source_target_pairs={{0,32},{4,36},{8,40},{12,44},{16,48},{20,52},{24,56},{28,60},{32,6... | collective-permute-start | bytes 24584 | tf_op jit(solution)/shard_map/ppermute | solution.py:32
  31.4 0.7 %collective-permute-start.11 = (bf16[8,512]{1,0:T(8,128)(2,1)S(1)}, bf16[8,512]{1,0:T(8,128)(2,1)S(1)}, u32[]{:S(2)}, u32[]{:S(2)}) collective-permute-start(bf16[8,512]{1,0:T(8,128)(2,1)S(1)} %get-tuple-element.120.refs_3_.refs_0_), channel_id=1, source_target_pairs={{0,16},{4,20},{8,24},{12,28},{16,32},{20,36},{24,40},{28,44},{32,4... | collective-permute-start | bytes 24584 | tf_op jit(solution)/shard_map/ppermute | solution.py:32
  32.1 1.9 %collective-permute-start.12 = (bf16[8,512]{1,0:T(8,128)(2,1)S(1)}, bf16[8,512]{1,0:T(8,128)(2,1)S(1)}, u32[]{:S(2)}, u32[]{:S(2)}) collective-permute-start(bf16[8,512]{1,0:T(8,128)(2,1)S(1)} %get-tuple-element.120.refs_3_.refs_0_), channel_id=1, source_target_pairs={{0,112},{4,116},{8,120},{12,124},{16,0},{20,4},{24,8},{28,12},{32,... | collective-permute-start | bytes 24584 | tf_op jit(solution)/shard_map/ppermute | solution.py:32
  34.0 4.8 %own_attention.1 = (f32[8,448]{1,0:T(8,128)S(1)}, f32[8,448]{1,0:T(8,128)S(1)}, f32[8,448]{1,0:T(8,128)S(1)}) custom-call(s32[8,256]{1,0:T(8,128)S(1)} %copy-done.1, s32[8]{0:T(128)S(1)} %copy-done.3, f32[8,128]{1,0:T(8,128)S(1)} %get-tuple-element.106.refs_0_.refs_2_, bf16[8,512]{1,0:T(8,128)(2,1)S(1)} %get-tuple-element.120.refs_3_.refs_0_, ...), custom_call_target="tpu_custom_call" | custom-call | tf_op jit(solution)/shard_map/own_attention/pallas_call | solution.py:114
  38.8 0.0 collective-permute-done.10.refs_1_
  38.8 0.0 collective-permute-done.11.refs_2_
  38.8 0.0 collective-permute-done.12.refs_3_
  38.9 0.9 %prompt_attention.1 = (f32[8,640]{1,0:T(8,128)S(1)}, f32[8,640]{1,0:T(8,128)S(1)}, f32[8,640]{1,0:T(8,128)S(1)}, f32[8,640]{1,0:T(8,128)S(1)}) custom-call(bf16[8,512]{1,0:T(8,128)(2,1)S(1)} %get-tuple-element.120.refs_3_.refs_0_, bf16[8,512]{1,0:T(8,128)(2,1)S(1)} %collective-permute-done.10.refs_1_, bf16[8,512]{1,0:T(8,128)(2,1)S(1)} %collective-permute-done.11.refs_2_, ...), custom_call_target="tpu_custom_call" | custom-call | tf_op jit(solution)/shard_map/prompt_attention/pallas_call | solution.py:114
  39.8 1.2 %collective-permute-start.14 = (f32[8,640]{1,0:T(8,128)S(1)}, f32[8,640]{1,0:T(8,128)S(1)}, u32[]{:S(2)}, u32[]{:S(2)}) collective-permute-start(f32[8,640]{1,0:T(8,128)S(1)} %get-tuple-element.126), channel_id=1, source_target_pairs={{0,96},{4,100},{8,104},{12,108},{16,112},{20,116},{24,120},{28,124... | collective-permute-start | bytes 61448 | tf_op jit(solution)/shard_map/ppermute | solution.py:32
  41.0 0.0 collective-permute-start.15
  41.1 1.4 %collective-permute-start.16 = (f32[8,640]{1,0:T(8,128)S(1)}, f32[8,640]{1,0:T(8,128)S(1)}, u32[]{:S(2)}, u32[]{:S(2)}) collective-permute-start(f32[8,640]{1,0:T(8,128)S(1)} %get-tuple-element.128), channel_id=1, source_target_pairs={{0,16},{4,20},{8,24},{12,28},{16,32},{20,36},{24,40},{28,44},{32,4... | collective-permute-start | bytes 61448 | tf_op jit(solution)/shard_map/ppermute | solution.py:32
  42.5 0.9 %collective-permute-done.14.refs_4_ = f32[8,640]{1,0:T(8,128)S(1)} collective-permute-done((f32[8,640]{1,0:T(8,128)S(1)}, f32[8,640]{1,0:T(8,128)S(1)}, u32[]{:S(2)}, u32[]{:S(2)}) %collective-permute-start.14) | collective-permute-done | bytes 20512 | tf_op jit(solution)/shard_map/ppermute | solution.py:32
  43.4 0.5 %collective-permute-done.15.refs_5_ = f32[8,640]{1,0:T(8,128)S(1)} collective-permute-done((f32[8,640]{1,0:T(8,128)S(1)}, f32[8,640]{1,0:T(8,128)S(1)}, u32[]{:S(2)}, u32[]{:S(2)}) %collective-permute-start.15) | collective-permute-done | bytes 20512 | tf_op jit(solution)/shard_map/ppermute | solution.py:32
  44.0 0.9 %collective-permute-done.16.refs_6_ = f32[8,640]{1,0:T(8,128)S(1)} collective-permute-done((f32[8,640]{1,0:T(8,128)S(1)}, f32[8,640]{1,0:T(8,128)S(1)}, u32[]{:S(2)}, u32[]{:S(2)}) %collective-permute-start.16) | collective-permute-done | bytes 20512 | tf_op jit(solution)/shard_map/ppermute | solution.py:32
  44.9 0.6 %combine.1 = (f32[8,448]{1,0:T(8,128)S(1)}, f32[8,448]{1,0:T(8,128)S(1)}, f32[8,448]{1,0:T(8,128)S(1)}, f32[8,448]{1,0:T(8,128)S(1)}) custom-call(f32[8,448]{1,0:T(8,128)S(1)} %get-tuple-element.117.refs_0_, f32[8,448]{1,0:T(8,128)S(1)} %get-tuple-element.118.refs_1_, f32[8,448]{1,0:T(8,128)S(1)} %get-tuple-element.119.refs_2_, ...), custom_call_target="tpu_custom_call" | custom-call | tf_op jit(solution)/shard_map/combine/pallas_call | solution.py:114
  45.5 2.0 %collective-permute-start.17 = (f32[8,448]{1,0:T(8,128)S(1)}, f32[8,448]{1,0:T(8,128)S(1)}, u32[]{:S(2)}, u32[]{:S(2)}) collective-permute-start(f32[8,448]{1,0:T(8,128)S(1)} %get-tuple-element.130), channel_id=1, source_target_pairs={{0,2},{1,3},{2,0},{3,1},{4,6},{5,7},{6,4},{7,5},{8,10},{9,11},{10,... | collective-permute-start | bytes 43016 | tf_op jit(solution)/shard_map/ppermute | solution.py:28
  47.5 0.0 collective-permute-start.18
  47.5 2.7 %collective-permute-start.19 = (f32[8,448]{1,0:T(8,128)S(1)}, f32[8,448]{1,0:T(8,128)S(1)}, u32[]{:S(2)}, u32[]{:S(2)}) collective-permute-start(f32[8,448]{1,0:T(8,128)S(1)} %get-tuple-element.132), channel_id=1, source_target_pairs={{0,3},{1,0},{2,1},{3,2},{4,7},{5,4},{6,5},{7,6},{8,11},{9,8},{10,9... | collective-permute-start | bytes 43016 | tf_op jit(solution)/shard_map/ppermute | solution.py:28
  50.2 1.1 %collective-permute-done.18 = f32[8,448]{1,0:T(8,128)S(1)} collective-permute-done((f32[8,448]{1,0:T(8,128)S(1)}, f32[8,448]{1,0:T(8,128)S(1)}, u32[]{:S(2)}, u32[]{:S(2)}) %collective-permute-start.18) | collective-permute-done | bytes 14368 | tf_op jit(solution)/shard_map/ppermute | solution.py:28
  51.3 0.6 %fusion = bf16[1,8,448]{2,1,0:T(8,128)(2,1)} fusion(f32[8,448]{1,0:T(8,128)S(1)} %collective-permute-done.19, f32[8,448]{1,0:T(8,128)S(1)} %collective-permute-done.18, f32[8,448]{1,0:T(8,128)S(1)} %collective-permute-done.17, f32[8,448]{1,0:T(8,128)S(1)} %get-tuple-element.129, bf16[8,448]{1,0:T(8,128)(2,1)S(1)} %get-tuple-element.109, pred[]{:T(512)S(6)} %eq.3), kind=kLoop, calls=%fused_computation.2 | loop fusion | flops 25088 | bytes 71681 | tf_op jit(solution)/shard_map/broadcast_in_dim | solution.py:721
  (10 shorter events, 0.0 us)
Async XLA Ops:
  1.1 8.2 %collective-permute-start = (bf16[448,128]{1,0:T(8,128)(2,1)S(1)}, bf16[448,128]{1,0:T(8,128)(2,1)S(1)}, u32[]{:S(2)}, u32[]{:S(2)}) collective-permute-start(bf16[448,128]{1,0:T(8,128)(2,1)S(1)} %window_page.1), channel_id=1, source_target_pairs={{0,4},{4,8},{8,12},{12,0},{16,20},{20,24},{24,28},{28,16},{32,36},... | collective-permute-start | bytes 344072 | tf_op jit(solution)/shard_map/ppermute | solution.py:40
  3.2 10.0 %collective-permute-start.4 = (bf16[448,128]{1,0:T(8,128)(2,1)S(1)}, bf16[448,128]{1,0:T(8,128)(2,1)S(1)}, u32[]{:S(2)}, u32[]{:S(2)}) collective-permute-start(bf16[448,128]{1,0:T(8,128)(2,1)S(1)} %window_page.1), channel_id=1, source_target_pairs={{0,12},{4,0},{8,4},{12,8},{16,28},{20,16},{24,20},{28,24},{32,44},... | collective-permute-start | bytes 344072 | tf_op jit(solution)/shard_map/ppermute | solution.py:40
  4.5 8.6 %collective-permute-start.5 = (bf16[448,128]{1,0:T(8,128)(2,1)S(1)}, bf16[448,128]{1,0:T(8,128)(2,1)S(1)}, u32[]{:S(2)}, u32[]{:S(2)}) collective-permute-start(bf16[448,128]{1,0:T(8,128)(2,1)S(1)} %window_page.1), channel_id=1, source_target_pairs={{0,8},{4,12},{8,0},{12,4},{16,24},{20,28},{24,16},{28,20},{32,40},... | collective-permute-start | bytes 344072 | tf_op jit(solution)/shard_map/ppermute | solution.py:40
  6.2 6.3 %collective-permute-start.2 = (bf16[8,448]{1,0:T(8,128)(2,1)}, bf16[8,448]{1,0:T(8,128)(2,1)S(1)}, u32[]{:S(2)}, u32[]{:S(2)}) collective-permute-start(bf16[8,448]{1,0:T(8,128)(2,1)} %refs_0_.2), channel_id=1, source_target_pairs={{0,3},{1,0},{2,1},{3,2},{4,7},{5,4},{6,5},{7,6},{8,11},{9,8},{10,9... | collective-permute-start | bytes 21512 | tf_op jit(solution)/shard_map/ppermute | solution.py:28
  8.9 4.2 %collective-permute-start.3 = (bf16[8,448]{1,0:T(8,128)(2,1)}, bf16[8,448]{1,0:T(8,128)(2,1)S(1)}, u32[]{:S(2)}, u32[]{:S(2)}) collective-permute-start(bf16[8,448]{1,0:T(8,128)(2,1)} %refs_0_.2), channel_id=1, source_target_pairs={{0,2},{1,3},{2,0},{3,1},{4,6},{5,7},{6,4},{7,5},{8,10},{9,11},{10,... | collective-permute-start | bytes 21512 | tf_op jit(solution)/shard_map/ppermute | solution.py:28
  9.3 12.9 %copy-start.2 = (bf16[8,448]{1,0:T(8,128)(2,1)S(1)}, bf16[8,448]{1,0:T(8,128)(2,1)}, u32[]{:S(2)}) copy-start(bf16[8,448]{1,0:T(8,128)(2,1)} %refs_0_.2) | copy-start | bytes 21508
  9.3 3.9 %collective-permute-start.1 = (bf16[8,448]{1,0:T(8,128)(2,1)}, bf16[8,448]{1,0:T(8,128)(2,1)S(1)}, u32[]{:S(2)}, u32[]{:S(2)}) collective-permute-start(bf16[8,448]{1,0:T(8,128)(2,1)} %refs_0_.2), channel_id=1, source_target_pairs={{0,1},{1,2},{2,3},{3,0},{4,5},{5,6},{6,7},{7,4},{8,9},{9,10},{10,1... | collective-permute-start | bytes 21512 | tf_op jit(solution)/shard_map/ppermute | solution.py:28
  13.3 12.9 %copy-start.1 = (s32[8,256]{1,0:T(8,128)S(1)}, s32[8,256]{1,0:T(8,128)}, u32[]{:S(2)}) copy-start(s32[8,256]{1,0:T(8,128)} %refs_0_.4) | copy-start | bytes 24580
  13.3 12.9 %copy-start.3 = (s32[8]{0:T(128)S(1)}, s32[8]{0:T(128)}, u32[]{:S(2)}) copy-start(s32[8]{0:T(128)} %refs_1_.2) | copy-start | bytes 100
  13.3 25.6 %collective-permute-start.13 = (bf16[4,448,128]{2,1,0:T(8,128)(2,1)S(1)}, bf16[4,448,128]{2,1,0:T(8,128)(2,1)S(1)}, u32[]{:S(2)}, u32[]{:S(2)}) collective-permute-start(bf16[4,448,128]{2,1,0:T(8,128)(2,1)S(1)} %pad_maximum_fusion.refs_4_), channel_id=1, source_target_pairs={{128,192},{132,196},{136,200},{140,204},{144,208},{148,212},{152,2... | collective-permute-start | bytes 1376264 | tf_op jit(solution)/shard_map/ppermute | solution.py:49
  22.2 6.4 %collective-permute-start.6 = (bf16[8,1792]{1,0:T(8,128)(2,1)S(1)}, bf16[8,1792]{1,0:T(8,128)(2,1)S(1)}, u32[]{:S(2)}, u32[]{:S(2)}) collective-permute-start(bf16[8,1792]{1,0:T(8,128)(2,1)S(1)} %linear_layer.1.refs_7_), channel_id=1, source_target_pairs={{0,130},{1,131},{2,128},{3,129},{130,0},{131,1},{128,2},{129,3},{4... | collective-permute-start | bytes 86024 | tf_op jit(solution)/shard_map/ppermute | solution.py:59
  22.3 6.3 %collective-permute-start.7 = (bf16[8,1792]{1,0:T(8,128)(2,1)S(1)}, bf16[8,1792]{1,0:T(8,128)(2,1)S(1)}, u32[]{:S(2)}, u32[]{:S(2)}) collective-permute-start(bf16[8,1792]{1,0:T(8,128)(2,1)S(1)} %linear_layer.1.refs_7_), channel_id=1, source_target_pairs={{0,129},{1,130},{2,131},{3,128},{129,0},{130,1},{131,2},{128,3},{4... | collective-permute-start | bytes 86024 | tf_op jit(solution)/shard_map/ppermute | solution.py:59
  25.8 3.3 %collective-permute-start.8 = (bf16[8,1792]{1,0:T(8,128)(2,1)S(1)}, bf16[8,1792]{1,0:T(8,128)(2,1)S(1)}, u32[]{:S(2)}, u32[]{:S(2)}) collective-permute-start(bf16[8,1792]{1,0:T(8,128)(2,1)S(1)} %linear_layer.1.refs_7_), channel_id=1, source_target_pairs={{0,131},{1,128},{2,129},{3,130},{131,0},{128,1},{129,2},{130,3},{4... | collective-permute-start | bytes 86024 | tf_op jit(solution)/shard_map/ppermute | solution.py:59
  25.8 3.3 %collective-permute-start.9 = (bf16[8,1792]{1,0:T(8,128)(2,1)S(1)}, bf16[8,1792]{1,0:T(8,128)(2,1)S(1)}, u32[]{:S(2)}, u32[]{:S(2)}) collective-permute-start(bf16[8,1792]{1,0:T(8,128)(2,1)S(1)} %linear_layer.1.refs_7_), channel_id=1, source_target_pairs={{0,128},{1,129},{2,130},{3,131},{128,0},{129,1},{130,2},{131,3},{4... | collective-permute-start | bytes 86024 | tf_op jit(solution)/shard_map/ppermute | solution.py:59
  30.1 8.7 %collective-permute-start.10 = (bf16[8,512]{1,0:T(8,128)(2,1)S(1)}, bf16[8,512]{1,0:T(8,128)(2,1)S(1)}, u32[]{:S(2)}, u32[]{:S(2)}) collective-permute-start(bf16[8,512]{1,0:T(8,128)(2,1)S(1)} %get-tuple-element.120.refs_3_.refs_0_), channel_id=1, source_target_pairs={{0,32},{4,36},{8,40},{12,44},{16,48},{20,52},{24,56},{28,60},{32,6... | collective-permute-start | bytes 24584 | tf_op jit(solution)/shard_map/ppermute | solution.py:32
  31.4 7.5 %collective-permute-start.11 = (bf16[8,512]{1,0:T(8,128)(2,1)S(1)}, bf16[8,512]{1,0:T(8,128)(2,1)S(1)}, u32[]{:S(2)}, u32[]{:S(2)}) collective-permute-start(bf16[8,512]{1,0:T(8,128)(2,1)S(1)} %get-tuple-element.120.refs_3_.refs_0_), channel_id=1, source_target_pairs={{0,16},{4,20},{8,24},{12,28},{16,32},{20,36},{24,40},{28,44},{32,4... | collective-permute-start | bytes 24584 | tf_op jit(solution)/shard_map/ppermute | solution.py:32
  32.1 6.8 %collective-permute-start.12 = (bf16[8,512]{1,0:T(8,128)(2,1)S(1)}, bf16[8,512]{1,0:T(8,128)(2,1)S(1)}, u32[]{:S(2)}, u32[]{:S(2)}) collective-permute-start(bf16[8,512]{1,0:T(8,128)(2,1)S(1)} %get-tuple-element.120.refs_3_.refs_0_), channel_id=1, source_target_pairs={{0,112},{4,116},{8,120},{12,124},{16,0},{20,4},{24,8},{28,12},{32,... | collective-permute-start | bytes 24584 | tf_op jit(solution)/shard_map/ppermute | solution.py:32
  34.0 10.9 %copy-start = (bf16[1,448,1792]{2,1,0:T(8,128)(2,1)S(1)}, bf16[1,448,1792]{2,1,0:T(8,128)(2,1)}, u32[]{:S(2)}) copy-start(bf16[1,448,1792]{2,1,0:T(8,128)(2,1)} %refs_8_.1) | copy-start | bytes 4816900
  39.8 3.6 %collective-permute-start.14 = (f32[8,640]{1,0:T(8,128)S(1)}, f32[8,640]{1,0:T(8,128)S(1)}, u32[]{:S(2)}, u32[]{:S(2)}) collective-permute-start(f32[8,640]{1,0:T(8,128)S(1)} %get-tuple-element.126), channel_id=1, source_target_pairs={{0,96},{4,100},{8,104},{12,108},{16,112},{20,116},{24,120},{28,124... | collective-permute-start | bytes 61448 | tf_op jit(solution)/shard_map/ppermute | solution.py:32
  41.0 2.9 %collective-permute-start.15 = (f32[8,640]{1,0:T(8,128)S(1)}, f32[8,640]{1,0:T(8,128)S(1)}, u32[]{:S(2)}, u32[]{:S(2)}) collective-permute-start(f32[8,640]{1,0:T(8,128)S(1)} %get-tuple-element.127), channel_id=1, source_target_pairs={{0,112},{4,116},{8,120},{12,124},{16,0},{20,4},{24,8},{28,12},{32,... | collective-permute-start | bytes 61448 | tf_op jit(solution)/shard_map/ppermute | solution.py:32
  41.1 3.8 %collective-permute-start.16 = (f32[8,640]{1,0:T(8,128)S(1)}, f32[8,640]{1,0:T(8,128)S(1)}, u32[]{:S(2)}, u32[]{:S(2)}) collective-permute-start(f32[8,640]{1,0:T(8,128)S(1)} %get-tuple-element.128), channel_id=1, source_target_pairs={{0,16},{4,20},{8,24},{12,28},{16,32},{20,36},{24,40},{28,44},{32,4... | collective-permute-start | bytes 61448 | tf_op jit(solution)/shard_map/ppermute | solution.py:32
  45.5 4.7 %collective-permute-start.17 = (f32[8,448]{1,0:T(8,128)S(1)}, f32[8,448]{1,0:T(8,128)S(1)}, u32[]{:S(2)}, u32[]{:S(2)}) collective-permute-start(f32[8,448]{1,0:T(8,128)S(1)} %get-tuple-element.130), channel_id=1, source_target_pairs={{0,2},{1,3},{2,0},{3,1},{4,6},{5,7},{6,4},{7,5},{8,10},{9,11},{10,... | collective-permute-start | bytes 43016 | tf_op jit(solution)/shard_map/ppermute | solution.py:28
  47.5 3.8 %collective-permute-start.18 = (f32[8,448]{1,0:T(8,128)S(1)}, f32[8,448]{1,0:T(8,128)S(1)}, u32[]{:S(2)}, u32[]{:S(2)}) collective-permute-start(f32[8,448]{1,0:T(8,128)S(1)} %get-tuple-element.131), channel_id=1, source_target_pairs={{0,1},{1,2},{2,3},{3,0},{4,5},{5,6},{6,7},{7,4},{8,9},{9,10},{10,1... | collective-permute-start | bytes 43016 | tf_op jit(solution)/shard_map/ppermute | solution.py:28
  47.5 3.8 %collective-permute-start.19 = (f32[8,448]{1,0:T(8,128)S(1)}, f32[8,448]{1,0:T(8,128)S(1)}, u32[]{:S(2)}, u32[]{:S(2)}) collective-permute-start(f32[8,448]{1,0:T(8,128)S(1)} %get-tuple-element.132), channel_id=1, source_target_pairs={{0,3},{1,0},{2,1},{3,2},{4,7},{5,4},{6,5},{7,6},{8,11},{9,8},{10,9... | collective-permute-start | bytes 43016 | tf_op jit(solution)/shard_map/ppermute | solution.py:28

commit v14 on v12

--- a/solution.py
+++ b/solution.py
@@ -265,17 +265,13 @@
     p3,
     gain,
     qk_w,
-    v_hbm,
+    v_w,
     one,
     asked,
     key_new,
     value_new,
-    v_w,
-    sem,
 ):
     rows, share = one.shape
-    copy = pltpu.make_async_copy(v_hbm.at[0], v_w, sem)
-    copy.start()
     heads = share // HD
     layer_one = sum(ref[...].astype(jnp.float32) for ref in (p0, p1, p2, p3)).astype(jnp.bfloat16)
     rounded = layer_one.astype(jnp.float32)
@@ -299,15 +295,14 @@
     query = jnp.where(lane == share + 1, tags[:, 1:2], query)
     asked[...] = query.astype(jnp.bfloat16)
     key_new[...] = key[:, :share].astype(jnp.bfloat16)
-    copy.wait()
     value_new[...] = lax.dot_general(
         normed, v_w[...], FLAT, preferred_element_type=jnp.float32
     ).astype(jnp.bfloat16)
 
 
-def project(tags, pieces, near, value_w):
+def project(tags, pieces, near):
     rows = pieces[0].shape[0]
-    share = value_w.shape[1]
+    share = near["value_w"].shape[0]
     return kernel_call(
         project_kernel,
         1,
@@ -318,9 +313,9 @@
             jax.ShapeDtypeStruct((rows, share), jnp.bfloat16),
             jax.ShapeDtypeStruct((rows, share), jnp.bfloat16),
         ],
-        [VMEM] * 7 + [HBM],
-        [pltpu.VMEM(value_w.shape[1:], jnp.bfloat16), pltpu.SemaphoreType.DMA],
-        (tags, *pieces, near["gain"], near["query_key_w"], value_w),
+        [VMEM] * 8,
+        [],
+        (tags, *pieces, near["gain"], near["query_key_w"], near["value_w"]),
     )
 
 
@@ -501,7 +496,7 @@
         for h in range(1, heads):
             there = rows_whole[:, h * share : (h + 1) * share]
             slab = jnp.where(((ids[2] + steps) & (heads - 1)) == h, there, slab)
-        ref[...] = slab
+        ref[...] = slab.astype(jnp.bfloat16)
 
 
 def own_slabs(ids, *refs):
@@ -513,7 +508,7 @@
         combine_kernel,
         1,
         "combine",
-        [jax.ShapeDtypeStruct(own[0].shape, jnp.float32)] * 4,
+        [jax.ShapeDtypeStruct(own[0].shape, jnp.bfloat16)] * 4,
         [VMEM] * 9,
         [],
         (*own, *parts, update, out_w),
@@ -530,7 +525,7 @@
     "conv_state",
     "value_w",
 )
-WINDOW_NEAR = ("gain", "query_key_w")
+WINDOW_NEAR = ("gain", "value_w", "query_key_w")
 
 
 def bring_near(arrays):
@@ -684,7 +679,7 @@
     )
     near["own_pages"], tags = bring_windows(table, ends, own_pages)
     swapped = [section_swap(update, k) for k in (2, 1, 3, 0)]
-    one_share, packed, key_new, value_new = project(tags, swapped, near, value_w)
+    one_share, packed, key_new, value_new = project(tags, swapped, near)
     asked = [packed] + [z_shift(packed, k) for k in (2, 1, 7)]
     own = own_attention(tags, packed, key_new, value_new, near)
     asked, own = lax.optimization_barrier((asked, own))
@@ -692,9 +687,9 @@
     parts = [answers[0]] + [z_shift(answers[at], -k) for at, k in ((1, 2), (2, 1), (3, 7))]
     slabs = combine(own, parts, update, out_w)
     here = lax.axis_index("section") == 1
-    total = jnp.where(here, one_share.astype(jnp.float32), 0.0) + slabs[0]
+    total = jnp.where(here, one_share.astype(jnp.float32), 0.0) + slabs[0].astype(jnp.float32)
     for piece in [head_shift(slabs[k], k) for k in (2, 1, 3)]:
-        total = total + piece
+        total = total + piece.astype(jnp.float32)
     return total.astype(jnp.bfloat16)[None]
 
 

time: 50.9 us -> 50.2 us (0.986)
  Pallas kernels: 10.8 us -> 10.2 us
    pallas_call x8, Pallas kernels: 10.8 us -> 10.2 us  [kernel_call(): pl.pallas_call(run, out_shape=out_shape, in_specs=in_specs, out_specs=jax...]
  transfers between devices with their start and end apart: 20 -> 20, of which waited for: 6 -> 5; matrix products, arithmetic and copies ran while one was open for 0% -> 0% of each run, Pallas kernels for 16% -> 15%
where the time goes in v14:
time: 50.2 us; the launch traced here: 49.9 us
  starting transfers between devices  33.8 us (67%)
  Pallas kernels  10.2 us (20%)
  waiting for transfers between devices  5.09 us (10%)
  other arithmetic  0.67 us (1%)
    pallas_call x8, Pallas kernels, kernel_call(): pl.pallas_call(run, out_shape=out_shape, in_specs=in_specs, out_specs=jax...  10.2 us
    ppermute x1, starting transfers between devices, far_swap(): lax.ppermute(value, ('section', 'req'), [(count + i, count + (i + count /...  8.82 us
    ppermute x6, starting transfers between devices, z_shift(): lax.ppermute(value, 'req', [(z * XN + i, (z + steps) % ZN * XN + i) for z...  7.99 us
    ppermute x6, starting transfers between devices, head_shift(): lax.ppermute(value, 'head', [(i, (i + steps) % count) for i in range(coun...  7.84 us
    ppermute x3, starting transfers between devices, x_shift(): lax.ppermute(value, 'req', [(z * XN + i, z * XN + (i + steps) % XN) for z...  5.12 us
    ppermute x4, starting transfers between devices, section_swap(): lax.ppermute(value, ('section', 'head'), there + [(b, a) for a, b in there])  4.01 us
    ppermute x6, waiting for transfers between devices, z_shift(): lax.ppermute(value, 'req', [(z * XN + i, (z + steps) % ZN * XN + i) for z...  2.97 us
    ppermute x6, waiting for transfers between devices, head_shift(): lax.ppermute(value, 'head', [(i, (i + steps) % count) for i in range(coun...  2.09 us
  transfers between devices with their start and end apart: 20, of which 5 were waited for; matrix products, arithmetic and copies ran while one was open for 0% of the time, Pallas kernels for 15%

profile of v14, /device:TPU:1, one launch (start us, length us, event | category | flops | bytes accessed | tf_op | source)
XLA Modules:
  0.0 49.9 jit_solution(2000211204549714593)
XLA Ops:
  0.0 1.0 %window_page.1 = bf16[448,128]{1,0:T(8,128)(2,1)S(1)} custom-call(bf16[1,2,448,128]{3,2,1,0:T(8,128)(2,1)} %bitcast.18), custom_call_target="tpu_custom_call" | custom-call | bytes 16777216 | tf_op jit(solution)/shard_map/window_page/pallas_call | solution.py:114
  1.1 2.1 %collective-permute-start = (bf16[448,128]{1,0:T(8,128)(2,1)S(1)}, bf16[448,128]{1,0:T(8,128)(2,1)S(1)}, u32[]{:S(2)}, u32[]{:S(2)}) collective-permute-start(bf16[448,128]{1,0:T(8,128)(2,1)S(1)} %window_page.1), channel_id=1, source_target_pairs={{0,4},{4,8},{8,12},{12,0},{16,20},{20,24},{24,28},{28,16},{32,36},... | collective-permute-start | bytes 344072 | tf_op jit(solution)/shard_map/ppermute | solution.py:40
  3.2 1.4 %collective-permute-start.4 = (bf16[448,128]{1,0:T(8,128)(2,1)S(1)}, bf16[448,128]{1,0:T(8,128)(2,1)S(1)}, u32[]{:S(2)}, u32[]{:S(2)}) collective-permute-start(bf16[448,128]{1,0:T(8,128)(2,1)S(1)} %window_page.1), channel_id=1, source_target_pairs={{0,12},{4,0},{8,4},{12,8},{16,28},{20,16},{24,20},{28,24},{32,44},... | collective-permute-start | bytes 344072 | tf_op jit(solution)/shard_map/ppermute | solution.py:40
  4.5 1.6 %collective-permute-start.5 = (bf16[448,128]{1,0:T(8,128)(2,1)S(1)}, bf16[448,128]{1,0:T(8,128)(2,1)S(1)}, u32[]{:S(2)}, u32[]{:S(2)}) collective-permute-start(bf16[448,128]{1,0:T(8,128)(2,1)S(1)} %window_page.1), channel_id=1, source_target_pairs={{0,8},{4,12},{8,0},{12,4},{16,24},{20,28},{24,16},{28,20},{32,40},... | collective-permute-start | bytes 344072 | tf_op jit(solution)/shard_map/ppermute | solution.py:40
  6.2 2.7 %collective-permute-start.2 = (bf16[8,448]{1,0:T(8,128)(2,1)}, bf16[8,448]{1,0:T(8,128)(2,1)S(1)}, u32[]{:S(2)}, u32[]{:S(2)}) collective-permute-start(bf16[8,448]{1,0:T(8,128)(2,1)} %refs_0_.2), channel_id=1, source_target_pairs={{0,3},{1,0},{2,1},{3,2},{4,7},{5,4},{6,5},{7,6},{8,11},{9,8},{10,9... | collective-permute-start | bytes 21512 | tf_op jit(solution)/shard_map/ppermute | solution.py:28
  8.9 0.3 collective-permute-start.3
  9.3 0.0 collective-permute-done
  9.3 0.7 %collective-permute-start.1 = (bf16[8,448]{1,0:T(8,128)(2,1)}, bf16[8,448]{1,0:T(8,128)(2,1)S(1)}, u32[]{:S(2)}, u32[]{:S(2)}) collective-permute-start(bf16[8,448]{1,0:T(8,128)(2,1)} %refs_0_.2), channel_id=1, source_target_pairs={{0,1},{1,2},{2,3},{3,0},{4,5},{5,6},{6,7},{7,4},{8,9},{9,10},{10,1... | collective-permute-start | bytes 21512 | tf_op jit(solution)/shard_map/ppermute | solution.py:28
  10.0 2.5 %bring_near.1 = (bf16[8,2,448]{2,1,0:T(2,128)(2,1)S(1)}, f32[3,448]{1,0:T(4,128)S(1)}, bf16[1792,128]{1,0:T(8,128)(2,1)S(1)}, f32[1,1792]{1,0:T(1,128)S(1)}, f32...) custom-call(bf16[8,2,448]{2,1,0:T(2,128)(2,1)} %refs_0_.1, ...), custom_call_target="tpu_custom_call" | custom-call | bytes 14588672 | tf_op jit(solution)/shard_map/bring_near/pallas_call | solution.py:114
  12.4 0.0 collective-permute-done.2.refs_2_
  12.4 0.7 %collective-permute-done.3.refs_3_ = bf16[8,448]{1,0:T(8,128)(2,1)S(1)} collective-permute-done((bf16[8,448]{1,0:T(8,128)(2,1)}, bf16[8,448]{1,0:T(8,128)(2,1)S(1)}, u32[]{:S(2)}, u32[]{:S(2)}) %collective-permute-start.3) | collective-permute-done | bytes 7200 | tf_op jit(solution)/shard_map/ppermute | solution.py:28
  13.1 0.0 collective-permute-done.4
  13.1 0.0 collective-permute-done.5
  13.1 0.1 collective-permute-done.1.refs_1_
  13.2 0.1 pad_maximum_fusion.refs_4_
  13.3 0.0 copy-start.2
  13.3 0.0 copy-start.3
  13.3 8.8 %collective-permute-start.13 = (bf16[4,448,128]{2,1,0:T(8,128)(2,1)S(1)}, bf16[4,448,128]{2,1,0:T(8,128)(2,1)S(1)}, u32[]{:S(2)}, u32[]{:S(2)}) collective-permute-start(bf16[4,448,128]{2,1,0:T(8,128)(2,1)S(1)} %pad_maximum_fusion.refs_4_), channel_id=1, source_target_pairs={{128,192},{132,196},{136,200},{140,204},{144,208},{148,212},{152,2... | collective-permute-start | bytes 1376264 | tf_op jit(solution)/shard_map/ppermute | solution.py:49
  22.2 0.1 collective-permute-start.6
  22.3 3.6 %collective-permute-start.7 = (bf16[8,1792]{1,0:T(8,128)(2,1)S(1)}, bf16[8,1792]{1,0:T(8,128)(2,1)S(1)}, u32[]{:S(2)}, u32[]{:S(2)}) collective-permute-start(bf16[8,1792]{1,0:T(8,128)(2,1)S(1)} %linear_layer.1.refs_7_), channel_id=1, source_target_pairs={{0,129},{1,130},{2,131},{3,128},{129,0},{130,1},{131,2},{128,3},{4... | collective-permute-start | bytes 86024 | tf_op jit(solution)/shard_map/ppermute | solution.py:59
  25.8 0.0 collective-permute-start.8
  25.8 0.3 collective-permute-start.9
  26.2 3.0 %bring_windows.1 = (bf16[8,2,2,448,128]{4,3,2,1,0:T(8,128)(2,1)S(1)}, f32[8,128]{1,0:T(8,128)S(1)}) custom-call(s32[8,256]{1,0:T(8,128)S(1)} %copy-done.2, s32[8]{0:T(128)S(1)} %copy-done.3, bf16[16,2,448,128]{3,2,1,0:T(8,128)(2,1)} %bitcast.15), custom_call_target="tpu_custom_call" | custom-call | bytes 7340032 | tf_op jit(solution)/shard_map/bring_windows/pallas_call | solution.py:114
  29.2 0.0 collective-permute-done.6.refs_1_
  29.2 0.0 collective-permute-done.7.refs_2_
  29.2 0.0 collective-permute-done.8.refs_3_
  29.2 0.0 collective-permute-done.9.refs_4_
  29.2 1.0 %project.1 = (bf16[8,448]{1,0:T(8,128)(2,1)S(1)}, bf16[8,512]{1,0:T(8,128)(2,1)S(1)}, bf16[8,448]{1,0:T(8,128)(2,1)S(1)}, bf16[8,448]{1,0:T(8,128)(2,1)S(1)}) custom-call(f32[8,128]{1,0:T(8,128)S(1)} %get-tuple-element.106.refs_0_, bf16[8,1792]{1,0:T(8,128)(2,1)S(1)} %collective-permute-done.6.refs_1_, bf16[8,1792]{1,0:T(8,128)(2,1)S(1)} %collective-permute-done.7.refs_2_, ...), custom_call_target="tpu_custom_call" | custom-call | tf_op jit(solution)/shard_map/project/pallas_call | solution.py:114
  30.2 1.2 %collective-permute-start.10 = (bf16[8,512]{1,0:T(8,128)(2,1)S(1)}, bf16[8,512]{1,0:T(8,128)(2,1)S(1)}, u32[]{:S(2)}, u32[]{:S(2)}) collective-permute-start(bf16[8,512]{1,0:T(8,128)(2,1)S(1)} %get-tuple-element.120.refs_1_.refs_0_), channel_id=1, source_target_pairs={{0,32},{4,36},{8,40},{12,44},{16,48},{20,52},{24,56},{28,60},{32,6... | collective-permute-start | bytes 24584 | tf_op jit(solution)/shard_map/ppermute | solution.py:32
  31.4 0.8 %collective-permute-start.11 = (bf16[8,512]{1,0:T(8,128)(2,1)S(1)}, bf16[8,512]{1,0:T(8,128)(2,1)S(1)}, u32[]{:S(2)}, u32[]{:S(2)}) collective-permute-start(bf16[8,512]{1,0:T(8,128)(2,1)S(1)} %get-tuple-element.120.refs_1_.refs_0_), channel_id=1, source_target_pairs={{0,16},{4,20},{8,24},{12,28},{16,32},{20,36},{24,40},{28,44},{32,4... | collective-permute-start | bytes 24584 | tf_op jit(solution)/shard_map/ppermute | solution.py:32
  32.2 1.9 %collective-permute-start.12 = (bf16[8,512]{1,0:T(8,128)(2,1)S(1)}, bf16[8,512]{1,0:T(8,128)(2,1)S(1)}, u32[]{:S(2)}, u32[]{:S(2)}) collective-permute-start(bf16[8,512]{1,0:T(8,128)(2,1)S(1)} %get-tuple-element.120.refs_1_.refs_0_), channel_id=1, source_target_pairs={{0,112},{4,116},{8,120},{12,124},{16,0},{20,4},{24,8},{28,12},{32,... | collective-permute-start | bytes 24584 | tf_op jit(solution)/shard_map/ppermute | solution.py:32
  34.1 1.2 %own_attention.1 = (f32[8,448]{1,0:T(8,128)S(1)}, f32[8,448]{1,0:T(8,128)S(1)}, f32[8,448]{1,0:T(8,128)S(1)}) custom-call(f32[8,128]{1,0:T(8,128)S(1)} %get-tuple-element.106.refs_0_, bf16[8,512]{1,0:T(8,128)(2,1)S(1)} %get-tuple-element.120.refs_1_.refs_0_, bf16[8,448]{1,0:T(8,128)(2,1)S(1)} %get-tuple-element.111.refs_2_, ...), custom_call_target="tpu_custom_call" | custom-call | tf_op jit(solution)/shard_map/own_attention/pallas_call | solution.py:114
  35.3 0.0 collective-permute-done.10.refs_1_
  35.3 0.0 collective-permute-done.11.refs_2_
  35.3 0.0 collective-permute-done.12.refs_3_
  35.4 0.9 %prompt_attention.1 = (f32[8,640]{1,0:T(8,128)S(1)}, f32[8,640]{1,0:T(8,128)S(1)}, f32[8,640]{1,0:T(8,128)S(1)}, f32[8,640]{1,0:T(8,128)S(1)}) custom-call(bf16[8,512]{1,0:T(8,128)(2,1)S(1)} %get-tuple-element.120.refs_1_.refs_0_, bf16[8,512]{1,0:T(8,128)(2,1)S(1)} %collective-permute-done.10.refs_1_, bf16[8,512]{1,0:T(8,128)(2,1)S(1)} %collective-permute-done.11.refs_2_, ...), custom_call_target="tpu_custom_call" | custom-call | tf_op jit(solution)/shard_map/prompt_attention/pallas_call | solution.py:114
  36.3 2.6 %collective-permute-start.14 = (f32[8,640]{1,0:T(8,128)S(1)}, f32[8,640]{1,0:T(8,128)S(1)}, u32[]{:S(2)}, u32[]{:S(2)}) collective-permute-start(f32[8,640]{1,0:T(8,128)S(1)} %get-tuple-element.126), channel_id=1, source_target_pairs={{0,96},{4,100},{8,104},{12,108},{16,112},{20,116},{24,120},{28,124... | collective-permute-start | bytes 61448 | tf_op jit(solution)/shard_map/ppermute | solution.py:32
  39.0 0.6 %collective-permute-start.15 = (f32[8,640]{1,0:T(8,128)S(1)}, f32[8,640]{1,0:T(8,128)S(1)}, u32[]{:S(2)}, u32[]{:S(2)}) collective-permute-start(f32[8,640]{1,0:T(8,128)S(1)} %get-tuple-element.127), channel_id=1, source_target_pairs={{0,112},{4,116},{8,120},{12,124},{16,0},{20,4},{24,8},{28,12},{32,... | collective-permute-start | bytes 61448 | tf_op jit(solution)/shard_map/ppermute | solution.py:32
  39.5 0.9 %collective-permute-start.16 = (f32[8,640]{1,0:T(8,128)S(1)}, f32[8,640]{1,0:T(8,128)S(1)}, u32[]{:S(2)}, u32[]{:S(2)}) collective-permute-start(f32[8,640]{1,0:T(8,128)S(1)} %get-tuple-element.128), channel_id=1, source_target_pairs={{0,16},{4,20},{8,24},{12,28},{16,32},{20,36},{24,40},{28,44},{32,4... | collective-permute-start | bytes 61448 | tf_op jit(solution)/shard_map/ppermute | solution.py:32
  40.4 0.0 collective-permute-done.14.refs_4_
  40.4 1.5 %collective-permute-done.15.refs_5_ = f32[8,640]{1,0:T(8,128)S(1)} collective-permute-done((f32[8,640]{1,0:T(8,128)S(1)}, f32[8,640]{1,0:T(8,128)S(1)}, u32[]{:S(2)}, u32[]{:S(2)}) %collective-permute-start.15) | collective-permute-done | bytes 20512 | tf_op jit(solution)/shard_map/ppermute | solution.py:32
  41.9 1.5 %collective-permute-done.16.refs_6_ = f32[8,640]{1,0:T(8,128)S(1)} collective-permute-done((f32[8,640]{1,0:T(8,128)S(1)}, f32[8,640]{1,0:T(8,128)S(1)}, u32[]{:S(2)}, u32[]{:S(2)}) %collective-permute-start.16) | collective-permute-done | bytes 20512 | tf_op jit(solution)/shard_map/ppermute | solution.py:32
  43.4 0.5 %combine.1 = (bf16[8,448]{1,0:T(8,128)(2,1)S(1)}, bf16[8,448]{1,0:T(8,128)(2,1)S(1)}, bf16[8,448]{1,0:T(8,128)(2,1)S(1)}, bf16[8,448]{1,0:T(8,128)(2,1)S(1)}) custom-call(f32[8,448]{1,0:T(8,128)S(1)} %get-tuple-element.117.refs_0_, f32[8,448]{1,0:T(8,128)S(1)} %get-tuple-element.118.refs_1_, f32[8,448]{1,0:T(8,128)S(1)} %get-tuple-element.119.refs_2_, ...), custom_call_target="tpu_custom_call" | custom-call | tf_op jit(solution)/shard_map/combine/pallas_call | solution.py:114
  43.9 1.4 %collective-permute-start.17 = (bf16[8,448]{1,0:T(8,128)(2,1)S(1)}, bf16[8,448]{1,0:T(8,128)(2,1)S(1)}, u32[]{:S(2)}, u32[]{:S(2)}) collective-permute-start(bf16[8,448]{1,0:T(8,128)(2,1)S(1)} %get-tuple-element.130), channel_id=1, source_target_pairs={{0,2},{1,3},{2,0},{3,1},{4,6},{5,7},{6,4},{7,5},{8,10},{9,11},{10,... | collective-permute-start | bytes 21512 | tf_op jit(solution)/shard_map/ppermute | solution.py:28
  45.3 0.5 %collective-permute-start.18 = (bf16[8,448]{1,0:T(8,128)(2,1)S(1)}, bf16[8,448]{1,0:T(8,128)(2,1)S(1)}, u32[]{:S(2)}, u32[]{:S(2)}) collective-permute-start(bf16[8,448]{1,0:T(8,128)(2,1)S(1)} %get-tuple-element.131), channel_id=1, source_target_pairs={{0,1},{1,2},{2,3},{3,0},{4,5},{5,6},{6,7},{7,4},{8,9},{9,10},{10,1... | collective-permute-start | bytes 21512 | tf_op jit(solution)/shard_map/ppermute | solution.py:28
  45.9 2.1 %collective-permute-start.19 = (bf16[8,448]{1,0:T(8,128)(2,1)S(1)}, bf16[8,448]{1,0:T(8,128)(2,1)S(1)}, u32[]{:S(2)}, u32[]{:S(2)}) collective-permute-start(bf16[8,448]{1,0:T(8,128)(2,1)S(1)} %get-tuple-element.132), channel_id=1, source_target_pairs={{0,3},{1,0},{2,1},{3,2},{4,7},{5,4},{6,5},{7,6},{8,11},{9,8},{10,9... | collective-permute-start | bytes 21512 | tf_op jit(solution)/shard_map/ppermute | solution.py:28
  48.0 1.3 %collective-permute-done.18 = bf16[8,448]{1,0:T(8,128)(2,1)S(1)} collective-permute-done((bf16[8,448]{1,0:T(8,128)(2,1)S(1)}, bf16[8,448]{1,0:T(8,128)(2,1)S(1)}, u32[]{:S(2)}, u32[]{:S(2)}) %collective-permute-start.18) | collective-permute-done | bytes 7200 | tf_op jit(solution)/shard_map/ppermute | solution.py:28
  49.3 0.6 %fusion = bf16[1,8,448]{2,1,0:T(8,128)(2,1)} fusion(bf16[8,448]{1,0:T(8,128)(2,1)S(1)} %collective-permute-done.19, bf16[8,448]{1,0:T(8,128)(2,1)S(1)} %collective-permute-done.18, bf16[8,448]{1,0:T(8,128)(2,1)S(1)} %collective-permute-done.17, bf16[8,448]{1,0:T(8,128)(2,1)S(1)} %get-tuple-element.129, bf16[8,448]{1,0:T(8,128)(2,1)S(1)} %get-tuple-element.109, ...), kind=kLoop, calls=%fused_computation.2 | loop fusion | flops 39424 | bytes 43009 | tf_op jit(solution)/shard_map/broadcast_in_dim | solution.py:693
  (10 shorter events, 0.0 us)
Async XLA Ops:
  1.1 8.2 %collective-permute-start = (bf16[448,128]{1,0:T(8,128)(2,1)S(1)}, bf16[448,128]{1,0:T(8,128)(2,1)S(1)}, u32[]{:S(2)}, u32[]{:S(2)}) collective-permute-start(bf16[448,128]{1,0:T(8,128)(2,1)S(1)} %window_page.1), channel_id=1, source_target_pairs={{0,4},{4,8},{8,12},{12,0},{16,20},{20,24},{24,28},{28,16},{32,36},... | collective-permute-start | bytes 344072 | tf_op jit(solution)/shard_map/ppermute | solution.py:40
  3.2 10.0 %collective-permute-start.4 = (bf16[448,128]{1,0:T(8,128)(2,1)S(1)}, bf16[448,128]{1,0:T(8,128)(2,1)S(1)}, u32[]{:S(2)}, u32[]{:S(2)}) collective-permute-start(bf16[448,128]{1,0:T(8,128)(2,1)S(1)} %window_page.1), channel_id=1, source_target_pairs={{0,12},{4,0},{8,4},{12,8},{16,28},{20,16},{24,20},{28,24},{32,44},... | collective-permute-start | bytes 344072 | tf_op jit(solution)/shard_map/ppermute | solution.py:40
  4.5 8.6 %collective-permute-start.5 = (bf16[448,128]{1,0:T(8,128)(2,1)S(1)}, bf16[448,128]{1,0:T(8,128)(2,1)S(1)}, u32[]{:S(2)}, u32[]{:S(2)}) collective-permute-start(bf16[448,128]{1,0:T(8,128)(2,1)S(1)} %window_page.1), channel_id=1, source_target_pairs={{0,8},{4,12},{8,0},{12,4},{16,24},{20,28},{24,16},{28,20},{32,40},... | collective-permute-start | bytes 344072 | tf_op jit(solution)/shard_map/ppermute | solution.py:40
  6.2 6.3 %collective-permute-start.2 = (bf16[8,448]{1,0:T(8,128)(2,1)}, bf16[8,448]{1,0:T(8,128)(2,1)S(1)}, u32[]{:S(2)}, u32[]{:S(2)}) collective-permute-start(bf16[8,448]{1,0:T(8,128)(2,1)} %refs_0_.2), channel_id=1, source_target_pairs={{0,3},{1,0},{2,1},{3,2},{4,7},{5,4},{6,5},{7,6},{8,11},{9,8},{10,9... | collective-permute-start | bytes 21512 | tf_op jit(solution)/shard_map/ppermute | solution.py:28
  8.9 4.2 %collective-permute-start.3 = (bf16[8,448]{1,0:T(8,128)(2,1)}, bf16[8,448]{1,0:T(8,128)(2,1)S(1)}, u32[]{:S(2)}, u32[]{:S(2)}) collective-permute-start(bf16[8,448]{1,0:T(8,128)(2,1)} %refs_0_.2), channel_id=1, source_target_pairs={{0,2},{1,3},{2,0},{3,1},{4,6},{5,7},{6,4},{7,5},{8,10},{9,11},{10,... | collective-permute-start | bytes 21512 | tf_op jit(solution)/shard_map/ppermute | solution.py:28
  9.3 12.9 %copy-start.1 = (bf16[8,448]{1,0:T(8,128)(2,1)S(1)}, bf16[8,448]{1,0:T(8,128)(2,1)}, u32[]{:S(2)}) copy-start(bf16[8,448]{1,0:T(8,128)(2,1)} %refs_0_.2) | copy-start | bytes 21508
  9.3 3.9 %collective-permute-start.1 = (bf16[8,448]{1,0:T(8,128)(2,1)}, bf16[8,448]{1,0:T(8,128)(2,1)S(1)}, u32[]{:S(2)}, u32[]{:S(2)}) collective-permute-start(bf16[8,448]{1,0:T(8,128)(2,1)} %refs_0_.2), channel_id=1, source_target_pairs={{0,1},{1,2},{2,3},{3,0},{4,5},{5,6},{6,7},{7,4},{8,9},{9,10},{10,1... | collective-permute-start | bytes 21512 | tf_op jit(solution)/shard_map/ppermute | solution.py:28
  13.3 12.9 %copy-start.2 = (s32[8,256]{1,0:T(8,128)S(1)}, s32[8,256]{1,0:T(8,128)}, u32[]{:S(2)}) copy-start(s32[8,256]{1,0:T(8,128)} %refs_0_.3) | copy-start | bytes 24580
  13.3 12.9 %copy-start.3 = (s32[8]{0:T(128)S(1)}, s32[8]{0:T(128)}, u32[]{:S(2)}) copy-start(s32[8]{0:T(128)} %refs_1_.1) | copy-start | bytes 100
  13.3 22.1 %collective-permute-start.13 = (bf16[4,448,128]{2,1,0:T(8,128)(2,1)S(1)}, bf16[4,448,128]{2,1,0:T(8,128)(2,1)S(1)}, u32[]{:S(2)}, u32[]{:S(2)}) collective-permute-start(bf16[4,448,128]{2,1,0:T(8,128)(2,1)S(1)} %pad_maximum_fusion.refs_4_), channel_id=1, source_target_pairs={{128,192},{132,196},{136,200},{140,204},{144,208},{148,212},{152,2... | collective-permute-start | bytes 1376264 | tf_op jit(solution)/shard_map/ppermute | solution.py:49
  22.2 7.0 %collective-permute-start.6 = (bf16[8,1792]{1,0:T(8,128)(2,1)S(1)}, bf16[8,1792]{1,0:T(8,128)(2,1)S(1)}, u32[]{:S(2)}, u32[]{:S(2)}) collective-permute-start(bf16[8,1792]{1,0:T(8,128)(2,1)S(1)} %linear_layer.1.refs_7_), channel_id=1, source_target_pairs={{0,130},{1,131},{2,128},{3,129},{130,0},{131,1},{128,2},{129,3},{4... | collective-permute-start | bytes 86024 | tf_op jit(solution)/shard_map/ppermute | solution.py:59
  22.3 6.9 %collective-permute-start.7 = (bf16[8,1792]{1,0:T(8,128)(2,1)S(1)}, bf16[8,1792]{1,0:T(8,128)(2,1)S(1)}, u32[]{:S(2)}, u32[]{:S(2)}) collective-permute-start(bf16[8,1792]{1,0:T(8,128)(2,1)S(1)} %linear_layer.1.refs_7_), channel_id=1, source_target_pairs={{0,129},{1,130},{2,131},{3,128},{129,0},{130,1},{131,2},{128,3},{4... | collective-permute-start | bytes 86024 | tf_op jit(solution)/shard_map/ppermute | solution.py:59
  25.8 3.4 %collective-permute-start.8 = (bf16[8,1792]{1,0:T(8,128)(2,1)S(1)}, bf16[8,1792]{1,0:T(8,128)(2,1)S(1)}, u32[]{:S(2)}, u32[]{:S(2)}) collective-permute-start(bf16[8,1792]{1,0:T(8,128)(2,1)S(1)} %linear_layer.1.refs_7_), channel_id=1, source_target_pairs={{0,131},{1,128},{2,129},{3,130},{131,0},{128,1},{129,2},{130,3},{4... | collective-permute-start | bytes 86024 | tf_op jit(solution)/shard_map/ppermute | solution.py:59
  25.8 3.4 %collective-permute-start.9 = (bf16[8,1792]{1,0:T(8,128)(2,1)S(1)}, bf16[8,1792]{1,0:T(8,128)(2,1)S(1)}, u32[]{:S(2)}, u32[]{:S(2)}) collective-permute-start(bf16[8,1792]{1,0:T(8,128)(2,1)S(1)} %linear_layer.1.refs_7_), channel_id=1, source_target_pairs={{0,128},{1,129},{2,130},{3,131},{128,0},{129,1},{130,2},{131,3},{4... | collective-permute-start | bytes 86024 | tf_op jit(solution)/shard_map/ppermute | solution.py:59
  30.2 5.1 %collective-permute-start.10 = (bf16[8,512]{1,0:T(8,128)(2,1)S(1)}, bf16[8,512]{1,0:T(8,128)(2,1)S(1)}, u32[]{:S(2)}, u32[]{:S(2)}) collective-permute-start(bf16[8,512]{1,0:T(8,128)(2,1)S(1)} %get-tuple-element.120.refs_1_.refs_0_), channel_id=1, source_target_pairs={{0,32},{4,36},{8,40},{12,44},{16,48},{20,52},{24,56},{28,60},{32,6... | collective-permute-start | bytes 24584 | tf_op jit(solution)/shard_map/ppermute | solution.py:32
  31.4 3.9 %collective-permute-start.11 = (bf16[8,512]{1,0:T(8,128)(2,1)S(1)}, bf16[8,512]{1,0:T(8,128)(2,1)S(1)}, u32[]{:S(2)}, u32[]{:S(2)}) collective-permute-start(bf16[8,512]{1,0:T(8,128)(2,1)S(1)} %get-tuple-element.120.refs_1_.refs_0_), channel_id=1, source_target_pairs={{0,16},{4,20},{8,24},{12,28},{16,32},{20,36},{24,40},{28,44},{32,4... | collective-permute-start | bytes 24584 | tf_op jit(solution)/shard_map/ppermute | solution.py:32
  32.2 3.1 %collective-permute-start.12 = (bf16[8,512]{1,0:T(8,128)(2,1)S(1)}, bf16[8,512]{1,0:T(8,128)(2,1)S(1)}, u32[]{:S(2)}, u32[]{:S(2)}) collective-permute-start(bf16[8,512]{1,0:T(8,128)(2,1)S(1)} %get-tuple-element.120.refs_1_.refs_0_), channel_id=1, source_target_pairs={{0,112},{4,116},{8,120},{12,124},{16,0},{20,4},{24,8},{28,12},{32,... | collective-permute-start | bytes 24584 | tf_op jit(solution)/shard_map/ppermute | solution.py:32
  34.1 9.3 %copy-start = (bf16[1,448,1792]{2,1,0:T(8,128)(2,1)S(1)}, bf16[1,448,1792]{2,1,0:T(8,128)(2,1)}, u32[]{:S(2)}) copy-start(bf16[1,448,1792]{2,1,0:T(8,128)(2,1)} %refs_8_.1) | copy-start | bytes 4816900
  36.3 4.1 %collective-permute-start.14 = (f32[8,640]{1,0:T(8,128)S(1)}, f32[8,640]{1,0:T(8,128)S(1)}, u32[]{:S(2)}, u32[]{:S(2)}) collective-permute-start(f32[8,640]{1,0:T(8,128)S(1)} %get-tuple-element.126), channel_id=1, source_target_pairs={{0,96},{4,100},{8,104},{12,108},{16,112},{20,116},{24,120},{28,124... | collective-permute-start | bytes 61448 | tf_op jit(solution)/shard_map/ppermute | solution.py:32
  39.0 3.0 %collective-permute-start.15 = (f32[8,640]{1,0:T(8,128)S(1)}, f32[8,640]{1,0:T(8,128)S(1)}, u32[]{:S(2)}, u32[]{:S(2)}) collective-permute-start(f32[8,640]{1,0:T(8,128)S(1)} %get-tuple-element.127), channel_id=1, source_target_pairs={{0,112},{4,116},{8,120},{12,124},{16,0},{20,4},{24,8},{28,12},{32,... | collective-permute-start | bytes 61448 | tf_op jit(solution)/shard_map/ppermute | solution.py:32
  39.5 3.8 %collective-permute-start.16 = (f32[8,640]{1,0:T(8,128)S(1)}, f32[8,640]{1,0:T(8,128)S(1)}, u32[]{:S(2)}, u32[]{:S(2)}) collective-permute-start(f32[8,640]{1,0:T(8,128)S(1)} %get-tuple-element.128), channel_id=1, source_target_pairs={{0,16},{4,20},{8,24},{12,28},{16,32},{20,36},{24,40},{28,44},{32,4... | collective-permute-start | bytes 61448 | tf_op jit(solution)/shard_map/ppermute | solution.py:32
  43.9 4.1 %collective-permute-start.17 = (bf16[8,448]{1,0:T(8,128)(2,1)S(1)}, bf16[8,448]{1,0:T(8,128)(2,1)S(1)}, u32[]{:S(2)}, u32[]{:S(2)}) collective-permute-start(bf16[8,448]{1,0:T(8,128)(2,1)S(1)} %get-tuple-element.130), channel_id=1, source_target_pairs={{0,2},{1,3},{2,0},{3,1},{4,6},{5,7},{6,4},{7,5},{8,10},{9,11},{10,... | collective-permute-start | bytes 21512 | tf_op jit(solution)/shard_map/ppermute | solution.py:28
  45.3 4.0 %collective-permute-start.18 = (bf16[8,448]{1,0:T(8,128)(2,1)S(1)}, bf16[8,448]{1,0:T(8,128)(2,1)S(1)}, u32[]{:S(2)}, u32[]{:S(2)}) collective-permute-start(bf16[8,448]{1,0:T(8,128)(2,1)S(1)} %get-tuple-element.131), channel_id=1, source_target_pairs={{0,1},{1,2},{2,3},{3,0},{4,5},{5,6},{6,7},{7,4},{8,9},{9,10},{10,1... | collective-permute-start | bytes 21512 | tf_op jit(solution)/shard_map/ppermute | solution.py:28
  45.9 3.5 %collective-permute-start.19 = (bf16[8,448]{1,0:T(8,128)(2,1)S(1)}, bf16[8,448]{1,0:T(8,128)(2,1)S(1)}, u32[]{:S(2)}, u32[]{:S(2)}) collective-permute-start(bf16[8,448]{1,0:T(8,128)(2,1)S(1)} %get-tuple-element.132), channel_id=1, source_target_pairs={{0,3},{1,0},{2,1},{3,2},{4,7},{5,4},{6,5},{7,6},{8,11},{9,8},{10,9... | collective-permute-start | bytes 21512 | tf_op jit(solution)/shard_map/ppermute | solution.py:28

commit v15 on v14

--- a/solution.py
+++ b/solution.py
@@ -570,14 +570,22 @@
     rows = tags.shape[0]
     total = own_hbm.shape[0]
     copies = []
+    spans = []
     for r in range(rows):
-        for slot, logical in enumerate(window_pages(lengths, r)):
+        first, last = window_pages(lengths, r)
+        spans.append(first != last)
+        for slot, logical in enumerate((first, last)):
             page = jnp.clip(table[r, logical] - GROUPS - ids[1] * total, 0, total - 1)
             copies.append(
                 pltpu.make_async_copy(own_hbm.at[page], own_near.at[r, slot], sems.at[r, slot])
             )
-    for copy in copies:
-        copy.start()
+        copies[2 * r].start()
+        pl.when(spans[r])(copies[2 * r + 1].start)
+
+        @pl.when(jnp.logical_not(spans[r]))
+        def _():
+            own_near[r, 1] = jnp.zeros(own_near.shape[2:], own_near.dtype)
+
     row = lax.broadcasted_iota(jnp.int32, tags.shape, 0)
     lane = lanes_of(tags.shape)
     marks = jnp.zeros(tags.shape, jnp.int32)
@@ -589,8 +597,9 @@
         for at, mark in enumerate((table[r, 0], start, length, first * PAGE, second)):
             marks = jnp.where((row == r) & (lane == at), mark, marks)
     tags[...] = marks.astype(jnp.float32)
-    for copy in copies:
-        copy.wait()
+    for r in range(rows):
+        copies[2 * r].wait()
+        pl.when(spans[r])(copies[2 * r + 1].wait)
 
 
 def bring_windows(table, lengths, own_pages):

time: 50.2 us -> 50.2 us (level)
  transfers between devices with their start and end apart: 20 -> 20, of which waited for: 5 -> 6; matrix products, arithmetic and copies ran while one was open for 0% -> 0% of each run, Pallas kernels for 15% -> 15%
where the time goes in v15:
time: 50.2 us; the launch traced here: 50 us
  starting transfers between devices  33.9 us (68%)
  Pallas kernels  9.98 us (20%)
  waiting for transfers between devices  5.26 us (10%)
  other arithmetic  0.67 us (1%)
    pallas_call x8, Pallas kernels, kernel_call(): pl.pallas_call(run, out_shape=out_shape, in_specs=in_specs, out_specs=jax...  9.98 us
    ppermute x1, starting transfers between devices, far_swap(): lax.ppermute(value, ('section', 'req'), [(count + i, count + (i + count /...  8.82 us
    ppermute x6, starting transfers between devices, z_shift(): lax.ppermute(value, 'req', [(z * XN + i, (z + steps) % ZN * XN + i) for z...  8.08 us
    ppermute x6, starting transfers between devices, head_shift(): lax.ppermute(value, 'head', [(i, (i + steps) % count) for i in range(coun...  7.92 us
    ppermute x3, starting transfers between devices, x_shift(): lax.ppermute(value, 'req', [(z * XN + i, z * XN + (i + steps) % XN) for z...  5.12 us
    ppermute x4, starting transfers between devices, section_swap(): lax.ppermute(value, ('section', 'head'), there + [(b, a) for a, b in there])  4.01 us
    ppermute x6, waiting for transfers between devices, z_shift(): lax.ppermute(value, 'req', [(z * XN + i, (z + steps) % ZN * XN + i) for z...  2.98 us
    ppermute x6, waiting for transfers between devices, head_shift(): lax.ppermute(value, 'head', [(i, (i + steps) % count) for i in range(coun...  2.09 us
  transfers between devices with their start and end apart: 20, of which 6 were waited for; matrix products, arithmetic and copies ran while one was open for 0% of the time, Pallas kernels for 15%

profile of v15, /device:TPU:1, one launch (start us, length us, event | category | flops | bytes accessed | tf_op | source)
XLA Modules:
  0.0 50.0 jit_solution(5419699181301696489)
XLA Ops:
  0.0 1.0 %window_page.1 = bf16[448,128]{1,0:T(8,128)(2,1)S(1)} custom-call(bf16[1,2,448,128]{3,2,1,0:T(8,128)(2,1)} %bitcast.18), custom_call_target="tpu_custom_call" | custom-call | bytes 16777216 | tf_op jit(solution)/shard_map/window_page/pallas_call | solution.py:114
  1.1 2.1 %collective-permute-start = (bf16[448,128]{1,0:T(8,128)(2,1)S(1)}, bf16[448,128]{1,0:T(8,128)(2,1)S(1)}, u32[]{:S(2)}, u32[]{:S(2)}) collective-permute-start(bf16[448,128]{1,0:T(8,128)(2,1)S(1)} %window_page.1), channel_id=1, source_target_pairs={{0,4},{4,8},{8,12},{12,0},{16,20},{20,24},{24,28},{28,16},{32,36},... | collective-permute-start | bytes 344072 | tf_op jit(solution)/shard_map/ppermute | solution.py:40
  3.2 1.4 %collective-permute-start.4 = (bf16[448,128]{1,0:T(8,128)(2,1)S(1)}, bf16[448,128]{1,0:T(8,128)(2,1)S(1)}, u32[]{:S(2)}, u32[]{:S(2)}) collective-permute-start(bf16[448,128]{1,0:T(8,128)(2,1)S(1)} %window_page.1), channel_id=1, source_target_pairs={{0,12},{4,0},{8,4},{12,8},{16,28},{20,16},{24,20},{28,24},{32,44},... | collective-permute-start | bytes 344072 | tf_op jit(solution)/shard_map/ppermute | solution.py:40
  4.5 1.6 %collective-permute-start.5 = (bf16[448,128]{1,0:T(8,128)(2,1)S(1)}, bf16[448,128]{1,0:T(8,128)(2,1)S(1)}, u32[]{:S(2)}, u32[]{:S(2)}) collective-permute-start(bf16[448,128]{1,0:T(8,128)(2,1)S(1)} %window_page.1), channel_id=1, source_target_pairs={{0,8},{4,12},{8,0},{12,4},{16,24},{20,28},{24,16},{28,20},{32,40},... | collective-permute-start | bytes 344072 | tf_op jit(solution)/shard_map/ppermute | solution.py:40
  6.2 2.7 %collective-permute-start.2 = (bf16[8,448]{1,0:T(8,128)(2,1)}, bf16[8,448]{1,0:T(8,128)(2,1)S(1)}, u32[]{:S(2)}, u32[]{:S(2)}) collective-permute-start(bf16[8,448]{1,0:T(8,128)(2,1)} %refs_0_.2), channel_id=1, source_target_pairs={{0,3},{1,0},{2,1},{3,2},{4,7},{5,4},{6,5},{7,6},{8,11},{9,8},{10,9... | collective-permute-start | bytes 21512 | tf_op jit(solution)/shard_map/ppermute | solution.py:28
  8.9 0.3 collective-permute-start.3
  9.3 0.0 collective-permute-done
  9.3 0.7 %collective-permute-start.1 = (bf16[8,448]{1,0:T(8,128)(2,1)}, bf16[8,448]{1,0:T(8,128)(2,1)S(1)}, u32[]{:S(2)}, u32[]{:S(2)}) collective-permute-start(bf16[8,448]{1,0:T(8,128)(2,1)} %refs_0_.2), channel_id=1, source_target_pairs={{0,1},{1,2},{2,3},{3,0},{4,5},{5,6},{6,7},{7,4},{8,9},{9,10},{10,1... | collective-permute-start | bytes 21512 | tf_op jit(solution)/shard_map/ppermute | solution.py:28
  10.0 2.5 %bring_near.1 = (bf16[8,2,448]{2,1,0:T(2,128)(2,1)S(1)}, f32[3,448]{1,0:T(4,128)S(1)}, bf16[1792,128]{1,0:T(8,128)(2,1)S(1)}, f32[1,1792]{1,0:T(1,128)S(1)}, f32...) custom-call(bf16[8,2,448]{2,1,0:T(2,128)(2,1)} %refs_0_.1, ...), custom_call_target="tpu_custom_call" | custom-call | bytes 14588672 | tf_op jit(solution)/shard_map/bring_near/pallas_call | solution.py:114
  12.4 0.0 collective-permute-done.2.refs_2_
  12.4 0.7 %collective-permute-done.3.refs_3_ = bf16[8,448]{1,0:T(8,128)(2,1)S(1)} collective-permute-done((bf16[8,448]{1,0:T(8,128)(2,1)}, bf16[8,448]{1,0:T(8,128)(2,1)S(1)}, u32[]{:S(2)}, u32[]{:S(2)}) %collective-permute-start.3) | collective-permute-done | bytes 7200 | tf_op jit(solution)/shard_map/ppermute | solution.py:28
  13.1 0.0 collective-permute-done.4
  13.1 0.0 collective-permute-done.5
  13.1 0.1 collective-permute-done.1.refs_1_
  13.2 0.1 pad_maximum_fusion.refs_4_
  13.3 0.0 copy-start.2
  13.3 0.0 copy-start.3
  13.3 8.8 %collective-permute-start.13 = (bf16[4,448,128]{2,1,0:T(8,128)(2,1)S(1)}, bf16[4,448,128]{2,1,0:T(8,128)(2,1)S(1)}, u32[]{:S(2)}, u32[]{:S(2)}) collective-permute-start(bf16[4,448,128]{2,1,0:T(8,128)(2,1)S(1)} %pad_maximum_fusion.refs_4_), channel_id=1, source_target_pairs={{128,192},{132,196},{136,200},{140,204},{144,208},{148,212},{152,2... | collective-permute-start | bytes 1376264 | tf_op jit(solution)/shard_map/ppermute | solution.py:49
  22.2 0.1 collective-permute-start.6
  22.3 3.6 %collective-permute-start.7 = (bf16[8,1792]{1,0:T(8,128)(2,1)S(1)}, bf16[8,1792]{1,0:T(8,128)(2,1)S(1)}, u32[]{:S(2)}, u32[]{:S(2)}) collective-permute-start(bf16[8,1792]{1,0:T(8,128)(2,1)S(1)} %linear_layer.1.refs_7_), channel_id=1, source_target_pairs={{0,129},{1,130},{2,131},{3,128},{129,0},{130,1},{131,2},{128,3},{4... | collective-permute-start | bytes 86024 | tf_op jit(solution)/shard_map/ppermute | solution.py:59
  25.8 0.0 collective-permute-start.8
  25.8 0.3 collective-permute-start.9
  26.2 2.7 %bring_windows.1 = (bf16[8,2,2,448,128]{4,3,2,1,0:T(8,128)(2,1)S(1)}, f32[8,128]{1,0:T(8,128)S(1)}) custom-call(s32[8,256]{1,0:T(8,128)S(1)} %copy-done.2, s32[8]{0:T(128)S(1)} %copy-done.3, bf16[16,2,448,128]{3,2,1,0:T(8,128)(2,1)} %bitcast.15), custom_call_target="tpu_custom_call" | custom-call | bytes 7340032 | tf_op jit(solution)/shard_map/bring_windows/pallas_call | solution.py:114
  28.9 0.0 collective-permute-done.6.refs_1_
  29.0 0.0 collective-permute-done.7.refs_2_
  29.0 0.2 collective-permute-done.8.refs_3_
  29.1 0.0 collective-permute-done.9.refs_4_
  29.1 1.0 %project.1 = (bf16[8,448]{1,0:T(8,128)(2,1)S(1)}, bf16[8,512]{1,0:T(8,128)(2,1)S(1)}, bf16[8,448]{1,0:T(8,128)(2,1)S(1)}, bf16[8,448]{1,0:T(8,128)(2,1)S(1)}) custom-call(f32[8,128]{1,0:T(8,128)S(1)} %get-tuple-element.106.refs_0_, bf16[8,1792]{1,0:T(8,128)(2,1)S(1)} %collective-permute-done.6.refs_1_, bf16[8,1792]{1,0:T(8,128)(2,1)S(1)} %collective-permute-done.7.refs_2_, ...), custom_call_target="tpu_custom_call" | custom-call | tf_op jit(solution)/shard_map/project/pallas_call | solution.py:114
  30.1 1.2 %collective-permute-start.10 = (bf16[8,512]{1,0:T(8,128)(2,1)S(1)}, bf16[8,512]{1,0:T(8,128)(2,1)S(1)}, u32[]{:S(2)}, u32[]{:S(2)}) collective-permute-start(bf16[8,512]{1,0:T(8,128)(2,1)S(1)} %get-tuple-element.120.refs_1_.refs_0_), channel_id=1, source_target_pairs={{0,32},{4,36},{8,40},{12,44},{16,48},{20,52},{24,56},{28,60},{32,6... | collective-permute-start | bytes 24584 | tf_op jit(solution)/shard_map/ppermute | solution.py:32
  31.4 0.7 %collective-permute-start.11 = (bf16[8,512]{1,0:T(8,128)(2,1)S(1)}, bf16[8,512]{1,0:T(8,128)(2,1)S(1)}, u32[]{:S(2)}, u32[]{:S(2)}) collective-permute-start(bf16[8,512]{1,0:T(8,128)(2,1)S(1)} %get-tuple-element.120.refs_1_.refs_0_), channel_id=1, source_target_pairs={{0,16},{4,20},{8,24},{12,28},{16,32},{20,36},{24,40},{28,44},{32,4... | collective-permute-start | bytes 24584 | tf_op jit(solution)/shard_map/ppermute | solution.py:32
  32.1 1.9 %collective-permute-start.12 = (bf16[8,512]{1,0:T(8,128)(2,1)S(1)}, bf16[8,512]{1,0:T(8,128)(2,1)S(1)}, u32[]{:S(2)}, u32[]{:S(2)}) collective-permute-start(bf16[8,512]{1,0:T(8,128)(2,1)S(1)} %get-tuple-element.120.refs_1_.refs_0_), channel_id=1, source_target_pairs={{0,112},{4,116},{8,120},{12,124},{16,0},{20,4},{24,8},{28,12},{32,... | collective-permute-start | bytes 24584 | tf_op jit(solution)/shard_map/ppermute | solution.py:32
  34.0 1.2 %own_attention.1 = (f32[8,448]{1,0:T(8,128)S(1)}, f32[8,448]{1,0:T(8,128)S(1)}, f32[8,448]{1,0:T(8,128)S(1)}) custom-call(f32[8,128]{1,0:T(8,128)S(1)} %get-tuple-element.106.refs_0_, bf16[8,512]{1,0:T(8,128)(2,1)S(1)} %get-tuple-element.120.refs_1_.refs_0_, bf16[8,448]{1,0:T(8,128)(2,1)S(1)} %get-tuple-element.111.refs_2_, ...), custom_call_target="tpu_custom_call" | custom-call | tf_op jit(solution)/shard_map/own_attention/pallas_call | solution.py:114
  35.2 0.0 collective-permute-done.11.refs_2_
  35.3 0.0 collective-permute-done.12.refs_3_
  35.3 0.9 %prompt_attention.1 = (f32[8,640]{1,0:T(8,128)S(1)}, f32[8,640]{1,0:T(8,128)S(1)}, f32[8,640]{1,0:T(8,128)S(1)}, f32[8,640]{1,0:T(8,128)S(1)}) custom-call(bf16[8,512]{1,0:T(8,128)(2,1)S(1)} %get-tuple-element.120.refs_1_.refs_0_, bf16[8,512]{1,0:T(8,128)(2,1)S(1)} %collective-permute-done.10.refs_1_, bf16[8,512]{1,0:T(8,128)(2,1)S(1)} %collective-permute-done.11.refs_2_, ...), custom_call_target="tpu_custom_call" | custom-call | tf_op jit(solution)/shard_map/prompt_attention/pallas_call | solution.py:114
  36.2 2.7 %collective-permute-start.14 = (f32[8,640]{1,0:T(8,128)S(1)}, f32[8,640]{1,0:T(8,128)S(1)}, u32[]{:S(2)}, u32[]{:S(2)}) collective-permute-start(f32[8,640]{1,0:T(8,128)S(1)} %get-tuple-element.126), channel_id=1, source_target_pairs={{0,96},{4,100},{8,104},{12,108},{16,112},{20,116},{24,120},{28,124... | collective-permute-start | bytes 61448 | tf_op jit(solution)/shard_map/ppermute | solution.py:32
  39.0 0.6 %collective-permute-start.15 = (f32[8,640]{1,0:T(8,128)S(1)}, f32[8,640]{1,0:T(8,128)S(1)}, u32[]{:S(2)}, u32[]{:S(2)}) collective-permute-start(f32[8,640]{1,0:T(8,128)S(1)} %get-tuple-element.127), channel_id=1, source_target_pairs={{0,112},{4,116},{8,120},{12,124},{16,0},{20,4},{24,8},{28,12},{32,... | collective-permute-start | bytes 61448 | tf_op jit(solution)/shard_map/ppermute | solution.py:32
  39.6 0.9 %collective-permute-start.16 = (f32[8,640]{1,0:T(8,128)S(1)}, f32[8,640]{1,0:T(8,128)S(1)}, u32[]{:S(2)}, u32[]{:S(2)}) collective-permute-start(f32[8,640]{1,0:T(8,128)S(1)} %get-tuple-element.128), channel_id=1, source_target_pairs={{0,16},{4,20},{8,24},{12,28},{16,32},{20,36},{24,40},{28,44},{32,4... | collective-permute-start | bytes 61448 | tf_op jit(solution)/shard_map/ppermute | solution.py:32
  40.4 1.5 %collective-permute-done.15.refs_5_ = f32[8,640]{1,0:T(8,128)S(1)} collective-permute-done((f32[8,640]{1,0:T(8,128)S(1)}, f32[8,640]{1,0:T(8,128)S(1)}, u32[]{:S(2)}, u32[]{:S(2)}) %collective-permute-start.15) | collective-permute-done | bytes 20512 | tf_op jit(solution)/shard_map/ppermute | solution.py:32
  41.9 1.5 %collective-permute-done.16.refs_6_ = f32[8,640]{1,0:T(8,128)S(1)} collective-permute-done((f32[8,640]{1,0:T(8,128)S(1)}, f32[8,640]{1,0:T(8,128)S(1)}, u32[]{:S(2)}, u32[]{:S(2)}) %collective-permute-start.16) | collective-permute-done | bytes 20512 | tf_op jit(solution)/shard_map/ppermute | solution.py:32
  43.4 0.5 %combine.1 = (bf16[8,448]{1,0:T(8,128)(2,1)S(1)}, bf16[8,448]{1,0:T(8,128)(2,1)S(1)}, bf16[8,448]{1,0:T(8,128)(2,1)S(1)}, bf16[8,448]{1,0:T(8,128)(2,1)S(1)}) custom-call(f32[8,448]{1,0:T(8,128)S(1)} %get-tuple-element.117.refs_0_, f32[8,448]{1,0:T(8,128)S(1)} %get-tuple-element.118.refs_1_, f32[8,448]{1,0:T(8,128)S(1)} %get-tuple-element.119.refs_2_, ...), custom_call_target="tpu_custom_call" | custom-call | tf_op jit(solution)/shard_map/combine/pallas_call | solution.py:114
  43.9 1.5 %collective-permute-start.17 = (bf16[8,448]{1,0:T(8,128)(2,1)S(1)}, bf16[8,448]{1,0:T(8,128)(2,1)S(1)}, u32[]{:S(2)}, u32[]{:S(2)}) collective-permute-start(bf16[8,448]{1,0:T(8,128)(2,1)S(1)} %get-tuple-element.130), channel_id=1, source_target_pairs={{0,2},{1,3},{2,0},{3,1},{4,6},{5,7},{6,4},{7,5},{8,10},{9,11},{10,... | collective-permute-start | bytes 21512 | tf_op jit(solution)/shard_map/ppermute | solution.py:28
  45.4 0.4 collective-permute-start.18
  45.9 2.2 %collective-permute-start.19 = (bf16[8,448]{1,0:T(8,128)(2,1)S(1)}, bf16[8,448]{1,0:T(8,128)(2,1)S(1)}, u32[]{:S(2)}, u32[]{:S(2)}) collective-permute-start(bf16[8,448]{1,0:T(8,128)(2,1)S(1)} %get-tuple-element.132), channel_id=1, source_target_pairs={{0,3},{1,0},{2,1},{3,2},{4,7},{5,4},{6,5},{7,6},{8,11},{9,8},{10,9... | collective-permute-start | bytes 21512 | tf_op jit(solution)/shard_map/ppermute | solution.py:28
  48.1 0.0 collective-permute-done.17
  48.1 1.3 %collective-permute-done.18 = bf16[8,448]{1,0:T(8,128)(2,1)S(1)} collective-permute-done((bf16[8,448]{1,0:T(8,128)(2,1)S(1)}, bf16[8,448]{1,0:T(8,128)(2,1)S(1)}, u32[]{:S(2)}, u32[]{:S(2)}) %collective-permute-start.18) | collective-permute-done | bytes 7200 | tf_op jit(solution)/shard_map/ppermute | solution.py:28
  49.4 0.0 collective-permute-done.19
  49.4 0.6 %fusion = bf16[1,8,448]{2,1,0:T(8,128)(2,1)} fusion(bf16[8,448]{1,0:T(8,128)(2,1)S(1)} %collective-permute-done.19, bf16[8,448]{1,0:T(8,128)(2,1)S(1)} %collective-permute-done.18, bf16[8,448]{1,0:T(8,128)(2,1)S(1)} %collective-permute-done.17, bf16[8,448]{1,0:T(8,128)(2,1)S(1)} %get-tuple-element.129, bf16[8,448]{1,0:T(8,128)(2,1)S(1)} %get-tuple-element.109, ...), kind=kLoop, calls=%fused_computation.2 | loop fusion | flops 39424 | bytes 43009 | tf_op jit(solution)/shard_map/broadcast_in_dim | solution.py:702
  (10 shorter events, 0.0 us)
Async XLA Ops:
  1.1 8.2 %collective-permute-start = (bf16[448,128]{1,0:T(8,128)(2,1)S(1)}, bf16[448,128]{1,0:T(8,128)(2,1)S(1)}, u32[]{:S(2)}, u32[]{:S(2)}) collective-permute-start(bf16[448,128]{1,0:T(8,128)(2,1)S(1)} %window_page.1), channel_id=1, source_target_pairs={{0,4},{4,8},{8,12},{12,0},{16,20},{20,24},{24,28},{28,16},{32,36},... | collective-permute-start | bytes 344072 | tf_op jit(solution)/shard_map/ppermute | solution.py:40
  3.2 10.0 %collective-permute-start.4 = (bf16[448,128]{1,0:T(8,128)(2,1)S(1)}, bf16[448,128]{1,0:T(8,128)(2,1)S(1)}, u32[]{:S(2)}, u32[]{:S(2)}) collective-permute-start(bf16[448,128]{1,0:T(8,128)(2,1)S(1)} %window_page.1), channel_id=1, source_target_pairs={{0,12},{4,0},{8,4},{12,8},{16,28},{20,16},{24,20},{28,24},{32,44},... | collective-permute-start | bytes 344072 | tf_op jit(solution)/shard_map/ppermute | solution.py:40
  4.5 8.6 %collective-permute-start.5 = (bf16[448,128]{1,0:T(8,128)(2,1)S(1)}, bf16[448,128]{1,0:T(8,128)(2,1)S(1)}, u32[]{:S(2)}, u32[]{:S(2)}) collective-permute-start(bf16[448,128]{1,0:T(8,128)(2,1)S(1)} %window_page.1), channel_id=1, source_target_pairs={{0,8},{4,12},{8,0},{12,4},{16,24},{20,28},{24,16},{28,20},{32,40},... | collective-permute-start | bytes 344072 | tf_op jit(solution)/shard_map/ppermute | solution.py:40
  6.2 6.3 %collective-permute-start.2 = (bf16[8,448]{1,0:T(8,128)(2,1)}, bf16[8,448]{1,0:T(8,128)(2,1)S(1)}, u32[]{:S(2)}, u32[]{:S(2)}) collective-permute-start(bf16[8,448]{1,0:T(8,128)(2,1)} %refs_0_.2), channel_id=1, source_target_pairs={{0,3},{1,0},{2,1},{3,2},{4,7},{5,4},{6,5},{7,6},{8,11},{9,8},{10,9... | collective-permute-start | bytes 21512 | tf_op jit(solution)/shard_map/ppermute | solution.py:28
  8.9 4.2 %collective-permute-start.3 = (bf16[8,448]{1,0:T(8,128)(2,1)}, bf16[8,448]{1,0:T(8,128)(2,1)S(1)}, u32[]{:S(2)}, u32[]{:S(2)}) collective-permute-start(bf16[8,448]{1,0:T(8,128)(2,1)} %refs_0_.2), channel_id=1, source_target_pairs={{0,2},{1,3},{2,0},{3,1},{4,6},{5,7},{6,4},{7,5},{8,10},{9,11},{10,... | collective-permute-start | bytes 21512 | tf_op jit(solution)/shard_map/ppermute | solution.py:28
  9.3 12.9 %copy-start.1 = (bf16[8,448]{1,0:T(8,128)(2,1)S(1)}, bf16[8,448]{1,0:T(8,128)(2,1)}, u32[]{:S(2)}) copy-start(bf16[8,448]{1,0:T(8,128)(2,1)} %refs_0_.2) | copy-start | bytes 21508
  9.3 3.9 %collective-permute-start.1 = (bf16[8,448]{1,0:T(8,128)(2,1)}, bf16[8,448]{1,0:T(8,128)(2,1)S(1)}, u32[]{:S(2)}, u32[]{:S(2)}) collective-permute-start(bf16[8,448]{1,0:T(8,128)(2,1)} %refs_0_.2), channel_id=1, source_target_pairs={{0,1},{1,2},{2,3},{3,0},{4,5},{5,6},{6,7},{7,4},{8,9},{9,10},{10,1... | collective-permute-start | bytes 21512 | tf_op jit(solution)/shard_map/ppermute | solution.py:28
  13.3 12.9 %copy-start.2 = (s32[8,256]{1,0:T(8,128)S(1)}, s32[8,256]{1,0:T(8,128)}, u32[]{:S(2)}) copy-start(s32[8,256]{1,0:T(8,128)} %refs_0_.3) | copy-start | bytes 24580
  13.3 12.9 %copy-start.3 = (s32[8]{0:T(128)S(1)}, s32[8]{0:T(128)}, u32[]{:S(2)}) copy-start(s32[8]{0:T(128)} %refs_1_.1) | copy-start | bytes 100
  13.3 22.0 %collective-permute-start.13 = (bf16[4,448,128]{2,1,0:T(8,128)(2,1)S(1)}, bf16[4,448,128]{2,1,0:T(8,128)(2,1)S(1)}, u32[]{:S(2)}, u32[]{:S(2)}) collective-permute-start(bf16[4,448,128]{2,1,0:T(8,128)(2,1)S(1)} %pad_maximum_fusion.refs_4_), channel_id=1, source_target_pairs={{128,192},{132,196},{136,200},{140,204},{144,208},{148,212},{152,2... | collective-permute-start | bytes 1376264 | tf_op jit(solution)/shard_map/ppermute | solution.py:49
  22.2 6.8 %collective-permute-start.6 = (bf16[8,1792]{1,0:T(8,128)(2,1)S(1)}, bf16[8,1792]{1,0:T(8,128)(2,1)S(1)}, u32[]{:S(2)}, u32[]{:S(2)}) collective-permute-start(bf16[8,1792]{1,0:T(8,128)(2,1)S(1)} %linear_layer.1.refs_7_), channel_id=1, source_target_pairs={{0,130},{1,131},{2,128},{3,129},{130,0},{131,1},{128,2},{129,3},{4... | collective-permute-start | bytes 86024 | tf_op jit(solution)/shard_map/ppermute | solution.py:59
  22.3 6.7 %collective-permute-start.7 = (bf16[8,1792]{1,0:T(8,128)(2,1)S(1)}, bf16[8,1792]{1,0:T(8,128)(2,1)S(1)}, u32[]{:S(2)}, u32[]{:S(2)}) collective-permute-start(bf16[8,1792]{1,0:T(8,128)(2,1)S(1)} %linear_layer.1.refs_7_), channel_id=1, source_target_pairs={{0,129},{1,130},{2,131},{3,128},{129,0},{130,1},{131,2},{128,3},{4... | collective-permute-start | bytes 86024 | tf_op jit(solution)/shard_map/ppermute | solution.py:59
  25.8 3.3 %collective-permute-start.8 = (bf16[8,1792]{1,0:T(8,128)(2,1)S(1)}, bf16[8,1792]{1,0:T(8,128)(2,1)S(1)}, u32[]{:S(2)}, u32[]{:S(2)}) collective-permute-start(bf16[8,1792]{1,0:T(8,128)(2,1)S(1)} %linear_layer.1.refs_7_), channel_id=1, source_target_pairs={{0,131},{1,128},{2,129},{3,130},{131,0},{128,1},{129,2},{130,3},{4... | collective-permute-start | bytes 86024 | tf_op jit(solution)/shard_map/ppermute | solution.py:59
  25.8 3.3 %collective-permute-start.9 = (bf16[8,1792]{1,0:T(8,128)(2,1)S(1)}, bf16[8,1792]{1,0:T(8,128)(2,1)S(1)}, u32[]{:S(2)}, u32[]{:S(2)}) collective-permute-start(bf16[8,1792]{1,0:T(8,128)(2,1)S(1)} %linear_layer.1.refs_7_), channel_id=1, source_target_pairs={{0,128},{1,129},{2,130},{3,131},{128,0},{129,1},{130,2},{131,3},{4... | collective-permute-start | bytes 86024 | tf_op jit(solution)/shard_map/ppermute | solution.py:59
  30.1 5.1 %collective-permute-start.10 = (bf16[8,512]{1,0:T(8,128)(2,1)S(1)}, bf16[8,512]{1,0:T(8,128)(2,1)S(1)}, u32[]{:S(2)}, u32[]{:S(2)}) collective-permute-start(bf16[8,512]{1,0:T(8,128)(2,1)S(1)} %get-tuple-element.120.refs_1_.refs_0_), channel_id=1, source_target_pairs={{0,32},{4,36},{8,40},{12,44},{16,48},{20,52},{24,56},{28,60},{32,6... | collective-permute-start | bytes 24584 | tf_op jit(solution)/shard_map/ppermute | solution.py:32
  31.4 3.9 %collective-permute-start.11 = (bf16[8,512]{1,0:T(8,128)(2,1)S(1)}, bf16[8,512]{1,0:T(8,128)(2,1)S(1)}, u32[]{:S(2)}, u32[]{:S(2)}) collective-permute-start(bf16[8,512]{1,0:T(8,128)(2,1)S(1)} %get-tuple-element.120.refs_1_.refs_0_), channel_id=1, source_target_pairs={{0,16},{4,20},{8,24},{12,28},{16,32},{20,36},{24,40},{28,44},{32,4... | collective-permute-start | bytes 24584 | tf_op jit(solution)/shard_map/ppermute | solution.py:32
  32.1 3.2 %collective-permute-start.12 = (bf16[8,512]{1,0:T(8,128)(2,1)S(1)}, bf16[8,512]{1,0:T(8,128)(2,1)S(1)}, u32[]{:S(2)}, u32[]{:S(2)}) collective-permute-start(bf16[8,512]{1,0:T(8,128)(2,1)S(1)} %get-tuple-element.120.refs_1_.refs_0_), channel_id=1, source_target_pairs={{0,112},{4,116},{8,120},{12,124},{16,0},{20,4},{24,8},{28,12},{32,... | collective-permute-start | bytes 24584 | tf_op jit(solution)/shard_map/ppermute | solution.py:32
  34.0 9.4 %copy-start = (bf16[1,448,1792]{2,1,0:T(8,128)(2,1)S(1)}, bf16[1,448,1792]{2,1,0:T(8,128)(2,1)}, u32[]{:S(2)}) copy-start(bf16[1,448,1792]{2,1,0:T(8,128)(2,1)} %refs_8_.1) | copy-start | bytes 4816900
  36.2 4.2 %collective-permute-start.14 = (f32[8,640]{1,0:T(8,128)S(1)}, f32[8,640]{1,0:T(8,128)S(1)}, u32[]{:S(2)}, u32[]{:S(2)}) collective-permute-start(f32[8,640]{1,0:T(8,128)S(1)} %get-tuple-element.126), channel_id=1, source_target_pairs={{0,96},{4,100},{8,104},{12,108},{16,112},{20,116},{24,120},{28,124... | collective-permute-start | bytes 61448 | tf_op jit(solution)/shard_map/ppermute | solution.py:32
  39.0 3.0 %collective-permute-start.15 = (f32[8,640]{1,0:T(8,128)S(1)}, f32[8,640]{1,0:T(8,128)S(1)}, u32[]{:S(2)}, u32[]{:S(2)}) collective-permute-start(f32[8,640]{1,0:T(8,128)S(1)} %get-tuple-element.127), channel_id=1, source_target_pairs={{0,112},{4,116},{8,120},{12,124},{16,0},{20,4},{24,8},{28,12},{32,... | collective-permute-start | bytes 61448 | tf_op jit(solution)/shard_map/ppermute | solution.py:32
  39.6 3.8 %collective-permute-start.16 = (f32[8,640]{1,0:T(8,128)S(1)}, f32[8,640]{1,0:T(8,128)S(1)}, u32[]{:S(2)}, u32[]{:S(2)}) collective-permute-start(f32[8,640]{1,0:T(8,128)S(1)} %get-tuple-element.128), channel_id=1, source_target_pairs={{0,16},{4,20},{8,24},{12,28},{16,32},{20,36},{24,40},{28,44},{32,4... | collective-permute-start | bytes 61448 | tf_op jit(solution)/shard_map/ppermute | solution.py:32
  43.9 4.2 %collective-permute-start.17 = (bf16[8,448]{1,0:T(8,128)(2,1)S(1)}, bf16[8,448]{1,0:T(8,128)(2,1)S(1)}, u32[]{:S(2)}, u32[]{:S(2)}) collective-permute-start(bf16[8,448]{1,0:T(8,128)(2,1)S(1)} %get-tuple-element.130), channel_id=1, source_target_pairs={{0,2},{1,3},{2,0},{3,1},{4,6},{5,7},{6,4},{7,5},{8,10},{9,11},{10,... | collective-permute-start | bytes 21512 | tf_op jit(solution)/shard_map/ppermute | solution.py:28
  45.4 4.0 %collective-permute-start.18 = (bf16[8,448]{1,0:T(8,128)(2,1)S(1)}, bf16[8,448]{1,0:T(8,128)(2,1)S(1)}, u32[]{:S(2)}, u32[]{:S(2)}) collective-permute-start(bf16[8,448]{1,0:T(8,128)(2,1)S(1)} %get-tuple-element.131), channel_id=1, source_target_pairs={{0,1},{1,2},{2,3},{3,0},{4,5},{5,6},{6,7},{7,4},{8,9},{9,10},{10,1... | collective-permute-start | bytes 21512 | tf_op jit(solution)/shard_map/ppermute | solution.py:28
  45.9 3.6 %collective-permute-start.19 = (bf16[8,448]{1,0:T(8,128)(2,1)S(1)}, bf16[8,448]{1,0:T(8,128)(2,1)S(1)}, u32[]{:S(2)}, u32[]{:S(2)}) collective-permute-start(bf16[8,448]{1,0:T(8,128)(2,1)S(1)} %get-tuple-element.132), channel_id=1, source_target_pairs={{0,3},{1,0},{2,1},{3,2},{4,7},{5,4},{6,5},{7,6},{8,11},{9,8},{10,9... | collective-permute-start | bytes 21512 | tf_op jit(solution)/shard_map/ppermute | solution.py:28

commit v16 on v15

--- a/solution.py
+++ b/solution.py
@@ -674,7 +674,8 @@
     }
 
     page = window_page(pages_first)
-    row_pages = [x_shift(page, k) for k in (1, 3, 2)]
+    far_first = [x_shift(page, k) for k in (2, 1, 3)]
+    row_pages = [far_first[1], far_first[2], far_first[0]]
     row_pages[0], last_tokens, stored = lax.optimization_barrier((row_pages[0], tokens, stored))
     received = [head_shift(last_tokens, 1), head_shift(tokens, 3), head_shift(tokens, 2)]
     near, received, row_pages = lax.optimization_barrier((bring_near(stored), received, row_pages))

time: 50.2 us -> 50.5 us (level)
  no operation moved by 1% of the time
where the time goes in v16:
time: 50.5 us; the launch traced here: 50.2 us
  starting transfers between devices  34.3 us (68%)
  Pallas kernels  9.91 us (20%)
  waiting for transfers between devices  5.17 us (10%)
  other arithmetic  0.67 us (1%)
    pallas_call x8, Pallas kernels, kernel_call(): pl.pallas_call(run, out_shape=out_shape, in_specs=in_specs, out_specs=jax...  9.91 us
    ppermute x1, starting transfers between devices, far_swap(): lax.ppermute(value, ('section', 'req'), [(count + i, count + (i + count /...  8.82 us
    ppermute x6, starting transfers between devices, head_shift(): lax.ppermute(value, 'head', [(i, (i + steps) % count) for i in range(coun...  8.25 us
    ppermute x6, starting transfers between devices, z_shift(): lax.ppermute(value, 'req', [(z * XN + i, (z + steps) % ZN * XN + i) for z...  8.08 us
    ppermute x3, starting transfers between devices, x_shift(): lax.ppermute(value, 'req', [(z * XN + i, z * XN + (i + steps) % XN) for z...  5.12 us
    ppermute x4, starting transfers between devices, section_swap(): lax.ppermute(value, ('section', 'head'), there + [(b, a) for a, b in there])  4.01 us
    ppermute x6, waiting for transfers between devices, z_shift(): lax.ppermute(value, 'req', [(z * XN + i, (z + steps) % ZN * XN + i) for z...  2.98 us
    ppermute x6, waiting for transfers between devices, head_shift(): lax.ppermute(value, 'head', [(i, (i + steps) % count) for i in range(coun...  1.94 us
  transfers between devices with their start and end apart: 20, of which 6 were waited for; matrix products, arithmetic and copies ran while one was open for 0% of the time, Pallas kernels for 15%

profile of v16, /device:TPU:1, one launch (start us, length us, event | category | flops | bytes accessed | tf_op | source)
XLA Modules:
  0.0 50.2 jit_solution(5419699181301696489)
XLA Ops:
  0.0 1.0 %window_page.1 = bf16[448,128]{1,0:T(8,128)(2,1)S(1)} custom-call(bf16[1,2,448,128]{3,2,1,0:T(8,128)(2,1)} %bitcast.18), custom_call_target="tpu_custom_call" | custom-call | bytes 16777216 | tf_op jit(solution)/shard_map/window_page/pallas_call | solution.py:114
  1.1 2.1 %collective-permute-start = (bf16[448,128]{1,0:T(8,128)(2,1)S(1)}, bf16[448,128]{1,0:T(8,128)(2,1)S(1)}, u32[]{:S(2)}, u32[]{:S(2)}) collective-permute-start(bf16[448,128]{1,0:T(8,128)(2,1)S(1)} %window_page.1), channel_id=1, source_target_pairs={{0,4},{4,8},{8,12},{12,0},{16,20},{20,24},{24,28},{28,16},{32,36},... | collective-permute-start | bytes 344072 | tf_op jit(solution)/shard_map/ppermute | solution.py:40
  3.2 1.4 %collective-permute-start.4 = (bf16[448,128]{1,0:T(8,128)(2,1)S(1)}, bf16[448,128]{1,0:T(8,128)(2,1)S(1)}, u32[]{:S(2)}, u32[]{:S(2)}) collective-permute-start(bf16[448,128]{1,0:T(8,128)(2,1)S(1)} %window_page.1), channel_id=1, source_target_pairs={{0,12},{4,0},{8,4},{12,8},{16,28},{20,16},{24,20},{28,24},{32,44},... | collective-permute-start | bytes 344072 | tf_op jit(solution)/shard_map/ppermute | solution.py:40
  4.5 1.6 %collective-permute-start.5 = (bf16[448,128]{1,0:T(8,128)(2,1)S(1)}, bf16[448,128]{1,0:T(8,128)(2,1)S(1)}, u32[]{:S(2)}, u32[]{:S(2)}) collective-permute-start(bf16[448,128]{1,0:T(8,128)(2,1)S(1)} %window_page.1), channel_id=1, source_target_pairs={{0,8},{4,12},{8,0},{12,4},{16,24},{20,28},{24,16},{28,20},{32,40},... | collective-permute-start | bytes 344072 | tf_op jit(solution)/shard_map/ppermute | solution.py:40
  6.2 2.7 %collective-permute-start.2 = (bf16[8,448]{1,0:T(8,128)(2,1)}, bf16[8,448]{1,0:T(8,128)(2,1)S(1)}, u32[]{:S(2)}, u32[]{:S(2)}) collective-permute-start(bf16[8,448]{1,0:T(8,128)(2,1)} %refs_0_.2), channel_id=1, source_target_pairs={{0,3},{1,0},{2,1},{3,2},{4,7},{5,4},{6,5},{7,6},{8,11},{9,8},{10,9... | collective-permute-start | bytes 21512 | tf_op jit(solution)/shard_map/ppermute | solution.py:28
  8.9 0.3 collective-permute-start.3
  9.3 0.0 collective-permute-done
  9.3 0.7 %collective-permute-start.1 = (bf16[8,448]{1,0:T(8,128)(2,1)}, bf16[8,448]{1,0:T(8,128)(2,1)S(1)}, u32[]{:S(2)}, u32[]{:S(2)}) collective-permute-start(bf16[8,448]{1,0:T(8,128)(2,1)} %refs_0_.2), channel_id=1, source_target_pairs={{0,1},{1,2},{2,3},{3,0},{4,5},{5,6},{6,7},{7,4},{8,9},{9,10},{10,1... | collective-permute-start | bytes 21512 | tf_op jit(solution)/shard_map/ppermute | solution.py:28
  10.0 2.5 %bring_near.1 = (bf16[8,2,448]{2,1,0:T(2,128)(2,1)S(1)}, f32[3,448]{1,0:T(4,128)S(1)}, bf16[1792,128]{1,0:T(8,128)(2,1)S(1)}, f32[1,1792]{1,0:T(1,128)S(1)}, f32...) custom-call(bf16[8,2,448]{2,1,0:T(2,128)(2,1)} %refs_0_.1, ...), custom_call_target="tpu_custom_call" | custom-call | bytes 14588672 | tf_op jit(solution)/shard_map/bring_near/pallas_call | solution.py:114
  12.4 0.0 collective-permute-done.2.refs_2_
  12.4 0.7 %collective-permute-done.3.refs_3_ = bf16[8,448]{1,0:T(8,128)(2,1)S(1)} collective-permute-done((bf16[8,448]{1,0:T(8,128)(2,1)}, bf16[8,448]{1,0:T(8,128)(2,1)S(1)}, u32[]{:S(2)}, u32[]{:S(2)}) %collective-permute-start.3) | collective-permute-done | bytes 7200 | tf_op jit(solution)/shard_map/ppermute | solution.py:28
  13.1 0.0 collective-permute-done.4
  13.1 0.0 collective-permute-done.5
  13.1 0.1 collective-permute-done.1.refs_1_
  13.2 0.1 pad_maximum_fusion.refs_4_
  13.3 0.0 copy-start.2
  13.3 0.0 copy-start.3
  13.3 8.8 %collective-permute-start.13 = (bf16[4,448,128]{2,1,0:T(8,128)(2,1)S(1)}, bf16[4,448,128]{2,1,0:T(8,128)(2,1)S(1)}, u32[]{:S(2)}, u32[]{:S(2)}) collective-permute-start(bf16[4,448,128]{2,1,0:T(8,128)(2,1)S(1)} %pad_maximum_fusion.refs_4_), channel_id=1, source_target_pairs={{128,192},{132,196},{136,200},{140,204},{144,208},{148,212},{152,2... | collective-permute-start | bytes 1376264 | tf_op jit(solution)/shard_map/ppermute | solution.py:49
  22.2 0.1 collective-permute-start.6
  22.3 3.6 %collective-permute-start.7 = (bf16[8,1792]{1,0:T(8,128)(2,1)S(1)}, bf16[8,1792]{1,0:T(8,128)(2,1)S(1)}, u32[]{:S(2)}, u32[]{:S(2)}) collective-permute-start(bf16[8,1792]{1,0:T(8,128)(2,1)S(1)} %linear_layer.1.refs_7_), channel_id=1, source_target_pairs={{0,129},{1,130},{2,131},{3,128},{129,0},{130,1},{131,2},{128,3},{4... | collective-permute-start | bytes 86024 | tf_op jit(solution)/shard_map/ppermute | solution.py:59
  25.8 0.0 collective-permute-start.8
  25.8 0.3 collective-permute-start.9
  26.2 2.7 %bring_windows.1 = (bf16[8,2,2,448,128]{4,3,2,1,0:T(8,128)(2,1)S(1)}, f32[8,128]{1,0:T(8,128)S(1)}) custom-call(s32[8,256]{1,0:T(8,128)S(1)} %copy-done.2, s32[8]{0:T(128)S(1)} %copy-done.3, bf16[16,2,448,128]{3,2,1,0:T(8,128)(2,1)} %bitcast.15), custom_call_target="tpu_custom_call" | custom-call | bytes 7340032 | tf_op jit(solution)/shard_map/bring_windows/pallas_call | solution.py:114
  28.9 0.0 collective-permute-done.7.refs_2_
  28.9 0.2 collective-permute-done.8.refs_3_
  29.1 1.0 %project.1 = (bf16[8,448]{1,0:T(8,128)(2,1)S(1)}, bf16[8,512]{1,0:T(8,128)(2,1)S(1)}, bf16[8,448]{1,0:T(8,128)(2,1)S(1)}, bf16[8,448]{1,0:T(8,128)(2,1)S(1)}) custom-call(f32[8,128]{1,0:T(8,128)S(1)} %get-tuple-element.106.refs_0_, bf16[8,1792]{1,0:T(8,128)(2,1)S(1)} %collective-permute-done.6.refs_1_, bf16[8,1792]{1,0:T(8,128)(2,1)S(1)} %collective-permute-done.7.refs_2_, ...), custom_call_target="tpu_custom_call" | custom-call | tf_op jit(solution)/shard_map/project/pallas_call | solution.py:114
  30.1 1.2 %collective-permute-start.10 = (bf16[8,512]{1,0:T(8,128)(2,1)S(1)}, bf16[8,512]{1,0:T(8,128)(2,1)S(1)}, u32[]{:S(2)}, u32[]{:S(2)}) collective-permute-start(bf16[8,512]{1,0:T(8,128)(2,1)S(1)} %get-tuple-element.120.refs_1_.refs_0_), channel_id=1, source_target_pairs={{0,32},{4,36},{8,40},{12,44},{16,48},{20,52},{24,56},{28,60},{32,6... | collective-permute-start | bytes 24584 | tf_op jit(solution)/shard_map/ppermute | solution.py:32
  31.4 0.7 %collective-permute-start.11 = (bf16[8,512]{1,0:T(8,128)(2,1)S(1)}, bf16[8,512]{1,0:T(8,128)(2,1)S(1)}, u32[]{:S(2)}, u32[]{:S(2)}) collective-permute-start(bf16[8,512]{1,0:T(8,128)(2,1)S(1)} %get-tuple-element.120.refs_1_.refs_0_), channel_id=1, source_target_pairs={{0,16},{4,20},{8,24},{12,28},{16,32},{20,36},{24,40},{28,44},{32,4... | collective-permute-start | bytes 24584 | tf_op jit(solution)/shard_map/ppermute | solution.py:32
  32.1 1.9 %collective-permute-start.12 = (bf16[8,512]{1,0:T(8,128)(2,1)S(1)}, bf16[8,512]{1,0:T(8,128)(2,1)S(1)}, u32[]{:S(2)}, u32[]{:S(2)}) collective-permute-start(bf16[8,512]{1,0:T(8,128)(2,1)S(1)} %get-tuple-element.120.refs_1_.refs_0_), channel_id=1, source_target_pairs={{0,112},{4,116},{8,120},{12,124},{16,0},{20,4},{24,8},{28,12},{32,... | collective-permute-start | bytes 24584 | tf_op jit(solution)/shard_map/ppermute | solution.py:32
  34.0 1.2 %own_attention.1 = (f32[8,448]{1,0:T(8,128)S(1)}, f32[8,448]{1,0:T(8,128)S(1)}, f32[8,448]{1,0:T(8,128)S(1)}) custom-call(f32[8,128]{1,0:T(8,128)S(1)} %get-tuple-element.106.refs_0_, bf16[8,512]{1,0:T(8,128)(2,1)S(1)} %get-tuple-element.120.refs_1_.refs_0_, bf16[8,448]{1,0:T(8,128)(2,1)S(1)} %get-tuple-element.111.refs_2_, ...), custom_call_target="tpu_custom_call" | custom-call | tf_op jit(solution)/shard_map/own_attention/pallas_call | solution.py:114
  35.2 0.0 collective-permute-done.10.refs_1_
  35.2 0.0 collective-permute-done.11.refs_2_
  35.3 0.0 collective-permute-done.13.refs_5_
  35.3 0.9 %prompt_attention.1 = (f32[8,640]{1,0:T(8,128)S(1)}, f32[8,640]{1,0:T(8,128)S(1)}, f32[8,640]{1,0:T(8,128)S(1)}, f32[8,640]{1,0:T(8,128)S(1)}) custom-call(bf16[8,512]{1,0:T(8,128)(2,1)S(1)} %get-tuple-element.120.refs_1_.refs_0_, bf16[8,512]{1,0:T(8,128)(2,1)S(1)} %collective-permute-done.10.refs_1_, bf16[8,512]{1,0:T(8,128)(2,1)S(1)} %collective-permute-done.11.refs_2_, ...), custom_call_target="tpu_custom_call" | custom-call | tf_op jit(solution)/shard_map/prompt_attention/pallas_call | solution.py:114
  36.2 2.7 %collective-permute-start.14 = (f32[8,640]{1,0:T(8,128)S(1)}, f32[8,640]{1,0:T(8,128)S(1)}, u32[]{:S(2)}, u32[]{:S(2)}) collective-permute-start(f32[8,640]{1,0:T(8,128)S(1)} %get-tuple-element.126), channel_id=1, source_target_pairs={{0,96},{4,100},{8,104},{12,108},{16,112},{20,116},{24,120},{28,124... | collective-permute-start | bytes 61448 | tf_op jit(solution)/shard_map/ppermute | solution.py:32
  39.0 0.6 %collective-permute-start.15 = (f32[8,640]{1,0:T(8,128)S(1)}, f32[8,640]{1,0:T(8,128)S(1)}, u32[]{:S(2)}, u32[]{:S(2)}) collective-permute-start(f32[8,640]{1,0:T(8,128)S(1)} %get-tuple-element.127), channel_id=1, source_target_pairs={{0,112},{4,116},{8,120},{12,124},{16,0},{20,4},{24,8},{28,12},{32,... | collective-permute-start | bytes 61448 | tf_op jit(solution)/shard_map/ppermute | solution.py:32
  39.6 0.9 %collective-permute-start.16 = (f32[8,640]{1,0:T(8,128)S(1)}, f32[8,640]{1,0:T(8,128)S(1)}, u32[]{:S(2)}, u32[]{:S(2)}) collective-permute-start(f32[8,640]{1,0:T(8,128)S(1)} %get-tuple-element.128), channel_id=1, source_target_pairs={{0,16},{4,20},{8,24},{12,28},{16,32},{20,36},{24,40},{28,44},{32,4... | collective-permute-start | bytes 61448 | tf_op jit(solution)/shard_map/ppermute | solution.py:32
  40.4 0.0 collective-permute-done.14.refs_4_
  40.4 1.5 %collective-permute-done.15.refs_5_ = f32[8,640]{1,0:T(8,128)S(1)} collective-permute-done((f32[8,640]{1,0:T(8,128)S(1)}, f32[8,640]{1,0:T(8,128)S(1)}, u32[]{:S(2)}, u32[]{:S(2)}) %collective-permute-start.15) | collective-permute-done | bytes 20512 | tf_op jit(solution)/shard_map/ppermute | solution.py:32
  41.9 1.5 %collective-permute-done.16.refs_6_ = f32[8,640]{1,0:T(8,128)S(1)} collective-permute-done((f32[8,640]{1,0:T(8,128)S(1)}, f32[8,640]{1,0:T(8,128)S(1)}, u32[]{:S(2)}, u32[]{:S(2)}) %collective-permute-start.16) | collective-permute-done | bytes 20512 | tf_op jit(solution)/shard_map/ppermute | solution.py:32
  43.4 0.5 %combine.1 = (bf16[8,448]{1,0:T(8,128)(2,1)S(1)}, bf16[8,448]{1,0:T(8,128)(2,1)S(1)}, bf16[8,448]{1,0:T(8,128)(2,1)S(1)}, bf16[8,448]{1,0:T(8,128)(2,1)S(1)}) custom-call(f32[8,448]{1,0:T(8,128)S(1)} %get-tuple-element.117.refs_0_, f32[8,448]{1,0:T(8,128)S(1)} %get-tuple-element.118.refs_1_, f32[8,448]{1,0:T(8,128)S(1)} %get-tuple-element.119.refs_2_, ...), custom_call_target="tpu_custom_call" | custom-call | tf_op jit(solution)/shard_map/combine/pallas_call | solution.py:114
  43.9 1.8 %collective-permute-start.17 = (bf16[8,448]{1,0:T(8,128)(2,1)S(1)}, bf16[8,448]{1,0:T(8,128)(2,1)S(1)}, u32[]{:S(2)}, u32[]{:S(2)}) collective-permute-start(bf16[8,448]{1,0:T(8,128)(2,1)S(1)} %get-tuple-element.130), channel_id=1, source_target_pairs={{0,2},{1,3},{2,0},{3,1},{4,6},{5,7},{6,4},{7,5},{8,10},{9,11},{10,... | collective-permute-start | bytes 21512 | tf_op jit(solution)/shard_map/ppermute | solution.py:28
  45.7 0.1 collective-permute-start.18
  45.9 2.6 %collective-permute-start.19 = (bf16[8,448]{1,0:T(8,128)(2,1)S(1)}, bf16[8,448]{1,0:T(8,128)(2,1)S(1)}, u32[]{:S(2)}, u32[]{:S(2)}) collective-permute-start(bf16[8,448]{1,0:T(8,128)(2,1)S(1)} %get-tuple-element.132), channel_id=1, source_target_pairs={{0,3},{1,0},{2,1},{3,2},{4,7},{5,4},{6,5},{7,6},{8,11},{9,8},{10,9... | collective-permute-start | bytes 21512 | tf_op jit(solution)/shard_map/ppermute | solution.py:28
  48.4 0.0 collective-permute-done.17
  48.4 1.2 %collective-permute-done.18 = bf16[8,448]{1,0:T(8,128)(2,1)S(1)} collective-permute-done((bf16[8,448]{1,0:T(8,128)(2,1)S(1)}, bf16[8,448]{1,0:T(8,128)(2,1)S(1)}, u32[]{:S(2)}, u32[]{:S(2)}) %collective-permute-start.18) | collective-permute-done | bytes 7200 | tf_op jit(solution)/shard_map/ppermute | solution.py:28
  49.6 0.0 collective-permute-done.19
  49.6 0.6 %fusion = bf16[1,8,448]{2,1,0:T(8,128)(2,1)} fusion(bf16[8,448]{1,0:T(8,128)(2,1)S(1)} %collective-permute-done.19, bf16[8,448]{1,0:T(8,128)(2,1)S(1)} %collective-permute-done.18, bf16[8,448]{1,0:T(8,128)(2,1)S(1)} %collective-permute-done.17, bf16[8,448]{1,0:T(8,128)(2,1)S(1)} %get-tuple-element.129, bf16[8,448]{1,0:T(8,128)(2,1)S(1)} %get-tuple-element.109, ...), kind=kLoop, calls=%fused_computation.2 | loop fusion | flops 39424 | bytes 43009 | tf_op jit(solution)/shard_map/broadcast_in_dim | solution.py:703
  (10 shorter events, 0.0 us)
Async XLA Ops:
  1.1 8.2 %collective-permute-start = (bf16[448,128]{1,0:T(8,128)(2,1)S(1)}, bf16[448,128]{1,0:T(8,128)(2,1)S(1)}, u32[]{:S(2)}, u32[]{:S(2)}) collective-permute-start(bf16[448,128]{1,0:T(8,128)(2,1)S(1)} %window_page.1), channel_id=1, source_target_pairs={{0,4},{4,8},{8,12},{12,0},{16,20},{20,24},{24,28},{28,16},{32,36},... | collective-permute-start | bytes 344072 | tf_op jit(solution)/shard_map/ppermute | solution.py:40
  3.2 10.0 %collective-permute-start.4 = (bf16[448,128]{1,0:T(8,128)(2,1)S(1)}, bf16[448,128]{1,0:T(8,128)(2,1)S(1)}, u32[]{:S(2)}, u32[]{:S(2)}) collective-permute-start(bf16[448,128]{1,0:T(8,128)(2,1)S(1)} %window_page.1), channel_id=1, source_target_pairs={{0,12},{4,0},{8,4},{12,8},{16,28},{20,16},{24,20},{28,24},{32,44},... | collective-permute-start | bytes 344072 | tf_op jit(solution)/shard_map/ppermute | solution.py:40
  4.5 8.6 %collective-permute-start.5 = (bf16[448,128]{1,0:T(8,128)(2,1)S(1)}, bf16[448,128]{1,0:T(8,128)(2,1)S(1)}, u32[]{:S(2)}, u32[]{:S(2)}) collective-permute-start(bf16[448,128]{1,0:T(8,128)(2,1)S(1)} %window_page.1), channel_id=1, source_target_pairs={{0,8},{4,12},{8,0},{12,4},{16,24},{20,28},{24,16},{28,20},{32,40},... | collective-permute-start | bytes 344072 | tf_op jit(solution)/shard_map/ppermute | solution.py:40
  6.2 6.3 %collective-permute-start.2 = (bf16[8,448]{1,0:T(8,128)(2,1)}, bf16[8,448]{1,0:T(8,128)(2,1)S(1)}, u32[]{:S(2)}, u32[]{:S(2)}) collective-permute-start(bf16[8,448]{1,0:T(8,128)(2,1)} %refs_0_.2), channel_id=1, source_target_pairs={{0,3},{1,0},{2,1},{3,2},{4,7},{5,4},{6,5},{7,6},{8,11},{9,8},{10,9... | collective-permute-start | bytes 21512 | tf_op jit(solution)/shard_map/ppermute | solution.py:28
  8.9 4.2 %collective-permute-start.3 = (bf16[8,448]{1,0:T(8,128)(2,1)}, bf16[8,448]{1,0:T(8,128)(2,1)S(1)}, u32[]{:S(2)}, u32[]{:S(2)}) collective-permute-start(bf16[8,448]{1,0:T(8,128)(2,1)} %refs_0_.2), channel_id=1, source_target_pairs={{0,2},{1,3},{2,0},{3,1},{4,6},{5,7},{6,4},{7,5},{8,10},{9,11},{10,... | collective-permute-start | bytes 21512 | tf_op jit(solution)/shard_map/ppermute | solution.py:28
  9.3 12.9 %copy-start.1 = (bf16[8,448]{1,0:T(8,128)(2,1)S(1)}, bf16[8,448]{1,0:T(8,128)(2,1)}, u32[]{:S(2)}) copy-start(bf16[8,448]{1,0:T(8,128)(2,1)} %refs_0_.2) | copy-start | bytes 21508
  9.3 3.9 %collective-permute-start.1 = (bf16[8,448]{1,0:T(8,128)(2,1)}, bf16[8,448]{1,0:T(8,128)(2,1)S(1)}, u32[]{:S(2)}, u32[]{:S(2)}) collective-permute-start(bf16[8,448]{1,0:T(8,128)(2,1)} %refs_0_.2), channel_id=1, source_target_pairs={{0,1},{1,2},{2,3},{3,0},{4,5},{5,6},{6,7},{7,4},{8,9},{9,10},{10,1... | collective-permute-start | bytes 21512 | tf_op jit(solution)/shard_map/ppermute | solution.py:28
  13.3 12.9 %copy-start.2 = (s32[8,256]{1,0:T(8,128)S(1)}, s32[8,256]{1,0:T(8,128)}, u32[]{:S(2)}) copy-start(s32[8,256]{1,0:T(8,128)} %refs_0_.3) | copy-start | bytes 24580
  13.3 12.9 %copy-start.3 = (s32[8]{0:T(128)S(1)}, s32[8]{0:T(128)}, u32[]{:S(2)}) copy-start(s32[8]{0:T(128)} %refs_1_.1) | copy-start | bytes 100
  13.3 22.0 %collective-permute-start.13 = (bf16[4,448,128]{2,1,0:T(8,128)(2,1)S(1)}, bf16[4,448,128]{2,1,0:T(8,128)(2,1)S(1)}, u32[]{:S(2)}, u32[]{:S(2)}) collective-permute-start(bf16[4,448,128]{2,1,0:T(8,128)(2,1)S(1)} %pad_maximum_fusion.refs_4_), channel_id=1, source_target_pairs={{128,192},{132,196},{136,200},{140,204},{144,208},{148,212},{152,2... | collective-permute-start | bytes 1376264 | tf_op jit(solution)/shard_map/ppermute | solution.py:49
  22.2 6.7 %collective-permute-start.6 = (bf16[8,1792]{1,0:T(8,128)(2,1)S(1)}, bf16[8,1792]{1,0:T(8,128)(2,1)S(1)}, u32[]{:S(2)}, u32[]{:S(2)}) collective-permute-start(bf16[8,1792]{1,0:T(8,128)(2,1)S(1)} %linear_layer.1.refs_7_), channel_id=1, source_target_pairs={{0,130},{1,131},{2,128},{3,129},{130,0},{131,1},{128,2},{129,3},{4... | collective-permute-start | bytes 86024 | tf_op jit(solution)/shard_map/ppermute | solution.py:59
  22.3 6.6 %collective-permute-start.7 = (bf16[8,1792]{1,0:T(8,128)(2,1)S(1)}, bf16[8,1792]{1,0:T(8,128)(2,1)S(1)}, u32[]{:S(2)}, u32[]{:S(2)}) collective-permute-start(bf16[8,1792]{1,0:T(8,128)(2,1)S(1)} %linear_layer.1.refs_7_), channel_id=1, source_target_pairs={{0,129},{1,130},{2,131},{3,128},{129,0},{130,1},{131,2},{128,3},{4... | collective-permute-start | bytes 86024 | tf_op jit(solution)/shard_map/ppermute | solution.py:59
  25.8 3.3 %collective-permute-start.8 = (bf16[8,1792]{1,0:T(8,128)(2,1)S(1)}, bf16[8,1792]{1,0:T(8,128)(2,1)S(1)}, u32[]{:S(2)}, u32[]{:S(2)}) collective-permute-start(bf16[8,1792]{1,0:T(8,128)(2,1)S(1)} %linear_layer.1.refs_7_), channel_id=1, source_target_pairs={{0,131},{1,128},{2,129},{3,130},{131,0},{128,1},{129,2},{130,3},{4... | collective-permute-start | bytes 86024 | tf_op jit(solution)/shard_map/ppermute | solution.py:59
  25.8 3.3 %collective-permute-start.9 = (bf16[8,1792]{1,0:T(8,128)(2,1)S(1)}, bf16[8,1792]{1,0:T(8,128)(2,1)S(1)}, u32[]{:S(2)}, u32[]{:S(2)}) collective-permute-start(bf16[8,1792]{1,0:T(8,128)(2,1)S(1)} %linear_layer.1.refs_7_), channel_id=1, source_target_pairs={{0,128},{1,129},{2,130},{3,131},{128,0},{129,1},{130,2},{131,3},{4... | collective-permute-start | bytes 86024 | tf_op jit(solution)/shard_map/ppermute | solution.py:59
  30.1 5.1 %collective-permute-start.10 = (bf16[8,512]{1,0:T(8,128)(2,1)S(1)}, bf16[8,512]{1,0:T(8,128)(2,1)S(1)}, u32[]{:S(2)}, u32[]{:S(2)}) collective-permute-start(bf16[8,512]{1,0:T(8,128)(2,1)S(1)} %get-tuple-element.120.refs_1_.refs_0_), channel_id=1, source_target_pairs={{0,32},{4,36},{8,40},{12,44},{16,48},{20,52},{24,56},{28,60},{32,6... | collective-permute-start | bytes 24584 | tf_op jit(solution)/shard_map/ppermute | solution.py:32
  31.4 3.9 %collective-permute-start.11 = (bf16[8,512]{1,0:T(8,128)(2,1)S(1)}, bf16[8,512]{1,0:T(8,128)(2,1)S(1)}, u32[]{:S(2)}, u32[]{:S(2)}) collective-permute-start(bf16[8,512]{1,0:T(8,128)(2,1)S(1)} %get-tuple-element.120.refs_1_.refs_0_), channel_id=1, source_target_pairs={{0,16},{4,20},{8,24},{12,28},{16,32},{20,36},{24,40},{28,44},{32,4... | collective-permute-start | bytes 24584 | tf_op jit(solution)/shard_map/ppermute | solution.py:32
  32.1 3.2 %collective-permute-start.12 = (bf16[8,512]{1,0:T(8,128)(2,1)S(1)}, bf16[8,512]{1,0:T(8,128)(2,1)S(1)}, u32[]{:S(2)}, u32[]{:S(2)}) collective-permute-start(bf16[8,512]{1,0:T(8,128)(2,1)S(1)} %get-tuple-element.120.refs_1_.refs_0_), channel_id=1, source_target_pairs={{0,112},{4,116},{8,120},{12,124},{16,0},{20,4},{24,8},{28,12},{32,... | collective-permute-start | bytes 24584 | tf_op jit(solution)/shard_map/ppermute | solution.py:32
  34.0 9.4 %copy-start = (bf16[1,448,1792]{2,1,0:T(8,128)(2,1)S(1)}, bf16[1,448,1792]{2,1,0:T(8,128)(2,1)}, u32[]{:S(2)}) copy-start(bf16[1,448,1792]{2,1,0:T(8,128)(2,1)} %refs_8_.1) | copy-start | bytes 4816900
  36.2 4.2 %collective-permute-start.14 = (f32[8,640]{1,0:T(8,128)S(1)}, f32[8,640]{1,0:T(8,128)S(1)}, u32[]{:S(2)}, u32[]{:S(2)}) collective-permute-start(f32[8,640]{1,0:T(8,128)S(1)} %get-tuple-element.126), channel_id=1, source_target_pairs={{0,96},{4,100},{8,104},{12,108},{16,112},{20,116},{24,120},{28,124... | collective-permute-start | bytes 61448 | tf_op jit(solution)/shard_map/ppermute | solution.py:32
  39.0 3.0 %collective-permute-start.15 = (f32[8,640]{1,0:T(8,128)S(1)}, f32[8,640]{1,0:T(8,128)S(1)}, u32[]{:S(2)}, u32[]{:S(2)}) collective-permute-start(f32[8,640]{1,0:T(8,128)S(1)} %get-tuple-element.127), channel_id=1, source_target_pairs={{0,112},{4,116},{8,120},{12,124},{16,0},{20,4},{24,8},{28,12},{32,... | collective-permute-start | bytes 61448 | tf_op jit(solution)/shard_map/ppermute | solution.py:32
  39.6 3.8 %collective-permute-start.16 = (f32[8,640]{1,0:T(8,128)S(1)}, f32[8,640]{1,0:T(8,128)S(1)}, u32[]{:S(2)}, u32[]{:S(2)}) collective-permute-start(f32[8,640]{1,0:T(8,128)S(1)} %get-tuple-element.128), channel_id=1, source_target_pairs={{0,16},{4,20},{8,24},{12,28},{16,32},{20,36},{24,40},{28,44},{32,4... | collective-permute-start | bytes 61448 | tf_op jit(solution)/shard_map/ppermute | solution.py:32
  43.9 4.5 %collective-permute-start.17 = (bf16[8,448]{1,0:T(8,128)(2,1)S(1)}, bf16[8,448]{1,0:T(8,128)(2,1)S(1)}, u32[]{:S(2)}, u32[]{:S(2)}) collective-permute-start(bf16[8,448]{1,0:T(8,128)(2,1)S(1)} %get-tuple-element.130), channel_id=1, source_target_pairs={{0,2},{1,3},{2,0},{3,1},{4,6},{5,7},{6,4},{7,5},{8,10},{9,11},{10,... | collective-permute-start | bytes 21512 | tf_op jit(solution)/shard_map/ppermute | solution.py:28
  45.7 3.8 %collective-permute-start.18 = (bf16[8,448]{1,0:T(8,128)(2,1)S(1)}, bf16[8,448]{1,0:T(8,128)(2,1)S(1)}, u32[]{:S(2)}, u32[]{:S(2)}) collective-permute-start(bf16[8,448]{1,0:T(8,128)(2,1)S(1)} %get-tuple-element.131), channel_id=1, source_target_pairs={{0,1},{1,2},{2,3},{3,0},{4,5},{5,6},{6,7},{7,4},{8,9},{9,10},{10,1... | collective-permute-start | bytes 21512 | tf_op jit(solution)/shard_map/ppermute | solution.py:28
  45.9 3.7 %collective-permute-start.19 = (bf16[8,448]{1,0:T(8,128)(2,1)S(1)}, bf16[8,448]{1,0:T(8,128)(2,1)S(1)}, u32[]{:S(2)}, u32[]{:S(2)}) collective-permute-start(bf16[8,448]{1,0:T(8,128)(2,1)S(1)} %get-tuple-element.132), channel_id=1, source_target_pairs={{0,3},{1,0},{2,1},{3,2},{4,7},{5,4},{6,5},{7,6},{8,11},{9,8},{10,9... | collective-permute-start | bytes 21512 | tf_op jit(solution)/shard_map/ppermute | solution.py:28
